TPU v7x, 512 devices: a whole 4x8x8 slice. The times are simulated.
512 devices in a mesh: tm: 32 (over y, x), blk: 16 (over z, core).
Axes of the slice: x: 4, y: 8, z: 8, core: 2. Of those that a mesh axis runs over, the one named last changes fastest.
Arguments:
- panel_strip: bfloat16 [32, 8192, 2304], P('tm', 'blk'), may hold values from -6 to 6
- pivot_inverses: bfloat16 [32, 2, 256, 256], P('tm'), may hold values from -0.0234375 to 0.0234375
- coupling: float32 [32, 256, 256], P('tm'), may hold values from -0.375 to 0.375
- pivot_nodes: int32 [3, 256], replicated, may hold values from 0 to 8191, as said below
Outputs:
- trailing: bfloat16 [32, 8192, 1792], P('tm', 'blk')
- reduced: float32 [32, 256, 256], P('tm')
Inputs may be any that keep to these rules, and one draw needn't show every extreme that they name: `pivot_nodes`: entry j of every row is a node of the range [(j // 16) * 512, (j // 16 + 1) * 512); all 768 entries differ.
All inputs are finite; a program needn't handle non-finite values.
Results may differ from a plain program's by a relative error of at most 0.0068.
Values may be sent and summed in bfloat16 or wider, within the bound.
No kernel may reach another device: no remote copies, remote signals or barrier semaphores. Data moves between devices by JAX's collectives and lax.ppermute only.
A program may use at most 128 MiB of HBM per device.

v0:
```python
import jax
import jax.numpy as jnp
from jax import lax
from jax.sharding import PartitionSpec as P


def passed_along(x, axis, by):
    count = lax.axis_size(axis)
    pairs = [(i, i + by) for i in range(count) if 0 <= i + by < count]
    return lax.ppermute(x, axis, pairs)


def matmul_high(left, right):
    return jnp.dot(left, right, precision=lax.Precision.HIGHEST, preferred_element_type=jnp.float32)


def body(panel_strip, pivot_inverses, coupling, pivot_nodes):
    strip_block = panel_strip[0]
    inverse_pair = pivot_inverses[0]
    coupling_here = coupling[0]
    panel_width = inverse_pair.shape[-1]
    rows_here = strip_block.shape[0]
    blk_count = lax.axis_size("blk")
    per_device = panel_width // blk_count
    my_index = lax.axis_index("blk")
    local_rows = (
        lax.dynamic_slice_in_dim(pivot_nodes, my_index * per_device, per_device, 1)
        - my_index * rows_here
    )
    picker = (
        local_rows[:, :, None] == lax.broadcasted_iota(jnp.int32, (3, per_device, rows_here), 2)
    ).astype(jnp.bfloat16)
    factor_one = jnp.dot(
        strip_block[:, :panel_width], inverse_pair[0], preferred_element_type=jnp.float32
    ).astype(jnp.bfloat16)
    picked_one = jnp.dot(
        picker[0], strip_block[:, panel_width:], preferred_element_type=jnp.float32
    ).astype(jnp.bfloat16)
    columns = factor_one
    updated = (
        strip_block[:, panel_width:].astype(jnp.float32)
        - jnp.dot(
            columns,
            lax.all_gather(picked_one, "blk", axis=0, tiled=True),
            preferred_element_type=jnp.float32,
        )
    ).astype(jnp.bfloat16)
    factor_two = jnp.dot(
        updated[:, :panel_width], inverse_pair[1], preferred_element_type=jnp.float32
    ).astype(jnp.bfloat16)
    picked_two = jnp.dot(
        picker[1], updated[:, panel_width:], preferred_element_type=jnp.float32
    ).astype(jnp.bfloat16)
    columns = factor_two
    trailing = (
        updated[:, panel_width:].astype(jnp.float32)
        - jnp.dot(
            columns,
            lax.all_gather(picked_two, "blk", axis=0, tiled=True),
            preferred_element_type=jnp.float32,
        )
    ).astype(jnp.bfloat16)
    edge_rows = jnp.dot(
        picker[2], trailing[:, :panel_width], preferred_element_type=jnp.float32
    ).astype(jnp.bfloat16)
    boundary_block = lax.all_gather(edge_rows, "blk", axis=0, tiled=True).astype(jnp.float32)
    position = lax.axis_index("tm")

    def advance(turn_index, current):
        incoming = passed_along(current, "tm", 1)

        def apply_map(operand):
            return (
                matmul_high(matmul_high(coupling_here, operand), coupling_here.T) + boundary_block
            )

        def keep_state(operand):
            return current

        return lax.cond(position == turn_index, apply_map, keep_state, incoming)

    reduced = lax.fori_loop(1, lax.axis_size("tm"), advance, boundary_block)
    return (trailing[None], reduced[None])


def solution(mesh):
    placed = (P("tm", "blk", None), P("tm", None, None, None), P("tm", None, None), P())
    return jax.shard_map(
        body,
        mesh=mesh,
        in_specs=placed,
        out_specs=(P("tm", "blk", None), P("tm", None, None)),
        check_vma=False,
    )
```

profile of v0, /device:TPU:32, one launch (start us, length us, event | category | flops | bytes accessed | tf_op | source)
XLA Modules:
  0.0 484.5 jit_solution(10073837723274590851)
XLA Ops:
  8.1 2.6 convolution_convert_fusion.1
  10.7 46.4 %all-gather.2.cloned.1.call-done = bf16[256,2048]{1,0:T(8,128)(2,1)} async-done(((bf16[16,2048]{1,0:T(8,128)(2,1)}), bf16[256,2048]{1,0:T(8,128)(2,1)}) %all-gather.2.cloned.1.call-update) | async-done | bytes 1048592 | tf_op jit(solution)/shard_map/all_gather | solution.py:44
  57.1 2.8 subtract_convert_fusion
  60.3 18.0 %all_gather.10 = bf16[256,1792]{1,0:T(8,128)(2,1)S(1)} all-gather(bf16[16,1792]{1,0:T(8,128)(2,1)S(1)} %convolution_convert_fusion), channel_id=1, replica_groups=mesh['tm'=32,'blk'=16] {'blk'}, dimensions={0}, use_global_device_ids=true | all-gather | bytes 974848 | tf_op jit(solution)/shard_map/all_gather | solution.py:59
  78.3 3.0 subtract_convert_fusion.1
  82.4 15.1 %all_gather.11 = bf16[256,256]{1,0:T(8,128)(2,1)S(1)} all-gather(bf16[16,256]{1,0:T(8,128)(2,1)S(1)} %convolution_convert_fusion.4), channel_id=1, replica_groups=mesh['tm'=32,'blk'=16] {'blk'}, dimensions={0}, use_global_device_ids=true | all-gather | bytes 139264 | tf_op jit(solution)/shard_map/all_gather | solution.py:66
  97.6 379.3 %while.16 = (s32[]{:T(128)}, f32[256,256]{1,0:T(8,128)S(1)}, s32[]{:T(128)}, f32[256,256]{1,0:T(8,128)S(1)}, f32[256,256]{1,0:T(8,128)S(1)}, /*index=5*/s32[]{:T(128)}) while((s32[]{:T(128)}, f32[256,256]{1,0:T(8,128)S(1)}, s32[]{:T(128)}, f32[256,256]{1,0:T(8,128)S(1)}, f32[256,256]{1,0:T(8,128)S(1)}, /*index=5*/s32[]{:T(128)}) %tuple.51), condition=%wide.region_3.0_spmd, body=%wide.region_0.0_spmd.sunk | while | flops 402718720 | bytes 2883739 | solution.py:82
  97.6 3.4 collective-permute-start
  101.0 10.4 %collective-permute-done = f32[256,256]{1,0:T(8,128)S(1)} collective-permute-done((f32[256,256]{1,0:T(8,128)S(1)}, f32[256,256]{1,0:T(8,128)S(1)}, u32[]{:S(2)}, u32[]{:S(2)}) %collective-permute-start) | collective-permute-done | bytes 262176 | tf_op jit(solution)/shard_map/while/body/eval_jaxpr/ppermute | solution.py:10
  111.4 1.9 collective-permute-start
  113.3 11.0 %collective-permute-done = f32[256,256]{1,0:T(8,128)S(1)} collective-permute-done((f32[256,256]{1,0:T(8,128)S(1)}, f32[256,256]{1,0:T(8,128)S(1)}, u32[]{:S(2)}, u32[]{:S(2)}) %collective-permute-start) | collective-permute-done | bytes 262176 | tf_op jit(solution)/shard_map/while/body/eval_jaxpr/ppermute | solution.py:10
  124.3 1.9 collective-permute-start
  126.3 10.1 %collective-permute-done = f32[256,256]{1,0:T(8,128)S(1)} collective-permute-done((f32[256,256]{1,0:T(8,128)S(1)}, f32[256,256]{1,0:T(8,128)S(1)}, u32[]{:S(2)}, u32[]{:S(2)}) %collective-permute-start) | collective-permute-done | bytes 262176 | tf_op jit(solution)/shard_map/while/body/eval_jaxpr/ppermute | solution.py:10
  136.4 1.9 collective-permute-start
  138.3 9.7 %collective-permute-done = f32[256,256]{1,0:T(8,128)S(1)} collective-permute-done((f32[256,256]{1,0:T(8,128)S(1)}, f32[256,256]{1,0:T(8,128)S(1)}, u32[]{:S(2)}, u32[]{:S(2)}) %collective-permute-start) | collective-permute-done | bytes 262176 | tf_op jit(solution)/shard_map/while/body/eval_jaxpr/ppermute | solution.py:10
  147.9 1.9 collective-permute-start
  149.9 9.7 %collective-permute-done = f32[256,256]{1,0:T(8,128)S(1)} collective-permute-done((f32[256,256]{1,0:T(8,128)S(1)}, f32[256,256]{1,0:T(8,128)S(1)}, u32[]{:S(2)}, u32[]{:S(2)}) %collective-permute-start) | collective-permute-done | bytes 262176 | tf_op jit(solution)/shard_map/while/body/eval_jaxpr/ppermute | solution.py:10
  159.5 1.9 collective-permute-start
  161.4 9.7 %collective-permute-done = f32[256,256]{1,0:T(8,128)S(1)} collective-permute-done((f32[256,256]{1,0:T(8,128)S(1)}, f32[256,256]{1,0:T(8,128)S(1)}, u32[]{:S(2)}, u32[]{:S(2)}) %collective-permute-start) | collective-permute-done | bytes 262176 | tf_op jit(solution)/shard_map/while/body/eval_jaxpr/ppermute | solution.py:10
  171.1 1.9 collective-permute-start
  173.0 9.7 %collective-permute-done = f32[256,256]{1,0:T(8,128)S(1)} collective-permute-done((f32[256,256]{1,0:T(8,128)S(1)}, f32[256,256]{1,0:T(8,128)S(1)}, u32[]{:S(2)}, u32[]{:S(2)}) %collective-permute-start) | collective-permute-done | bytes 262176 | tf_op jit(solution)/shard_map/while/body/eval_jaxpr/ppermute | solution.py:10
  182.7 1.9 collective-permute-start
  184.6 9.8 %collective-permute-done = f32[256,256]{1,0:T(8,128)S(1)} collective-permute-done((f32[256,256]{1,0:T(8,128)S(1)}, f32[256,256]{1,0:T(8,128)S(1)}, u32[]{:S(2)}, u32[]{:S(2)}) %collective-permute-start) | collective-permute-done | bytes 262176 | tf_op jit(solution)/shard_map/while/body/eval_jaxpr/ppermute | solution.py:10
  194.4 1.9 collective-permute-start
  196.3 10.9 %collective-permute-done = f32[256,256]{1,0:T(8,128)S(1)} collective-permute-done((f32[256,256]{1,0:T(8,128)S(1)}, f32[256,256]{1,0:T(8,128)S(1)}, u32[]{:S(2)}, u32[]{:S(2)}) %collective-permute-start) | collective-permute-done | bytes 262176 | tf_op jit(solution)/shard_map/while/body/eval_jaxpr/ppermute | solution.py:10
  207.3 1.9 collective-permute-start
  209.2 12.1 %collective-permute-done = f32[256,256]{1,0:T(8,128)S(1)} collective-permute-done((f32[256,256]{1,0:T(8,128)S(1)}, f32[256,256]{1,0:T(8,128)S(1)}, u32[]{:S(2)}, u32[]{:S(2)}) %collective-permute-start) | collective-permute-done | bytes 262176 | tf_op jit(solution)/shard_map/while/body/eval_jaxpr/ppermute | solution.py:10
  221.3 1.9 collective-permute-start
  223.3 11.6 %collective-permute-done = f32[256,256]{1,0:T(8,128)S(1)} collective-permute-done((f32[256,256]{1,0:T(8,128)S(1)}, f32[256,256]{1,0:T(8,128)S(1)}, u32[]{:S(2)}, u32[]{:S(2)}) %collective-permute-start) | collective-permute-done | bytes 262176 | tf_op jit(solution)/shard_map/while/body/eval_jaxpr/ppermute | solution.py:10
  234.9 1.9 collective-permute-start
  236.8 10.8 %collective-permute-done = f32[256,256]{1,0:T(8,128)S(1)} collective-permute-done((f32[256,256]{1,0:T(8,128)S(1)}, f32[256,256]{1,0:T(8,128)S(1)}, u32[]{:S(2)}, u32[]{:S(2)}) %collective-permute-start) | collective-permute-done | bytes 262176 | tf_op jit(solution)/shard_map/while/body/eval_jaxpr/ppermute | solution.py:10
  247.6 1.9 collective-permute-start
  249.5 9.9 %collective-permute-done = f32[256,256]{1,0:T(8,128)S(1)} collective-permute-done((f32[256,256]{1,0:T(8,128)S(1)}, f32[256,256]{1,0:T(8,128)S(1)}, u32[]{:S(2)}, u32[]{:S(2)}) %collective-permute-start) | collective-permute-done | bytes 262176 | tf_op jit(solution)/shard_map/while/body/eval_jaxpr/ppermute | solution.py:10
  259.4 1.9 collective-permute-start
  261.3 9.7 %collective-permute-done = f32[256,256]{1,0:T(8,128)S(1)} collective-permute-done((f32[256,256]{1,0:T(8,128)S(1)}, f32[256,256]{1,0:T(8,128)S(1)}, u32[]{:S(2)}, u32[]{:S(2)}) %collective-permute-start) | collective-permute-done | bytes 262176 | tf_op jit(solution)/shard_map/while/body/eval_jaxpr/ppermute | solution.py:10
  271.0 1.9 collective-permute-start
  272.9 9.7 %collective-permute-done = f32[256,256]{1,0:T(8,128)S(1)} collective-permute-done((f32[256,256]{1,0:T(8,128)S(1)}, f32[256,256]{1,0:T(8,128)S(1)}, u32[]{:S(2)}, u32[]{:S(2)}) %collective-permute-start) | collective-permute-done | bytes 262176 | tf_op jit(solution)/shard_map/while/body/eval_jaxpr/ppermute | solution.py:10
  282.5 1.9 collective-permute-start
  284.5 9.7 %collective-permute-done = f32[256,256]{1,0:T(8,128)S(1)} collective-permute-done((f32[256,256]{1,0:T(8,128)S(1)}, f32[256,256]{1,0:T(8,128)S(1)}, u32[]{:S(2)}, u32[]{:S(2)}) %collective-permute-start) | collective-permute-done | bytes 262176 | tf_op jit(solution)/shard_map/while/body/eval_jaxpr/ppermute | solution.py:10
  294.9 1.9 collective-permute-start
  296.9 9.7 %collective-permute-done = f32[256,256]{1,0:T(8,128)S(1)} collective-permute-done((f32[256,256]{1,0:T(8,128)S(1)}, f32[256,256]{1,0:T(8,128)S(1)}, u32[]{:S(2)}, u32[]{:S(2)}) %collective-permute-start) | collective-permute-done | bytes 262176 | tf_op jit(solution)/shard_map/while/body/eval_jaxpr/ppermute | solution.py:10
  306.5 1.9 collective-permute-start
  308.4 10.1 %collective-permute-done = f32[256,256]{1,0:T(8,128)S(1)} collective-permute-done((f32[256,256]{1,0:T(8,128)S(1)}, f32[256,256]{1,0:T(8,128)S(1)}, u32[]{:S(2)}, u32[]{:S(2)}) %collective-permute-start) | collective-permute-done | bytes 262176 | tf_op jit(solution)/shard_map/while/body/eval_jaxpr/ppermute | solution.py:10
  318.5 1.9 collective-permute-start
  320.4 11.2 %collective-permute-done = f32[256,256]{1,0:T(8,128)S(1)} collective-permute-done((f32[256,256]{1,0:T(8,128)S(1)}, f32[256,256]{1,0:T(8,128)S(1)}, u32[]{:S(2)}, u32[]{:S(2)}) %collective-permute-start) | collective-permute-done | bytes 262176 | tf_op jit(solution)/shard_map/while/body/eval_jaxpr/ppermute | solution.py:10
  331.6 1.9 collective-permute-start
  333.6 12.3 %collective-permute-done = f32[256,256]{1,0:T(8,128)S(1)} collective-permute-done((f32[256,256]{1,0:T(8,128)S(1)}, f32[256,256]{1,0:T(8,128)S(1)}, u32[]{:S(2)}, u32[]{:S(2)}) %collective-permute-start) | collective-permute-done | bytes 262176 | tf_op jit(solution)/shard_map/while/body/eval_jaxpr/ppermute | solution.py:10
  345.9 1.9 collective-permute-start
  347.8 11.6 %collective-permute-done = f32[256,256]{1,0:T(8,128)S(1)} collective-permute-done((f32[256,256]{1,0:T(8,128)S(1)}, f32[256,256]{1,0:T(8,128)S(1)}, u32[]{:S(2)}, u32[]{:S(2)}) %collective-permute-start) | collective-permute-done | bytes 262176 | tf_op jit(solution)/shard_map/while/body/eval_jaxpr/ppermute | solution.py:10
  359.4 1.9 collective-permute-start
  361.3 10.8 %collective-permute-done = f32[256,256]{1,0:T(8,128)S(1)} collective-permute-done((f32[256,256]{1,0:T(8,128)S(1)}, f32[256,256]{1,0:T(8,128)S(1)}, u32[]{:S(2)}, u32[]{:S(2)}) %collective-permute-start) | collective-permute-done | bytes 262176 | tf_op jit(solution)/shard_map/while/body/eval_jaxpr/ppermute | solution.py:10
  372.1 1.9 collective-permute-start
  374.0 9.8 %collective-permute-done = f32[256,256]{1,0:T(8,128)S(1)} collective-permute-done((f32[256,256]{1,0:T(8,128)S(1)}, f32[256,256]{1,0:T(8,128)S(1)}, u32[]{:S(2)}, u32[]{:S(2)}) %collective-permute-start) | collective-permute-done | bytes 262176 | tf_op jit(solution)/shard_map/while/body/eval_jaxpr/ppermute | solution.py:10
  383.9 1.9 collective-permute-start
  385.8 9.7 %collective-permute-done = f32[256,256]{1,0:T(8,128)S(1)} collective-permute-done((f32[256,256]{1,0:T(8,128)S(1)}, f32[256,256]{1,0:T(8,128)S(1)}, u32[]{:S(2)}, u32[]{:S(2)}) %collective-permute-start) | collective-permute-done | bytes 262176 | tf_op jit(solution)/shard_map/while/body/eval_jaxpr/ppermute | solution.py:10
  395.5 1.9 collective-permute-start
  397.4 9.7 %collective-permute-done = f32[256,256]{1,0:T(8,128)S(1)} collective-permute-done((f32[256,256]{1,0:T(8,128)S(1)}, f32[256,256]{1,0:T(8,128)S(1)}, u32[]{:S(2)}, u32[]{:S(2)}) %collective-permute-start) | collective-permute-done | bytes 262176 | tf_op jit(solution)/shard_map/while/body/eval_jaxpr/ppermute | solution.py:10
  407.0 1.9 collective-permute-start
  409.0 9.7 %collective-permute-done = f32[256,256]{1,0:T(8,128)S(1)} collective-permute-done((f32[256,256]{1,0:T(8,128)S(1)}, f32[256,256]{1,0:T(8,128)S(1)}, u32[]{:S(2)}, u32[]{:S(2)}) %collective-permute-start) | collective-permute-done | bytes 262176 | tf_op jit(solution)/shard_map/while/body/eval_jaxpr/ppermute | solution.py:10
  420.5 9.7 %collective-permute-done = f32[256,256]{1,0:T(8,128)S(1)} collective-permute-done((f32[256,256]{1,0:T(8,128)S(1)}, f32[256,256]{1,0:T(8,128)S(1)}, u32[]{:S(2)}, u32[]{:S(2)}) %collective-permute-start) | collective-permute-done | bytes 262176 | tf_op jit(solution)/shard_map/while/body/eval_jaxpr/ppermute | solution.py:10
  432.1 10.1 %collective-permute-done = f32[256,256]{1,0:T(8,128)S(1)} collective-permute-done((f32[256,256]{1,0:T(8,128)S(1)}, f32[256,256]{1,0:T(8,128)S(1)}, u32[]{:S(2)}, u32[]{:S(2)}) %collective-permute-start) | collective-permute-done | bytes 262176 | tf_op jit(solution)/shard_map/while/body/eval_jaxpr/ppermute | solution.py:10
  444.1 9.7 %collective-permute-done = f32[256,256]{1,0:T(8,128)S(1)} collective-permute-done((f32[256,256]{1,0:T(8,128)S(1)}, f32[256,256]{1,0:T(8,128)S(1)}, u32[]{:S(2)}, u32[]{:S(2)}) %collective-permute-start) | collective-permute-done | bytes 262176 | tf_op jit(solution)/shard_map/while/body/eval_jaxpr/ppermute | solution.py:10
  455.7 9.7 %collective-permute-done = f32[256,256]{1,0:T(8,128)S(1)} collective-permute-done((f32[256,256]{1,0:T(8,128)S(1)}, f32[256,256]{1,0:T(8,128)S(1)}, u32[]{:S(2)}, u32[]{:S(2)}) %collective-permute-start) | collective-permute-done | bytes 262176 | tf_op jit(solution)/shard_map/while/body/eval_jaxpr/ppermute | solution.py:10
  467.3 9.7 %collective-permute-done = f32[256,256]{1,0:T(8,128)S(1)} collective-permute-done((f32[256,256]{1,0:T(8,128)S(1)}, f32[256,256]{1,0:T(8,128)S(1)}, u32[]{:S(2)}, u32[]{:S(2)}) %collective-permute-start) | collective-permute-done | bytes 262176 | tf_op jit(solution)/shard_map/while/body/eval_jaxpr/ppermute | solution.py:10
  (52 shorter events, 14.3 us)
Async XLA Ops:
  7.2 50.0 %copy-start.2 = (bf16[1,2,256,256]{3,2,1,0:T(8,128)(2,1)S(1)}, bf16[1,2,256,256]{3,2,1,0:T(8,128)(2,1)}, u32[]{:S(2)}) copy-start(bf16[1,2,256,256]{3,2,1,0:T(8,128)(2,1)} %param.9) | copy-start | bytes 786436
  7.2 50.0 %all-gather.2.cloned.1.call-start = ((), (), s32[]{:S(2)}) async-start(), calls=%async_computation | async-start | bytes 1114112 | tf_op jit(solution)/shard_map/all_gather | solution.py:44
  78.3 19.3 %copy-start = (f32[1,256,256]{2,1,0:T(8,128)S(1)}, f32[1,256,256]{2,1,0:T(8,128)}, u32[]{:S(2)}) copy-start(f32[1,256,256]{2,1,0:T(8,128)} %param.10) | copy-start | bytes 786436
  97.6 13.8 %collective-permute-start = (f32[256,256]{1,0:T(8,128)S(1)}, f32[256,256]{1,0:T(8,128)S(1)}, u32[]{:S(2)}, u32[]{:S(2)}) collective-permute-start(f32[256,256]{1,0:T(8,128)S(1)} %get-tuple-element.162), channel_id=1, source_target_pairs={{0,16},{16,32},{32,48},{48,64},{64,80},{80,96},{96,112},{112,128},... | collective-permute-start | bytes 786440 | tf_op jit(solution)/shard_map/while/body/eval_jaxpr/ppermute | solution.py:10
  111.4 13.0 %collective-permute-start = (f32[256,256]{1,0:T(8,128)S(1)}, f32[256,256]{1,0:T(8,128)S(1)}, u32[]{:S(2)}, u32[]{:S(2)}) collective-permute-start(f32[256,256]{1,0:T(8,128)S(1)} %get-tuple-element.162), channel_id=1, source_target_pairs={{0,16},{16,32},{32,48},{48,64},{64,80},{80,96},{96,112},{112,128},... | collective-permute-start | bytes 786440 | tf_op jit(solution)/shard_map/while/body/eval_jaxpr/ppermute | solution.py:10
  124.3 12.0 %collective-permute-start = (f32[256,256]{1,0:T(8,128)S(1)}, f32[256,256]{1,0:T(8,128)S(1)}, u32[]{:S(2)}, u32[]{:S(2)}) collective-permute-start(f32[256,256]{1,0:T(8,128)S(1)} %get-tuple-element.162), channel_id=1, source_target_pairs={{0,16},{16,32},{32,48},{48,64},{64,80},{80,96},{96,112},{112,128},... | collective-permute-start | bytes 786440 | tf_op jit(solution)/shard_map/while/body/eval_jaxpr/ppermute | solution.py:10
  136.4 11.6 %collective-permute-start = (f32[256,256]{1,0:T(8,128)S(1)}, f32[256,256]{1,0:T(8,128)S(1)}, u32[]{:S(2)}, u32[]{:S(2)}) collective-permute-start(f32[256,256]{1,0:T(8,128)S(1)} %get-tuple-element.162), channel_id=1, source_target_pairs={{0,16},{16,32},{32,48},{48,64},{64,80},{80,96},{96,112},{112,128},... | collective-permute-start | bytes 786440 | tf_op jit(solution)/shard_map/while/body/eval_jaxpr/ppermute | solution.py:10
  147.9 11.6 %collective-permute-start = (f32[256,256]{1,0:T(8,128)S(1)}, f32[256,256]{1,0:T(8,128)S(1)}, u32[]{:S(2)}, u32[]{:S(2)}) collective-permute-start(f32[256,256]{1,0:T(8,128)S(1)} %get-tuple-element.162), channel_id=1, source_target_pairs={{0,16},{16,32},{32,48},{48,64},{64,80},{80,96},{96,112},{112,128},... | collective-permute-start | bytes 786440 | tf_op jit(solution)/shard_map/while/body/eval_jaxpr/ppermute | solution.py:10
  159.5 11.6 %collective-permute-start = (f32[256,256]{1,0:T(8,128)S(1)}, f32[256,256]{1,0:T(8,128)S(1)}, u32[]{:S(2)}, u32[]{:S(2)}) collective-permute-start(f32[256,256]{1,0:T(8,128)S(1)} %get-tuple-element.162), channel_id=1, source_target_pairs={{0,16},{16,32},{32,48},{48,64},{64,80},{80,96},{96,112},{112,128},... | collective-permute-start | bytes 786440 | tf_op jit(solution)/shard_map/while/body/eval_jaxpr/ppermute | solution.py:10
  171.1 11.6 %collective-permute-start = (f32[256,256]{1,0:T(8,128)S(1)}, f32[256,256]{1,0:T(8,128)S(1)}, u32[]{:S(2)}, u32[]{:S(2)}) collective-permute-start(f32[256,256]{1,0:T(8,128)S(1)} %get-tuple-element.162), channel_id=1, source_target_pairs={{0,16},{16,32},{32,48},{48,64},{64,80},{80,96},{96,112},{112,128},... | collective-permute-start | bytes 786440 | tf_op jit(solution)/shard_map/while/body/eval_jaxpr/ppermute | solution.py:10
  182.7 11.8 %collective-permute-start = (f32[256,256]{1,0:T(8,128)S(1)}, f32[256,256]{1,0:T(8,128)S(1)}, u32[]{:S(2)}, u32[]{:S(2)}) collective-permute-start(f32[256,256]{1,0:T(8,128)S(1)} %get-tuple-element.162), channel_id=1, source_target_pairs={{0,16},{16,32},{32,48},{48,64},{64,80},{80,96},{96,112},{112,128},... | collective-permute-start | bytes 786440 | tf_op jit(solution)/shard_map/while/body/eval_jaxpr/ppermute | solution.py:10
  194.4 12.8 %collective-permute-start = (f32[256,256]{1,0:T(8,128)S(1)}, f32[256,256]{1,0:T(8,128)S(1)}, u32[]{:S(2)}, u32[]{:S(2)}) collective-permute-start(f32[256,256]{1,0:T(8,128)S(1)} %get-tuple-element.162), channel_id=1, source_target_pairs={{0,16},{16,32},{32,48},{48,64},{64,80},{80,96},{96,112},{112,128},... | collective-permute-start | bytes 786440 | tf_op jit(solution)/shard_map/while/body/eval_jaxpr/ppermute | solution.py:10
  207.3 14.1 %collective-permute-start = (f32[256,256]{1,0:T(8,128)S(1)}, f32[256,256]{1,0:T(8,128)S(1)}, u32[]{:S(2)}, u32[]{:S(2)}) collective-permute-start(f32[256,256]{1,0:T(8,128)S(1)} %get-tuple-element.162), channel_id=1, source_target_pairs={{0,16},{16,32},{32,48},{48,64},{64,80},{80,96},{96,112},{112,128},... | collective-permute-start | bytes 786440 | tf_op jit(solution)/shard_map/while/body/eval_jaxpr/ppermute | solution.py:10
  221.3 13.5 %collective-permute-start = (f32[256,256]{1,0:T(8,128)S(1)}, f32[256,256]{1,0:T(8,128)S(1)}, u32[]{:S(2)}, u32[]{:S(2)}) collective-permute-start(f32[256,256]{1,0:T(8,128)S(1)} %get-tuple-element.162), channel_id=1, source_target_pairs={{0,16},{16,32},{32,48},{48,64},{64,80},{80,96},{96,112},{112,128},... | collective-permute-start | bytes 786440 | tf_op jit(solution)/shard_map/while/body/eval_jaxpr/ppermute | solution.py:10
  234.9 12.7 %collective-permute-start = (f32[256,256]{1,0:T(8,128)S(1)}, f32[256,256]{1,0:T(8,128)S(1)}, u32[]{:S(2)}, u32[]{:S(2)}) collective-permute-start(f32[256,256]{1,0:T(8,128)S(1)} %get-tuple-element.162), channel_id=1, source_target_pairs={{0,16},{16,32},{32,48},{48,64},{64,80},{80,96},{96,112},{112,128},... | collective-permute-start | bytes 786440 | tf_op jit(solution)/shard_map/while/body/eval_jaxpr/ppermute | solution.py:10
  247.6 11.8 %collective-permute-start = (f32[256,256]{1,0:T(8,128)S(1)}, f32[256,256]{1,0:T(8,128)S(1)}, u32[]{:S(2)}, u32[]{:S(2)}) collective-permute-start(f32[256,256]{1,0:T(8,128)S(1)} %get-tuple-element.162), channel_id=1, source_target_pairs={{0,16},{16,32},{32,48},{48,64},{64,80},{80,96},{96,112},{112,128},... | collective-permute-start | bytes 786440 | tf_op jit(solution)/shard_map/while/body/eval_jaxpr/ppermute | solution.py:10
  259.4 11.6 %collective-permute-start = (f32[256,256]{1,0:T(8,128)S(1)}, f32[256,256]{1,0:T(8,128)S(1)}, u32[]{:S(2)}, u32[]{:S(2)}) collective-permute-start(f32[256,256]{1,0:T(8,128)S(1)} %get-tuple-element.162), channel_id=1, source_target_pairs={{0,16},{16,32},{32,48},{48,64},{64,80},{80,96},{96,112},{112,128},... | collective-permute-start | bytes 786440 | tf_op jit(solution)/shard_map/while/body/eval_jaxpr/ppermute | solution.py:10
  271.0 11.6 %collective-permute-start = (f32[256,256]{1,0:T(8,128)S(1)}, f32[256,256]{1,0:T(8,128)S(1)}, u32[]{:S(2)}, u32[]{:S(2)}) collective-permute-start(f32[256,256]{1,0:T(8,128)S(1)} %get-tuple-element.162), channel_id=1, source_target_pairs={{0,16},{16,32},{32,48},{48,64},{64,80},{80,96},{96,112},{112,128},... | collective-permute-start | bytes 786440 | tf_op jit(solution)/shard_map/while/body/eval_jaxpr/ppermute | solution.py:10
  282.5 11.6 %collective-permute-start = (f32[256,256]{1,0:T(8,128)S(1)}, f32[256,256]{1,0:T(8,128)S(1)}, u32[]{:S(2)}, u32[]{:S(2)}) collective-permute-start(f32[256,256]{1,0:T(8,128)S(1)} %get-tuple-element.162), channel_id=1, source_target_pairs={{0,16},{16,32},{32,48},{48,64},{64,80},{80,96},{96,112},{112,128},... | collective-permute-start | bytes 786440 | tf_op jit(solution)/shard_map/while/body/eval_jaxpr/ppermute | solution.py:10
  294.9 11.6 %collective-permute-start = (f32[256,256]{1,0:T(8,128)S(1)}, f32[256,256]{1,0:T(8,128)S(1)}, u32[]{:S(2)}, u32[]{:S(2)}) collective-permute-start(f32[256,256]{1,0:T(8,128)S(1)} %get-tuple-element.162), channel_id=1, source_target_pairs={{0,16},{16,32},{32,48},{48,64},{64,80},{80,96},{96,112},{112,128},... | collective-permute-start | bytes 786440 | tf_op jit(solution)/shard_map/while/body/eval_jaxpr/ppermute | solution.py:10
  306.5 12.0 %collective-permute-start = (f32[256,256]{1,0:T(8,128)S(1)}, f32[256,256]{1,0:T(8,128)S(1)}, u32[]{:S(2)}, u32[]{:S(2)}) collective-permute-start(f32[256,256]{1,0:T(8,128)S(1)} %get-tuple-element.162), channel_id=1, source_target_pairs={{0,16},{16,32},{32,48},{48,64},{64,80},{80,96},{96,112},{112,128},... | collective-permute-start | bytes 786440 | tf_op jit(solution)/shard_map/while/body/eval_jaxpr/ppermute | solution.py:10
  318.5 13.1 %collective-permute-start = (f32[256,256]{1,0:T(8,128)S(1)}, f32[256,256]{1,0:T(8,128)S(1)}, u32[]{:S(2)}, u32[]{:S(2)}) collective-permute-start(f32[256,256]{1,0:T(8,128)S(1)} %get-tuple-element.162), channel_id=1, source_target_pairs={{0,16},{16,32},{32,48},{48,64},{64,80},{80,96},{96,112},{112,128},... | collective-permute-start | bytes 786440 | tf_op jit(solution)/shard_map/while/body/eval_jaxpr/ppermute | solution.py:10
  331.6 14.3 %collective-permute-start = (f32[256,256]{1,0:T(8,128)S(1)}, f32[256,256]{1,0:T(8,128)S(1)}, u32[]{:S(2)}, u32[]{:S(2)}) collective-permute-start(f32[256,256]{1,0:T(8,128)S(1)} %get-tuple-element.162), channel_id=1, source_target_pairs={{0,16},{16,32},{32,48},{48,64},{64,80},{80,96},{96,112},{112,128},... | collective-permute-start | bytes 786440 | tf_op jit(solution)/shard_map/while/body/eval_jaxpr/ppermute | solution.py:10
  345.9 13.5 %collective-permute-start = (f32[256,256]{1,0:T(8,128)S(1)}, f32[256,256]{1,0:T(8,128)S(1)}, u32[]{:S(2)}, u32[]{:S(2)}) collective-permute-start(f32[256,256]{1,0:T(8,128)S(1)} %get-tuple-element.162), channel_id=1, source_target_pairs={{0,16},{16,32},{32,48},{48,64},{64,80},{80,96},{96,112},{112,128},... | collective-permute-start | bytes 786440 | tf_op jit(solution)/shard_map/while/body/eval_jaxpr/ppermute | solution.py:10
  359.4 12.7 %collective-permute-start = (f32[256,256]{1,0:T(8,128)S(1)}, f32[256,256]{1,0:T(8,128)S(1)}, u32[]{:S(2)}, u32[]{:S(2)}) collective-permute-start(f32[256,256]{1,0:T(8,128)S(1)} %get-tuple-element.162), channel_id=1, source_target_pairs={{0,16},{16,32},{32,48},{48,64},{64,80},{80,96},{96,112},{112,128},... | collective-permute-start | bytes 786440 | tf_op jit(solution)/shard_map/while/body/eval_jaxpr/ppermute | solution.py:10
  372.1 11.8 %collective-permute-start = (f32[256,256]{1,0:T(8,128)S(1)}, f32[256,256]{1,0:T(8,128)S(1)}, u32[]{:S(2)}, u32[]{:S(2)}) collective-permute-start(f32[256,256]{1,0:T(8,128)S(1)} %get-tuple-element.162), channel_id=1, source_target_pairs={{0,16},{16,32},{32,48},{48,64},{64,80},{80,96},{96,112},{112,128},... | collective-permute-start | bytes 786440 | tf_op jit(solution)/shard_map/while/body/eval_jaxpr/ppermute | solution.py:10
  383.9 11.6 %collective-permute-start = (f32[256,256]{1,0:T(8,128)S(1)}, f32[256,256]{1,0:T(8,128)S(1)}, u32[]{:S(2)}, u32[]{:S(2)}) collective-permute-start(f32[256,256]{1,0:T(8,128)S(1)} %get-tuple-element.162), channel_id=1, source_target_pairs={{0,16},{16,32},{32,48},{48,64},{64,80},{80,96},{96,112},{112,128},... | collective-permute-start | bytes 786440 | tf_op jit(solution)/shard_map/while/body/eval_jaxpr/ppermute | solution.py:10
  395.5 11.6 %collective-permute-start = (f32[256,256]{1,0:T(8,128)S(1)}, f32[256,256]{1,0:T(8,128)S(1)}, u32[]{:S(2)}, u32[]{:S(2)}) collective-permute-start(f32[256,256]{1,0:T(8,128)S(1)} %get-tuple-element.162), channel_id=1, source_target_pairs={{0,16},{16,32},{32,48},{48,64},{64,80},{80,96},{96,112},{112,128},... | collective-permute-start | bytes 786440 | tf_op jit(solution)/shard_map/while/body/eval_jaxpr/ppermute | solution.py:10
  407.0 11.6 %collective-permute-start = (f32[256,256]{1,0:T(8,128)S(1)}, f32[256,256]{1,0:T(8,128)S(1)}, u32[]{:S(2)}, u32[]{:S(2)}) collective-permute-start(f32[256,256]{1,0:T(8,128)S(1)} %get-tuple-element.162), channel_id=1, source_target_pairs={{0,16},{16,32},{32,48},{48,64},{64,80},{80,96},{96,112},{112,128},... | collective-permute-start | bytes 786440 | tf_op jit(solution)/shard_map/while/body/eval_jaxpr/ppermute | solution.py:10
  418.6 11.6 %collective-permute-start = (f32[256,256]{1,0:T(8,128)S(1)}, f32[256,256]{1,0:T(8,128)S(1)}, u32[]{:S(2)}, u32[]{:S(2)}) collective-permute-start(f32[256,256]{1,0:T(8,128)S(1)} %get-tuple-element.162), channel_id=1, source_target_pairs={{0,16},{16,32},{32,48},{48,64},{64,80},{80,96},{96,112},{112,128},... | collective-permute-start | bytes 786440 | tf_op jit(solution)/shard_map/while/body/eval_jaxpr/ppermute | solution.py:10
  430.2 12.0 %collective-permute-start = (f32[256,256]{1,0:T(8,128)S(1)}, f32[256,256]{1,0:T(8,128)S(1)}, u32[]{:S(2)}, u32[]{:S(2)}) collective-permute-start(f32[256,256]{1,0:T(8,128)S(1)} %get-tuple-element.162), channel_id=1, source_target_pairs={{0,16},{16,32},{32,48},{48,64},{64,80},{80,96},{96,112},{112,128},... | collective-permute-start | bytes 786440 | tf_op jit(solution)/shard_map/while/body/eval_jaxpr/ppermute | solution.py:10
  442.2 11.6 %collective-permute-start = (f32[256,256]{1,0:T(8,128)S(1)}, f32[256,256]{1,0:T(8,128)S(1)}, u32[]{:S(2)}, u32[]{:S(2)}) collective-permute-start(f32[256,256]{1,0:T(8,128)S(1)} %get-tuple-element.162), channel_id=1, source_target_pairs={{0,16},{16,32},{32,48},{48,64},{64,80},{80,96},{96,112},{112,128},... | collective-permute-start | bytes 786440 | tf_op jit(solution)/shard_map/while/body/eval_jaxpr/ppermute | solution.py:10
  453.8 11.6 %collective-permute-start = (f32[256,256]{1,0:T(8,128)S(1)}, f32[256,256]{1,0:T(8,128)S(1)}, u32[]{:S(2)}, u32[]{:S(2)}) collective-permute-start(f32[256,256]{1,0:T(8,128)S(1)} %get-tuple-element.162), channel_id=1, source_target_pairs={{0,16},{16,32},{32,48},{48,64},{64,80},{80,96},{96,112},{112,128},... | collective-permute-start | bytes 786440 | tf_op jit(solution)/shard_map/while/body/eval_jaxpr/ppermute | solution.py:10
  465.4 11.6 %collective-permute-start = (f32[256,256]{1,0:T(8,128)S(1)}, f32[256,256]{1,0:T(8,128)S(1)}, u32[]{:S(2)}, u32[]{:S(2)}) collective-permute-start(f32[256,256]{1,0:T(8,128)S(1)} %get-tuple-element.162), channel_id=1, source_target_pairs={{0,16},{16,32},{32,48},{48,64},{64,80},{80,96},{96,112},{112,128},... | collective-permute-start | bytes 786440 | tf_op jit(solution)/shard_map/while/body/eval_jaxpr/ppermute | solution.py:10
  476.9 0.7 copy-start.1
Sparse Core Ops, SparseCore 0:
  10.9 46.2 all-gather.1
where the time goes:
time: 486 us; the launch traced here: 484 us
  waiting for transfers between devices  364 us (75%)
  starting transfers between devices  60.7 us (12%)
  blocking collectives  33.1 us (7%)
  between operations  14.1 us (3%)
  matrix products  10.7 us (2%)
    ppermute x31, waiting for transfers between devices, passed_along(): return lax.ppermute(x, axis, pairs)  317 us
    ppermute x31, starting transfers between devices, passed_along(): return lax.ppermute(x, axis, pairs)  60.6 us
    all_gather x1, waiting for transfers between devices, body(): lax.all_gather(picked_one, 'blk', axis=0, tiled=True)  46.4 us
    all_gather x1, blocking collectives, body(): lax.all_gather(picked_two, 'blk', axis=0, tiled=True)  18 us
    all_gather x1, blocking collectives, body(): lax.all_gather(edge_rows, 'blk', axis=0, tiled=True).astype(jnp.float32)  15.1 us
  transfers between devices with their start and end apart: 32, of which 32 were waited for; matrix products, arithmetic and copies ran while one was open for 0% of the time, Pallas kernels for 0%

commit v1 on v0

v1 whole, which is shorter than its diff:
```python
import jax
import jax.numpy as jnp
from jax import lax
from jax.sharding import PartitionSpec as P


def passed_along(x, axis, by):
    count = lax.axis_size(axis)
    return lax.ppermute(x, axis, [(i, i + by) for i in range(count - by)])


def matmul_high(left, right):
    return jnp.dot(left, right, precision=lax.Precision.HIGHEST, preferred_element_type=jnp.float32)


def rounded_dot(left, right):
    return jnp.dot(left, right, preferred_element_type=jnp.float32).astype(jnp.bfloat16)


def reduced_by(block, factor, rows):
    product = jnp.dot(factor, rows, preferred_element_type=jnp.float32)
    return (block.astype(jnp.float32) - product).astype(jnp.bfloat16)


def body(panel_strip, pivot_inverses, coupling, pivot_nodes):
    strip = panel_strip[0]
    first_inverse, second_inverse = pivot_inverses[0, 0], pivot_inverses[0, 1]
    coupling_here = coupling[0]
    w = coupling_here.shape[0]
    rows_here = strip.shape[0]
    per_device = w // lax.axis_size("blk")
    my_index = lax.axis_index("blk")
    local_rows = (
        lax.dynamic_slice_in_dim(pivot_nodes, my_index * per_device, per_device, 1)
        - my_index * rows_here
    ).reshape(-1)
    picker = (
        local_rows[:, None] == lax.broadcasted_iota(jnp.int32, (3 * per_device, rows_here), 1)
    ).astype(jnp.bfloat16)
    picked = rounded_dot(picker, strip)
    rows_one, rows_two, rows_edge = (
        picked[i * per_device:(i + 1) * per_device] for i in range(3)
    )

    near = lax.all_gather(
        jnp.concatenate(
            [rows_one[:, w:3 * w], rows_two[:, :w], rows_two[:, 2 * w:3 * w], rows_edge[:, :3 * w]], 1
        ),
        "blk", axis=0, tiled=True,
    )
    far = lax.all_gather(
        jnp.concatenate([rows_one[:, 3 * w:], rows_two[:, 3 * w:]], 1), "blk", axis=0, tiled=True
    )
    one_next, one_edge = near[:, :w], near[:, w:2 * w]
    two_panel, two_edge = near[:, 2 * w:3 * w], near[:, 3 * w:4 * w]
    edge = near[:, 4 * w:]

    factor_at_two = rounded_dot(two_panel, first_inverse)
    factor_at_edge = rounded_dot(edge[:, :w], first_inverse)
    second_edge = reduced_by(two_edge, factor_at_two, one_edge)
    edge_updated = reduced_by(edge[:, w:], factor_at_edge, near[:, :2 * w])
    edge_factor_two = rounded_dot(edge_updated[:, :w], second_inverse)
    boundary = reduced_by(edge_updated[:, w:], edge_factor_two, second_edge)

    count = lax.axis_size("tm")
    span = coupling_here
    current = boundary.astype(jnp.float32)
    step = 1
    while step < count:
        incoming = passed_along(current.astype(jnp.bfloat16), "tm", step).astype(jnp.float32)
        current = matmul_high(matmul_high(span, incoming), span.T) + current
        if 2 * step < count:
            span = matmul_high(span, passed_along(span, "tm", step))
        step *= 2
    reduced = current

    factor_one = rounded_dot(strip[:, :w], first_inverse)
    next_panel = reduced_by(strip[:, w:2 * w], factor_one, one_next)
    factor_two = rounded_dot(next_panel, second_inverse)
    far_one, far_two = jnp.split(far, 2, 1)
    second_far = reduced_by(far_two, factor_at_two, far_one)
    one_rows = jnp.concatenate([one_edge, far_one], 1)
    two_rows = jnp.concatenate([second_edge, second_far], 1)
    updated = reduced_by(strip[:, 2 * w:], factor_one, one_rows)
    trailing = reduced_by(updated, factor_two, two_rows)
    return (trailing[None], reduced[None])


def solution(mesh):
    placed = (P("tm", "blk", None), P("tm", None, None, None), P("tm", None, None), P())
    return jax.shard_map(
        body,
        mesh=mesh,
        in_specs=placed,
        out_specs=(P("tm", "blk", None), P("tm", None, None)),
        check_vma=False,
    )
```

time: 486 us -> 130 us (0.27)
  the two profiles are of different devices: /device:TPU:32 before, /device:TPU:40 now
where the time goes in v1:
time: 130 us; the launch traced here: 129 us
  waiting for transfers between devices  34.6 us (27%)
  blocking collectives  26.1 us (20%)
  matrix products  25.3 us (19%)
  starting transfers between devices  24.4 us (19%)
  between operations  14.4 us (11%)
  local copies, waits for them, and re-layouts  2.66 us (2%)
  other arithmetic  1.44 us (1%)
    ppermute x9, waiting for transfers between devices, passed_along(): return lax.ppermute(x, axis, [(i, i + by) for i in range(count - by)])  34.6 us
    all_gather x1, blocking collectives, body(): lax.all_gather(jnp.concatenate([rows_one[:, w:3 * w], rows_two[:, :w], ro...  26.1 us
    ppermute x9, starting transfers between devices, passed_along(): return lax.ppermute(x, axis, [(i, i + by) for i in range(count - by)])  24.4 us
    dot_general x6, matrix products, reduced_by(): product = jnp.dot(factor, rows, preferred_element_type=jnp.float32)  8.68 us
    dot_general x14, matrix products, matmul_high(): jnp.dot(left, right, precision=lax.Precision.HIGHEST, preferred_element_t...  8.61 us
    dot_general x4, matrix products, rounded_dot(): jnp.dot(left, right, preferred_element_type=jnp.float32)  7.99 us
  transfers between devices with their start and end apart: 10, of which 7 were waited for; matrix products, arithmetic and copies ran while one was open for 16% of the time, Pallas kernels for 0%

profile of v1, /device:TPU:40, one launch (start us, length us, event | category | flops | bytes accessed | tf_op | source)
XLA Modules:
  0.0 128.9 jit_solution(8305294757422915728)
XLA Ops:
  7.2 0.0 copy-start.1
  7.2 0.0 all-gather.2.cloned.1.call-start
  7.2 0.8 dynamic-slice_subtract_fusion
  8.0 0.1 eq.10
  8.1 2.2 %convolution_convert_fusion = bf16[48,2304]{1,0:T(8,128)(2,1)S(1)} fusion(s32[48]{0:T(128)S(1)} %eq.10, bf16[1,512,2304]{2,1,0:T(8,128)(2,1)} %param.4), kind=kOutput, calls=%fused_computation.2 | convolution fusion | flops 113381376 | bytes 2580672 | tf_op jit(solution)/shard_map/dot_general | solution.py:17
  10.3 0.6 pad_maximum_fusion
  11.0 0.0 all-gather.2.cloned.1.call-update
  11.0 0.0 copy-done.1
  11.0 3.4 %collective-permute-start = (f32[256,256]{1,0:T(8,128)S(1)}, f32[256,256]{1,0:T(8,128)}, u32[]{:S(2)}, u32[]{:S(2)}) collective-permute-start(f32[256,256]{1,0:T(8,128)S(1)} %bitcast.64), channel_id=1, source_target_pairs={{0,16},{16,32},{32,48},{48,64},{64,80},{80,96},{96,112},{112,128},... | collective-permute-start | bytes 786440 | tf_op jit(solution)/shard_map/ppermute | solution.py:9
  14.5 0.0 copy-start
  14.5 26.1 %all_gather.6 = bf16[256,1792]{1,0:T(8,128)(2,1)S(1)} all-gather(bf16[16,1792]{1,0:T(8,128)(2,1)S(1)} %pad_maximum_fusion.1), channel_id=1, replica_groups=mesh['tm'=32,'blk'=16] {'blk'}, dimensions={0}, use_global_device_ids=true | all-gather | bytes 974848 | tf_op jit(solution)/shard_map/all_gather | solution.py:45
  40.6 1.9 %convolution_convert_fusion.5 = bf16[256,256]{1,0:T(8,128)(2,1)} fusion(bf16[256,1792]{1,0:T(8,128)(2,1)S(1)} %all_gather.6, bf16[1,2,256,256]{3,2,1,0:T(8,128)(2,1)} %param.5), kind=kOutput, calls=%fused_computation.24 | convolution fusion | flops 33619968 | bytes 393216 | tf_op jit(solution)/shard_map/dot_general | solution.py:17
  42.5 2.0 %fusion.3 = bf16[256,512]{1,0:T(8,128)(2,1)} fusion(bf16[256,1792]{1,0:T(8,128)(2,1)S(1)} %all_gather.6, bf16[1,2,256,256]{3,2,1,0:T(8,128)(2,1)} %param.5), kind=kOutput, calls=%fused_computation.11 | convolution fusion | flops 101122048 | bytes 1048576 | tf_op jit(solution)/shard_map/dot_general | solution.py:21
  44.4 1.7 %fusion.5 = bf16[256,256]{1,0:T(8,128)(2,1)} fusion(bf16[256,256]{1,0:T(8,128)(2,1)} %convolution_convert_fusion.5, bf16[256,1792]{1,0:T(8,128)(2,1)S(1)} %all_gather.6), kind=kOutput, calls=%fused_computation.20 | convolution fusion | flops 33751040 | bytes 524288 | tf_op jit(solution)/shard_map/dot_general | solution.py:21
  46.2 2.1 %fusion.6 = bf16[256,256]{1,0:T(8,128)(2,1)} fusion(bf16[256,256]{1,0:T(8,128)(2,1)} %fusion.5, bf16[256,512]{1,0:T(8,128)(2,1)} %fusion.3, bf16[1,2,256,256]{3,2,1,0:T(8,128)(2,1)} %param.5), kind=kOutput, calls=%fused_computation.21 | convolution fusion | flops 67371008 | bytes 655360 | tf_op jit(solution)/shard_map/dot_general | solution.py:21
  48.3 3.5 %collective-permute-start.4 = (bf16[256,256]{1,0:T(8,128)(2,1)}, bf16[256,256]{1,0:T(8,128)(2,1)}, u32[]{:S(2)}, u32[]{:S(2)}) collective-permute-start(bf16[256,256]{1,0:T(8,128)(2,1)} %fusion.6), channel_id=1, source_target_pairs={{0,16},{16,32},{32,48},{48,64},{64,80},{80,96},{96,112},{112,128},... | collective-permute-start | bytes 393224 | tf_op jit(solution)/shard_map/ppermute | solution.py:9
  51.8 0.0 copy-done
  51.8 1.8 %convolution_convert_fusion.2 = bf16[512,256]{1,0:T(8,128)(2,1)} fusion(bf16[512,2304]{1,0:T(8,128)(2,1)S(1)} %bitcast.61, bf16[1,2,256,256]{3,2,1,0:T(8,128)(2,1)} %param.5), kind=kOutput, calls=%fused_computation.9 | convolution fusion | flops 67239936 | bytes 655360 | tf_op jit(solution)/shard_map/dot_general | solution.py:17
  53.6 2.1 %convolution_convert_fusion.1 = bf16[512,256]{1,0:T(8,128)(2,1)} fusion(bf16[512,256]{1,0:T(8,128)(2,1)} %convolution_convert_fusion.2, bf16[512,2304]{1,0:T(8,128)(2,1)S(1)} %bitcast.62, bf16[256,1792]{1,0:T(8,128)(2,1)S(1)} %all_gather.6, bf16[1,2,256,256]{3,2,1,0:T(8,128)(2,1)} %param.5), kind=kOutput, calls=%fused_computation.8 | convolution fusion | flops 134742016 | bytes 1048576 | tf_op jit(solution)/shard_map/dot_general | solution.py:17
  55.7 0.0 copy-done.2
  55.7 2.7 %collective-permute-done.4 = bf16[256,256]{1,0:T(8,128)(2,1)} collective-permute-done((bf16[256,256]{1,0:T(8,128)(2,1)}, bf16[256,256]{1,0:T(8,128)(2,1)}, u32[]{:S(2)}, u32[]{:S(2)}) %collective-permute-start.4) | collective-permute-done | bytes 131104 | tf_op jit(solution)/shard_map/ppermute | solution.py:9
  58.3 1.2 fusion.42
  59.6 1.5 %fusion.51 = (bf16[256,256]{1,0:T(8,128)(2,1)S(1)}, f32[256,256]{1,0:T(8,128)S(1)}) fusion(bf16[256,256]{1,0:T(8,128)(2,1)} %fusion.6, f32[256,256]{1,0:T(8,128)S(1)} %fusion.42, f32[1,256,256]{2,1,0:T(8,128)S(1)} %copy-done.1), kind=kOutput, calls=%fused_computation.66 | convolution fusion | flops 201523200 | bytes 1048576 | tf_op jit(solution)/shard_map/dot_general | solution.py:13
  61.1 2.6 %collective-permute-start.5 = (bf16[256,256]{1,0:T(8,128)(2,1)S(1)}, bf16[256,256]{1,0:T(8,128)(2,1)S(1)}, u32[]{:S(2)}, u32[]{:S(2)}) collective-permute-start(bf16[256,256]{1,0:T(8,128)(2,1)S(1)} %get-tuple-element.6), channel_id=1, source_target_pairs={{0,32},{16,48},{32,64},{48,80},{64,96},{80,112},{96,128},{112,144}... | collective-permute-start | bytes 393224 | tf_op jit(solution)/shard_map/ppermute | solution.py:9
  63.7 0.0 collective-permute-done
  63.7 1.3 %fusion.44 = f32[256,256]{1,0:T(8,128)S(1)} fusion(f32[256,256]{1,0:T(8,128)} %collective-permute-done, f32[1,256,256]{2,1,0:T(8,128)S(1)} %copy-done.1), kind=kOutput, calls=%fused_computation.59 | convolution fusion | flops 201326592 | bytes 786432 | tf_op jit(solution)/shard_map/dot_general | solution.py:13
  65.0 4.7 %collective-permute-start.1 = (f32[256,256]{1,0:T(8,128)S(1)}, f32[256,256]{1,0:T(8,128)S(1)}, u32[]{:S(2)}, u32[]{:S(2)}) collective-permute-start(f32[256,256]{1,0:T(8,128)S(1)} %fusion.44), channel_id=1, source_target_pairs={{0,32},{16,48},{32,64},{48,80},{64,96},{80,112},{96,128},{112,144}... | collective-permute-start | bytes 786440 | tf_op jit(solution)/shard_map/ppermute | solution.py:9
  69.7 0.6 collective-permute-done.5
  70.4 0.3 fusion.58
  70.6 0.4 fusion.52
  71.0 2.4 %collective-permute-start.6 = (bf16[256,256]{1,0:T(8,128)(2,1)S(1)}, bf16[256,256]{1,0:T(8,128)(2,1)S(1)}, u32[]{:S(2)}, u32[]{:S(2)}) collective-permute-start(bf16[256,256]{1,0:T(8,128)(2,1)S(1)} %get-tuple-element.8), channel_id=1, source_target_pairs={{0,64},{16,80},{32,96},{48,112},{64,128},{80,144},{96,160},{112,17... | collective-permute-start | bytes 393224 | tf_op jit(solution)/shard_map/ppermute | solution.py:9
  73.5 4.7 %collective-permute-done.1 = f32[256,256]{1,0:T(8,128)S(1)} collective-permute-done((f32[256,256]{1,0:T(8,128)S(1)}, f32[256,256]{1,0:T(8,128)S(1)}, u32[]{:S(2)}, u32[]{:S(2)}) %collective-permute-start.1) | collective-permute-done | bytes 262176 | tf_op jit(solution)/shard_map/ppermute | solution.py:9
  78.2 0.4 fusion.55
  78.6 2.7 %collective-permute-start.2 = (f32[256,256]{1,0:T(8,128)S(1)}, f32[256,256]{1,0:T(8,128)S(1)}, u32[]{:S(2)}, u32[]{:S(2)}) collective-permute-start(f32[256,256]{1,0:T(8,128)S(1)} %fusion.55), channel_id=1, source_target_pairs={{0,64},{16,80},{32,96},{48,112},{64,128},{80,144},{96,160},{112,17... | collective-permute-start | bytes 786440 | tf_op jit(solution)/shard_map/ppermute | solution.py:9
  81.3 0.0 collective-permute-done.6
  81.3 0.3 fusion.59
  81.5 0.4 fusion.53
  82.0 1.9 %collective-permute-start.7 = (bf16[256,256]{1,0:T(8,128)(2,1)S(1)}, bf16[256,256]{1,0:T(8,128)(2,1)S(1)}, u32[]{:S(2)}, u32[]{:S(2)}) collective-permute-start(bf16[256,256]{1,0:T(8,128)(2,1)S(1)} %get-tuple-element.10), channel_id=1, source_target_pairs={{0,128},{16,144},{32,160},{48,176},{64,192},{80,208},{96,224},{112... | collective-permute-start | bytes 393224 | tf_op jit(solution)/shard_map/ppermute | solution.py:9
  83.9 6.6 %collective-permute-done.2 = f32[256,256]{1,0:T(8,128)S(1)} collective-permute-done((f32[256,256]{1,0:T(8,128)S(1)}, f32[256,256]{1,0:T(8,128)S(1)}, u32[]{:S(2)}, u32[]{:S(2)}) %collective-permute-start.2) | collective-permute-done | bytes 262176 | tf_op jit(solution)/shard_map/ppermute | solution.py:9
  90.4 0.4 fusion.56
  90.8 1.9 %collective-permute-start.3 = (f32[256,256]{1,0:T(8,128)S(1)}, f32[256,256]{1,0:T(8,128)S(1)}, u32[]{:S(2)}, u32[]{:S(2)}) collective-permute-start(f32[256,256]{1,0:T(8,128)S(1)} %fusion.56), channel_id=1, source_target_pairs={{0,128},{16,144},{32,160},{48,176},{64,192},{80,208},{96,224},{112... | collective-permute-start | bytes 786440 | tf_op jit(solution)/shard_map/ppermute | solution.py:9
  92.8 11.0 %collective-permute-done.7 = bf16[256,256]{1,0:T(8,128)(2,1)S(1)} collective-permute-done((bf16[256,256]{1,0:T(8,128)(2,1)S(1)}, bf16[256,256]{1,0:T(8,128)(2,1)S(1)}, u32[]{:S(2)}, u32[]{:S(2)}) %collective-permute-start.7) | collective-permute-done | bytes 131104 | tf_op jit(solution)/shard_map/ppermute | solution.py:9
  103.7 0.3 fusion.60
  104.0 0.4 fusion.54
  104.4 1.3 %collective-permute-start.8 = (bf16[256,256]{1,0:T(8,128)(2,1)S(1)}, bf16[256,256]{1,0:T(8,128)(2,1)S(1)}, u32[]{:S(2)}, u32[]{:S(2)}) collective-permute-start(bf16[256,256]{1,0:T(8,128)(2,1)S(1)} %get-tuple-element.12), channel_id=1, source_target_pairs={{0,256},{16,272},{32,288},{48,304},{64,320},{80,336},{96,352},{112... | collective-permute-start | bytes 393224 | tf_op jit(solution)/shard_map/ppermute | solution.py:9
  105.7 1.3 collective-permute-done.3
  107.0 0.4 fusion.57
  107.4 0.0 slice-start
  107.4 0.0 copy-start.5
  107.4 7.8 %collective-permute-done.8 = bf16[256,256]{1,0:T(8,128)(2,1)S(1)} collective-permute-done((bf16[256,256]{1,0:T(8,128)(2,1)S(1)}, bf16[256,256]{1,0:T(8,128)(2,1)S(1)}, u32[]{:S(2)}, u32[]{:S(2)}) %collective-permute-start.8) | collective-permute-done | bytes 131104 | tf_op jit(solution)/shard_map/ppermute | solution.py:9
  115.2 0.3 fusion.61
  115.5 1.1 fusion.4
  116.6 1.2 split.8
  117.8 0.0 slice-done
  117.8 0.0 copy-done.5
  117.8 0.0 copy-start.3
  117.8 0.0 copy-start.6
  117.8 0.6 subtract_convert_fusion.1
  118.4 0.7 copy-done.3
  119.2 0.0 copy-done.6
  119.2 0.4 fusion.1
  119.6 0.6 copy-done.4
  120.1 0.0 copy-done.7
  120.2 1.9 %fusion = bf16[1,512,1792]{2,1,0:T(8,128)(2,1)} fusion(bf16[512,256]{1,0:T(8,128)(2,1)S(1)} %copy-done.4, bf16[512,1792]{1,0:T(8,128)(2,1)S(1)} %subtract_convert_fusion.1, bf16[256,1536]{1,0:T(8,128)(2,1)S(1)} %fusion.1, bf16[256,256]{1,0:T(8,128)(2,1)S(1)} %copy-done.7), kind=kOutput, calls=%fused_computation.4 | convolution fusion | flops 474349568 | bytes 4849664 | tf_op jit(solution)/shard_map/dot_general | solution.py:21
  (9 shorter events, 0.0 us)
Async XLA Ops:
  7.2 3.8 %copy-start.1 = (f32[1,256,256]{2,1,0:T(8,128)S(1)}, f32[1,256,256]{2,1,0:T(8,128)}, u32[]{:S(2)}) copy-start(f32[1,256,256]{2,1,0:T(8,128)} %param.6) | copy-start | bytes 786436
  7.2 109.4 %all-gather.2.cloned.1.call-start = ((), (), s32[]{:S(2)}) async-start(), calls=%async_computation | async-start | bytes 1671168 | tf_op jit(solution)/shard_map/all_gather | solution.py:51
  11.0 52.7 %collective-permute-start = (f32[256,256]{1,0:T(8,128)S(1)}, f32[256,256]{1,0:T(8,128)}, u32[]{:S(2)}, u32[]{:S(2)}) collective-permute-start(f32[256,256]{1,0:T(8,128)S(1)} %bitcast.64), channel_id=1, source_target_pairs={{0,16},{16,32},{32,48},{48,64},{64,80},{80,96},{96,112},{112,128},... | collective-permute-start | bytes 786440 | tf_op jit(solution)/shard_map/ppermute | solution.py:9
  14.5 37.3 %copy-start = (bf16[1,512,2304]{2,1,0:T(8,128)(2,1)S(1)}, bf16[1,512,2304]{2,1,0:T(8,128)(2,1)}, u32[]{:S(2)}) copy-start(bf16[1,512,2304]{2,1,0:T(8,128)(2,1)} %param.4) | copy-start | bytes 7077892
  40.6 15.1 %copy-start.2 = (bf16[256,1792]{1,0:T(8,128)(2,1)}, bf16[256,1792]{1,0:T(8,128)(2,1)S(1)}, u32[]{:S(2)}) copy-start(bf16[256,1792]{1,0:T(8,128)(2,1)S(1)} %all_gather.6) | copy-start | bytes 2752516
  48.3 10.1 %collective-permute-start.4 = (bf16[256,256]{1,0:T(8,128)(2,1)}, bf16[256,256]{1,0:T(8,128)(2,1)}, u32[]{:S(2)}, u32[]{:S(2)}) collective-permute-start(bf16[256,256]{1,0:T(8,128)(2,1)} %fusion.6), channel_id=1, source_target_pairs={{0,16},{16,32},{32,48},{48,64},{64,80},{80,96},{96,112},{112,128},... | collective-permute-start | bytes 393224 | tf_op jit(solution)/shard_map/ppermute | solution.py:9
  61.1 9.3 %collective-permute-start.5 = (bf16[256,256]{1,0:T(8,128)(2,1)S(1)}, bf16[256,256]{1,0:T(8,128)(2,1)S(1)}, u32[]{:S(2)}, u32[]{:S(2)}) collective-permute-start(bf16[256,256]{1,0:T(8,128)(2,1)S(1)} %get-tuple-element.6), channel_id=1, source_target_pairs={{0,32},{16,48},{32,64},{48,80},{64,96},{80,112},{96,128},{112,144}... | collective-permute-start | bytes 393224 | tf_op jit(solution)/shard_map/ppermute | solution.py:9
  65.0 13.2 %collective-permute-start.1 = (f32[256,256]{1,0:T(8,128)S(1)}, f32[256,256]{1,0:T(8,128)S(1)}, u32[]{:S(2)}, u32[]{:S(2)}) collective-permute-start(f32[256,256]{1,0:T(8,128)S(1)} %fusion.44), channel_id=1, source_target_pairs={{0,32},{16,48},{32,64},{48,80},{64,96},{80,112},{96,128},{112,144}... | collective-permute-start | bytes 786440 | tf_op jit(solution)/shard_map/ppermute | solution.py:9
  71.0 10.2 %collective-permute-start.6 = (bf16[256,256]{1,0:T(8,128)(2,1)S(1)}, bf16[256,256]{1,0:T(8,128)(2,1)S(1)}, u32[]{:S(2)}, u32[]{:S(2)}) collective-permute-start(bf16[256,256]{1,0:T(8,128)(2,1)S(1)} %get-tuple-element.8), channel_id=1, source_target_pairs={{0,64},{16,80},{32,96},{48,112},{64,128},{80,144},{96,160},{112,17... | collective-permute-start | bytes 393224 | tf_op jit(solution)/shard_map/ppermute | solution.py:9
  78.6 11.8 %collective-permute-start.2 = (f32[256,256]{1,0:T(8,128)S(1)}, f32[256,256]{1,0:T(8,128)S(1)}, u32[]{:S(2)}, u32[]{:S(2)}) collective-permute-start(f32[256,256]{1,0:T(8,128)S(1)} %fusion.55), channel_id=1, source_target_pairs={{0,64},{16,80},{32,96},{48,112},{64,128},{80,144},{96,160},{112,17... | collective-permute-start | bytes 786440 | tf_op jit(solution)/shard_map/ppermute | solution.py:9
  82.0 21.7 %collective-permute-start.7 = (bf16[256,256]{1,0:T(8,128)(2,1)S(1)}, bf16[256,256]{1,0:T(8,128)(2,1)S(1)}, u32[]{:S(2)}, u32[]{:S(2)}) collective-permute-start(bf16[256,256]{1,0:T(8,128)(2,1)S(1)} %get-tuple-element.10), channel_id=1, source_target_pairs={{0,128},{16,144},{32,160},{48,176},{64,192},{80,208},{96,224},{112... | collective-permute-start | bytes 393224 | tf_op jit(solution)/shard_map/ppermute | solution.py:9
  90.8 16.1 %collective-permute-start.3 = (f32[256,256]{1,0:T(8,128)S(1)}, f32[256,256]{1,0:T(8,128)S(1)}, u32[]{:S(2)}, u32[]{:S(2)}) collective-permute-start(f32[256,256]{1,0:T(8,128)S(1)} %fusion.56), channel_id=1, source_target_pairs={{0,128},{16,144},{32,160},{48,176},{64,192},{80,208},{96,224},{112... | collective-permute-start | bytes 786440 | tf_op jit(solution)/shard_map/ppermute | solution.py:9
  104.4 10.8 %collective-permute-start.8 = (bf16[256,256]{1,0:T(8,128)(2,1)S(1)}, bf16[256,256]{1,0:T(8,128)(2,1)S(1)}, u32[]{:S(2)}, u32[]{:S(2)}) collective-permute-start(bf16[256,256]{1,0:T(8,128)(2,1)S(1)} %get-tuple-element.12), channel_id=1, source_target_pairs={{0,256},{16,272},{32,288},{48,304},{64,320},{80,336},{96,352},{112... | collective-permute-start | bytes 393224 | tf_op jit(solution)/shard_map/ppermute | solution.py:9
  107.4 10.4 %slice-start = ((bf16[256,1792]{1,0:T(8,128)(2,1)}), bf16[256,256]{1,0:T(8,128)(2,1)S(1)}, s32[]{:S(2)}) async-start(bf16[256,1792]{1,0:T(8,128)(2,1)} %copy-done.2), calls=%async_computation.1 | async-start | bytes 262144 | tf_op jit(solution)/shard_map/slice | solution.py:54
  107.4 10.4 %copy-start.5 = (bf16[512,256]{1,0:T(8,128)(2,1)S(1)}, bf16[512,256]{1,0:T(8,128)(2,1)}, u32[]{:S(2)}) copy-start(bf16[512,256]{1,0:T(8,128)(2,1)} %convolution_convert_fusion.2) | copy-start | bytes 786436
  117.8 1.4 %copy-start.3 = (bf16[256,3072]{1,0:T(8,128)(2,1)S(1)}, bf16[256,3072]{1,0:T(8,128)(2,1)}, u32[]{:S(2)}) copy-start(bf16[256,3072]{1,0:T(8,128)(2,1)} %all-gather.2.cloned.1.call-done) | copy-start | bytes 4718596
  117.8 1.4 %copy-start.6 = (bf16[256,256]{1,0:T(8,128)(2,1)S(1)}, bf16[256,256]{1,0:T(8,128)(2,1)}, u32[]{:S(2)}) copy-start(bf16[256,256]{1,0:T(8,128)(2,1)} %convolution_convert_fusion.5) | copy-start | bytes 393220
  119.2 1.0 copy-start.4
  119.2 1.0 copy-start.7
Sparse Core Ops, SparseCore 0:
  11.1 46.6 all-gather.1

commit v2 on v1

v2 whole, which is shorter than its diff:
```python
import jax
import jax.numpy as jnp
from jax import lax
from jax.experimental import pallas as pl
from jax.experimental.pallas import tpu as pltpu
from jax.sharding import PartitionSpec as P

BF16 = jnp.bfloat16
F32 = jnp.float32


def passed_along(x, axis, by):
    count = lax.axis_size(axis)
    return lax.ppermute(x, axis, [(i, i + by) for i in range(count - by)])


def matmul_high(left, right):
    return jnp.dot(left, right, precision=lax.Precision.HIGHEST, preferred_element_type=F32)


def rounded_dot(left, right):
    return jnp.dot(left, right, preferred_element_type=F32).astype(BF16)


def reduced_by(block, factor, rows):
    product = jnp.dot(factor, rows, preferred_element_type=F32)
    return (block.astype(F32) - product).astype(BF16)


def pick_kernel(w, per, chunks, nodes_ref, strip_hbm, near_ref, far_ref, strip_ref, sems):
    rows = strip_ref.shape[0]
    cols = strip_ref.shape[1] // chunks

    def part(i):
        at = pl.ds(i * cols, cols)
        return pltpu.make_async_copy(strip_hbm.at[:, at], strip_ref.at[:, at], sems.at[i])

    for i in range(chunks):
        part(i).start()
    me = lax.axis_index("blk")
    at_row = lax.broadcasted_iota(jnp.int32, (3 * per, rows), 0)
    at_lane = lax.broadcasted_iota(jnp.int32, (3 * per, rows), 1)
    wanted = jnp.zeros((3 * per, rows), jnp.int32)
    for k in range(3):
        for i in range(per):
            node = nodes_ref[k, me * per + i] - me * rows
            wanted = jnp.where(at_row == k * per + i, node, wanted)
    picker = (wanted == at_lane).astype(F32).astype(BF16)
    far_width = strip_ref.shape[1] - 3 * w
    for i in range(chunks):
        part(i).wait()
        at = pl.ds(i * cols, cols)
        got = jnp.dot(picker, strip_ref[:, at], preferred_element_type=F32).astype(BF16)
        one, two, edge = got[:per], got[per:2 * per], got[2 * per:]
        if i == 0:
            near_ref[:, :2 * w] = one[:, w:]
            near_ref[:, 2 * w:3 * w] = two[:, :w]
            near_ref[:, 3 * w:4 * w] = two[:, 2 * w:]
            near_ref[:, 4 * w:] = edge
        else:
            far_ref[:, (i - 1) * cols:i * cols] = one
            far_ref[:, far_width + (i - 1) * cols:far_width + i * cols] = two


def picked_rows(pivot_nodes, strip, w, per):
    rows, width = strip.shape
    chunks = width // (3 * w)
    return pl.pallas_call(
        lambda *refs: pick_kernel(w, per, chunks, *refs),
        out_shape=(
            jax.ShapeDtypeStruct((per, 7 * w), BF16),
            jax.ShapeDtypeStruct((per, 2 * (width - 3 * w)), BF16),
        ),
        in_specs=[pl.BlockSpec(memory_space=pltpu.SMEM), pl.BlockSpec(memory_space=pl.ANY)],
        out_specs=(pl.BlockSpec(memory_space=pltpu.VMEM), pl.BlockSpec(memory_space=pltpu.VMEM)),
        scratch_shapes=[pltpu.VMEM((rows, width), BF16), pltpu.SemaphoreType.DMA((chunks,))],
        cost_estimate=pl.CostEstimate(
            flops=2 * 3 * per * rows * width, bytes_accessed=2 * rows * width, transcendentals=0
        ),
        name="pick",
    )(pivot_nodes, strip)


def boundary_kernel(w, near_ref, inverse_ref, boundary_ref, factor_ref, second_ref):
    near = near_ref[...]
    one_edge = near[:, w:2 * w]
    edge = near[:, 4 * w:]
    factor_at_two = rounded_dot(near[:, 2 * w:3 * w], inverse_ref[0])
    factor_at_edge = rounded_dot(edge[:, :w], inverse_ref[0])
    updated = reduced_by(edge[:, w:], factor_at_edge, near[:, :2 * w])
    second_edge = reduced_by(near[:, 3 * w:4 * w], factor_at_two, one_edge)
    factor_two = rounded_dot(updated[:, :w], inverse_ref[1])
    boundary_ref[...] = reduced_by(updated[:, w:], factor_two, second_edge)
    factor_ref[...] = factor_at_two
    second_ref[...] = second_edge


def boundary_of(near, inverses):
    w = near.shape[0]
    block = jax.ShapeDtypeStruct((w, w), BF16)
    vmem = pl.BlockSpec(memory_space=pltpu.VMEM)
    return pl.pallas_call(
        lambda *refs: boundary_kernel(w, *refs),
        out_shape=(block, block, block),
        in_specs=[vmem, vmem],
        out_specs=(vmem, vmem, vmem),
        cost_estimate=pl.CostEstimate(flops=14 * w * w * w, bytes_accessed=12 * w * 2 * w, transcendentals=0),
        name="boundary",
    )(near, inverses)


def trailing_kernel(
    w, per, panels_ref, block_ref, inverse_ref, near_ref, factor_ref, second_ref, own_ref, other_ref,
    out_ref, one_ref, two_ref, far_ref,
):
    step = pl.program_id(0)
    half = far_ref.shape[1] // 2

    def finish(one_rows, two_rows):
        updated = reduced_by(block_ref[...], one_ref[...], one_rows)
        out_ref[...] = reduced_by(updated, two_ref[...], two_rows)

    @pl.when(step == 0)
    def _():
        me = lax.axis_index("blk")
        chip, core = me // 2, lax.rem(me, 2)
        chips = far_ref.shape[0] // (2 * per)
        for m, shift in enumerate(chip_shifts(chips)):
            source = 2 * lax.rem(chip + chips - shift, chips)
            for ref, which in ((own_ref, core), (other_ref, 1 - core)):
                at = pl.multiple_of((source + which) * per, per)
                far_ref[pl.ds(at, per), :] = ref[m * per:(m + 1) * per, :]
        one_ref[...] = rounded_dot(panels_ref[:, :w], inverse_ref[0])
        panel = reduced_by(panels_ref[:, w:], one_ref[...], near_ref[:, :w])
        two_ref[...] = rounded_dot(panel, inverse_ref[1])
        finish(near_ref[:, w:], second_ref[...])

    @pl.when(step > 0)
    def _():
        at = pl.multiple_of((step - 1) * w, w)
        one_rows = far_ref[:, pl.ds(at, w)]
        finish(one_rows, reduced_by(far_ref[:, pl.ds(half + at, w)], factor_ref[...], one_rows))


def trailing_of(strip, inverses, near, factor_at_two, second_edge, own, other, per):
    rows, width = strip.shape
    w = near.shape[0]
    fixed = lambda i: (0, 0)
    return pl.pallas_call(
        lambda *refs: trailing_kernel(w, per, *refs),
        out_shape=jax.ShapeDtypeStruct((rows, width - 2 * w), BF16),
        grid=(width // w - 2,),
        in_specs=[
            pl.BlockSpec((rows, 2 * w), fixed),
            pl.BlockSpec((rows, w), lambda i: (0, i + 2)),
            pl.BlockSpec((2, w, w), lambda i: (0, 0, 0)),
            pl.BlockSpec((w, 2 * w), fixed),
            pl.BlockSpec((w, w), fixed),
            pl.BlockSpec((w, w), fixed),
            pl.BlockSpec(own.shape, fixed),
            pl.BlockSpec(own.shape, fixed),
        ],
        out_specs=pl.BlockSpec((rows, w), lambda i: (0, i)),
        scratch_shapes=[
            pltpu.VMEM((rows, w), BF16),
            pltpu.VMEM((rows, w), BF16),
            pltpu.VMEM((w, own.shape[1]), BF16),
        ],
        cost_estimate=pl.CostEstimate(
            flops=4 * rows * w * width, bytes_accessed=4 * rows * width + 4 * w * width, transcendentals=0
        ),
        name="trailing",
    )(strip, strip, inverses, near, factor_at_two, second_edge, own, other)


def chip_shifts(chips):
    return [0] + [s for by in range(1, chips // 2) for s in (by, chips - by)] + [chips // 2]


def body(panel_strip, pivot_inverses, coupling, pivot_nodes):
    strip = panel_strip[0]
    inverses = pivot_inverses[0]
    span = coupling[0]
    w = span.shape[0]
    blocks = lax.axis_size("blk")
    per = w // blocks

    back_one, back_two, back_three = (passed_along(span, "tm", by) for by in (1, 2, 3))

    near_here, far_here = picked_rows(pivot_nodes, strip, w, per)
    near = lax.all_gather(near_here, "blk", axis=0, tiled=True)
    boundary, factor_at_two, second_edge = boundary_of(near, inverses)
    back_one, back_two, back_three, boundary, far_here = lax.optimization_barrier(
        (back_one, back_two, back_three, boundary, far_here)
    )

    shifts = chip_shifts(blocks // 2)
    far_from = {0: far_here}

    def send_far(gate, which):
        gate, block = lax.optimization_barrier((gate, far_here))
        for shift in which:
            pairs = [(i, (i + 2 * shift) % blocks) for i in range(blocks)]
            far_from[shift] = lax.ppermute(block, "blk", pairs)
        return gate

    def arrived(value, which):
        value, *blocks_in = lax.optimization_barrier((value, *(far_from[s] for s in which)))
        far_from.update(zip(which, blocks_in))
        return value

    def advance(current, incoming, reach):
        return matmul_high(matmul_high(reach, incoming.astype(F32)), reach.T) + current

    groups = [shifts[6:], shifts[3:6], shifts[1:3]]

    incoming = passed_along(boundary, "tm", 1)
    span_two = send_far(matmul_high(span, back_one), groups[0])
    span_four = matmul_high(span_two, matmul_high(back_two, back_three))
    current = advance(boundary.astype(F32), incoming, span)

    current, span_four = lax.optimization_barrier((current, span_four))
    incoming = passed_along(current.astype(BF16), "tm", 2)
    current = send_far(current, groups[1])
    span_eight = matmul_high(span_four, passed_along(span_four, "tm", 4))
    incoming = arrived(incoming, groups[0])
    current = advance(current, incoming, span_two)

    current, span_eight = lax.optimization_barrier((current, span_eight))
    incoming = passed_along(current.astype(BF16), "tm", 4)
    current = send_far(current, groups[2])
    incoming = arrived(incoming, groups[1])
    current = advance(current, incoming, span_four)

    current = arrived(current, groups[2])
    incoming = passed_along(current.astype(BF16), "tm", 8)
    own = jnp.concatenate([far_from[s] for s in shifts], 0)
    other = lax.ppermute(own, "blk", [(i, i ^ 1) for i in range(blocks)])
    span_sixteen = matmul_high(span_eight, passed_along(span_eight, "tm", 8))
    incoming, other, span_sixteen = lax.optimization_barrier((incoming, other, span_sixteen))
    current = advance(current, incoming, span_eight)

    current, other = lax.optimization_barrier((current, other))
    incoming = passed_along(current.astype(BF16), "tm", 16)
    trailing = trailing_of(strip, inverses, near, factor_at_two, second_edge, own, other, per)
    incoming, trailing = lax.optimization_barrier((incoming, trailing))
    current = advance(current, incoming, span_sixteen)
    return (trailing[None], current[None])


def solution(mesh):
    placed = (P("tm", "blk", None), P("tm", None, None, None), P("tm", None, None), P())
    return jax.shard_map(
        body,
        mesh=mesh,
        in_specs=placed,
        out_specs=(P("tm", "blk", None), P("tm", None, None)),
        check_vma=False,
    )
```

time: 130 us -> 145 us (1.12)
  the two profiles are of different devices: /device:TPU:40 before, /device:TPU:12 now
where the time goes in v2:
time: 145 us; the launch traced here: 144 us
  starting transfers between devices  66.2 us (46%)
  waiting for transfers between devices  29 us (20%)
  blocking collectives  27.3 us (19%)
  Pallas kernels  13.9 us (10%)
  matrix products  6.75 us (5%)
    ppermute x10, starting transfers between devices, passed_along(): return lax.ppermute(x, axis, [(i, i + by) for i in range(count - by)])  39.8 us
    all_gather x1, blocking collectives, body(): near = lax.all_gather(near_here, 'blk', axis=0, tiled=True)  27.3 us
    ppermute x7, starting transfers between devices, send_far(): far_from[shift] = lax.ppermute(block, 'blk', pairs)  24.5 us
    ppermute x10, waiting for transfers between devices, passed_along(): return lax.ppermute(x, axis, [(i, i + by) for i in range(count - by)])  23.9 us
    pallas_call x1, Pallas kernels, trailing_of(): pl.pallas_call(lambda *refs: trailing_kernel(w, per, *refs), out_shape=ja...  8.02 us
    dot_general x15, matrix products, matmul_high(): jnp.dot(left, right, precision=lax.Precision.HIGHEST, preferred_element_t...  6.75 us
    ppermute x7, waiting for transfers between devices, send_far(): far_from[shift] = lax.ppermute(block, 'blk', pairs)  5.07 us
    pallas_call x1, Pallas kernels, picked_rows(): pl.pallas_call(lambda *refs: pick_kernel(w, per, chunks, *refs), out_shap...  3.34 us
  transfers between devices with their start and end apart: 18, of which 5 were waited for; matrix products, arithmetic and copies ran while one was open for 2% of the time, Pallas kernels for 10%

profile of v2, /device:TPU:12, one launch (start us, length us, event | category | flops | bytes accessed | tf_op | source)
XLA Modules:
  0.0 144.4 jit_solution(14533738560007265781)
XLA Ops:
  0.6 0.0 copy-start
  0.6 3.6 %collective-permute-start.2 = (f32[256,256]{1,0:T(8,128)}, f32[256,256]{1,0:T(8,128)S(1)}, u32[]{:S(2)}, u32[]{:S(2)}) collective-permute-start(f32[256,256]{1,0:T(8,128)} %bitcast.46), channel_id=1, source_target_pairs={{0,48},{16,64},{32,80},{48,96},{64,112},{80,128},{96,144},{112,160... | collective-permute-start | bytes 786440 | tf_op jit(solution)/shard_map/ppermute | solution.py:14
  4.2 4.6 %collective-permute-start.1 = (f32[256,256]{1,0:T(8,128)}, f32[256,256]{1,0:T(8,128)S(1)}, u32[]{:S(2)}, u32[]{:S(2)}) collective-permute-start(f32[256,256]{1,0:T(8,128)} %bitcast.47), channel_id=1, source_target_pairs={{0,32},{16,48},{32,64},{48,80},{64,96},{80,112},{96,128},{112,144}... | collective-permute-start | bytes 786440 | tf_op jit(solution)/shard_map/ppermute | solution.py:14
  8.9 2.8 %collective-permute-start = (f32[256,256]{1,0:T(8,128)}, f32[256,256]{1,0:T(8,128)S(1)}, u32[]{:S(2)}, u32[]{:S(2)}) collective-permute-start(f32[256,256]{1,0:T(8,128)} %bitcast.48), channel_id=1, source_target_pairs={{0,16},{16,32},{32,48},{48,64},{64,80},{80,96},{96,112},{112,128},... | collective-permute-start | bytes 786440 | tf_op jit(solution)/shard_map/ppermute | solution.py:14
  11.7 3.3 %pick.1 = (bf16[16,1792]{1,0:T(8,128)(2,1)}, bf16[16,3072]{1,0:T(8,128)(2,1)}) custom-call(s32[3,256]{1,0:T(4,128)} %refs_0_.1, bf16[512,2304]{1,0:T(8,128)(2,1)} %bitcast.43), custom_call_target="tpu_custom_call" | custom-call | flops 113246208 | bytes 2359296 | tf_op jit(solution)/shard_map/pick/pallas_call | solution.py:68
  15.0 27.3 %all_gather.3.refs_0_.refs_3_ = bf16[256,1792]{1,0:T(8,128)(2,1)} all-gather(bf16[16,1792]{1,0:T(8,128)(2,1)} %get-tuple-element.39), channel_id=1, replica_groups=mesh['tm'=32,'blk'=16] {'blk'}, dimensions={0}, use_global_device_ids=true | all-gather | bytes 974848 | tf_op jit(solution)/shard_map/all_gather | solution.py:191
  42.3 2.5 %boundary.1 = (bf16[256,256]{1,0:T(8,128)(2,1)}, bf16[256,256]{1,0:T(8,128)(2,1)}, bf16[256,256]{1,0:T(8,128)(2,1)}) custom-call(bf16[256,1792]{1,0:T(8,128)(2,1)} %all_gather.3.refs_0_.refs_3_, bf16[2,256,256]{2,1,0:T(8,128)(2,1)} %bitcast.50), custom_call_target="tpu_custom_call" | custom-call | flops 234881024 | bytes 1572864 | tf_op jit(solution)/shard_map/boundary/pallas_call | solution.py:102
  44.9 0.0 copy-start.3
  44.9 0.0 copy-start.4
  44.9 0.0 collective-permute-done.2
  44.9 0.0 collective-permute-done.1
  44.9 0.0 collective-permute-done
  44.9 0.0 copy-done
  44.9 0.6 convolution_bitcast_fusion
  45.5 4.0 %collective-permute-start.3 = (bf16[256,256]{1,0:T(8,128)(2,1)}, bf16[256,256]{1,0:T(8,128)(2,1)S(1)}, u32[]{:S(2)}, u32[]{:S(2)}) collective-permute-start(bf16[256,256]{1,0:T(8,128)(2,1)} %get-tuple-element.45), channel_id=1, source_target_pairs={{0,16},{16,32},{32,48},{48,64},{64,80},{80,96},{96,112},{112,128},... | collective-permute-start | bytes 393224 | tf_op jit(solution)/shard_map/ppermute | solution.py:14
  49.5 0.4 fusion.8
  49.9 0.6 fusion.9
  50.5 2.9 %collective-permute-done.3 = bf16[256,256]{1,0:T(8,128)(2,1)S(1)} collective-permute-done((bf16[256,256]{1,0:T(8,128)(2,1)}, bf16[256,256]{1,0:T(8,128)(2,1)S(1)}, u32[]{:S(2)}, u32[]{:S(2)}) %collective-permute-start.3) | collective-permute-done | bytes 131104 | tf_op jit(solution)/shard_map/ppermute | solution.py:14
  53.4 0.3 fusion.3
  53.7 0.0 copy-done.3
  53.7 0.6 convert_add_fusion
  54.4 5.8 %collective-permute-start.4 = (bf16[256,256]{1,0:T(8,128)(2,1)S(1)}, bf16[256,256]{1,0:T(8,128)(2,1)S(1)}, u32[]{:S(2)}, u32[]{:S(2)}) collective-permute-start(bf16[256,256]{1,0:T(8,128)(2,1)S(1)} %convert_element_type.21), channel_id=1, source_target_pairs={{0,32},{16,48},{32,64},{48,80},{64,96},{80,112},{96,128},{112,144}... | collective-permute-start | bytes 393224 | tf_op jit(solution)/shard_map/ppermute | solution.py:14
  60.2 0.0 copy-done.4
  60.2 3.4 %collective-permute-start.6 = (bf16[16,3072]{1,0:T(8,128)(2,1)S(1)}, bf16[16,3072]{1,0:T(8,128)(2,1)S(1)}, u32[]{:S(2)}, u32[]{:S(2)}) collective-permute-start(bf16[16,3072]{1,0:T(8,128)(2,1)S(1)} %copy-done.4), channel_id=1, source_target_pairs={{0,8},{1,9},{2,10},{3,11},{4,12},{5,13},{6,14},{7,15},{8,0},{9,1},... | collective-permute-start | bytes 294920 | tf_op jit(solution)/shard_map/ppermute | solution.py:204
  63.6 4.2 %collective-permute-start.5 = (bf16[16,3072]{1,0:T(8,128)(2,1)S(1)}, bf16[16,3072]{1,0:T(8,128)(2,1)S(1)}, u32[]{:S(2)}, u32[]{:S(2)}) collective-permute-start(bf16[16,3072]{1,0:T(8,128)(2,1)S(1)} %copy-done.4), channel_id=1, source_target_pairs={{0,10},{1,11},{2,12},{3,13},{4,14},{5,15},{6,0},{7,1},{8,2},{9,3},... | collective-permute-start | bytes 294920 | tf_op jit(solution)/shard_map/ppermute | solution.py:204
  67.8 3.4 %collective-permute-start.11 = (bf16[16,3072]{1,0:T(8,128)(2,1)S(1)}, bf16[16,3072]{1,0:T(8,128)(2,1)S(1)}, u32[]{:S(2)}, u32[]{:S(2)}) collective-permute-start(bf16[16,3072]{1,0:T(8,128)(2,1)S(1)} %copy-done.4), channel_id=1, source_target_pairs={{0,6},{1,7},{2,8},{3,9},{4,10},{5,11},{6,12},{7,13},{8,14},{9,15},... | collective-permute-start | bytes 294920 | tf_op jit(solution)/shard_map/ppermute | solution.py:204
  71.2 5.5 %collective-permute-start.10 = (bf16[16,3072]{1,0:T(8,128)(2,1)S(1)}, bf16[16,3072]{1,0:T(8,128)(2,1)S(1)}, u32[]{:S(2)}, u32[]{:S(2)}) collective-permute-start(bf16[16,3072]{1,0:T(8,128)(2,1)S(1)} %copy-done.4), channel_id=1, source_target_pairs={{0,12},{1,13},{2,14},{3,15},{4,0},{5,1},{6,2},{7,3},{8,4},{9,5},{1... | collective-permute-start | bytes 294920 | tf_op jit(solution)/shard_map/ppermute | solution.py:204
  76.7 0.0 collective-permute-done.6
  76.7 1.9 %collective-permute-start.9 = (bf16[16,3072]{1,0:T(8,128)(2,1)S(1)}, bf16[16,3072]{1,0:T(8,128)(2,1)S(1)}, u32[]{:S(2)}, u32[]{:S(2)}) collective-permute-start(bf16[16,3072]{1,0:T(8,128)(2,1)S(1)} %copy-done.4), channel_id=1, source_target_pairs={{0,4},{1,5},{2,6},{3,7},{4,8},{5,9},{6,10},{7,11},{8,12},{9,13},{1... | collective-permute-start | bytes 294920 | tf_op jit(solution)/shard_map/ppermute | solution.py:204
  78.7 0.0 collective-permute-done.5
  78.7 4.7 %collective-permute-start.7 = (f32[256,256]{1,0:T(8,128)S(1)}, f32[256,256]{1,0:T(8,128)S(1)}, u32[]{:S(2)}, u32[]{:S(2)}) collective-permute-start(f32[256,256]{1,0:T(8,128)S(1)} %fusion.9), channel_id=1, source_target_pairs={{0,64},{16,80},{32,96},{48,112},{64,128},{80,144},{96,160},{112,17... | collective-permute-start | bytes 786440 | tf_op jit(solution)/shard_map/ppermute | solution.py:14
  83.4 0.0 collective-permute-done.4
  83.4 0.4 fusion.10
  83.8 0.4 convolution_add_fusion.3
  84.2 3.1 %collective-permute-done.7 = f32[256,256]{1,0:T(8,128)S(1)} collective-permute-done((f32[256,256]{1,0:T(8,128)S(1)}, f32[256,256]{1,0:T(8,128)S(1)}, u32[]{:S(2)}, u32[]{:S(2)}) %collective-permute-start.7) | collective-permute-done | bytes 262176 | tf_op jit(solution)/shard_map/ppermute | solution.py:14
  87.3 0.4 fusion.11
  87.7 4.4 %collective-permute-start.8 = (bf16[256,256]{1,0:T(8,128)(2,1)S(1)}, bf16[256,256]{1,0:T(8,128)(2,1)S(1)}, u32[]{:S(2)}, u32[]{:S(2)}) collective-permute-start(bf16[256,256]{1,0:T(8,128)(2,1)S(1)} %convert_element_type.22), channel_id=1, source_target_pairs={{0,64},{16,80},{32,96},{48,112},{64,128},{80,144},{96,160},{112,17... | collective-permute-start | bytes 393224 | tf_op jit(solution)/shard_map/ppermute | solution.py:14
  92.1 4.2 %collective-permute-start.13 = (bf16[16,3072]{1,0:T(8,128)(2,1)S(1)}, bf16[16,3072]{1,0:T(8,128)(2,1)S(1)}, u32[]{:S(2)}, u32[]{:S(2)}) collective-permute-start(bf16[16,3072]{1,0:T(8,128)(2,1)S(1)} %copy-done.4), channel_id=1, source_target_pairs={{0,14},{1,15},{2,0},{3,1},{4,2},{5,3},{6,4},{7,5},{8,6},{9,7},{10,... | collective-permute-start | bytes 294920 | tf_op jit(solution)/shard_map/ppermute | solution.py:204
  96.3 0.0 collective-permute-done.11
  96.3 1.9 %collective-permute-start.12 = (bf16[16,3072]{1,0:T(8,128)(2,1)S(1)}, bf16[16,3072]{1,0:T(8,128)(2,1)S(1)}, u32[]{:S(2)}, u32[]{:S(2)}) collective-permute-start(bf16[16,3072]{1,0:T(8,128)(2,1)S(1)} %copy-done.4), channel_id=1, source_target_pairs={{0,2},{1,3},{2,4},{3,5},{4,6},{5,7},{6,8},{7,9},{8,10},{9,11},{10,... | collective-permute-start | bytes 294920 | tf_op jit(solution)/shard_map/ppermute | solution.py:204
  98.2 0.0 collective-permute-done.10
  98.2 0.0 collective-permute-done.9
  98.2 0.0 collective-permute-done.8
  98.2 0.3 fusion.12
  98.5 0.4 convolution_add_fusion.2
  98.9 0.0 collective-permute-done.13
  98.9 5.1 %collective-permute-done.12 = bf16[16,3072]{1,0:T(8,128)(2,1)S(1)} collective-permute-done((bf16[16,3072]{1,0:T(8,128)(2,1)S(1)}, bf16[16,3072]{1,0:T(8,128)(2,1)S(1)}, u32[]{:S(2)}, u32[]{:S(2)}) %collective-permute-start.12) | collective-permute-done | bytes 98336 | tf_op jit(solution)/shard_map/ppermute | solution.py:204
  104.1 0.0 copy-start.1
  104.1 1.9 %collective-permute-start.15 = (bf16[128,3072]{1,0:T(8,128)(2,1)S(1)}, bf16[128,3072]{1,0:T(8,128)(2,1)S(1)}, u32[]{:S(2)}, u32[]{:S(2)}) collective-permute-start(bf16[128,3072]{1,0:T(8,128)(2,1)S(1)} %constant_dynamic-update-slice_fusion.refs_6_), channel_id=1, source_target_pairs={{0,1},{1,0},{2,3},{3,2},{4,5},{5,4},{6,7},{7,6},{8,9},{9,8},{10,11... | collective-permute-start | bytes 2359304 | tf_op jit(solution)/shard_map/ppermute | solution.py:238
  106.0 4.5 %collective-permute-start.16 = (f32[256,256]{1,0:T(8,128)S(1)}, f32[256,256]{1,0:T(8,128)S(1)}, u32[]{:S(2)}, u32[]{:S(2)}) collective-permute-start(f32[256,256]{1,0:T(8,128)S(1)} %fusion.11), channel_id=1, source_target_pairs={{0,128},{16,144},{32,160},{48,176},{64,192},{80,208},{96,224},{112... | collective-permute-start | bytes 786440 | tf_op jit(solution)/shard_map/ppermute | solution.py:14
  110.5 1.9 %collective-permute-start.14 = (bf16[256,256]{1,0:T(8,128)(2,1)S(1)}, bf16[256,256]{1,0:T(8,128)(2,1)S(1)}, u32[]{:S(2)}, u32[]{:S(2)}) collective-permute-start(bf16[256,256]{1,0:T(8,128)(2,1)S(1)} %convert_element_type.23), channel_id=1, source_target_pairs={{0,128},{16,144},{32,160},{48,176},{64,192},{80,208},{96,224},{112... | collective-permute-start | bytes 393224 | tf_op jit(solution)/shard_map/ppermute | solution.py:14
  112.5 13.0 %collective-permute-done.16 = f32[256,256]{1,0:T(8,128)S(1)} collective-permute-done((f32[256,256]{1,0:T(8,128)S(1)}, f32[256,256]{1,0:T(8,128)S(1)}, u32[]{:S(2)}, u32[]{:S(2)}) %collective-permute-start.16) | collective-permute-done | bytes 262176 | tf_op jit(solution)/shard_map/ppermute | solution.py:14
  125.5 0.4 fusion.13
  125.9 5.0 %collective-permute-done.14 = bf16[256,256]{1,0:T(8,128)(2,1)S(1)} collective-permute-done((bf16[256,256]{1,0:T(8,128)(2,1)S(1)}, bf16[256,256]{1,0:T(8,128)(2,1)S(1)}, u32[]{:S(2)}, u32[]{:S(2)}) %collective-permute-start.14) | collective-permute-done | bytes 131104 | tf_op jit(solution)/shard_map/ppermute | solution.py:14
  130.8 0.0 collective-permute-done.15.refs_7_
  130.8 0.3 fusion.14
  131.1 0.4 convolution_add_fusion.1
  131.6 3.4 %collective-permute-start.17 = (bf16[256,256]{1,0:T(8,128)(2,1)S(1)}, bf16[256,256]{1,0:T(8,128)(2,1)S(1)}, u32[]{:S(2)}, u32[]{:S(2)}) collective-permute-start(bf16[256,256]{1,0:T(8,128)(2,1)S(1)} %convert_element_type.24), channel_id=1, source_target_pairs={{0,256},{16,272},{32,288},{48,304},{64,320},{80,336},{96,352},{112... | collective-permute-start | bytes 393224 | tf_op jit(solution)/shard_map/ppermute | solution.py:14
  135.0 0.0 copy-done.1
  135.0 0.0 copy-done.2
  135.0 8.0 %trailing.1 = bf16[512,1792]{1,0:T(8,128)(2,1)} custom-call(bf16[512,2304]{1,0:T(8,128)(2,1)} %bitcast.44, bf16[512,2304]{1,0:T(8,128)(2,1)} %bitcast.45, bf16[2,256,256]{2,1,0:T(8,128)(2,1)} %bitcast.51, bf16[256,1792]{1,0:T(8,128)(2,1)} %all_gather.3.refs_0_.refs_3_, bf16[256,256]{1,0:T(8,128)(2,1)} %get-tuple-element.70.refs_4_, ...), custom_call_target="tpu_custom_call" | custom-call | flops 1207959552 | bytes 7077888 | tf_op jit(solution)/shard_map/trailing/pallas_call | solution.py:149
  143.0 0.0 collective-permute-done.17
  143.0 0.3 fusion.15
  143.3 1.1 fusion
  (13 shorter events, 0.1 us)
Async XLA Ops:
  0.6 44.3 %copy-start = (f32[1,256,256]{2,1,0:T(8,128)S(1)}, f32[1,256,256]{2,1,0:T(8,128)}, u32[]{:S(2)}) copy-start(f32[1,256,256]{2,1,0:T(8,128)} %param.6) | copy-start | bytes 786436
  0.6 44.3 %collective-permute-start.2 = (f32[256,256]{1,0:T(8,128)}, f32[256,256]{1,0:T(8,128)S(1)}, u32[]{:S(2)}, u32[]{:S(2)}) collective-permute-start(f32[256,256]{1,0:T(8,128)} %bitcast.46), channel_id=1, source_target_pairs={{0,48},{16,64},{32,80},{48,96},{64,112},{80,128},{96,144},{112,160... | collective-permute-start | bytes 786440 | tf_op jit(solution)/shard_map/ppermute | solution.py:14
  4.2 40.7 %collective-permute-start.1 = (f32[256,256]{1,0:T(8,128)}, f32[256,256]{1,0:T(8,128)S(1)}, u32[]{:S(2)}, u32[]{:S(2)}) collective-permute-start(f32[256,256]{1,0:T(8,128)} %bitcast.47), channel_id=1, source_target_pairs={{0,32},{16,48},{32,64},{48,80},{64,96},{80,112},{96,128},{112,144}... | collective-permute-start | bytes 786440 | tf_op jit(solution)/shard_map/ppermute | solution.py:14
  8.9 36.0 %collective-permute-start = (f32[256,256]{1,0:T(8,128)}, f32[256,256]{1,0:T(8,128)S(1)}, u32[]{:S(2)}, u32[]{:S(2)}) collective-permute-start(f32[256,256]{1,0:T(8,128)} %bitcast.48), channel_id=1, source_target_pairs={{0,16},{16,32},{32,48},{48,64},{64,80},{80,96},{96,112},{112,128},... | collective-permute-start | bytes 786440 | tf_op jit(solution)/shard_map/ppermute | solution.py:14
  44.9 8.8 %copy-start.3 = (bf16[256,256]{1,0:T(8,128)(2,1)S(1)}, bf16[256,256]{1,0:T(8,128)(2,1)}, u32[]{:S(2)}) copy-start(bf16[256,256]{1,0:T(8,128)(2,1)} %get-tuple-element.45) | copy-start | bytes 393220
  44.9 15.3 %copy-start.4 = (bf16[16,3072]{1,0:T(8,128)(2,1)S(1)}, bf16[16,3072]{1,0:T(8,128)(2,1)}, u32[]{:S(2)}) copy-start(bf16[16,3072]{1,0:T(8,128)(2,1)} %get-tuple-element.58) | copy-start | bytes 294916
  45.5 7.9 %collective-permute-start.3 = (bf16[256,256]{1,0:T(8,128)(2,1)}, bf16[256,256]{1,0:T(8,128)(2,1)S(1)}, u32[]{:S(2)}, u32[]{:S(2)}) collective-permute-start(bf16[256,256]{1,0:T(8,128)(2,1)} %get-tuple-element.45), channel_id=1, source_target_pairs={{0,16},{16,32},{32,48},{48,64},{64,80},{80,96},{96,112},{112,128},... | collective-permute-start | bytes 393224 | tf_op jit(solution)/shard_map/ppermute | solution.py:14
  54.4 29.0 %collective-permute-start.4 = (bf16[256,256]{1,0:T(8,128)(2,1)S(1)}, bf16[256,256]{1,0:T(8,128)(2,1)S(1)}, u32[]{:S(2)}, u32[]{:S(2)}) collective-permute-start(bf16[256,256]{1,0:T(8,128)(2,1)S(1)} %convert_element_type.21), channel_id=1, source_target_pairs={{0,32},{16,48},{32,64},{48,80},{64,96},{80,112},{96,128},{112,144}... | collective-permute-start | bytes 393224 | tf_op jit(solution)/shard_map/ppermute | solution.py:14
  60.2 16.5 %collective-permute-start.6 = (bf16[16,3072]{1,0:T(8,128)(2,1)S(1)}, bf16[16,3072]{1,0:T(8,128)(2,1)S(1)}, u32[]{:S(2)}, u32[]{:S(2)}) collective-permute-start(bf16[16,3072]{1,0:T(8,128)(2,1)S(1)} %copy-done.4), channel_id=1, source_target_pairs={{0,8},{1,9},{2,10},{3,11},{4,12},{5,13},{6,14},{7,15},{8,0},{9,1},... | collective-permute-start | bytes 294920 | tf_op jit(solution)/shard_map/ppermute | solution.py:204
  63.6 15.1 %collective-permute-start.5 = (bf16[16,3072]{1,0:T(8,128)(2,1)S(1)}, bf16[16,3072]{1,0:T(8,128)(2,1)S(1)}, u32[]{:S(2)}, u32[]{:S(2)}) collective-permute-start(bf16[16,3072]{1,0:T(8,128)(2,1)S(1)} %copy-done.4), channel_id=1, source_target_pairs={{0,10},{1,11},{2,12},{3,13},{4,14},{5,15},{6,0},{7,1},{8,2},{9,3},... | collective-permute-start | bytes 294920 | tf_op jit(solution)/shard_map/ppermute | solution.py:204
  67.8 28.4 %collective-permute-start.11 = (bf16[16,3072]{1,0:T(8,128)(2,1)S(1)}, bf16[16,3072]{1,0:T(8,128)(2,1)S(1)}, u32[]{:S(2)}, u32[]{:S(2)}) collective-permute-start(bf16[16,3072]{1,0:T(8,128)(2,1)S(1)} %copy-done.4), channel_id=1, source_target_pairs={{0,6},{1,7},{2,8},{3,9},{4,10},{5,11},{6,12},{7,13},{8,14},{9,15},... | collective-permute-start | bytes 294920 | tf_op jit(solution)/shard_map/ppermute | solution.py:204
  71.2 27.0 %collective-permute-start.10 = (bf16[16,3072]{1,0:T(8,128)(2,1)S(1)}, bf16[16,3072]{1,0:T(8,128)(2,1)S(1)}, u32[]{:S(2)}, u32[]{:S(2)}) collective-permute-start(bf16[16,3072]{1,0:T(8,128)(2,1)S(1)} %copy-done.4), channel_id=1, source_target_pairs={{0,12},{1,13},{2,14},{3,15},{4,0},{5,1},{6,2},{7,3},{8,4},{9,5},{1... | collective-permute-start | bytes 294920 | tf_op jit(solution)/shard_map/ppermute | solution.py:204
  76.7 21.5 %collective-permute-start.9 = (bf16[16,3072]{1,0:T(8,128)(2,1)S(1)}, bf16[16,3072]{1,0:T(8,128)(2,1)S(1)}, u32[]{:S(2)}, u32[]{:S(2)}) collective-permute-start(bf16[16,3072]{1,0:T(8,128)(2,1)S(1)} %copy-done.4), channel_id=1, source_target_pairs={{0,4},{1,5},{2,6},{3,7},{4,8},{5,9},{6,10},{7,11},{8,12},{9,13},{1... | collective-permute-start | bytes 294920 | tf_op jit(solution)/shard_map/ppermute | solution.py:204
  78.7 8.6 %collective-permute-start.7 = (f32[256,256]{1,0:T(8,128)S(1)}, f32[256,256]{1,0:T(8,128)S(1)}, u32[]{:S(2)}, u32[]{:S(2)}) collective-permute-start(f32[256,256]{1,0:T(8,128)S(1)} %fusion.9), channel_id=1, source_target_pairs={{0,64},{16,80},{32,96},{48,112},{64,128},{80,144},{96,160},{112,17... | collective-permute-start | bytes 786440 | tf_op jit(solution)/shard_map/ppermute | solution.py:14
  87.7 10.6 %collective-permute-start.8 = (bf16[256,256]{1,0:T(8,128)(2,1)S(1)}, bf16[256,256]{1,0:T(8,128)(2,1)S(1)}, u32[]{:S(2)}, u32[]{:S(2)}) collective-permute-start(bf16[256,256]{1,0:T(8,128)(2,1)S(1)} %convert_element_type.22), channel_id=1, source_target_pairs={{0,64},{16,80},{32,96},{48,112},{64,128},{80,144},{96,160},{112,17... | collective-permute-start | bytes 393224 | tf_op jit(solution)/shard_map/ppermute | solution.py:14
  92.1 6.9 %collective-permute-start.13 = (bf16[16,3072]{1,0:T(8,128)(2,1)S(1)}, bf16[16,3072]{1,0:T(8,128)(2,1)S(1)}, u32[]{:S(2)}, u32[]{:S(2)}) collective-permute-start(bf16[16,3072]{1,0:T(8,128)(2,1)S(1)} %copy-done.4), channel_id=1, source_target_pairs={{0,14},{1,15},{2,0},{3,1},{4,2},{5,3},{6,4},{7,5},{8,6},{9,7},{10,... | collective-permute-start | bytes 294920 | tf_op jit(solution)/shard_map/ppermute | solution.py:204
  96.3 7.7 %collective-permute-start.12 = (bf16[16,3072]{1,0:T(8,128)(2,1)S(1)}, bf16[16,3072]{1,0:T(8,128)(2,1)S(1)}, u32[]{:S(2)}, u32[]{:S(2)}) collective-permute-start(bf16[16,3072]{1,0:T(8,128)(2,1)S(1)} %copy-done.4), channel_id=1, source_target_pairs={{0,2},{1,3},{2,4},{3,5},{4,6},{5,7},{6,8},{7,9},{8,10},{9,11},{10,... | collective-permute-start | bytes 294920 | tf_op jit(solution)/shard_map/ppermute | solution.py:204
  104.1 30.9 %copy-start.1 = (bf16[128,3072]{1,0:T(8,128)(2,1)}, bf16[128,3072]{1,0:T(8,128)(2,1)S(1)}, u32[]{:S(2)}) copy-start(bf16[128,3072]{1,0:T(8,128)(2,1)S(1)} %constant_dynamic-update-slice_fusion.refs_6_) | copy-start | bytes 2359300
  104.1 26.7 %collective-permute-start.15 = (bf16[128,3072]{1,0:T(8,128)(2,1)S(1)}, bf16[128,3072]{1,0:T(8,128)(2,1)S(1)}, u32[]{:S(2)}, u32[]{:S(2)}) collective-permute-start(bf16[128,3072]{1,0:T(8,128)(2,1)S(1)} %constant_dynamic-update-slice_fusion.refs_6_), channel_id=1, source_target_pairs={{0,1},{1,0},{2,3},{3,2},{4,5},{5,4},{6,7},{7,6},{8,9},{9,8},{10,11... | collective-permute-start | bytes 2359304 | tf_op jit(solution)/shard_map/ppermute | solution.py:238
  106.0 19.4 %collective-permute-start.16 = (f32[256,256]{1,0:T(8,128)S(1)}, f32[256,256]{1,0:T(8,128)S(1)}, u32[]{:S(2)}, u32[]{:S(2)}) collective-permute-start(f32[256,256]{1,0:T(8,128)S(1)} %fusion.11), channel_id=1, source_target_pairs={{0,128},{16,144},{32,160},{48,176},{64,192},{80,208},{96,224},{112... | collective-permute-start | bytes 786440 | tf_op jit(solution)/shard_map/ppermute | solution.py:14
  110.5 20.3 %collective-permute-start.14 = (bf16[256,256]{1,0:T(8,128)(2,1)S(1)}, bf16[256,256]{1,0:T(8,128)(2,1)S(1)}, u32[]{:S(2)}, u32[]{:S(2)}) collective-permute-start(bf16[256,256]{1,0:T(8,128)(2,1)S(1)} %convert_element_type.23), channel_id=1, source_target_pairs={{0,128},{16,144},{32,160},{48,176},{64,192},{80,208},{96,224},{112... | collective-permute-start | bytes 393224 | tf_op jit(solution)/shard_map/ppermute | solution.py:14
  130.8 4.2 %copy-start.2 = (bf16[128,3072]{1,0:T(8,128)(2,1)}, bf16[128,3072]{1,0:T(8,128)(2,1)S(1)}, u32[]{:S(2)}) copy-start(bf16[128,3072]{1,0:T(8,128)(2,1)S(1)} %collective-permute-done.15.refs_7_) | copy-start | bytes 2359300
  131.6 11.5 %collective-permute-start.17 = (bf16[256,256]{1,0:T(8,128)(2,1)S(1)}, bf16[256,256]{1,0:T(8,128)(2,1)S(1)}, u32[]{:S(2)}, u32[]{:S(2)}) collective-permute-start(bf16[256,256]{1,0:T(8,128)(2,1)S(1)} %convert_element_type.24), channel_id=1, source_target_pairs={{0,256},{16,272},{32,288},{48,304},{64,320},{80,336},{96,352},{112... | collective-permute-start | bytes 393224 | tf_op jit(solution)/shard_map/ppermute | solution.py:14

commit v3 on v2

--- a/solution.py
+++ b/solution.py
@@ -38,14 +38,16 @@
     for i in range(chunks):
         part(i).start()
     me = lax.axis_index("blk")
-    at_row = lax.broadcasted_iota(jnp.int32, (3 * per, rows), 0)
-    at_lane = lax.broadcasted_iota(jnp.int32, (3 * per, rows), 1)
-    wanted = jnp.zeros((3 * per, rows), jnp.int32)
+    lanes = 128
+    at_row = lax.broadcasted_iota(jnp.int32, (3 * per, lanes), 0)
+    at_lane = lax.broadcasted_iota(jnp.int32, (3 * per, lanes), 1)
+    wanted = jnp.zeros((3 * per, lanes), jnp.int32)
     for k in range(3):
         for i in range(per):
-            node = nodes_ref[k, me * per + i] - me * rows
-            wanted = jnp.where(at_row == k * per + i, node, wanted)
-    picker = (wanted == at_lane).astype(F32).astype(BF16)
+            wanted = jnp.where(at_row == k * per + i, nodes_ref[k, me * per + i] - me * rows, wanted)
+    picker = jnp.concatenate(
+        [(wanted == at_lane + first).astype(F32).astype(BF16) for first in range(0, rows, lanes)], 1
+    )
     far_width = strip_ref.shape[1] - 3 * w
     for i in range(chunks):
         part(i).wait()
@@ -110,11 +112,10 @@
 
 
 def trailing_kernel(
-    w, per, panels_ref, block_ref, inverse_ref, near_ref, factor_ref, second_ref, own_ref, other_ref,
-    out_ref, one_ref, two_ref, far_ref,
+    w, panels_ref, block_ref, inverse_ref, near_ref, factor_ref, second_ref, far_one_ref, far_two_ref,
+    out_ref, one_ref, two_ref,
 ):
     step = pl.program_id(0)
-    half = far_ref.shape[1] // 2
 
     def finish(one_rows, two_rows):
         updated = reduced_by(block_ref[...], one_ref[...], one_rows)
@@ -122,14 +123,6 @@
 
     @pl.when(step == 0)
     def _():
-        me = lax.axis_index("blk")
-        chip, core = me // 2, lax.rem(me, 2)
-        chips = far_ref.shape[0] // (2 * per)
-        for m, shift in enumerate(chip_shifts(chips)):
-            source = 2 * lax.rem(chip + chips - shift, chips)
-            for ref, which in ((own_ref, core), (other_ref, 1 - core)):
-                at = pl.multiple_of((source + which) * per, per)
-                far_ref[pl.ds(at, per), :] = ref[m * per:(m + 1) * per, :]
         one_ref[...] = rounded_dot(panels_ref[:, :w], inverse_ref[0])
         panel = reduced_by(panels_ref[:, w:], one_ref[...], near_ref[:, :w])
         two_ref[...] = rounded_dot(panel, inverse_ref[1])
@@ -137,19 +130,19 @@
 
     @pl.when(step > 0)
     def _():
-        at = pl.multiple_of((step - 1) * w, w)
-        one_rows = far_ref[:, pl.ds(at, w)]
-        finish(one_rows, reduced_by(far_ref[:, pl.ds(half + at, w)], factor_ref[...], one_rows))
-
-
-def trailing_of(strip, inverses, near, factor_at_two, second_edge, own, other, per):
+        one_rows = far_one_ref[...]
+        finish(one_rows, reduced_by(far_two_ref[...], factor_ref[...], one_rows))
+
+
+def trailing_of(strip, inverses, near, factor_at_two, second_edge, far):
     rows, width = strip.shape
     w = near.shape[0]
+    steps = width // w - 2
     fixed = lambda i: (0, 0)
     return pl.pallas_call(
-        lambda *refs: trailing_kernel(w, per, *refs),
+        lambda *refs: trailing_kernel(w, *refs),
         out_shape=jax.ShapeDtypeStruct((rows, width - 2 * w), BF16),
-        grid=(width // w - 2,),
+        grid=(steps,),
         in_specs=[
             pl.BlockSpec((rows, 2 * w), fixed),
             pl.BlockSpec((rows, w), lambda i: (0, i + 2)),
@@ -157,24 +150,16 @@
             pl.BlockSpec((w, 2 * w), fixed),
             pl.BlockSpec((w, w), fixed),
             pl.BlockSpec((w, w), fixed),
-            pl.BlockSpec(own.shape, fixed),
-            pl.BlockSpec(own.shape, fixed),
+            pl.BlockSpec((w, w), lambda i: (0, jnp.maximum(i - 1, 0))),
+            pl.BlockSpec((w, w), lambda i: (0, steps - 1 + jnp.maximum(i - 1, 0))),
         ],
         out_specs=pl.BlockSpec((rows, w), lambda i: (0, i)),
-        scratch_shapes=[
-            pltpu.VMEM((rows, w), BF16),
-            pltpu.VMEM((rows, w), BF16),
-            pltpu.VMEM((w, own.shape[1]), BF16),
-        ],
+        scratch_shapes=[pltpu.VMEM((rows, w), BF16), pltpu.VMEM((rows, w), BF16)],
         cost_estimate=pl.CostEstimate(
             flops=4 * rows * w * width, bytes_accessed=4 * rows * width + 4 * w * width, transcendentals=0
         ),
         name="trailing",
-    )(strip, strip, inverses, near, factor_at_two, second_edge, own, other)
-
-
-def chip_shifts(chips):
-    return [0] + [s for by in range(1, chips // 2) for s in (by, chips - by)] + [chips // 2]
+    )(strip, strip, inverses, near, factor_at_two, second_edge, far, far)
 
 
 def body(panel_strip, pivot_inverses, coupling, pivot_nodes):
@@ -190,59 +175,39 @@
     near_here, far_here = picked_rows(pivot_nodes, strip, w, per)
     near = lax.all_gather(near_here, "blk", axis=0, tiled=True)
     boundary, factor_at_two, second_edge = boundary_of(near, inverses)
-    back_one, back_two, back_three, boundary, far_here = lax.optimization_barrier(
-        (back_one, back_two, back_three, boundary, far_here)
+    back_one, back_two, back_three, boundary = lax.optimization_barrier(
+        (back_one, back_two, back_three, boundary)
     )
-
-    shifts = chip_shifts(blocks // 2)
-    far_from = {0: far_here}
-
-    def send_far(gate, which):
-        gate, block = lax.optimization_barrier((gate, far_here))
-        for shift in which:
-            pairs = [(i, (i + 2 * shift) % blocks) for i in range(blocks)]
-            far_from[shift] = lax.ppermute(block, "blk", pairs)
-        return gate
-
-    def arrived(value, which):
-        value, *blocks_in = lax.optimization_barrier((value, *(far_from[s] for s in which)))
-        far_from.update(zip(which, blocks_in))
-        return value
 
     def advance(current, incoming, reach):
         return matmul_high(matmul_high(reach, incoming.astype(F32)), reach.T) + current
 
-    groups = [shifts[6:], shifts[3:6], shifts[1:3]]
-
     incoming = passed_along(boundary, "tm", 1)
-    span_two = send_far(matmul_high(span, back_one), groups[0])
+    span_two = matmul_high(span, back_one)
     span_four = matmul_high(span_two, matmul_high(back_two, back_three))
+    incoming, span_four = lax.optimization_barrier((incoming, span_four))
+    passed_four = passed_along(span_four, "tm", 4)
+    span_four, far_here = lax.optimization_barrier((span_four, far_here))
+    far = lax.all_to_all(jnp.tile(far_here, (blocks, 1)), "blk", 0, 0, tiled=True)
     current = advance(boundary.astype(F32), incoming, span)
 
-    current, span_four = lax.optimization_barrier((current, span_four))
     incoming = passed_along(current.astype(BF16), "tm", 2)
-    current = send_far(current, groups[1])
-    span_eight = matmul_high(span_four, passed_along(span_four, "tm", 4))
-    incoming = arrived(incoming, groups[0])
     current = advance(current, incoming, span_two)
 
+    span_eight = matmul_high(span_four, passed_four)
     current, span_eight = lax.optimization_barrier((current, span_eight))
     incoming = passed_along(current.astype(BF16), "tm", 4)
-    current = send_far(current, groups[2])
-    incoming = arrived(incoming, groups[1])
+    passed_eight = passed_along(span_eight, "tm", 8)
     current = advance(current, incoming, span_four)
 
-    current = arrived(current, groups[2])
     incoming = passed_along(current.astype(BF16), "tm", 8)
-    own = jnp.concatenate([far_from[s] for s in shifts], 0)
-    other = lax.ppermute(own, "blk", [(i, i ^ 1) for i in range(blocks)])
-    span_sixteen = matmul_high(span_eight, passed_along(span_eight, "tm", 8))
-    incoming, other, span_sixteen = lax.optimization_barrier((incoming, other, span_sixteen))
+    span_sixteen = matmul_high(span_eight, passed_eight)
+    incoming, span_sixteen = lax.optimization_barrier((incoming, span_sixteen))
     current = advance(current, incoming, span_eight)
 
-    current, other = lax.optimization_barrier((current, other))
+    current, far = lax.optimization_barrier((current, far))
     incoming = passed_along(current.astype(BF16), "tm", 16)
-    trailing = trailing_of(strip, inverses, near, factor_at_two, second_edge, own, other, per)
+    trailing = trailing_of(strip, inverses, near, factor_at_two, second_edge, far)
     incoming, trailing = lax.optimization_barrier((incoming, trailing))
     current = advance(current, incoming, span_sixteen)
     return (trailing[None], current[None])

time: 145 us -> 124 us (0.86)
  the two profiles are of different devices: /device:TPU:12 before, /device:TPU:68 now
where the time goes in v3:
time: 124 us; the launch traced here: 123 us
  starting transfers between devices  64.3 us (52%)
  blocking collectives  24.3 us (20%)
  Pallas kernels  13.9 us (11%)
  waiting for transfers between devices  11.5 us (9%)
  matrix products  6.77 us (5%)
  local copies, waits for them, and re-layouts  1.34 us (1%)
    ppermute x10, starting transfers between devices, passed_along(): return lax.ppermute(x, axis, [(i, i + by) for i in range(count - by)])  57.9 us
    all_gather x1, blocking collectives, body(): near = lax.all_gather(near_here, 'blk', axis=0, tiled=True)  24.3 us
    ppermute x10, waiting for transfers between devices, passed_along(): return lax.ppermute(x, axis, [(i, i + by) for i in range(count - by)])  10.1 us
    pallas_call x1, Pallas kernels, trailing_of(): pl.pallas_call(lambda *refs: trailing_kernel(w, *refs), out_shape=jax.Sha...  7.88 us
    dot_general x15, matrix products, matmul_high(): jnp.dot(left, right, precision=lax.Precision.HIGHEST, preferred_element_t...  6.77 us
    all_to_all x1, starting transfers between devices, body(): lax.all_to_all(jnp.tile(far_here, (blocks, 1)), 'blk', 0, 0, tiled=True)  6.35 us
    pallas_call x1, Pallas kernels, picked_rows(): pl.pallas_call(lambda *refs: pick_kernel(w, per, chunks, *refs), out_shap...  3.46 us
    pallas_call x1, Pallas kernels, boundary_of(): pl.pallas_call(lambda *refs: boundary_kernel(w, *refs), out_shape=(block,...  2.58 us
  transfers between devices with their start and end apart: 11, of which 5 were waited for; matrix products, arithmetic and copies ran while one was open for 4% of the time, Pallas kernels for 11%

profile of v3, /device:TPU:68, one launch (start us, length us, event | category | flops | bytes accessed | tf_op | source)
XLA Modules:
  0.0 122.9 jit_solution(4670633962904906936)
XLA Ops:
  0.6 3.5 %collective-permute-start.2 = (f32[256,256]{1,0:T(8,128)}, f32[256,256]{1,0:T(8,128)S(1)}, u32[]{:S(2)}, u32[]{:S(2)}) collective-permute-start(f32[256,256]{1,0:T(8,128)} %bitcast.47), channel_id=1, source_target_pairs={{0,48},{16,64},{32,80},{48,96},{64,112},{80,128},{96,144},{112,160... | collective-permute-start | bytes 786440 | tf_op jit(solution)/shard_map/ppermute | solution.py:14
  4.1 4.6 %collective-permute-start.1 = (f32[256,256]{1,0:T(8,128)}, f32[256,256]{1,0:T(8,128)S(1)}, u32[]{:S(2)}, u32[]{:S(2)}) collective-permute-start(f32[256,256]{1,0:T(8,128)} %bitcast.48), channel_id=1, source_target_pairs={{0,32},{16,48},{32,64},{48,80},{64,96},{80,112},{96,128},{112,144}... | collective-permute-start | bytes 786440 | tf_op jit(solution)/shard_map/ppermute | solution.py:14
  8.7 2.8 %collective-permute-start = (f32[256,256]{1,0:T(8,128)}, f32[256,256]{1,0:T(8,128)S(1)}, u32[]{:S(2)}, u32[]{:S(2)}) collective-permute-start(f32[256,256]{1,0:T(8,128)} %bitcast.49), channel_id=1, source_target_pairs={{0,16},{16,32},{32,48},{48,64},{64,80},{80,96},{96,112},{112,128},... | collective-permute-start | bytes 786440 | tf_op jit(solution)/shard_map/ppermute | solution.py:14
  11.5 0.0 copy-start.1
  11.6 3.5 %pick.1 = (bf16[16,1792]{1,0:T(8,128)(2,1)}, bf16[16,3072]{1,0:T(8,128)(2,1)}) custom-call(s32[3,256]{1,0:T(4,128)} %refs_0_.1, bf16[512,2304]{1,0:T(8,128)(2,1)} %bitcast.42), custom_call_target="tpu_custom_call" | custom-call | flops 113246208 | bytes 2359296 | tf_op jit(solution)/shard_map/pick/pallas_call | solution.py:70
  15.0 24.3 %all_gather.3.refs_0_.refs_3_ = bf16[256,1792]{1,0:T(8,128)(2,1)} all-gather(bf16[16,1792]{1,0:T(8,128)(2,1)} %get-tuple-element.23), channel_id=1, replica_groups=mesh['tm'=32,'blk'=16] {'blk'}, dimensions={0}, use_global_device_ids=true | all-gather | bytes 974848 | tf_op jit(solution)/shard_map/all_gather | solution.py:176
  39.3 0.0 copy-start.3
  39.3 2.6 %boundary.1 = (bf16[256,256]{1,0:T(8,128)(2,1)}, bf16[256,256]{1,0:T(8,128)(2,1)}, bf16[256,256]{1,0:T(8,128)(2,1)}) custom-call(bf16[256,1792]{1,0:T(8,128)(2,1)} %all_gather.3.refs_0_.refs_3_, bf16[2,256,256]{2,1,0:T(8,128)(2,1)} %bitcast.51), custom_call_target="tpu_custom_call" | custom-call | flops 234881024 | bytes 1572864 | tf_op jit(solution)/shard_map/boundary/pallas_call | solution.py:104
  41.9 0.0 collective-permute-done.2
  41.9 0.0 collective-permute-done.1
  41.9 0.0 collective-permute-done
  41.9 0.0 copy-done.1
  41.9 0.6 fusion.6
  42.5 4.0 %collective-permute-start.3 = (bf16[256,256]{1,0:T(8,128)(2,1)}, bf16[256,256]{1,0:T(8,128)(2,1)S(1)}, u32[]{:S(2)}, u32[]{:S(2)}) collective-permute-start(bf16[256,256]{1,0:T(8,128)(2,1)} %get-tuple-element.26), channel_id=1, source_target_pairs={{0,16},{16,32},{32,48},{48,64},{64,80},{80,96},{96,112},{112,128},... | collective-permute-start | bytes 393224 | tf_op jit(solution)/shard_map/ppermute | solution.py:14
  46.5 0.4 fusion.9
  46.9 0.6 fusion.10
  47.5 2.9 %collective-permute-done.3 = bf16[256,256]{1,0:T(8,128)(2,1)S(1)} collective-permute-done((bf16[256,256]{1,0:T(8,128)(2,1)}, bf16[256,256]{1,0:T(8,128)(2,1)S(1)}, u32[]{:S(2)}, u32[]{:S(2)}) %collective-permute-start.3) | collective-permute-done | bytes 131104 | tf_op jit(solution)/shard_map/ppermute | solution.py:14
  50.3 0.0 copy-done.3
  50.3 1.3 %tile.2 = bf16[16,16,3072]{2,1,0:T(8,128)(2,1)} broadcast(bf16[16,3072]{1,0:T(8,128)(2,1)S(1)} %copy-done.3), dimensions={1,2} | broadcast | bytes 1671168 | tf_op jit(solution)/shard_map/tile | solution.py:191
  51.7 0.0 copy-start.2
  51.7 6.4 %all-to-all-start = ((bf16[16,16,3072]{2,1,0:T(8,128)(2,1)}), bf16[16,16,3072]{2,1,0:T(8,128)(2,1)S(1)}, u32[]{:S(2)}, u32[]{:S(2)}) async-start(bf16[16,16,3072]{2,1,0:T(8,128)(2,1)} %tile.2), calls=%async_computation | async-start | bytes 3145728 | tf_op jit(solution)/shard_map/all_to_all | solution.py:191
  58.0 0.3 fusion.4
  58.4 0.0 copy-done.2
  58.4 0.6 fusion.1
  59.0 5.8 %collective-permute-start.4 = (bf16[256,256]{1,0:T(8,128)(2,1)S(1)}, bf16[256,256]{1,0:T(8,128)(2,1)S(1)}, u32[]{:S(2)}, u32[]{:S(2)}) collective-permute-start(bf16[256,256]{1,0:T(8,128)(2,1)S(1)} %get-tuple-element.44), channel_id=1, source_target_pairs={{0,32},{16,48},{32,64},{48,80},{64,96},{80,112},{96,128},{112,144}... | collective-permute-start | bytes 393224 | tf_op jit(solution)/shard_map/ppermute | solution.py:14
  64.8 3.5 %collective-permute-start.5 = (f32[256,256]{1,0:T(8,128)S(1)}, f32[256,256]{1,0:T(8,128)S(1)}, u32[]{:S(2)}, u32[]{:S(2)}) collective-permute-start(f32[256,256]{1,0:T(8,128)S(1)} %fusion.10), channel_id=1, source_target_pairs={{0,64},{16,80},{32,96},{48,112},{64,128},{80,144},{96,160},{112,17... | collective-permute-start | bytes 786440 | tf_op jit(solution)/shard_map/ppermute | solution.py:14
  68.3 0.0 collective-permute-done.4
  68.3 0.4 fusion.11
  68.7 0.4 convolution_add_fusion.3
  69.1 4.8 %collective-permute-done.5 = f32[256,256]{1,0:T(8,128)S(1)} collective-permute-done((f32[256,256]{1,0:T(8,128)S(1)}, f32[256,256]{1,0:T(8,128)S(1)}, u32[]{:S(2)}, u32[]{:S(2)}) %collective-permute-start.5) | collective-permute-done | bytes 262176 | tf_op jit(solution)/shard_map/ppermute | solution.py:14
  73.9 0.4 fusion.12
  74.3 4.7 %collective-permute-start.6 = (bf16[256,256]{1,0:T(8,128)(2,1)S(1)}, bf16[256,256]{1,0:T(8,128)(2,1)S(1)}, u32[]{:S(2)}, u32[]{:S(2)}) collective-permute-start(bf16[256,256]{1,0:T(8,128)(2,1)S(1)} %convert_element_type.22), channel_id=1, source_target_pairs={{0,64},{16,80},{32,96},{48,112},{64,128},{80,144},{96,160},{112,17... | collective-permute-start | bytes 393224 | tf_op jit(solution)/shard_map/ppermute | solution.py:14
  79.0 5.7 %collective-permute-start.8 = (f32[256,256]{1,0:T(8,128)S(1)}, f32[256,256]{1,0:T(8,128)S(1)}, u32[]{:S(2)}, u32[]{:S(2)}) collective-permute-start(f32[256,256]{1,0:T(8,128)S(1)} %fusion.12), channel_id=1, source_target_pairs={{0,128},{16,144},{32,160},{48,176},{64,192},{80,208},{96,224},{112... | collective-permute-start | bytes 786440 | tf_op jit(solution)/shard_map/ppermute | solution.py:14
  84.7 0.0 collective-permute-done.6
  84.7 0.3 fusion.13
  85.0 0.4 fusion.8
  85.4 3.7 %collective-permute-start.7 = (bf16[256,256]{1,0:T(8,128)(2,1)S(1)}, bf16[256,256]{1,0:T(8,128)(2,1)S(1)}, u32[]{:S(2)}, u32[]{:S(2)}) collective-permute-start(bf16[256,256]{1,0:T(8,128)(2,1)S(1)} %get-tuple-element.46), channel_id=1, source_target_pairs={{0,128},{16,144},{32,160},{48,176},{64,192},{80,208},{96,224},{112... | collective-permute-start | bytes 393224 | tf_op jit(solution)/shard_map/ppermute | solution.py:14
  89.2 0.8 collective-permute-done.8
  90.0 0.4 fusion.14
  90.4 1.6 %collective-permute-done.7 = bf16[256,256]{1,0:T(8,128)(2,1)S(1)} collective-permute-done((bf16[256,256]{1,0:T(8,128)(2,1)S(1)}, bf16[256,256]{1,0:T(8,128)(2,1)S(1)}, u32[]{:S(2)}, u32[]{:S(2)}) %collective-permute-start.7) | collective-permute-done | bytes 131104 | tf_op jit(solution)/shard_map/ppermute | solution.py:14
  92.0 0.3 fusion.15
  92.3 0.4 convolution_add_fusion.1
  92.7 1.4 %all-to-all-done = bf16[16,16,3072]{2,1,0:T(8,128)(2,1)S(1)} async-done(((bf16[16,16,3072]{2,1,0:T(8,128)(2,1)}), bf16[16,16,3072]{2,1,0:T(8,128)(2,1)S(1)}, u32[]{:S(2)}, u32[]{:S(2)}) %all-to-all-start) | async-done | bytes 1572896 | tf_op jit(solution)/shard_map/all_to_all | solution.py:191
  94.1 0.0 copy-start
  94.1 19.5 %collective-permute-start.9 = (bf16[256,256]{1,0:T(8,128)(2,1)S(1)}, bf16[256,256]{1,0:T(8,128)(2,1)S(1)}, u32[]{:S(2)}, u32[]{:S(2)}) collective-permute-start(bf16[256,256]{1,0:T(8,128)(2,1)S(1)} %convert_element_type.24), channel_id=1, source_target_pairs={{0,256},{16,272},{32,288},{48,304},{64,320},{80,336},{96,352},{112... | collective-permute-start | bytes 393224 | tf_op jit(solution)/shard_map/ppermute | solution.py:14
  113.6 0.0 copy-done
  113.6 7.9 %trailing.1 = bf16[512,1792]{1,0:T(8,128)(2,1)} custom-call(bf16[512,2304]{1,0:T(8,128)(2,1)} %bitcast.43, bf16[512,2304]{1,0:T(8,128)(2,1)} %bitcast.44, bf16[2,256,256]{2,1,0:T(8,128)(2,1)} %bitcast.52, bf16[256,1792]{1,0:T(8,128)(2,1)} %all_gather.3.refs_0_.refs_3_, bf16[256,256]{1,0:T(8,128)(2,1)} %get-tuple-element.38.refs_4_, ...), custom_call_target="tpu_custom_call" | custom-call | flops 1207959552 | bytes 7077888 | tf_op jit(solution)/shard_map/trailing/pallas_call | solution.py:142
  121.5 0.0 collective-permute-done.9
  121.5 0.3 fusion.16
  121.8 1.1 fusion
  (2 shorter events, 0.0 us)
Async XLA Ops:
  0.6 41.2 %collective-permute-start.2 = (f32[256,256]{1,0:T(8,128)}, f32[256,256]{1,0:T(8,128)S(1)}, u32[]{:S(2)}, u32[]{:S(2)}) collective-permute-start(f32[256,256]{1,0:T(8,128)} %bitcast.47), channel_id=1, source_target_pairs={{0,48},{16,64},{32,80},{48,96},{64,112},{80,128},{96,144},{112,160... | collective-permute-start | bytes 786440 | tf_op jit(solution)/shard_map/ppermute | solution.py:14
  4.1 37.8 %collective-permute-start.1 = (f32[256,256]{1,0:T(8,128)}, f32[256,256]{1,0:T(8,128)S(1)}, u32[]{:S(2)}, u32[]{:S(2)}) collective-permute-start(f32[256,256]{1,0:T(8,128)} %bitcast.48), channel_id=1, source_target_pairs={{0,32},{16,48},{32,64},{48,80},{64,96},{80,112},{96,128},{112,144}... | collective-permute-start | bytes 786440 | tf_op jit(solution)/shard_map/ppermute | solution.py:14
  8.7 33.1 %collective-permute-start = (f32[256,256]{1,0:T(8,128)}, f32[256,256]{1,0:T(8,128)S(1)}, u32[]{:S(2)}, u32[]{:S(2)}) collective-permute-start(f32[256,256]{1,0:T(8,128)} %bitcast.49), channel_id=1, source_target_pairs={{0,16},{16,32},{32,48},{48,64},{64,80},{80,96},{96,112},{112,128},... | collective-permute-start | bytes 786440 | tf_op jit(solution)/shard_map/ppermute | solution.py:14
  11.5 30.3 %copy-start.1 = (f32[1,256,256]{2,1,0:T(8,128)S(1)}, f32[1,256,256]{2,1,0:T(8,128)}, u32[]{:S(2)}) copy-start(f32[1,256,256]{2,1,0:T(8,128)} %param.6) | copy-start | bytes 786436
  39.3 11.1 %copy-start.3 = (bf16[16,3072]{1,0:T(8,128)(2,1)S(1)}, bf16[16,3072]{1,0:T(8,128)(2,1)}, u32[]{:S(2)}) copy-start(bf16[16,3072]{1,0:T(8,128)(2,1)} %get-tuple-element.36) | copy-start | bytes 294916
  42.5 7.9 %collective-permute-start.3 = (bf16[256,256]{1,0:T(8,128)(2,1)}, bf16[256,256]{1,0:T(8,128)(2,1)S(1)}, u32[]{:S(2)}, u32[]{:S(2)}) collective-permute-start(bf16[256,256]{1,0:T(8,128)(2,1)} %get-tuple-element.26), channel_id=1, source_target_pairs={{0,16},{16,32},{32,48},{48,64},{64,80},{80,96},{96,112},{112,128},... | collective-permute-start | bytes 393224 | tf_op jit(solution)/shard_map/ppermute | solution.py:14
  51.7 6.7 %copy-start.2 = (bf16[256,256]{1,0:T(8,128)(2,1)S(1)}, bf16[256,256]{1,0:T(8,128)(2,1)}, u32[]{:S(2)}) copy-start(bf16[256,256]{1,0:T(8,128)(2,1)} %get-tuple-element.26) | copy-start | bytes 393220
  51.7 42.4 %all-to-all-start = ((bf16[16,16,3072]{2,1,0:T(8,128)(2,1)}), bf16[16,16,3072]{2,1,0:T(8,128)(2,1)S(1)}, u32[]{:S(2)}, u32[]{:S(2)}) async-start(bf16[16,16,3072]{2,1,0:T(8,128)(2,1)} %tile.2), calls=%async_computation | async-start | bytes 3145728 | tf_op jit(solution)/shard_map/all_to_all | solution.py:191
  59.0 9.3 %collective-permute-start.4 = (bf16[256,256]{1,0:T(8,128)(2,1)S(1)}, bf16[256,256]{1,0:T(8,128)(2,1)S(1)}, u32[]{:S(2)}, u32[]{:S(2)}) collective-permute-start(bf16[256,256]{1,0:T(8,128)(2,1)S(1)} %get-tuple-element.44), channel_id=1, source_target_pairs={{0,32},{16,48},{32,64},{48,80},{64,96},{80,112},{96,128},{112,144}... | collective-permute-start | bytes 393224 | tf_op jit(solution)/shard_map/ppermute | solution.py:14
  64.8 9.1 %collective-permute-start.5 = (f32[256,256]{1,0:T(8,128)S(1)}, f32[256,256]{1,0:T(8,128)S(1)}, u32[]{:S(2)}, u32[]{:S(2)}) collective-permute-start(f32[256,256]{1,0:T(8,128)S(1)} %fusion.10), channel_id=1, source_target_pairs={{0,64},{16,80},{32,96},{48,112},{64,128},{80,144},{96,160},{112,17... | collective-permute-start | bytes 786440 | tf_op jit(solution)/shard_map/ppermute | solution.py:14
  74.3 10.4 %collective-permute-start.6 = (bf16[256,256]{1,0:T(8,128)(2,1)S(1)}, bf16[256,256]{1,0:T(8,128)(2,1)S(1)}, u32[]{:S(2)}, u32[]{:S(2)}) collective-permute-start(bf16[256,256]{1,0:T(8,128)(2,1)S(1)} %convert_element_type.22), channel_id=1, source_target_pairs={{0,64},{16,80},{32,96},{48,112},{64,128},{80,144},{96,160},{112,17... | collective-permute-start | bytes 393224 | tf_op jit(solution)/shard_map/ppermute | solution.py:14
  79.0 11.0 %collective-permute-start.8 = (f32[256,256]{1,0:T(8,128)S(1)}, f32[256,256]{1,0:T(8,128)S(1)}, u32[]{:S(2)}, u32[]{:S(2)}) collective-permute-start(f32[256,256]{1,0:T(8,128)S(1)} %fusion.12), channel_id=1, source_target_pairs={{0,128},{16,144},{32,160},{48,176},{64,192},{80,208},{96,224},{112... | collective-permute-start | bytes 786440 | tf_op jit(solution)/shard_map/ppermute | solution.py:14
  85.4 6.6 %collective-permute-start.7 = (bf16[256,256]{1,0:T(8,128)(2,1)S(1)}, bf16[256,256]{1,0:T(8,128)(2,1)S(1)}, u32[]{:S(2)}, u32[]{:S(2)}) collective-permute-start(bf16[256,256]{1,0:T(8,128)(2,1)S(1)} %get-tuple-element.46), channel_id=1, source_target_pairs={{0,128},{16,144},{32,160},{48,176},{64,192},{80,208},{96,224},{112... | collective-permute-start | bytes 393224 | tf_op jit(solution)/shard_map/ppermute | solution.py:14
  94.1 19.6 %copy-start = (bf16[16,16,3072]{2,1,0:T(8,128)(2,1)}, bf16[16,16,3072]{2,1,0:T(8,128)(2,1)S(1)}, u32[]{:S(2)}) copy-start(bf16[16,16,3072]{2,1,0:T(8,128)(2,1)S(1)} %all-to-all-done) | copy-start | bytes 4718596
  94.1 27.4 %collective-permute-start.9 = (bf16[256,256]{1,0:T(8,128)(2,1)S(1)}, bf16[256,256]{1,0:T(8,128)(2,1)S(1)}, u32[]{:S(2)}, u32[]{:S(2)}) collective-permute-start(bf16[256,256]{1,0:T(8,128)(2,1)S(1)} %convert_element_type.24), channel_id=1, source_target_pairs={{0,256},{16,272},{32,288},{48,304},{64,320},{80,336},{96,352},{112... | collective-permute-start | bytes 393224 | tf_op jit(solution)/shard_map/ppermute | solution.py:14

commit v4 on v3

--- a/solution.py
+++ b/solution.py
@@ -27,7 +27,7 @@
     return (block.astype(F32) - product).astype(BF16)
 
 
-def pick_kernel(w, per, chunks, nodes_ref, strip_hbm, near_ref, far_ref, strip_ref, sems):
+def pick_kernel(w, per, chunks, nodes_hbm, strip_hbm, near_ref, far_ref, strip_ref, nodes_ref, sems):
     rows = strip_ref.shape[0]
     cols = strip_ref.shape[1] // chunks
 
@@ -35,8 +35,11 @@
         at = pl.ds(i * cols, cols)
         return pltpu.make_async_copy(strip_hbm.at[:, at], strip_ref.at[:, at], sems.at[i])
 
+    nodes = pltpu.make_async_copy(nodes_hbm, nodes_ref, sems.at[chunks])
+    nodes.start()
     for i in range(chunks):
         part(i).start()
+    nodes.wait()
     me = lax.axis_index("blk")
     lanes = 128
     at_row = lax.broadcasted_iota(jnp.int32, (3 * per, lanes), 0)
@@ -60,8 +63,9 @@
             near_ref[:, 3 * w:4 * w] = two[:, 2 * w:]
             near_ref[:, 4 * w:] = edge
         else:
-            far_ref[:, (i - 1) * cols:i * cols] = one
-            far_ref[:, far_width + (i - 1) * cols:far_width + i * cols] = two
+            for row in range(0, far_ref.shape[0], per):
+                far_ref[row:row + per, (i - 1) * cols:i * cols] = one
+                far_ref[row:row + per, far_width + (i - 1) * cols:far_width + i * cols] = two
 
 
 def picked_rows(pivot_nodes, strip, w, per):
@@ -69,13 +73,14 @@
     chunks = width // (3 * w)
     return pl.pallas_call(
         lambda *refs: pick_kernel(w, per, chunks, *refs),
-        out_shape=(
-            jax.ShapeDtypeStruct((per, 7 * w), BF16),
-            jax.ShapeDtypeStruct((per, 2 * (width - 3 * w)), BF16),
-        ),
-        in_specs=[pl.BlockSpec(memory_space=pltpu.SMEM), pl.BlockSpec(memory_space=pl.ANY)],
+        out_shape=(pltpu.VMEM((per, 7 * w), BF16), pltpu.VMEM((w, 2 * (width - 3 * w)), BF16)),
+        in_specs=[pl.BlockSpec(memory_space=pl.ANY), pl.BlockSpec(memory_space=pl.ANY)],
         out_specs=(pl.BlockSpec(memory_space=pltpu.VMEM), pl.BlockSpec(memory_space=pltpu.VMEM)),
-        scratch_shapes=[pltpu.VMEM((rows, width), BF16), pltpu.SemaphoreType.DMA((chunks,))],
+        scratch_shapes=[
+            pltpu.VMEM((rows, width), BF16),
+            pltpu.SMEM(pivot_nodes.shape, jnp.int32),
+            pltpu.SemaphoreType.DMA((chunks + 1,)),
+        ],
         cost_estimate=pl.CostEstimate(
             flops=2 * 3 * per * rows * width, bytes_accessed=2 * rows * width, transcendentals=0
         ),
@@ -99,7 +104,8 @@
 
 def boundary_of(near, inverses):
     w = near.shape[0]
-    block = jax.ShapeDtypeStruct((w, w), BF16)
+    block = pltpu.VMEM((w, w), BF16)
+    near = pltpu.with_memory_space_constraint(near, pltpu.VMEM)
     vmem = pl.BlockSpec(memory_space=pltpu.VMEM)
     return pl.pallas_call(
         lambda *refs: boundary_kernel(w, *refs),
@@ -112,10 +118,10 @@
 
 
 def trailing_kernel(
-    w, panels_ref, block_ref, inverse_ref, near_ref, factor_ref, second_ref, far_one_ref, far_two_ref,
-    out_ref, one_ref, two_ref,
+    w, panels_ref, block_ref, inverse_ref, near_ref, factor_ref, second_ref, far_ref, out_ref, one_ref, two_ref
 ):
     step = pl.program_id(0)
+    half = far_ref.shape[1] // 2
 
     def finish(one_rows, two_rows):
         updated = reduced_by(block_ref[...], one_ref[...], one_rows)
@@ -126,32 +132,32 @@
         one_ref[...] = rounded_dot(panels_ref[:, :w], inverse_ref[0])
         panel = reduced_by(panels_ref[:, w:], one_ref[...], near_ref[:, :w])
         two_ref[...] = rounded_dot(panel, inverse_ref[1])
-        finish(near_ref[:, w:], second_ref[...])
+        finish(near_ref[:, w:2 * w], second_ref[...])
 
     @pl.when(step > 0)
     def _():
-        one_rows = far_one_ref[...]
-        finish(one_rows, reduced_by(far_two_ref[...], factor_ref[...], one_rows))
+        at = pl.multiple_of((step - 1) * w, w)
+        one_rows = far_ref[:, pl.ds(at, w)]
+        finish(one_rows, reduced_by(far_ref[:, pl.ds(half + at, w)], factor_ref[...], one_rows))
+
+
+def in_vmem(*arrays):
+    return tuple(pltpu.with_memory_space_constraint(x, pltpu.VMEM) for x in arrays)
 
 
 def trailing_of(strip, inverses, near, factor_at_two, second_edge, far):
     rows, width = strip.shape
     w = near.shape[0]
-    steps = width // w - 2
-    fixed = lambda i: (0, 0)
+    vmem = pl.BlockSpec(memory_space=pltpu.VMEM)
     return pl.pallas_call(
         lambda *refs: trailing_kernel(w, *refs),
         out_shape=jax.ShapeDtypeStruct((rows, width - 2 * w), BF16),
-        grid=(steps,),
+        grid=(width // w - 2,),
         in_specs=[
-            pl.BlockSpec((rows, 2 * w), fixed),
+            pl.BlockSpec((rows, 2 * w), lambda i: (0, 0)),
             pl.BlockSpec((rows, w), lambda i: (0, i + 2)),
             pl.BlockSpec((2, w, w), lambda i: (0, 0, 0)),
-            pl.BlockSpec((w, 2 * w), fixed),
-            pl.BlockSpec((w, w), fixed),
-            pl.BlockSpec((w, w), fixed),
-            pl.BlockSpec((w, w), lambda i: (0, jnp.maximum(i - 1, 0))),
-            pl.BlockSpec((w, w), lambda i: (0, steps - 1 + jnp.maximum(i - 1, 0))),
+            vmem, vmem, vmem, vmem,
         ],
         out_specs=pl.BlockSpec((rows, w), lambda i: (0, i)),
         scratch_shapes=[pltpu.VMEM((rows, w), BF16), pltpu.VMEM((rows, w), BF16)],
@@ -159,7 +165,7 @@
             flops=4 * rows * w * width, bytes_accessed=4 * rows * width + 4 * w * width, transcendentals=0
         ),
         name="trailing",
-    )(strip, strip, inverses, near, factor_at_two, second_edge, far, far)
+    )(strip, strip, inverses, *in_vmem(near, factor_at_two, second_edge, far))
 
 
 def body(panel_strip, pivot_inverses, coupling, pivot_nodes):
@@ -174,6 +180,8 @@
 
     near_here, far_here = picked_rows(pivot_nodes, strip, w, per)
     near = lax.all_gather(near_here, "blk", axis=0, tiled=True)
+    near, far_here = lax.optimization_barrier((near, far_here))
+    far = lax.all_to_all(far_here, "blk", 0, 0, tiled=True)
     boundary, factor_at_two, second_edge = boundary_of(near, inverses)
     back_one, back_two, back_three, boundary = lax.optimization_barrier(
         (back_one, back_two, back_three, boundary)
@@ -182,31 +190,37 @@
     def advance(current, incoming, reach):
         return matmul_high(matmul_high(reach, incoming.astype(F32)), reach.T) + current
 
+    def half_product(reach, by):
+        half = lax.dynamic_slice_in_dim(reach, lax.axis_index("blk") % 2 * (w // 2), w // 2, 1)
+        return matmul_high(reach, passed_along(half, "tm", by))
+
+    def joined(half):
+        pairs = [[i, i + 1] for i in range(0, blocks, 2)]
+        return lax.all_gather(half, "blk", axis=1, tiled=True, axis_index_groups=pairs)
+
     incoming = passed_along(boundary, "tm", 1)
     span_two = matmul_high(span, back_one)
     span_four = matmul_high(span_two, matmul_high(back_two, back_three))
-    incoming, span_four = lax.optimization_barrier((incoming, span_four))
-    passed_four = passed_along(span_four, "tm", 4)
-    span_four, far_here = lax.optimization_barrier((span_four, far_here))
-    far = lax.all_to_all(jnp.tile(far_here, (blocks, 1)), "blk", 0, 0, tiled=True)
+    half_eight = half_product(span_four, 4)
     current = advance(boundary.astype(F32), incoming, span)
 
     incoming = passed_along(current.astype(BF16), "tm", 2)
+    incoming, half_eight = lax.optimization_barrier((incoming, half_eight))
     current = advance(current, incoming, span_two)
 
-    span_eight = matmul_high(span_four, passed_four)
-    current, span_eight = lax.optimization_barrier((current, span_eight))
     incoming = passed_along(current.astype(BF16), "tm", 4)
-    passed_eight = passed_along(span_eight, "tm", 8)
+    span_eight = joined(half_eight)
+    half_sixteen = half_product(span_eight, 8)
+    incoming, span_eight = lax.optimization_barrier((incoming, span_eight))
     current = advance(current, incoming, span_four)
 
     incoming = passed_along(current.astype(BF16), "tm", 8)
-    span_sixteen = matmul_high(span_eight, passed_eight)
-    incoming, span_sixteen = lax.optimization_barrier((incoming, span_sixteen))
+    incoming, half_sixteen = lax.optimization_barrier((incoming, half_sixteen))
     current = advance(current, incoming, span_eight)
 
     current, far = lax.optimization_barrier((current, far))
     incoming = passed_along(current.astype(BF16), "tm", 16)
+    span_sixteen = joined(half_sixteen)
     trailing = trailing_of(strip, inverses, near, factor_at_two, second_edge, far)
     incoming, trailing = lax.optimization_barrier((incoming, trailing))
     current = advance(current, incoming, span_sixteen)

time: 124 us -> 114 us (0.919)
  the two profiles are of different devices: /device:TPU:68 before, /device:TPU:1 now
where the time goes in v4:
time: 114 us; the launch traced here: 113 us
  starting transfers between devices  49.8 us (44%)
  blocking collectives  37.3 us (33%)
  Pallas kernels  10.9 us (10%)
  matrix products  8.66 us (8%)
  waiting for transfers between devices  3.43 us (3%)
  local copies, waits for them, and re-layouts  1.17 us (1%)
    ppermute x10, starting transfers between devices, passed_along(): return lax.ppermute(x, axis, [(i, i + by) for i in range(count - by)])  46 us
    all_gather x1, blocking collectives, body(): near = lax.all_gather(near_here, 'blk', axis=0, tiled=True)  27 us
    all_gather x2, blocking collectives, joined(): lax.all_gather(half, 'blk', axis=1, tiled=True, axis_index_groups=pairs)  10.3 us
    dot_general x15, matrix products, matmul_high(): jnp.dot(left, right, precision=lax.Precision.HIGHEST, preferred_element_t...  8.66 us
    pallas_call x1, Pallas kernels, trailing_of(): pl.pallas_call(lambda *refs: trailing_kernel(w, *refs), out_shape=jax.Sha...  7.24 us
    all_to_all x1, starting transfers between devices, body(): far = lax.all_to_all(far_here, 'blk', 0, 0, tiled=True)  3.79 us
    ppermute x10, waiting for transfers between devices, passed_along(): return lax.ppermute(x, axis, [(i, i + by) for i in range(count - by)])  3.42 us
  transfers between devices with their start and end apart: 11, of which 2 were waited for; matrix products, arithmetic and copies ran while one was open for 6% of the time, Pallas kernels for 10%

profile of v4, /device:TPU:1, one launch (start us, length us, event | category | flops | bytes accessed | tf_op | source)
XLA Modules:
  0.0 112.8 jit_solution(2371812988937724794)
XLA Ops:
  0.6 5.2 %collective-permute-start.2 = (f32[256,256]{1,0:T(8,128)}, f32[256,256]{1,0:T(8,128)S(1)}, u32[]{:S(2)}, u32[]{:S(2)}) collective-permute-start(f32[256,256]{1,0:T(8,128)} %bitcast.48), channel_id=1, source_target_pairs={{0,48},{16,64},{32,80},{48,96},{64,112},{80,128},{96,144},{112,160... | collective-permute-start | bytes 786440 | tf_op jit(solution)/shard_map/ppermute | solution.py:14
  5.9 4.2 %collective-permute-start.1 = (f32[256,256]{1,0:T(8,128)}, f32[256,256]{1,0:T(8,128)}, u32[]{:S(2)}, u32[]{:S(2)}) collective-permute-start(f32[256,256]{1,0:T(8,128)} %bitcast.49), channel_id=1, source_target_pairs={{0,32},{16,48},{32,64},{48,80},{64,96},{80,112},{96,128},{112,144}... | collective-permute-start | bytes 786440 | tf_op jit(solution)/shard_map/ppermute | solution.py:14
  10.0 3.2 %collective-permute-start = (f32[256,256]{1,0:T(8,128)}, f32[256,256]{1,0:T(8,128)}, u32[]{:S(2)}, u32[]{:S(2)}) collective-permute-start(f32[256,256]{1,0:T(8,128)} %bitcast.50), channel_id=1, source_target_pairs={{0,16},{16,32},{32,48},{48,64},{64,80},{80,96},{96,112},{112,128},... | collective-permute-start | bytes 786440 | tf_op jit(solution)/shard_map/ppermute | solution.py:14
  13.2 2.0 %pick.1 = (bf16[16,1792]{1,0:T(8,128)(2,1)S(1)}, bf16[256,3072]{1,0:T(8,128)(2,1)S(1)}) custom-call(s32[3,256]{1,0:T(4,128)} %refs_0_.1, bf16[512,2304]{1,0:T(8,128)(2,1)} %bitcast.45), custom_call_target="tpu_custom_call" | custom-call | flops 113246208 | bytes 2359296 | tf_op jit(solution)/shard_map/pick/pallas_call | solution.py:74
  15.2 0.0 copy-start
  15.3 1.1 %copy-done = bf16[256,3072]{1,0:T(8,128)(2,1)} copy-done((bf16[256,3072]{1,0:T(8,128)(2,1)}, bf16[256,3072]{1,0:T(8,128)(2,1)S(1)}, u32[]{:S(2)}) %copy-start) | copy-done | bytes 1572888
  16.4 27.0 %all_gather.9.refs_0_.refs_3_ = bf16[256,1792]{1,0:T(8,128)(2,1)S(1)} all-gather(bf16[16,1792]{1,0:T(8,128)(2,1)S(1)} %get-tuple-element.23), channel_id=1, replica_groups=mesh['tm'=32,'blk'=16] {'blk'}, dimensions={0}, use_global_device_ids=true | all-gather | bytes 974848 | tf_op jit(solution)/shard_map/all_gather | solution.py:182
  43.4 0.0 copy-start.1
  43.4 3.8 %all-to-all-start = ((bf16[16,16,3072]{2,1,0:T(8,128)(2,1)}), bf16[16,16,3072]{2,1,0:T(8,128)(2,1)S(1)}, u32[]{:S(2)}, u32[]{:S(2)}) async-start(bf16[16,16,3072]{2,1,0:T(8,128)(2,1)} %bitcast.44), calls=%async_computation | async-start | bytes 3145728 | tf_op jit(solution)/shard_map/all_to_all | solution.py:184
  47.2 1.6 %boundary.1 = (bf16[256,256]{1,0:T(8,128)(2,1)S(1)}, bf16[256,256]{1,0:T(8,128)(2,1)S(1)}, bf16[256,256]{1,0:T(8,128)(2,1)S(1)}) custom-call(bf16[256,1792]{1,0:T(8,128)(2,1)S(1)} %all_gather.9.refs_0_.refs_3_, bf16[2,256,256]{2,1,0:T(8,128)(2,1)} %bitcast.52), custom_call_target="tpu_custom_call" | custom-call | flops 234881024 | bytes 1572864 | tf_op jit(solution)/shard_map/boundary/pallas_call | solution.py:110
  48.8 0.0 collective-permute-done.2
  48.8 0.0 collective-permute-done.1
  48.8 0.0 collective-permute-done
  48.8 0.0 copy-done.1
  48.8 1.5 %fusion.6 = f32[256,256]{1,0:T(8,128)S(1)} fusion(f32[256,256]{1,0:T(8,128)} %collective-permute-done, f32[1,256,256]{2,1,0:T(8,128)S(1)} %copy-done.1), kind=kOutput, calls=%fused_computation.13 | convolution fusion | flops 201326592 | bytes 786432 | tf_op jit(solution)/shard_map/dot_general | solution.py:18
  50.4 2.1 %collective-permute-start.3 = (bf16[256,256]{1,0:T(8,128)(2,1)S(1)}, bf16[256,256]{1,0:T(8,128)(2,1)S(1)}, u32[]{:S(2)}, u32[]{:S(2)}) collective-permute-start(bf16[256,256]{1,0:T(8,128)(2,1)S(1)} %get-tuple-element.28), channel_id=1, source_target_pairs={{0,16},{16,32},{32,48},{48,64},{64,80},{80,96},{96,112},{112,128},... | collective-permute-start | bytes 393224 | tf_op jit(solution)/shard_map/ppermute | solution.py:14
  52.4 1.3 %fusion.10 = f32[256,256]{1,0:T(8,128)S(1)} fusion(f32[256,256]{1,0:T(8,128)} %collective-permute-done.1, f32[256,256]{1,0:T(8,128)S(1)} %collective-permute-done.2), kind=kOutput, calls=%fused_computation.17 | convolution fusion | flops 201326592 | bytes 786432 | tf_op jit(solution)/shard_map/dot_general | solution.py:18
  53.8 0.6 fusion.11
  54.4 3.2 %collective-permute-start.5 = (f32[256,128]{1,0:T(8,128)S(1)}, f32[256,128]{1,0:T(8,128)S(1)}, u32[]{:S(2)}, u32[]{:S(2)}) collective-permute-start(f32[256,128]{1,0:T(8,128)S(1)} %constant_dynamic-slice_fusion.1), channel_id=1, source_target_pairs={{0,64},{16,80},{32,96},{48,112},{64,128},{80,144},{96,160},{112,17... | collective-permute-start | bytes 393224 | tf_op jit(solution)/shard_map/ppermute | solution.py:14
  57.6 0.0 collective-permute-done.3
  57.6 0.3 fusion.4
  58.0 0.6 fusion.1
  58.6 4.7 %collective-permute-start.4 = (bf16[256,256]{1,0:T(8,128)(2,1)S(1)}, bf16[256,256]{1,0:T(8,128)(2,1)S(1)}, u32[]{:S(2)}, u32[]{:S(2)}) collective-permute-start(bf16[256,256]{1,0:T(8,128)(2,1)S(1)} %get-tuple-element.44), channel_id=1, source_target_pairs={{0,32},{16,48},{32,64},{48,80},{64,96},{80,112},{96,128},{112,144}... | collective-permute-start | bytes 393224 | tf_op jit(solution)/shard_map/ppermute | solution.py:14
  63.2 0.0 collective-permute-done.5
  63.3 0.4 fusion.12
  63.6 1.5 %collective-permute-done.4 = bf16[256,256]{1,0:T(8,128)(2,1)S(1)} collective-permute-done((bf16[256,256]{1,0:T(8,128)(2,1)S(1)}, bf16[256,256]{1,0:T(8,128)(2,1)S(1)}, u32[]{:S(2)}, u32[]{:S(2)}) %collective-permute-start.4) | collective-permute-done | bytes 131104 | tf_op jit(solution)/shard_map/ppermute | solution.py:14
  65.2 0.4 fusion.13
  65.6 0.4 fusion.8
  66.0 5.3 %collective-permute-start.6 = (bf16[256,256]{1,0:T(8,128)(2,1)S(1)}, bf16[256,256]{1,0:T(8,128)(2,1)S(1)}, u32[]{:S(2)}, u32[]{:S(2)}) collective-permute-start(bf16[256,256]{1,0:T(8,128)(2,1)S(1)} %get-tuple-element.46), channel_id=1, source_target_pairs={{0,64},{16,80},{32,96},{48,112},{64,128},{80,144},{96,160},{112,17... | collective-permute-start | bytes 393224 | tf_op jit(solution)/shard_map/ppermute | solution.py:14
  71.2 3.8 %all_gather.10 = f32[256,256]{1,0:T(8,128)S(1)} all-gather(f32[256,128]{1,0:T(8,128)S(1)} %fusion.12), channel_id=1, replica_groups={{0,1},{2,3},{4,5},{6,7},{8,9},{10,11},{12,13},{14,15},{16,17},{18,19},{..., dimensions={1}, use_global_device_ids=true | all-gather | bytes 393216 | tf_op jit(solution)/shard_map/all_gather | solution.py:199
  75.1 5.4 %collective-permute-start.8 = (f32[256,128]{1,0:T(8,128)S(1)}, f32[256,128]{1,0:T(8,128)S(1)}, u32[]{:S(2)}, u32[]{:S(2)}) collective-permute-start(f32[256,128]{1,0:T(8,128)S(1)} %constant_dynamic-slice_fusion), channel_id=1, source_target_pairs={{0,128},{16,144},{32,160},{48,176},{64,192},{80,208},{96,224},{112... | collective-permute-start | bytes 393224 | tf_op jit(solution)/shard_map/ppermute | solution.py:14
  80.5 0.0 collective-permute-done.6
  80.5 0.3 fusion.14
  80.8 0.4 fusion.9
  81.2 4.2 %collective-permute-start.7 = (bf16[256,256]{1,0:T(8,128)(2,1)S(1)}, bf16[256,256]{1,0:T(8,128)(2,1)S(1)}, u32[]{:S(2)}, u32[]{:S(2)}) collective-permute-start(bf16[256,256]{1,0:T(8,128)(2,1)S(1)} %get-tuple-element.48), channel_id=1, source_target_pairs={{0,128},{16,144},{32,160},{48,176},{64,192},{80,208},{96,224},{112... | collective-permute-start | bytes 393224 | tf_op jit(solution)/shard_map/ppermute | solution.py:14
  85.4 0.0 collective-permute-done.8
  85.4 0.4 fusion.15
  85.8 1.9 %collective-permute-done.7 = bf16[256,256]{1,0:T(8,128)(2,1)S(1)} collective-permute-done((bf16[256,256]{1,0:T(8,128)(2,1)S(1)}, bf16[256,256]{1,0:T(8,128)(2,1)S(1)}, u32[]{:S(2)}, u32[]{:S(2)}) %collective-permute-start.7) | collective-permute-done | bytes 131104 | tf_op jit(solution)/shard_map/ppermute | solution.py:14
  87.7 0.3 fusion.16
  87.9 0.4 convolution_add_fusion.1
  88.3 0.0 all-to-all-done
  88.4 0.7 convert_element_type.24
  89.0 8.6 %collective-permute-start.9 = (bf16[256,256]{1,0:T(8,128)(2,1)}, bf16[256,256]{1,0:T(8,128)(2,1)S(1)}, u32[]{:S(2)}, u32[]{:S(2)}) collective-permute-start(bf16[256,256]{1,0:T(8,128)(2,1)} %convert_element_type.24), channel_id=1, source_target_pairs={{0,256},{16,272},{32,288},{48,304},{64,320},{80,336},{96,352},{112... | collective-permute-start | bytes 393224 | tf_op jit(solution)/shard_map/ppermute | solution.py:14
  97.7 6.5 %all_gather.11 = f32[256,256]{1,0:T(8,128)S(1)} all-gather(f32[256,128]{1,0:T(8,128)S(1)} %fusion.15), channel_id=1, replica_groups={{0,1},{2,3},{4,5},{6,7},{8,9},{10,11},{12,13},{14,15},{16,17},{18,19},{..., dimensions={1}, use_global_device_ids=true | all-gather | bytes 393216 | tf_op jit(solution)/shard_map/all_gather | solution.py:199
  104.2 7.2 %trailing.1 = bf16[512,1792]{1,0:T(8,128)(2,1)} custom-call(bf16[512,2304]{1,0:T(8,128)(2,1)} %bitcast.46, bf16[512,2304]{1,0:T(8,128)(2,1)} %bitcast.47, bf16[2,256,256]{2,1,0:T(8,128)(2,1)} %bitcast.53, bf16[256,1792]{1,0:T(8,128)(2,1)S(1)} %all_gather.9.refs_0_.refs_3_, bf16[256,256]{1,0:T(8,128)(2,1)S(1)} %get-tuple-element.38.refs_4_, ...), custom_call_target="tpu_custom_call" | custom-call | flops 1207959552 | bytes 7077888 | tf_op jit(solution)/shard_map/trailing/pallas_call | solution.py:152
  111.4 0.0 collective-permute-done.9
  111.4 0.3 fusion.17
  111.7 1.1 fusion
  (2 shorter events, 0.0 us)
Async XLA Ops:
  0.6 48.2 %collective-permute-start.2 = (f32[256,256]{1,0:T(8,128)}, f32[256,256]{1,0:T(8,128)S(1)}, u32[]{:S(2)}, u32[]{:S(2)}) collective-permute-start(f32[256,256]{1,0:T(8,128)} %bitcast.48), channel_id=1, source_target_pairs={{0,48},{16,64},{32,80},{48,96},{64,112},{80,128},{96,144},{112,160... | collective-permute-start | bytes 786440 | tf_op jit(solution)/shard_map/ppermute | solution.py:14
  5.9 42.9 %collective-permute-start.1 = (f32[256,256]{1,0:T(8,128)}, f32[256,256]{1,0:T(8,128)}, u32[]{:S(2)}, u32[]{:S(2)}) collective-permute-start(f32[256,256]{1,0:T(8,128)} %bitcast.49), channel_id=1, source_target_pairs={{0,32},{16,48},{32,64},{48,80},{64,96},{80,112},{96,128},{112,144}... | collective-permute-start | bytes 786440 | tf_op jit(solution)/shard_map/ppermute | solution.py:14
  10.0 38.8 %collective-permute-start = (f32[256,256]{1,0:T(8,128)}, f32[256,256]{1,0:T(8,128)}, u32[]{:S(2)}, u32[]{:S(2)}) collective-permute-start(f32[256,256]{1,0:T(8,128)} %bitcast.50), channel_id=1, source_target_pairs={{0,16},{16,32},{32,48},{48,64},{64,80},{80,96},{96,112},{112,128},... | collective-permute-start | bytes 786440 | tf_op jit(solution)/shard_map/ppermute | solution.py:14
  15.2 1.1 %copy-start = (bf16[256,3072]{1,0:T(8,128)(2,1)}, bf16[256,3072]{1,0:T(8,128)(2,1)S(1)}, u32[]{:S(2)}) copy-start(bf16[256,3072]{1,0:T(8,128)(2,1)S(1)} %get-tuple-element.36) | copy-start | bytes 4718596
  43.4 5.4 %copy-start.1 = (f32[1,256,256]{2,1,0:T(8,128)S(1)}, f32[1,256,256]{2,1,0:T(8,128)}, u32[]{:S(2)}) copy-start(f32[1,256,256]{2,1,0:T(8,128)} %param.6) | copy-start | bytes 786436
  43.4 44.9 %all-to-all-start = ((bf16[16,16,3072]{2,1,0:T(8,128)(2,1)}), bf16[16,16,3072]{2,1,0:T(8,128)(2,1)S(1)}, u32[]{:S(2)}, u32[]{:S(2)}) async-start(bf16[16,16,3072]{2,1,0:T(8,128)(2,1)} %bitcast.44), calls=%async_computation | async-start | bytes 3145728 | tf_op jit(solution)/shard_map/all_to_all | solution.py:184
  50.4 7.2 %collective-permute-start.3 = (bf16[256,256]{1,0:T(8,128)(2,1)S(1)}, bf16[256,256]{1,0:T(8,128)(2,1)S(1)}, u32[]{:S(2)}, u32[]{:S(2)}) collective-permute-start(bf16[256,256]{1,0:T(8,128)(2,1)S(1)} %get-tuple-element.28), channel_id=1, source_target_pairs={{0,16},{16,32},{32,48},{48,64},{64,80},{80,96},{96,112},{112,128},... | collective-permute-start | bytes 393224 | tf_op jit(solution)/shard_map/ppermute | solution.py:14
  54.4 8.8 %collective-permute-start.5 = (f32[256,128]{1,0:T(8,128)S(1)}, f32[256,128]{1,0:T(8,128)S(1)}, u32[]{:S(2)}, u32[]{:S(2)}) collective-permute-start(f32[256,128]{1,0:T(8,128)S(1)} %constant_dynamic-slice_fusion.1), channel_id=1, source_target_pairs={{0,64},{16,80},{32,96},{48,112},{64,128},{80,144},{96,160},{112,17... | collective-permute-start | bytes 393224 | tf_op jit(solution)/shard_map/ppermute | solution.py:14
  58.6 6.6 %collective-permute-start.4 = (bf16[256,256]{1,0:T(8,128)(2,1)S(1)}, bf16[256,256]{1,0:T(8,128)(2,1)S(1)}, u32[]{:S(2)}, u32[]{:S(2)}) collective-permute-start(bf16[256,256]{1,0:T(8,128)(2,1)S(1)} %get-tuple-element.44), channel_id=1, source_target_pairs={{0,32},{16,48},{32,64},{48,80},{64,96},{80,112},{96,128},{112,144}... | collective-permute-start | bytes 393224 | tf_op jit(solution)/shard_map/ppermute | solution.py:14
  66.0 14.5 %collective-permute-start.6 = (bf16[256,256]{1,0:T(8,128)(2,1)S(1)}, bf16[256,256]{1,0:T(8,128)(2,1)S(1)}, u32[]{:S(2)}, u32[]{:S(2)}) collective-permute-start(bf16[256,256]{1,0:T(8,128)(2,1)S(1)} %get-tuple-element.46), channel_id=1, source_target_pairs={{0,64},{16,80},{32,96},{48,112},{64,128},{80,144},{96,160},{112,17... | collective-permute-start | bytes 393224 | tf_op jit(solution)/shard_map/ppermute | solution.py:14
  75.1 10.3 %collective-permute-start.8 = (f32[256,128]{1,0:T(8,128)S(1)}, f32[256,128]{1,0:T(8,128)S(1)}, u32[]{:S(2)}, u32[]{:S(2)}) collective-permute-start(f32[256,128]{1,0:T(8,128)S(1)} %constant_dynamic-slice_fusion), channel_id=1, source_target_pairs={{0,128},{16,144},{32,160},{48,176},{64,192},{80,208},{96,224},{112... | collective-permute-start | bytes 393224 | tf_op jit(solution)/shard_map/ppermute | solution.py:14
  81.2 6.5 %collective-permute-start.7 = (bf16[256,256]{1,0:T(8,128)(2,1)S(1)}, bf16[256,256]{1,0:T(8,128)(2,1)S(1)}, u32[]{:S(2)}, u32[]{:S(2)}) collective-permute-start(bf16[256,256]{1,0:T(8,128)(2,1)S(1)} %get-tuple-element.48), channel_id=1, source_target_pairs={{0,128},{16,144},{32,160},{48,176},{64,192},{80,208},{96,224},{112... | collective-permute-start | bytes 393224 | tf_op jit(solution)/shard_map/ppermute | solution.py:14
  89.0 22.4 %collective-permute-start.9 = (bf16[256,256]{1,0:T(8,128)(2,1)}, bf16[256,256]{1,0:T(8,128)(2,1)S(1)}, u32[]{:S(2)}, u32[]{:S(2)}) collective-permute-start(bf16[256,256]{1,0:T(8,128)(2,1)} %convert_element_type.24), channel_id=1, source_target_pairs={{0,256},{16,272},{32,288},{48,304},{64,320},{80,336},{96,352},{112... | collective-permute-start | bytes 393224 | tf_op jit(solution)/shard_map/ppermute | solution.py:14

commit v5 on v4

--- a/solution.py
+++ b/solution.py
@@ -73,9 +73,12 @@
     chunks = width // (3 * w)
     return pl.pallas_call(
         lambda *refs: pick_kernel(w, per, chunks, *refs),
-        out_shape=(pltpu.VMEM((per, 7 * w), BF16), pltpu.VMEM((w, 2 * (width - 3 * w)), BF16)),
+        out_shape=(
+            pltpu.VMEM((per, 7 * w), BF16),
+            pltpu.VMEM((w, 2 * (width - 3 * w)), BF16),
+        ),
         in_specs=[pl.BlockSpec(memory_space=pl.ANY), pl.BlockSpec(memory_space=pl.ANY)],
-        out_specs=(pl.BlockSpec(memory_space=pltpu.VMEM), pl.BlockSpec(memory_space=pltpu.VMEM)),
+        out_specs=tuple(pl.BlockSpec(memory_space=pltpu.VMEM) for _ in range(2)),
         scratch_shapes=[
             pltpu.VMEM((rows, width), BF16),
             pltpu.SMEM(pivot_nodes.shape, jnp.int32),
@@ -118,27 +121,38 @@
 
 
 def trailing_kernel(
-    w, panels_ref, block_ref, inverse_ref, near_ref, factor_ref, second_ref, far_ref, out_ref, one_ref, two_ref
+    w, strip_hbm, inverse_ref, near_ref, factor_ref, second_ref, far_ref, out_hbm, strip_ref, out_ref, sems
 ):
-    step = pl.program_id(0)
     half = far_ref.shape[1] // 2
-
-    def finish(one_rows, two_rows):
-        updated = reduced_by(block_ref[...], one_ref[...], one_rows)
-        out_ref[...] = reduced_by(updated, two_ref[...], two_rows)
-
-    @pl.when(step == 0)
-    def _():
-        one_ref[...] = rounded_dot(panels_ref[:, :w], inverse_ref[0])
-        panel = reduced_by(panels_ref[:, w:], one_ref[...], near_ref[:, :w])
-        two_ref[...] = rounded_dot(panel, inverse_ref[1])
-        finish(near_ref[:, w:2 * w], second_ref[...])
-
-    @pl.when(step > 0)
-    def _():
-        at = pl.multiple_of((step - 1) * w, w)
-        one_rows = far_ref[:, pl.ds(at, w)]
-        finish(one_rows, reduced_by(far_ref[:, pl.ds(half + at, w)], factor_ref[...], one_rows))
+    count = strip_ref.shape[1] // w
+
+    def part(i):
+        at = pl.ds(i * w, w)
+        return pltpu.make_async_copy(strip_hbm.at[:, at], strip_ref.at[:, at], sems.at[0, i])
+
+    def done_part(i):
+        at = pl.ds(i * w, w)
+        return pltpu.make_async_copy(out_ref.at[:, at], out_hbm.at[:, at], sems.at[1, i])
+
+    for i in range(count):
+        part(i).start()
+    part(0).wait()
+    first_factor = rounded_dot(strip_ref[:, :w], inverse_ref[0])
+    part(1).wait()
+    panel = reduced_by(strip_ref[:, w:2 * w], first_factor, near_ref[:, :w])
+    second_factor = rounded_dot(panel, inverse_ref[1])
+    for i in range(count - 2):
+        if i == 0:
+            one_rows, two_rows = near_ref[:, w:2 * w], second_ref[...]
+        else:
+            one_rows = far_ref[:, (i - 1) * w:i * w]
+            two_rows = reduced_by(far_ref[:, half + (i - 1) * w:half + i * w], factor_ref[...], one_rows)
+        part(i + 2).wait()
+        updated = reduced_by(strip_ref[:, (i + 2) * w:(i + 3) * w], first_factor, one_rows)
+        out_ref[:, i * w:(i + 1) * w] = reduced_by(updated, second_factor, two_rows)
+        done_part(i).start()
+    for i in range(count - 2):
+        done_part(i).wait()
 
 
 def in_vmem(*arrays):
@@ -152,20 +166,18 @@
     return pl.pallas_call(
         lambda *refs: trailing_kernel(w, *refs),
         out_shape=jax.ShapeDtypeStruct((rows, width - 2 * w), BF16),
-        grid=(width // w - 2,),
-        in_specs=[
-            pl.BlockSpec((rows, 2 * w), lambda i: (0, 0)),
-            pl.BlockSpec((rows, w), lambda i: (0, i + 2)),
-            pl.BlockSpec((2, w, w), lambda i: (0, 0, 0)),
-            vmem, vmem, vmem, vmem,
+        in_specs=[pl.BlockSpec(memory_space=pl.ANY)] + [vmem] * 5,
+        out_specs=pl.BlockSpec(memory_space=pl.ANY),
+        scratch_shapes=[
+            pltpu.VMEM((rows, width), BF16),
+            pltpu.VMEM((rows, width - 2 * w), BF16),
+            pltpu.SemaphoreType.DMA((2, width // w)),
         ],
-        out_specs=pl.BlockSpec((rows, w), lambda i: (0, i)),
-        scratch_shapes=[pltpu.VMEM((rows, w), BF16), pltpu.VMEM((rows, w), BF16)],
         cost_estimate=pl.CostEstimate(
             flops=4 * rows * w * width, bytes_accessed=4 * rows * width + 4 * w * width, transcendentals=0
         ),
         name="trailing",
-    )(strip, strip, inverses, *in_vmem(near, factor_at_two, second_edge, far))
+    )(strip, inverses, *in_vmem(near, factor_at_two, second_edge, far))
 
 
 def body(panel_strip, pivot_inverses, coupling, pivot_nodes):
@@ -190,37 +202,38 @@
     def advance(current, incoming, reach):
         return matmul_high(matmul_high(reach, incoming.astype(F32)), reach.T) + current
 
-    def half_product(reach, by):
-        half = lax.dynamic_slice_in_dim(reach, lax.axis_index("blk") % 2 * (w // 2), w // 2, 1)
-        return matmul_high(reach, passed_along(half, "tm", by))
-
     def joined(half):
         pairs = [[i, i + 1] for i in range(0, blocks, 2)]
         return lax.all_gather(half, "blk", axis=1, tiled=True, axis_index_groups=pairs)
 
-    incoming = passed_along(boundary, "tm", 1)
+    arriving = [passed_along(boundary, "tm", by) for by in (1, 2, 3)]
     span_two = matmul_high(span, back_one)
-    span_four = matmul_high(span_two, matmul_high(back_two, back_three))
-    half_eight = half_product(span_four, 4)
-    current = advance(boundary.astype(F32), incoming, span)
-
-    incoming = passed_along(current.astype(BF16), "tm", 2)
-    incoming, half_eight = lax.optimization_barrier((incoming, half_eight))
-    current = advance(current, incoming, span_two)
-
-    incoming = passed_along(current.astype(BF16), "tm", 4)
+    span_three = matmul_high(span_two, back_two)
+    span_four = matmul_high(span_three, back_three)
+    half_four = lax.dynamic_slice_in_dim(span_four, lax.axis_index("blk") % 2 * (w // 2), w // 2, 1)
+    half_eight = matmul_high(span_four, passed_along(half_four, "tm", 4))
+    current = boundary.astype(F32)
+    for incoming, reach in zip(arriving, (span, span_two, span_three)):
+        current = advance(current, incoming, reach)
+    wire = current.astype(BF16)
+
+    wire, half_eight = lax.optimization_barrier((wire, half_eight))
+    incoming = passed_along(wire, "tm", 4)
+    passed_eight = passed_along(half_eight, "tm", 8)
     span_eight = joined(half_eight)
-    half_sixteen = half_product(span_eight, 8)
     incoming, span_eight = lax.optimization_barrier((incoming, span_eight))
     current = advance(current, incoming, span_four)
-
-    incoming = passed_along(current.astype(BF16), "tm", 8)
-    incoming, half_sixteen = lax.optimization_barrier((incoming, half_sixteen))
+    wire = current.astype(BF16)
+
+    incoming = passed_along(wire, "tm", 8)
+    half_sixteen = matmul_high(span_eight, passed_eight)
+    span_sixteen = joined(half_sixteen)
+    incoming, span_sixteen = lax.optimization_barrier((incoming, span_sixteen))
     current = advance(current, incoming, span_eight)
-
-    current, far = lax.optimization_barrier((current, far))
-    incoming = passed_along(current.astype(BF16), "tm", 16)
-    span_sixteen = joined(half_sixteen)
+    wire = current.astype(BF16)
+
+    wire, factor_at_two = lax.optimization_barrier((wire, factor_at_two))
+    incoming = passed_along(wire, "tm", 16)
     trailing = trailing_of(strip, inverses, near, factor_at_two, second_edge, far)
     incoming, trailing = lax.optimization_barrier((incoming, trailing))
     current = advance(current, incoming, span_sixteen)

time: 114 us -> 108 us (0.947)
  the two profiles are of different devices: /device:TPU:1 before, /device:TPU:2 now
where the time goes in v5:
time: 108 us; the launch traced here: 107 us
  starting transfers between devices  54 us (50%)
  blocking collectives  29.6 us (27%)
  Pallas kernels  9.61 us (9%)
  matrix products  9.33 us (9%)
  waiting for transfers between devices  2.19 us (2%)
  local copies, waits for them, and re-layouts  1.16 us (1%)
    ppermute x11, starting transfers between devices, passed_along(): return lax.ppermute(x, axis, [(i, i + by) for i in range(count - by)])  50.1 us
    all_gather x1, blocking collectives, body(): near = lax.all_gather(near_here, 'blk', axis=0, tiled=True)  25.7 us
    dot_general x17, matrix products, matmul_high(): jnp.dot(left, right, precision=lax.Precision.HIGHEST, preferred_element_t...  9.33 us
    pallas_call x1, Pallas kernels, trailing_of(): pl.pallas_call(lambda *refs: trailing_kernel(w, *refs), out_shape=jax.Sha...  5.97 us
    all_gather x2, blocking collectives, joined(): lax.all_gather(half, 'blk', axis=1, tiled=True, axis_index_groups=pairs)  3.99 us
    all_to_all x1, starting transfers between devices, body(): far = lax.all_to_all(far_here, 'blk', 0, 0, tiled=True)  3.84 us
    ppermute x11, waiting for transfers between devices, passed_along(): return lax.ppermute(x, axis, [(i, i + by) for i in range(count - by)])  2.19 us
  transfers between devices with their start and end apart: 12, of which 2 were waited for; matrix products, arithmetic and copies ran while one was open for 7% of the time, Pallas kernels for 9%

profile of v5, /device:TPU:2, one launch (start us, length us, event | category | flops | bytes accessed | tf_op | source)
XLA Modules:
  0.0 106.9 jit_solution(2190885690794529237)
XLA Ops:
  0.6 3.5 %collective-permute-start.2 = (f32[256,256]{1,0:T(8,128)}, f32[256,256]{1,0:T(8,128)S(1)}, u32[]{:S(2)}, u32[]{:S(2)}) collective-permute-start(f32[256,256]{1,0:T(8,128)} %bitcast.49), channel_id=1, source_target_pairs={{0,48},{16,64},{32,80},{48,96},{64,112},{80,128},{96,144},{112,160... | collective-permute-start | bytes 786440 | tf_op jit(solution)/shard_map/ppermute | solution.py:14
  4.1 5.0 %collective-permute-start.1 = (f32[256,256]{1,0:T(8,128)}, f32[256,256]{1,0:T(8,128)}, u32[]{:S(2)}, u32[]{:S(2)}) collective-permute-start(f32[256,256]{1,0:T(8,128)} %bitcast.50), channel_id=1, source_target_pairs={{0,32},{16,48},{32,64},{48,80},{64,96},{80,112},{96,128},{112,144}... | collective-permute-start | bytes 786440 | tf_op jit(solution)/shard_map/ppermute | solution.py:14
  9.1 3.0 %collective-permute-start = (f32[256,256]{1,0:T(8,128)}, f32[256,256]{1,0:T(8,128)}, u32[]{:S(2)}, u32[]{:S(2)}) collective-permute-start(f32[256,256]{1,0:T(8,128)} %bitcast.51), channel_id=1, source_target_pairs={{0,16},{16,32},{32,48},{48,64},{64,80},{80,96},{96,112},{112,128},... | collective-permute-start | bytes 786440 | tf_op jit(solution)/shard_map/ppermute | solution.py:14
  12.2 2.0 %pick.1 = (bf16[16,1792]{1,0:T(8,128)(2,1)S(1)}, bf16[256,3072]{1,0:T(8,128)(2,1)S(1)}) custom-call(s32[3,256]{1,0:T(4,128)} %refs_0_.1, bf16[512,2304]{1,0:T(8,128)(2,1)} %bitcast.47), custom_call_target="tpu_custom_call" | custom-call | flops 113246208 | bytes 2359296 | tf_op jit(solution)/shard_map/pick/pallas_call | solution.py:74
  14.2 0.0 copy-start
  14.2 1.1 %copy-done = bf16[256,3072]{1,0:T(8,128)(2,1)} copy-done((bf16[256,3072]{1,0:T(8,128)(2,1)}, bf16[256,3072]{1,0:T(8,128)(2,1)S(1)}, u32[]{:S(2)}) %copy-start) | copy-done | bytes 1572888
  15.3 25.7 %all_gather.9.refs_0_.refs_2_ = bf16[256,1792]{1,0:T(8,128)(2,1)S(1)} all-gather(bf16[16,1792]{1,0:T(8,128)(2,1)S(1)} %get-tuple-element.23), channel_id=1, replica_groups=mesh['tm'=32,'blk'=16] {'blk'}, dimensions={0}, use_global_device_ids=true | all-gather | bytes 974848 | tf_op jit(solution)/shard_map/all_gather | solution.py:194
  41.0 0.0 copy-start.1
  41.0 3.8 %all-to-all-start = ((bf16[16,16,3072]{2,1,0:T(8,128)(2,1)}), bf16[16,16,3072]{2,1,0:T(8,128)(2,1)S(1)}, u32[]{:S(2)}, u32[]{:S(2)}) async-start(bf16[16,16,3072]{2,1,0:T(8,128)(2,1)} %bitcast.46), calls=%async_computation | async-start | bytes 3145728 | tf_op jit(solution)/shard_map/all_to_all | solution.py:196
  44.9 1.6 %boundary.1 = (bf16[256,256]{1,0:T(8,128)(2,1)S(1)}, bf16[256,256]{1,0:T(8,128)(2,1)S(1)}, bf16[256,256]{1,0:T(8,128)(2,1)S(1)}) custom-call(bf16[256,1792]{1,0:T(8,128)(2,1)S(1)} %all_gather.9.refs_0_.refs_2_, bf16[2,256,256]{2,1,0:T(8,128)(2,1)} %bitcast.53), custom_call_target="tpu_custom_call" | custom-call | flops 234881024 | bytes 1572864 | tf_op jit(solution)/shard_map/boundary/pallas_call | solution.py:113
  46.5 0.0 collective-permute-done.2
  46.5 0.0 collective-permute-done.1
  46.5 0.0 collective-permute-done
  46.5 2.8 %collective-permute-start.5 = (bf16[256,256]{1,0:T(8,128)(2,1)S(1)}, bf16[256,256]{1,0:T(8,128)(2,1)S(1)}, u32[]{:S(2)}, u32[]{:S(2)}) collective-permute-start(bf16[256,256]{1,0:T(8,128)(2,1)S(1)} %get-tuple-element.29), channel_id=1, source_target_pairs={{0,16},{16,32},{32,48},{48,64},{64,80},{80,96},{96,112},{112,128},... | collective-permute-start | bytes 393224 | tf_op jit(solution)/shard_map/ppermute | solution.py:14
  49.3 4.3 %collective-permute-start.4 = (bf16[256,256]{1,0:T(8,128)(2,1)S(1)}, bf16[256,256]{1,0:T(8,128)(2,1)S(1)}, u32[]{:S(2)}, u32[]{:S(2)}) collective-permute-start(bf16[256,256]{1,0:T(8,128)(2,1)S(1)} %get-tuple-element.29), channel_id=1, source_target_pairs={{0,32},{16,48},{32,64},{48,80},{64,96},{80,112},{96,128},{112,144}... | collective-permute-start | bytes 393224 | tf_op jit(solution)/shard_map/ppermute | solution.py:14
  53.6 4.7 %collective-permute-start.3 = (bf16[256,256]{1,0:T(8,128)(2,1)S(1)}, bf16[256,256]{1,0:T(8,128)(2,1)S(1)}, u32[]{:S(2)}, u32[]{:S(2)}) collective-permute-start(bf16[256,256]{1,0:T(8,128)(2,1)S(1)} %get-tuple-element.29), channel_id=1, source_target_pairs={{0,48},{16,64},{32,80},{48,96},{64,112},{80,128},{96,144},{112,160... | collective-permute-start | bytes 393224 | tf_op jit(solution)/shard_map/ppermute | solution.py:14
  58.3 0.0 copy-done.1
  58.3 1.5 %fusion.5 = f32[256,256]{1,0:T(8,128)S(1)} fusion(f32[256,256]{1,0:T(8,128)} %collective-permute-done, f32[1,256,256]{2,1,0:T(8,128)S(1)} %copy-done.1), kind=kOutput, calls=%fused_computation.10 | convolution fusion | flops 201326592 | bytes 786432 | tf_op jit(solution)/shard_map/dot_general | solution.py:18
  59.9 1.5 %fusion.10 = f32[256,256]{1,0:T(8,128)S(1)} fusion(f32[256,256]{1,0:T(8,128)S(1)} %fusion.5, f32[256,256]{1,0:T(8,128)} %collective-permute-done.1), kind=kOutput, calls=%fused_computation.15 | convolution fusion | flops 201326592 | bytes 786432 | tf_op jit(solution)/shard_map/dot_general | solution.py:18
  61.4 0.4 fusion.14
  61.8 4.7 %collective-permute-start.6 = (f32[256,128]{1,0:T(8,128)S(1)}, f32[256,128]{1,0:T(8,128)S(1)}, u32[]{:S(2)}, u32[]{:S(2)}) collective-permute-start(f32[256,128]{1,0:T(8,128)S(1)} %constant_dynamic-slice_fusion), channel_id=1, source_target_pairs={{0,64},{16,80},{32,96},{48,112},{64,128},{80,144},{96,160},{112,17... | collective-permute-start | bytes 393224 | tf_op jit(solution)/shard_map/ppermute | solution.py:14
  66.5 0.0 collective-permute-done.5
  66.6 0.3 fusion.3
  66.9 0.0 collective-permute-done.4
  66.9 0.4 fusion.12
  67.3 1.7 %collective-permute-done.6 = f32[256,128]{1,0:T(8,128)S(1)} collective-permute-done((f32[256,128]{1,0:T(8,128)S(1)}, f32[256,128]{1,0:T(8,128)S(1)}, u32[]{:S(2)}, u32[]{:S(2)}) %collective-permute-start.6) | collective-permute-done | bytes 131104 | tf_op jit(solution)/shard_map/ppermute | solution.py:14
  69.0 0.4 fusion.15
  69.4 0.0 collective-permute-done.3
  69.4 0.3 fusion.11
  69.7 0.6 fusion.1
  70.3 0.4 fusion.13
  70.7 0.4 fusion.7
  71.1 4.4 %collective-permute-start.7 = (bf16[256,256]{1,0:T(8,128)(2,1)S(1)}, bf16[256,256]{1,0:T(8,128)(2,1)S(1)}, u32[]{:S(2)}, u32[]{:S(2)}) collective-permute-start(bf16[256,256]{1,0:T(8,128)(2,1)S(1)} %get-tuple-element.31), channel_id=1, source_target_pairs={{0,64},{16,80},{32,96},{48,112},{64,128},{80,144},{96,160},{112,17... | collective-permute-start | bytes 393224 | tf_op jit(solution)/shard_map/ppermute | solution.py:14
  75.5 2.7 %collective-permute-start.9 = (f32[256,128]{1,0:T(8,128)S(1)}, f32[256,128]{1,0:T(8,128)S(1)}, u32[]{:S(2)}, u32[]{:S(2)}) collective-permute-start(f32[256,128]{1,0:T(8,128)S(1)} %fusion.15), channel_id=1, source_target_pairs={{0,128},{16,144},{32,160},{48,176},{64,192},{80,208},{96,224},{112... | collective-permute-start | bytes 393224 | tf_op jit(solution)/shard_map/ppermute | solution.py:14
  78.2 2.0 %all_gather.10 = f32[256,256]{1,0:T(8,128)S(1)} all-gather(f32[256,128]{1,0:T(8,128)S(1)} %fusion.15), channel_id=1, replica_groups={{0,1},{2,3},{4,5},{6,7},{8,9},{10,11},{12,13},{14,15},{16,17},{18,19},{..., dimensions={1}, use_global_device_ids=true | all-gather | bytes 393216 | tf_op jit(solution)/shard_map/all_gather | solution.py:207
  80.2 0.0 collective-permute-done.7
  80.2 0.3 fusion.16
  80.5 0.4 fusion.8
  80.9 3.5 %collective-permute-start.8 = (bf16[256,256]{1,0:T(8,128)(2,1)S(1)}, bf16[256,256]{1,0:T(8,128)(2,1)S(1)}, u32[]{:S(2)}, u32[]{:S(2)}) collective-permute-start(bf16[256,256]{1,0:T(8,128)(2,1)S(1)} %get-tuple-element.46), channel_id=1, source_target_pairs={{0,128},{16,144},{32,160},{48,176},{64,192},{80,208},{96,224},{112... | collective-permute-start | bytes 393224 | tf_op jit(solution)/shard_map/ppermute | solution.py:14
  84.4 0.0 collective-permute-done.9
  84.4 0.4 fusion.17
  84.8 2.0 %all_gather.11 = f32[256,256]{1,0:T(8,128)S(1)} all-gather(f32[256,128]{1,0:T(8,128)S(1)} %fusion.17), channel_id=1, replica_groups={{0,1},{2,3},{4,5},{6,7},{8,9},{10,11},{12,13},{14,15},{16,17},{18,19},{..., dimensions={1}, use_global_device_ids=true | all-gather | bytes 393216 | tf_op jit(solution)/shard_map/all_gather | solution.py:207
  86.8 0.4 collective-permute-done.8
  87.2 0.3 fusion.18
  87.5 0.4 fusion.9
  87.9 11.6 %collective-permute-start.10 = (bf16[256,256]{1,0:T(8,128)(2,1)S(1)}, bf16[256,256]{1,0:T(8,128)(2,1)S(1)}, u32[]{:S(2)}, u32[]{:S(2)}) collective-permute-start(bf16[256,256]{1,0:T(8,128)(2,1)S(1)} %get-tuple-element.37), channel_id=1, source_target_pairs={{0,256},{16,272},{32,288},{48,304},{64,320},{80,336},{96,352},{112... | collective-permute-start | bytes 393224 | tf_op jit(solution)/shard_map/ppermute | solution.py:14
  99.5 0.0 all-to-all-done
  99.5 6.0 %trailing.1 = bf16[512,1792]{1,0:T(8,128)(2,1)} custom-call(bf16[512,2304]{1,0:T(8,128)(2,1)} %bitcast.48, bf16[2,256,256]{2,1,0:T(8,128)(2,1)} %bitcast.54, bf16[256,1792]{1,0:T(8,128)(2,1)S(1)} %all_gather.9.refs_0_.refs_2_, bf16[256,256]{1,0:T(8,128)(2,1)S(1)} %get-tuple-element.38.refs_3_, bf16[256,256]{1,0:T(8,128)(2,1)S(1)} %get-tuple-element.39.refs_4_, ...), custom_call_target="tpu_custom_call" | custom-call | flops 1207959552 | bytes 7077888 | tf_op jit(solution)/shard_map/trailing/pallas_call | solution.py:166
  105.5 0.0 collective-permute-done.10
  105.5 0.3 fusion.19
  105.8 1.1 %fusion = f32[1,256,256]{2,1,0:T(8,128)} fusion(f32[256,256]{1,0:T(8,128)S(1)} %get-tuple-element.49, f32[256,256]{1,0:T(8,128)S(1)} %fusion.19, f32[256,256]{1,0:T(8,128)S(1)} %all_gather.11), kind=kOutput, calls=%fused_computation.1 | convolution fusion | flops 201392128 | bytes 1048576 | tf_op jit(solution)/shard_map/dot_general | solution.py:18
  (1 shorter events, 0.0 us)
Async XLA Ops:
  0.6 45.8 %collective-permute-start.2 = (f32[256,256]{1,0:T(8,128)}, f32[256,256]{1,0:T(8,128)S(1)}, u32[]{:S(2)}, u32[]{:S(2)}) collective-permute-start(f32[256,256]{1,0:T(8,128)} %bitcast.49), channel_id=1, source_target_pairs={{0,48},{16,64},{32,80},{48,96},{64,112},{80,128},{96,144},{112,160... | collective-permute-start | bytes 786440 | tf_op jit(solution)/shard_map/ppermute | solution.py:14
  4.1 42.4 %collective-permute-start.1 = (f32[256,256]{1,0:T(8,128)}, f32[256,256]{1,0:T(8,128)}, u32[]{:S(2)}, u32[]{:S(2)}) collective-permute-start(f32[256,256]{1,0:T(8,128)} %bitcast.50), channel_id=1, source_target_pairs={{0,32},{16,48},{32,64},{48,80},{64,96},{80,112},{96,128},{112,144}... | collective-permute-start | bytes 786440 | tf_op jit(solution)/shard_map/ppermute | solution.py:14
  9.1 37.4 %collective-permute-start = (f32[256,256]{1,0:T(8,128)}, f32[256,256]{1,0:T(8,128)}, u32[]{:S(2)}, u32[]{:S(2)}) collective-permute-start(f32[256,256]{1,0:T(8,128)} %bitcast.51), channel_id=1, source_target_pairs={{0,16},{16,32},{32,48},{48,64},{64,80},{80,96},{96,112},{112,128},... | collective-permute-start | bytes 786440 | tf_op jit(solution)/shard_map/ppermute | solution.py:14
  14.2 1.1 %copy-start = (bf16[256,3072]{1,0:T(8,128)(2,1)}, bf16[256,3072]{1,0:T(8,128)(2,1)S(1)}, u32[]{:S(2)}) copy-start(bf16[256,3072]{1,0:T(8,128)(2,1)S(1)} %get-tuple-element.40) | copy-start | bytes 4718596
  41.0 17.3 %copy-start.1 = (f32[1,256,256]{2,1,0:T(8,128)S(1)}, f32[1,256,256]{2,1,0:T(8,128)}, u32[]{:S(2)}) copy-start(f32[1,256,256]{2,1,0:T(8,128)} %param.6) | copy-start | bytes 786436
  41.0 58.5 %all-to-all-start = ((bf16[16,16,3072]{2,1,0:T(8,128)(2,1)}), bf16[16,16,3072]{2,1,0:T(8,128)(2,1)S(1)}, u32[]{:S(2)}, u32[]{:S(2)}) async-start(bf16[16,16,3072]{2,1,0:T(8,128)(2,1)} %bitcast.46), calls=%async_computation | async-start | bytes 3145728 | tf_op jit(solution)/shard_map/all_to_all | solution.py:196
  46.5 20.0 %collective-permute-start.5 = (bf16[256,256]{1,0:T(8,128)(2,1)S(1)}, bf16[256,256]{1,0:T(8,128)(2,1)S(1)}, u32[]{:S(2)}, u32[]{:S(2)}) collective-permute-start(bf16[256,256]{1,0:T(8,128)(2,1)S(1)} %get-tuple-element.29), channel_id=1, source_target_pairs={{0,16},{16,32},{32,48},{48,64},{64,80},{80,96},{96,112},{112,128},... | collective-permute-start | bytes 393224 | tf_op jit(solution)/shard_map/ppermute | solution.py:14
  49.3 17.6 %collective-permute-start.4 = (bf16[256,256]{1,0:T(8,128)(2,1)S(1)}, bf16[256,256]{1,0:T(8,128)(2,1)S(1)}, u32[]{:S(2)}, u32[]{:S(2)}) collective-permute-start(bf16[256,256]{1,0:T(8,128)(2,1)S(1)} %get-tuple-element.29), channel_id=1, source_target_pairs={{0,32},{16,48},{32,64},{48,80},{64,96},{80,112},{96,128},{112,144}... | collective-permute-start | bytes 393224 | tf_op jit(solution)/shard_map/ppermute | solution.py:14
  53.6 15.8 %collective-permute-start.3 = (bf16[256,256]{1,0:T(8,128)(2,1)S(1)}, bf16[256,256]{1,0:T(8,128)(2,1)S(1)}, u32[]{:S(2)}, u32[]{:S(2)}) collective-permute-start(bf16[256,256]{1,0:T(8,128)(2,1)S(1)} %get-tuple-element.29), channel_id=1, source_target_pairs={{0,48},{16,64},{32,80},{48,96},{64,112},{80,128},{96,144},{112,160... | collective-permute-start | bytes 393224 | tf_op jit(solution)/shard_map/ppermute | solution.py:14
  61.8 7.2 %collective-permute-start.6 = (f32[256,128]{1,0:T(8,128)S(1)}, f32[256,128]{1,0:T(8,128)S(1)}, u32[]{:S(2)}, u32[]{:S(2)}) collective-permute-start(f32[256,128]{1,0:T(8,128)S(1)} %constant_dynamic-slice_fusion), channel_id=1, source_target_pairs={{0,64},{16,80},{32,96},{48,112},{64,128},{80,144},{96,160},{112,17... | collective-permute-start | bytes 393224 | tf_op jit(solution)/shard_map/ppermute | solution.py:14
  71.1 9.1 %collective-permute-start.7 = (bf16[256,256]{1,0:T(8,128)(2,1)S(1)}, bf16[256,256]{1,0:T(8,128)(2,1)S(1)}, u32[]{:S(2)}, u32[]{:S(2)}) collective-permute-start(bf16[256,256]{1,0:T(8,128)(2,1)S(1)} %get-tuple-element.31), channel_id=1, source_target_pairs={{0,64},{16,80},{32,96},{48,112},{64,128},{80,144},{96,160},{112,17... | collective-permute-start | bytes 393224 | tf_op jit(solution)/shard_map/ppermute | solution.py:14
  75.5 8.9 %collective-permute-start.9 = (f32[256,128]{1,0:T(8,128)S(1)}, f32[256,128]{1,0:T(8,128)S(1)}, u32[]{:S(2)}, u32[]{:S(2)}) collective-permute-start(f32[256,128]{1,0:T(8,128)S(1)} %fusion.15), channel_id=1, source_target_pairs={{0,128},{16,144},{32,160},{48,176},{64,192},{80,208},{96,224},{112... | collective-permute-start | bytes 393224 | tf_op jit(solution)/shard_map/ppermute | solution.py:14
  80.9 6.3 %collective-permute-start.8 = (bf16[256,256]{1,0:T(8,128)(2,1)S(1)}, bf16[256,256]{1,0:T(8,128)(2,1)S(1)}, u32[]{:S(2)}, u32[]{:S(2)}) collective-permute-start(bf16[256,256]{1,0:T(8,128)(2,1)S(1)} %get-tuple-element.46), channel_id=1, source_target_pairs={{0,128},{16,144},{32,160},{48,176},{64,192},{80,208},{96,224},{112... | collective-permute-start | bytes 393224 | tf_op jit(solution)/shard_map/ppermute | solution.py:14
  87.9 17.6 %collective-permute-start.10 = (bf16[256,256]{1,0:T(8,128)(2,1)S(1)}, bf16[256,256]{1,0:T(8,128)(2,1)S(1)}, u32[]{:S(2)}, u32[]{:S(2)}) collective-permute-start(bf16[256,256]{1,0:T(8,128)(2,1)S(1)} %get-tuple-element.37), channel_id=1, source_target_pairs={{0,256},{16,272},{32,288},{48,304},{64,320},{80,336},{96,352},{112... | collective-permute-start | bytes 393224 | tf_op jit(solution)/shard_map/ppermute | solution.py:14

commit v6 on v5

--- a/solution.py
+++ b/solution.py
@@ -7,6 +7,7 @@
 
 BF16 = jnp.bfloat16
 F32 = jnp.float32
+VMEM_BYTES = 16 << 20
 
 
 def passed_along(x, axis, by):
@@ -51,7 +52,7 @@
     picker = jnp.concatenate(
         [(wanted == at_lane + first).astype(F32).astype(BF16) for first in range(0, rows, lanes)], 1
     )
-    far_width = strip_ref.shape[1] - 3 * w
+    width = far_ref.shape[1] // 2
     for i in range(chunks):
         part(i).wait()
         at = pl.ds(i * cols, cols)
@@ -63,9 +64,9 @@
             near_ref[:, 3 * w:4 * w] = two[:, 2 * w:]
             near_ref[:, 4 * w:] = edge
         else:
-            for row in range(0, far_ref.shape[0], per):
-                far_ref[row:row + per, (i - 1) * cols:i * cols] = one
-                far_ref[row:row + per, far_width + (i - 1) * cols:far_width + i * cols] = two
+            for row in range((i - 1) * per, far_ref.shape[0], 2 * per):
+                far_ref[row:row + per, :width] = one
+                far_ref[row:row + per, width:] = two
 
 
 def picked_rows(pivot_nodes, strip, w, per):
@@ -75,9 +76,9 @@
         lambda *refs: pick_kernel(w, per, chunks, *refs),
         out_shape=(
             pltpu.VMEM((per, 7 * w), BF16),
-            pltpu.VMEM((w, 2 * (width - 3 * w)), BF16),
+            pltpu.VMEM((w, width - 3 * w), BF16),
         ),
-        in_specs=[pl.BlockSpec(memory_space=pl.ANY), pl.BlockSpec(memory_space=pl.ANY)],
+        in_specs=[pl.BlockSpec(memory_space=pltpu.HBM), pl.BlockSpec(memory_space=pltpu.HBM)],
         out_specs=tuple(pl.BlockSpec(memory_space=pltpu.VMEM) for _ in range(2)),
         scratch_shapes=[
             pltpu.VMEM((rows, width), BF16),
@@ -91,7 +92,7 @@
     )(pivot_nodes, strip)
 
 
-def boundary_kernel(w, near_ref, inverse_ref, boundary_ref, factor_ref, second_ref):
+def boundary_kernel(w, near_ref, inverse_ref, boundary_ref, factor_ref, second_ref, ones_ref):
     near = near_ref[...]
     one_edge = near[:, w:2 * w]
     edge = near[:, 4 * w:]
@@ -103,6 +104,7 @@
     boundary_ref[...] = reduced_by(updated[:, w:], factor_two, second_edge)
     factor_ref[...] = factor_at_two
     second_ref[...] = second_edge
+    ones_ref[...] = near[:, :2 * w]
 
 
 def boundary_of(near, inverses):
@@ -112,46 +114,57 @@
     vmem = pl.BlockSpec(memory_space=pltpu.VMEM)
     return pl.pallas_call(
         lambda *refs: boundary_kernel(w, *refs),
-        out_shape=(block, block, block),
+        out_shape=(block, block, block, pltpu.VMEM((w, 2 * w), BF16)),
         in_specs=[vmem, vmem],
-        out_specs=(vmem, vmem, vmem),
+        out_specs=(vmem, vmem, vmem, vmem),
         cost_estimate=pl.CostEstimate(flops=14 * w * w * w, bytes_accessed=12 * w * 2 * w, transcendentals=0),
+        compiler_params=pltpu.CompilerParams(vmem_limit_bytes=VMEM_BYTES),
         name="boundary",
     )(near, inverses)
 
 
 def trailing_kernel(
-    w, strip_hbm, inverse_ref, near_ref, factor_ref, second_ref, far_ref, out_hbm, strip_ref, out_ref, sems
+    w, strip_hbm, inverse_ref, ones_ref, factor_ref, second_ref, own_ref, other_ref, out_hbm, strip_ref, out_ref, sems
 ):
-    half = far_ref.shape[1] // 2
+    half = own_ref.shape[1] // 2
+    per_half = half // w
     count = strip_ref.shape[1] // w
+    core = lax.rem(lax.axis_index("blk"), 2)
+
+    blocks = [0, 1, 2]
+    for which in (core, 1 - core):
+        blocks += [3 + which * per_half + k for k in range(per_half)]
+
+    def columns(block):
+        return pl.ds(block * w if isinstance(block, int) else pl.multiple_of(block * w, w), w)
 
     def part(i):
-        at = pl.ds(i * w, w)
-        return pltpu.make_async_copy(strip_hbm.at[:, at], strip_ref.at[:, at], sems.at[0, i])
+        at = columns(blocks[i])
+        return pltpu.make_async_copy(strip_hbm.at[:, at], strip_ref.at[:, i * w:(i + 1) * w], sems.at[0, i])
 
     def done_part(i):
-        at = pl.ds(i * w, w)
-        return pltpu.make_async_copy(out_ref.at[:, at], out_hbm.at[:, at], sems.at[1, i])
+        at = columns(blocks[i] - 2)
+        return pltpu.make_async_copy(out_ref.at[:, (i - 2) * w:(i - 1) * w], out_hbm.at[:, at], sems.at[1, i])
 
     for i in range(count):
         part(i).start()
     part(0).wait()
     first_factor = rounded_dot(strip_ref[:, :w], inverse_ref[0])
     part(1).wait()
-    panel = reduced_by(strip_ref[:, w:2 * w], first_factor, near_ref[:, :w])
+    panel = reduced_by(strip_ref[:, w:2 * w], first_factor, ones_ref[:, :w])
     second_factor = rounded_dot(panel, inverse_ref[1])
-    for i in range(count - 2):
-        if i == 0:
-            one_rows, two_rows = near_ref[:, w:2 * w], second_ref[...]
+    for i in range(2, count):
+        if i == 2:
+            one_rows, two_rows = ones_ref[:, w:2 * w], second_ref[...]
         else:
-            one_rows = far_ref[:, (i - 1) * w:i * w]
-            two_rows = reduced_by(far_ref[:, half + (i - 1) * w:half + i * w], factor_ref[...], one_rows)
-        part(i + 2).wait()
-        updated = reduced_by(strip_ref[:, (i + 2) * w:(i + 3) * w], first_factor, one_rows)
-        out_ref[:, i * w:(i + 1) * w] = reduced_by(updated, second_factor, two_rows)
+            ref, k = (own_ref, i - 3) if i - 3 < per_half else (other_ref, i - 3 - per_half)
+            one_rows = ref[:, k * w:(k + 1) * w]
+            two_rows = reduced_by(ref[:, half + k * w:half + (k + 1) * w], factor_ref[...], one_rows)
+        part(i).wait()
+        updated = reduced_by(strip_ref[:, i * w:(i + 1) * w], first_factor, one_rows)
+        out_ref[:, (i - 2) * w:(i - 1) * w] = reduced_by(updated, second_factor, two_rows)
         done_part(i).start()
-    for i in range(count - 2):
+    for i in range(2, count):
         done_part(i).wait()
 
 
@@ -159,14 +172,14 @@
     return tuple(pltpu.with_memory_space_constraint(x, pltpu.VMEM) for x in arrays)
 
 
-def trailing_of(strip, inverses, near, factor_at_two, second_edge, far):
+def trailing_of(strip, inverses, ones, factor_at_two, second_edge, own, other):
     rows, width = strip.shape
-    w = near.shape[0]
+    w = ones.shape[0]
     vmem = pl.BlockSpec(memory_space=pltpu.VMEM)
     return pl.pallas_call(
         lambda *refs: trailing_kernel(w, *refs),
         out_shape=jax.ShapeDtypeStruct((rows, width - 2 * w), BF16),
-        in_specs=[pl.BlockSpec(memory_space=pl.ANY)] + [vmem] * 5,
+        in_specs=[pl.BlockSpec(memory_space=pltpu.HBM)] + [vmem] * 6,
         out_specs=pl.BlockSpec(memory_space=pl.ANY),
         scratch_shapes=[
             pltpu.VMEM((rows, width), BF16),
@@ -177,7 +190,7 @@
             flops=4 * rows * w * width, bytes_accessed=4 * rows * width + 4 * w * width, transcendentals=0
         ),
         name="trailing",
-    )(strip, inverses, *in_vmem(near, factor_at_two, second_edge, far))
+    )(strip, inverses, *in_vmem(ones, factor_at_two, second_edge, own, other))
 
 
 def body(panel_strip, pivot_inverses, coupling, pivot_nodes):
@@ -192,9 +205,7 @@
 
     near_here, far_here = picked_rows(pivot_nodes, strip, w, per)
     near = lax.all_gather(near_here, "blk", axis=0, tiled=True)
-    near, far_here = lax.optimization_barrier((near, far_here))
-    far = lax.all_to_all(far_here, "blk", 0, 0, tiled=True)
-    boundary, factor_at_two, second_edge = boundary_of(near, inverses)
+    boundary, factor_at_two, second_edge, one_rows = boundary_of(near, inverses)
     back_one, back_two, back_three, boundary = lax.optimization_barrier(
         (back_one, back_two, back_three, boundary)
     )
@@ -207,6 +218,8 @@
         return lax.all_gather(half, "blk", axis=1, tiled=True, axis_index_groups=pairs)
 
     arriving = [passed_along(boundary, "tm", by) for by in (1, 2, 3)]
+    arriving[0], far_here = lax.optimization_barrier((arriving[0], far_here))
+    own = lax.all_to_all(far_here, "blk", 0, 0, tiled=True)
     span_two = matmul_high(span, back_one)
     span_three = matmul_high(span_two, back_two)
     span_four = matmul_high(span_three, back_three)
@@ -217,7 +230,6 @@
         current = advance(current, incoming, reach)
     wire = current.astype(BF16)
 
-    wire, half_eight = lax.optimization_barrier((wire, half_eight))
     incoming = passed_along(wire, "tm", 4)
     passed_eight = passed_along(half_eight, "tm", 8)
     span_eight = joined(half_eight)
@@ -226,15 +238,14 @@
     wire = current.astype(BF16)
 
     incoming = passed_along(wire, "tm", 8)
-    half_sixteen = matmul_high(span_eight, passed_eight)
-    span_sixteen = joined(half_sixteen)
-    incoming, span_sixteen = lax.optimization_barrier((incoming, span_sixteen))
+    other = lax.ppermute(own, "blk", [(i, i ^ 1) for i in range(blocks)])
+    span_sixteen = joined(matmul_high(span_eight, passed_eight))
     current = advance(current, incoming, span_eight)
     wire = current.astype(BF16)
 
     wire, factor_at_two = lax.optimization_barrier((wire, factor_at_two))
     incoming = passed_along(wire, "tm", 16)
-    trailing = trailing_of(strip, inverses, near, factor_at_two, second_edge, far)
+    trailing = trailing_of(strip, inverses, one_rows, factor_at_two, second_edge, own, other)
     incoming, trailing = lax.optimization_barrier((incoming, trailing))
     current = advance(current, incoming, span_sixteen)
     return (trailing[None], current[None])

time: 108 us -> 103 us (0.954)
  the two profiles are of different devices: /device:TPU:2 before, /device:TPU:1 now
where the time goes in v6:
time: 103 us
  starting transfers between devices  42.8 us (42%)
  blocking collectives  31.9 us (31%)
  waiting for transfers between devices  10.3 us (10%)
  Pallas kernels  9.49 us (9%)
  matrix products  7.44 us (7%)
    ppermute x11, starting transfers between devices, passed_along(): return lax.ppermute(x, axis, [(i, i + by) for i in range(count - by)])  36.2 us
    all_gather x1, blocking collectives, body(): near = lax.all_gather(near_here, 'blk', axis=0, tiled=True)  27 us
    all_to_all x1, waiting for transfers between devices, body(): own = lax.all_to_all(far_here, 'blk', 0, 0, tiled=True)  10.2 us
    dot_general x17, matrix products, matmul_high(): jnp.dot(left, right, precision=lax.Precision.HIGHEST, preferred_element_t...  7.44 us
    pallas_call x1, Pallas kernels, trailing_of(): pl.pallas_call(lambda *refs: trailing_kernel(w, *refs), out_shape=jax.Sha...  5.97 us
    all_gather x2, blocking collectives, joined(): lax.all_gather(half, 'blk', axis=1, tiled=True, axis_index_groups=pairs)  4.82 us
    all_to_all x1, starting transfers between devices, body(): own = lax.all_to_all(far_here, 'blk', 0, 0, tiled=True)  4.69 us
    pallas_call x1, Pallas kernels, picked_rows(): pl.pallas_call(lambda *refs: pick_kernel(w, per, chunks, *refs), out_shap...  2.86 us
  transfers between devices with their start and end apart: 13, of which 1 were waited for; matrix products, arithmetic and copies ran while one was open for 6% of the time, Pallas kernels for 9%

profile of v6, /device:TPU:1, one launch (start us, length us, event | category | flops | bytes accessed | tf_op | source)
XLA Modules:
  0.0 102.8 jit_solution(10574898356659248716)
XLA Ops:
  0.6 0.0 copy-start.1
  0.6 0.0 copy-start
  0.7 5.4 %collective-permute-start.2 = (f32[256,256]{1,0:T(8,128)}, f32[256,256]{1,0:T(8,128)S(1)}, u32[]{:S(2)}, u32[]{:S(2)}) collective-permute-start(f32[256,256]{1,0:T(8,128)} %bitcast.51), channel_id=1, source_target_pairs={{0,48},{16,64},{32,80},{48,96},{64,112},{80,128},{96,144},{112,160... | collective-permute-start | bytes 786440 | tf_op jit(solution)/shard_map/ppermute | solution.py:15
  6.0 3.5 %collective-permute-start.1 = (f32[256,256]{1,0:T(8,128)}, f32[256,256]{1,0:T(8,128)S(1)}, u32[]{:S(2)}, u32[]{:S(2)}) collective-permute-start(f32[256,256]{1,0:T(8,128)} %bitcast.52), channel_id=1, source_target_pairs={{0,32},{16,48},{32,64},{48,80},{64,96},{80,112},{96,128},{112,144}... | collective-permute-start | bytes 786440 | tf_op jit(solution)/shard_map/ppermute | solution.py:15
  9.5 2.5 %collective-permute-start = (f32[256,256]{1,0:T(8,128)}, f32[256,256]{1,0:T(8,128)S(1)}, u32[]{:S(2)}, u32[]{:S(2)}) collective-permute-start(f32[256,256]{1,0:T(8,128)} %bitcast.53), channel_id=1, source_target_pairs={{0,16},{16,32},{32,48},{48,64},{64,80},{80,96},{96,112},{112,128},... | collective-permute-start | bytes 786440 | tf_op jit(solution)/shard_map/ppermute | solution.py:15
  12.0 2.9 %pick.1 = (bf16[16,1792]{1,0:T(8,128)(2,1)S(1)}, bf16[256,1536]{1,0:T(8,128)(2,1)}) custom-call(s32[3,256]{1,0:T(4,128)} %refs_0_.1, bf16[512,2304]{1,0:T(8,128)(2,1)} %bitcast.49), custom_call_target="tpu_custom_call" | custom-call | flops 113246208 | bytes 2359296 | tf_op jit(solution)/shard_map/pick/pallas_call | solution.py:75
  14.9 27.0 %all_gather.9.refs_0_ = bf16[256,1792]{1,0:T(8,128)(2,1)S(1)} all-gather(bf16[16,1792]{1,0:T(8,128)(2,1)S(1)} %get-tuple-element.20), channel_id=1, replica_groups=mesh['tm'=32,'blk'=16] {'blk'}, dimensions={0}, use_global_device_ids=true | all-gather | bytes 974848 | tf_op jit(solution)/shard_map/all_gather | solution.py:207
  41.9 0.0 copy-done
  41.9 0.7 boundary.1
  42.6 0.0 collective-permute-done.2
  42.6 0.0 collective-permute-done.1
  42.6 0.0 collective-permute-done
  42.6 3.4 %collective-permute-start.5 = (bf16[256,256]{1,0:T(8,128)(2,1)S(1)}, bf16[256,256]{1,0:T(8,128)(2,1)S(1)}, u32[]{:S(2)}, u32[]{:S(2)}) collective-permute-start(bf16[256,256]{1,0:T(8,128)(2,1)S(1)} %get-tuple-element.24), channel_id=1, source_target_pairs={{0,16},{16,32},{32,48},{48,64},{64,80},{80,96},{96,112},{112,128},... | collective-permute-start | bytes 393224 | tf_op jit(solution)/shard_map/ppermute | solution.py:15
  46.0 4.7 %collective-permute-start.4 = (bf16[256,256]{1,0:T(8,128)(2,1)S(1)}, bf16[256,256]{1,0:T(8,128)(2,1)S(1)}, u32[]{:S(2)}, u32[]{:S(2)}) collective-permute-start(bf16[256,256]{1,0:T(8,128)(2,1)S(1)} %get-tuple-element.24), channel_id=1, source_target_pairs={{0,32},{16,48},{32,64},{48,80},{64,96},{80,112},{96,128},{112,144}... | collective-permute-start | bytes 393224 | tf_op jit(solution)/shard_map/ppermute | solution.py:15
  50.7 3.2 %collective-permute-start.3 = (bf16[256,256]{1,0:T(8,128)(2,1)S(1)}, bf16[256,256]{1,0:T(8,128)(2,1)S(1)}, u32[]{:S(2)}, u32[]{:S(2)}) collective-permute-start(bf16[256,256]{1,0:T(8,128)(2,1)S(1)} %get-tuple-element.24), channel_id=1, source_target_pairs={{0,48},{16,64},{32,80},{48,96},{64,112},{80,128},{96,144},{112,160... | collective-permute-start | bytes 393224 | tf_op jit(solution)/shard_map/ppermute | solution.py:15
  53.9 0.0 copy-done.1
  53.9 0.6 fusion.5
  54.5 0.6 fusion.10
  55.1 0.4 fusion.14
  55.5 4.4 %collective-permute-start.7 = (f32[256,128]{1,0:T(8,128)S(1)}, f32[256,128]{1,0:T(8,128)S(1)}, u32[]{:S(2)}, u32[]{:S(2)}) collective-permute-start(f32[256,128]{1,0:T(8,128)S(1)} %constant_dynamic-slice_fusion), channel_id=1, source_target_pairs={{0,64},{16,80},{32,96},{48,112},{64,128},{80,144},{96,160},{112,17... | collective-permute-start | bytes 393224 | tf_op jit(solution)/shard_map/ppermute | solution.py:15
  59.9 0.0 collective-permute-done.5
  59.9 4.7 %all-to-all-start = ((bf16[16,16,1536]{2,1,0:T(8,128)(2,1)}), bf16[16,16,1536]{2,1,0:T(8,128)(2,1)S(1)}, u32[]{:S(2)}, u32[]{:S(2)}) async-start(bf16[16,16,1536]{2,1,0:T(8,128)(2,1)} %bitcast.3), calls=%async_computation | async-start | bytes 1572864 | tf_op jit(solution)/shard_map/all_to_all | solution.py:222
  64.6 0.3 fusion.3
  65.0 0.6 fusion.1
  65.6 0.0 collective-permute-done.4
  65.6 0.4 fusion.12
  66.0 0.0 collective-permute-done.3
  66.0 0.3 fusion.11
  66.2 0.4 fusion.13
  66.6 0.4 fusion.7
  67.1 2.3 %collective-permute-start.6 = (bf16[256,256]{1,0:T(8,128)(2,1)S(1)}, bf16[256,256]{1,0:T(8,128)(2,1)S(1)}, u32[]{:S(2)}, u32[]{:S(2)}) collective-permute-start(bf16[256,256]{1,0:T(8,128)(2,1)S(1)} %get-tuple-element.38), channel_id=1, source_target_pairs={{0,64},{16,80},{32,96},{48,112},{64,128},{80,144},{96,160},{112,17... | collective-permute-start | bytes 393224 | tf_op jit(solution)/shard_map/ppermute | solution.py:15
  69.4 0.0 collective-permute-done.7
  69.4 0.4 fusion.15
  69.8 2.4 %collective-permute-start.11 = (f32[256,128]{1,0:T(8,128)S(1)}, f32[256,128]{1,0:T(8,128)S(1)}, u32[]{:S(2)}, u32[]{:S(2)}) collective-permute-start(f32[256,128]{1,0:T(8,128)S(1)} %fusion.15), channel_id=1, source_target_pairs={{0,128},{16,144},{32,160},{48,176},{64,192},{80,208},{96,224},{112... | collective-permute-start | bytes 393224 | tf_op jit(solution)/shard_map/ppermute | solution.py:15
  72.2 2.4 %all_gather.10 = f32[256,256]{1,0:T(8,128)S(1)} all-gather(f32[256,128]{1,0:T(8,128)S(1)} %fusion.15), channel_id=1, replica_groups={{0,1},{2,3},{4,5},{6,7},{8,9},{10,11},{12,13},{14,15},{16,17},{18,19},{..., dimensions={1}, use_global_device_ids=true | all-gather | bytes 393216 | tf_op jit(solution)/shard_map/all_gather | solution.py:218
  74.6 0.0 collective-permute-done.6
  74.6 0.3 fusion.16
  74.9 0.4 fusion.8
  75.3 1.8 %collective-permute-start.8 = (bf16[256,256]{1,0:T(8,128)(2,1)S(1)}, bf16[256,256]{1,0:T(8,128)(2,1)S(1)}, u32[]{:S(2)}, u32[]{:S(2)}) collective-permute-start(bf16[256,256]{1,0:T(8,128)(2,1)S(1)} %get-tuple-element.40), channel_id=1, source_target_pairs={{0,128},{16,144},{32,160},{48,176},{64,192},{80,208},{96,224},{112... | collective-permute-start | bytes 393224 | tf_op jit(solution)/shard_map/ppermute | solution.py:15
  77.1 10.2 %all-to-all-done = bf16[16,16,1536]{2,1,0:T(8,128)(2,1)S(1)} async-done(((bf16[16,16,1536]{2,1,0:T(8,128)(2,1)}), bf16[16,16,1536]{2,1,0:T(8,128)(2,1)S(1)}, u32[]{:S(2)}, u32[]{:S(2)}) %all-to-all-start) | async-done | bytes 786464 | tf_op jit(solution)/shard_map/all_to_all | solution.py:222
  87.3 1.9 %collective-permute-start.10 = (bf16[256,1536]{1,0:T(8,128)(2,1)S(1)}, bf16[256,1536]{1,0:T(8,128)(2,1)S(1)}, u32[]{:S(2)}, u32[]{:S(2)}) collective-permute-start(bf16[256,1536]{1,0:T(8,128)(2,1)S(1)} %bitcast.45), channel_id=1, source_target_pairs={{0,1},{1,0},{2,3},{3,2},{4,5},{5,4},{6,7},{7,6},{8,9},{9,8},{10,11... | collective-permute-start | bytes 2359304 | tf_op jit(solution)/shard_map/ppermute | solution.py:241
  89.3 0.0 collective-permute-done.11
  89.3 0.4 fusion.18
  89.6 0.0 collective-permute-done.8
  89.7 0.3 fusion.17
  89.9 0.4 fusion.9
  90.4 2.7 %collective-permute-start.9 = (bf16[256,256]{1,0:T(8,128)(2,1)S(1)}, bf16[256,256]{1,0:T(8,128)(2,1)S(1)}, u32[]{:S(2)}, u32[]{:S(2)}) collective-permute-start(bf16[256,256]{1,0:T(8,128)(2,1)S(1)} %get-tuple-element.31), channel_id=1, source_target_pairs={{0,256},{16,272},{32,288},{48,304},{64,320},{80,336},{96,352},{112... | collective-permute-start | bytes 393224 | tf_op jit(solution)/shard_map/ppermute | solution.py:15
  93.0 2.4 %all_gather.11 = f32[256,256]{1,0:T(8,128)S(1)} all-gather(f32[256,128]{1,0:T(8,128)S(1)} %fusion.18), channel_id=1, replica_groups={{0,1},{2,3},{4,5},{6,7},{8,9},{10,11},{12,13},{14,15},{16,17},{18,19},{..., dimensions={1}, use_global_device_ids=true | all-gather | bytes 393216 | tf_op jit(solution)/shard_map/all_gather | solution.py:218
  95.5 0.0 collective-permute-done.10.refs_6_
  95.5 6.0 %trailing.1 = bf16[512,1792]{1,0:T(8,128)(2,1)} custom-call(bf16[512,2304]{1,0:T(8,128)(2,1)} %bitcast.50, bf16[2,256,256]{2,1,0:T(8,128)(2,1)} %bitcast.47, bf16[256,512]{1,0:T(8,128)(2,1)S(1)} %get-tuple-element.32.refs_2_, bf16[256,256]{1,0:T(8,128)(2,1)S(1)} %get-tuple-element.33.refs_3_, bf16[256,256]{1,0:T(8,128)(2,1)S(1)} %get-tuple-element.34.refs_4_, ...), custom_call_target="tpu_custom_call" | custom-call | flops 1207959552 | bytes 7077888 | tf_op jit(solution)/shard_map/trailing/pallas_call | solution.py:179
  101.4 0.0 collective-permute-done.9
  101.4 0.3 fusion.19
  101.7 1.1 %fusion = f32[1,256,256]{2,1,0:T(8,128)} fusion(f32[256,256]{1,0:T(8,128)S(1)} %get-tuple-element.43, f32[256,256]{1,0:T(8,128)S(1)} %fusion.19, f32[256,256]{1,0:T(8,128)S(1)} %all_gather.11), kind=kOutput, calls=%fused_computation.1 | convolution fusion | flops 201392128 | bytes 1048576 | tf_op jit(solution)/shard_map/dot_general | solution.py:19
  (1 shorter events, 0.0 us)
Async XLA Ops:
  0.6 53.3 %copy-start.1 = (f32[1,256,256]{2,1,0:T(8,128)S(1)}, f32[1,256,256]{2,1,0:T(8,128)}, u32[]{:S(2)}) copy-start(f32[1,256,256]{2,1,0:T(8,128)} %param.6) | copy-start | bytes 786436
  0.6 41.3 %copy-start = (bf16[1,2,256,256]{3,2,1,0:T(8,128)(2,1)S(1)}, bf16[1,2,256,256]{3,2,1,0:T(8,128)(2,1)}, u32[]{:S(2)}) copy-start(bf16[1,2,256,256]{3,2,1,0:T(8,128)(2,1)} %param.5) | copy-start | bytes 786436
  0.7 41.9 %collective-permute-start.2 = (f32[256,256]{1,0:T(8,128)}, f32[256,256]{1,0:T(8,128)S(1)}, u32[]{:S(2)}, u32[]{:S(2)}) collective-permute-start(f32[256,256]{1,0:T(8,128)} %bitcast.51), channel_id=1, source_target_pairs={{0,48},{16,64},{32,80},{48,96},{64,112},{80,128},{96,144},{112,160... | collective-permute-start | bytes 786440 | tf_op jit(solution)/shard_map/ppermute | solution.py:15
  6.0 36.6 %collective-permute-start.1 = (f32[256,256]{1,0:T(8,128)}, f32[256,256]{1,0:T(8,128)S(1)}, u32[]{:S(2)}, u32[]{:S(2)}) collective-permute-start(f32[256,256]{1,0:T(8,128)} %bitcast.52), channel_id=1, source_target_pairs={{0,32},{16,48},{32,64},{48,80},{64,96},{80,112},{96,128},{112,144}... | collective-permute-start | bytes 786440 | tf_op jit(solution)/shard_map/ppermute | solution.py:15
  9.5 33.1 %collective-permute-start = (f32[256,256]{1,0:T(8,128)}, f32[256,256]{1,0:T(8,128)S(1)}, u32[]{:S(2)}, u32[]{:S(2)}) collective-permute-start(f32[256,256]{1,0:T(8,128)} %bitcast.53), channel_id=1, source_target_pairs={{0,16},{16,32},{32,48},{48,64},{64,80},{80,96},{96,112},{112,128},... | collective-permute-start | bytes 786440 | tf_op jit(solution)/shard_map/ppermute | solution.py:15
  42.6 17.3 %collective-permute-start.5 = (bf16[256,256]{1,0:T(8,128)(2,1)S(1)}, bf16[256,256]{1,0:T(8,128)(2,1)S(1)}, u32[]{:S(2)}, u32[]{:S(2)}) collective-permute-start(bf16[256,256]{1,0:T(8,128)(2,1)S(1)} %get-tuple-element.24), channel_id=1, source_target_pairs={{0,16},{16,32},{32,48},{48,64},{64,80},{80,96},{96,112},{112,128},... | collective-permute-start | bytes 393224 | tf_op jit(solution)/shard_map/ppermute | solution.py:15
  46.0 19.5 %collective-permute-start.4 = (bf16[256,256]{1,0:T(8,128)(2,1)S(1)}, bf16[256,256]{1,0:T(8,128)(2,1)S(1)}, u32[]{:S(2)}, u32[]{:S(2)}) collective-permute-start(bf16[256,256]{1,0:T(8,128)(2,1)S(1)} %get-tuple-element.24), channel_id=1, source_target_pairs={{0,32},{16,48},{32,64},{48,80},{64,96},{80,112},{96,128},{112,144}... | collective-permute-start | bytes 393224 | tf_op jit(solution)/shard_map/ppermute | solution.py:15
  50.7 15.3 %collective-permute-start.3 = (bf16[256,256]{1,0:T(8,128)(2,1)S(1)}, bf16[256,256]{1,0:T(8,128)(2,1)S(1)}, u32[]{:S(2)}, u32[]{:S(2)}) collective-permute-start(bf16[256,256]{1,0:T(8,128)(2,1)S(1)} %get-tuple-element.24), channel_id=1, source_target_pairs={{0,48},{16,64},{32,80},{48,96},{64,112},{80,128},{96,144},{112,160... | collective-permute-start | bytes 393224 | tf_op jit(solution)/shard_map/ppermute | solution.py:15
  55.5 13.9 %collective-permute-start.7 = (f32[256,128]{1,0:T(8,128)S(1)}, f32[256,128]{1,0:T(8,128)S(1)}, u32[]{:S(2)}, u32[]{:S(2)}) collective-permute-start(f32[256,128]{1,0:T(8,128)S(1)} %constant_dynamic-slice_fusion), channel_id=1, source_target_pairs={{0,64},{16,80},{32,96},{48,112},{64,128},{80,144},{96,160},{112,17... | collective-permute-start | bytes 393224 | tf_op jit(solution)/shard_map/ppermute | solution.py:15
  59.9 27.4 %all-to-all-start = ((bf16[16,16,1536]{2,1,0:T(8,128)(2,1)}), bf16[16,16,1536]{2,1,0:T(8,128)(2,1)S(1)}, u32[]{:S(2)}, u32[]{:S(2)}) async-start(bf16[16,16,1536]{2,1,0:T(8,128)(2,1)} %bitcast.3), calls=%async_computation | async-start | bytes 1572864 | tf_op jit(solution)/shard_map/all_to_all | solution.py:222
  67.1 7.6 %collective-permute-start.6 = (bf16[256,256]{1,0:T(8,128)(2,1)S(1)}, bf16[256,256]{1,0:T(8,128)(2,1)S(1)}, u32[]{:S(2)}, u32[]{:S(2)}) collective-permute-start(bf16[256,256]{1,0:T(8,128)(2,1)S(1)} %get-tuple-element.38), channel_id=1, source_target_pairs={{0,64},{16,80},{32,96},{48,112},{64,128},{80,144},{96,160},{112,17... | collective-permute-start | bytes 393224 | tf_op jit(solution)/shard_map/ppermute | solution.py:15
  69.8 19.5 %collective-permute-start.11 = (f32[256,128]{1,0:T(8,128)S(1)}, f32[256,128]{1,0:T(8,128)S(1)}, u32[]{:S(2)}, u32[]{:S(2)}) collective-permute-start(f32[256,128]{1,0:T(8,128)S(1)} %fusion.15), channel_id=1, source_target_pairs={{0,128},{16,144},{32,160},{48,176},{64,192},{80,208},{96,224},{112... | collective-permute-start | bytes 393224 | tf_op jit(solution)/shard_map/ppermute | solution.py:15
  75.3 14.3 %collective-permute-start.8 = (bf16[256,256]{1,0:T(8,128)(2,1)S(1)}, bf16[256,256]{1,0:T(8,128)(2,1)S(1)}, u32[]{:S(2)}, u32[]{:S(2)}) collective-permute-start(bf16[256,256]{1,0:T(8,128)(2,1)S(1)} %get-tuple-element.40), channel_id=1, source_target_pairs={{0,128},{16,144},{32,160},{48,176},{64,192},{80,208},{96,224},{112... | collective-permute-start | bytes 393224 | tf_op jit(solution)/shard_map/ppermute | solution.py:15
  87.3 8.1 %collective-permute-start.10 = (bf16[256,1536]{1,0:T(8,128)(2,1)S(1)}, bf16[256,1536]{1,0:T(8,128)(2,1)S(1)}, u32[]{:S(2)}, u32[]{:S(2)}) collective-permute-start(bf16[256,1536]{1,0:T(8,128)(2,1)S(1)} %bitcast.45), channel_id=1, source_target_pairs={{0,1},{1,0},{2,3},{3,2},{4,5},{5,4},{6,7},{7,6},{8,9},{9,8},{10,11... | collective-permute-start | bytes 2359304 | tf_op jit(solution)/shard_map/ppermute | solution.py:241
  90.4 11.1 %collective-permute-start.9 = (bf16[256,256]{1,0:T(8,128)(2,1)S(1)}, bf16[256,256]{1,0:T(8,128)(2,1)S(1)}, u32[]{:S(2)}, u32[]{:S(2)}) collective-permute-start(bf16[256,256]{1,0:T(8,128)(2,1)S(1)} %get-tuple-element.31), channel_id=1, source_target_pairs={{0,256},{16,272},{32,288},{48,304},{64,320},{80,336},{96,352},{112... | collective-permute-start | bytes 393224 | tf_op jit(solution)/shard_map/ppermute | solution.py:15

commit v7 on v6

--- a/solution.py
+++ b/solution.py
@@ -123,48 +123,61 @@
     )(near, inverses)
 
 
-def trailing_kernel(
-    w, strip_hbm, inverse_ref, ones_ref, factor_ref, second_ref, own_ref, other_ref, out_hbm, strip_ref, out_ref, sems
+def edge_kernel(
+    w, strip_hbm, inverse_ref, ones_ref, second_ref, out_hbm, one_ref, two_ref, strip_ref, edge_ref, sems
 ):
+    def part(i):
+        at = pl.ds(i * w, w)
+        return pltpu.make_async_copy(strip_hbm.at[:, at], strip_ref.at[:, at], sems.at[i])
+
+    for i in range(3):
+        part(i).start()
+    part(0).wait()
+    one_ref[...] = rounded_dot(strip_ref[:, :w], inverse_ref[0])
+    part(1).wait()
+    panel = reduced_by(strip_ref[:, w:2 * w], one_ref[...], ones_ref[:, :w])
+    two_ref[...] = rounded_dot(panel, inverse_ref[1])
+    part(2).wait()
+    updated = reduced_by(strip_ref[:, 2 * w:], one_ref[...], ones_ref[:, w:])
+    edge_ref[...] = reduced_by(updated, two_ref[...], second_ref[...])
+    done = pltpu.make_async_copy(edge_ref, out_hbm.at[:, pl.ds(0, w)], sems.at[3])
+    done.start()
+    done.wait()
+
+
+def far_kernel(
+    w, strip_hbm, begun_hbm, one_ref, two_ref, factor_ref, own_ref, other_ref, out_hbm, strip_ref, out_ref, sems
+):
+    del begun_hbm
     half = own_ref.shape[1] // 2
     per_half = half // w
-    count = strip_ref.shape[1] // w
+    count = 2 * per_half
     core = lax.rem(lax.axis_index("blk"), 2)
 
-    blocks = [0, 1, 2]
-    for which in (core, 1 - core):
-        blocks += [3 + which * per_half + k for k in range(per_half)]
+    blocks = [which * per_half + k for which in (core, 1 - core) for k in range(per_half)]
 
     def columns(block):
-        return pl.ds(block * w if isinstance(block, int) else pl.multiple_of(block * w, w), w)
+        return pl.ds(pl.multiple_of(block * w, w), w)
 
     def part(i):
-        at = columns(blocks[i])
+        at = columns(blocks[i] + 3)
         return pltpu.make_async_copy(strip_hbm.at[:, at], strip_ref.at[:, i * w:(i + 1) * w], sems.at[0, i])
 
     def done_part(i):
-        at = columns(blocks[i] - 2)
-        return pltpu.make_async_copy(out_ref.at[:, (i - 2) * w:(i - 1) * w], out_hbm.at[:, at], sems.at[1, i])
+        at = columns(blocks[i] + 1)
+        return pltpu.make_async_copy(out_ref.at[:, i * w:(i + 1) * w], out_hbm.at[:, at], sems.at[1, i])
 
     for i in range(count):
         part(i).start()
-    part(0).wait()
-    first_factor = rounded_dot(strip_ref[:, :w], inverse_ref[0])
-    part(1).wait()
-    panel = reduced_by(strip_ref[:, w:2 * w], first_factor, ones_ref[:, :w])
-    second_factor = rounded_dot(panel, inverse_ref[1])
-    for i in range(2, count):
-        if i == 2:
-            one_rows, two_rows = ones_ref[:, w:2 * w], second_ref[...]
-        else:
-            ref, k = (own_ref, i - 3) if i - 3 < per_half else (other_ref, i - 3 - per_half)
-            one_rows = ref[:, k * w:(k + 1) * w]
-            two_rows = reduced_by(ref[:, half + k * w:half + (k + 1) * w], factor_ref[...], one_rows)
+    for i in range(count):
+        ref, k = (own_ref, i) if i < per_half else (other_ref, i - per_half)
+        one_rows = ref[:, k * w:(k + 1) * w]
+        two_rows = reduced_by(ref[:, half + k * w:half + (k + 1) * w], factor_ref[...], one_rows)
         part(i).wait()
-        updated = reduced_by(strip_ref[:, i * w:(i + 1) * w], first_factor, one_rows)
-        out_ref[:, (i - 2) * w:(i - 1) * w] = reduced_by(updated, second_factor, two_rows)
+        updated = reduced_by(strip_ref[:, i * w:(i + 1) * w], one_ref[...], one_rows)
+        out_ref[:, i * w:(i + 1) * w] = reduced_by(updated, two_ref[...], two_rows)
         done_part(i).start()
-    for i in range(2, count):
+    for i in range(count):
         done_part(i).wait()
 
 
@@ -172,25 +185,56 @@
     return tuple(pltpu.with_memory_space_constraint(x, pltpu.VMEM) for x in arrays)
 
 
-def trailing_of(strip, inverses, ones, factor_at_two, second_edge, own, other):
+def trailing_edge(strip, inverses, ones, second_edge):
     rows, width = strip.shape
     w = ones.shape[0]
-    vmem = pl.BlockSpec(memory_space=pltpu.VMEM)
+    vmem, hbm = pl.BlockSpec(memory_space=pltpu.VMEM), pl.BlockSpec(memory_space=pl.ANY)
     return pl.pallas_call(
-        lambda *refs: trailing_kernel(w, *refs),
-        out_shape=jax.ShapeDtypeStruct((rows, width - 2 * w), BF16),
-        in_specs=[pl.BlockSpec(memory_space=pltpu.HBM)] + [vmem] * 6,
-        out_specs=pl.BlockSpec(memory_space=pl.ANY),
+        lambda *refs: edge_kernel(w, *refs),
+        out_shape=(
+            jax.ShapeDtypeStruct((rows, width - 2 * w), BF16),
+            pltpu.VMEM((rows, w), BF16),
+            pltpu.VMEM((rows, w), BF16),
+        ),
+        in_specs=[hbm, vmem, vmem, vmem],
+        out_specs=(hbm, vmem, vmem),
         scratch_shapes=[
-            pltpu.VMEM((rows, width), BF16),
-            pltpu.VMEM((rows, width - 2 * w), BF16),
-            pltpu.SemaphoreType.DMA((2, width // w)),
+            pltpu.VMEM((rows, 3 * w), BF16),
+            pltpu.VMEM((rows, w), BF16),
+            pltpu.SemaphoreType.DMA((4,)),
         ],
         cost_estimate=pl.CostEstimate(
-            flops=4 * rows * w * width, bytes_accessed=4 * rows * width + 4 * w * width, transcendentals=0
-        ),
-        name="trailing",
-    )(strip, inverses, *in_vmem(ones, factor_at_two, second_edge, own, other))
+            flops=10 * rows * w * w, bytes_accessed=12 * rows * w, transcendentals=0
+        ),
+        name="edge",
+    )(strip, inverses, *in_vmem(ones, second_edge))
+
+
+def trailing_far(strip, begun, factors, factor_at_two, own, other):
+    rows, width = strip.shape
+    w = factor_at_two.shape[0]
+    blocks = width // w - 3
+    vmem, hbm = pl.BlockSpec(memory_space=pltpu.VMEM), pl.BlockSpec(memory_space=pl.ANY)
+    return pl.pallas_call(
+        lambda *refs: far_kernel(w, *refs),
+        out_shape=jax.ShapeDtypeStruct(begun.shape, BF16),
+        in_specs=[hbm, hbm] + [vmem] * 5,
+        out_specs=hbm,
+        input_output_aliases={1: 0},
+        scratch_shapes=[
+            pltpu.VMEM((rows, blocks * w), BF16),
+            pltpu.VMEM((rows, blocks * w), BF16),
+            pltpu.SemaphoreType.DMA((2, blocks)),
+        ],
+        cost_estimate=pl.CostEstimate(
+            flops=w, bytes_accessed=w, transcendentals=0
+        ),
+        name="far",
+    )(strip, begun, *in_vmem(*factors, factor_at_two, own, other))
+
+
+def after(x, gate):
+    return lax.optimization_barrier((x, gate))[0]
 
 
 def body(panel_strip, pivot_inverses, coupling, pivot_nodes):
@@ -205,6 +249,8 @@
 
     near_here, far_here = picked_rows(pivot_nodes, strip, w, per)
     near = lax.all_gather(near_here, "blk", axis=0, tiled=True)
+    near, far_here = lax.optimization_barrier((near, far_here))
+    own = lax.all_to_all(far_here, "blk", 0, 0, tiled=True)
     boundary, factor_at_two, second_edge, one_rows = boundary_of(near, inverses)
     back_one, back_two, back_three, boundary = lax.optimization_barrier(
         (back_one, back_two, back_three, boundary)
@@ -218,8 +264,6 @@
         return lax.all_gather(half, "blk", axis=1, tiled=True, axis_index_groups=pairs)
 
     arriving = [passed_along(boundary, "tm", by) for by in (1, 2, 3)]
-    arriving[0], far_here = lax.optimization_barrier((arriving[0], far_here))
-    own = lax.all_to_all(far_here, "blk", 0, 0, tiled=True)
     span_two = matmul_high(span, back_one)
     span_three = matmul_high(span_two, back_two)
     span_four = matmul_high(span_three, back_three)
@@ -238,14 +282,16 @@
     wire = current.astype(BF16)
 
     incoming = passed_along(wire, "tm", 8)
-    other = lax.ppermute(own, "blk", [(i, i ^ 1) for i in range(blocks)])
-    span_sixteen = joined(matmul_high(span_eight, passed_eight))
+    other = lax.ppermute(after(own, wire), "blk", [(i, i ^ 1) for i in range(blocks)])
+    begun, *factors = trailing_edge(strip, inverses, after(one_rows, wire), second_edge)
+    half_sixteen = matmul_high(span_eight, passed_eight)
+    incoming, begun, half_sixteen = lax.optimization_barrier((incoming, begun, half_sixteen))
+    span_sixteen = joined(half_sixteen)
     current = advance(current, incoming, span_eight)
     wire = current.astype(BF16)
 
-    wire, factor_at_two = lax.optimization_barrier((wire, factor_at_two))
     incoming = passed_along(wire, "tm", 16)
-    trailing = trailing_of(strip, inverses, one_rows, factor_at_two, second_edge, own, other)
+    trailing = trailing_far(strip, begun, factors, factor_at_two, own, other)
     incoming, trailing = lax.optimization_barrier((incoming, trailing))
     current = advance(current, incoming, span_sixteen)
     return (trailing[None], current[None])

time: 103 us -> 102 us (level)
  waiting for transfers between devices: 10.3 us -> 0.03 us
  matrix products: 7.44 us -> 10.7 us
  starting transfers between devices: 42.8 us -> 45.7 us
  Pallas kernels: 9.49 us -> 11 us
  blocking collectives: 31.9 us -> 33.3 us
    all_to_all x1, waiting for transfers between devices: 10.2 us -> 0.01 us  [body(): own = lax.all_to_all(far_here, 'blk', 0, 0, tiled=True)]
    ppermute x11, starting transfers between devices: 36.2 us -> 39.6 us  [passed_along(): return lax.ppermute(x, axis, [(i, i + by) for i in range(count - by)])]
    dot_general x17, matrix products: 7.44 us -> 10.7 us  [matmul_high(): jnp.dot(left, right, precision=lax.Precision.HIGHEST, preferred_element_t...]
    pallas_call x1 -> x2, Pallas kernels: 5.97 us -> 7.52 us  [the longest x1 3.95 us: trailing_far(): pl.pallas_call(lambda *refs: far_kernel(w, *refs), out_shape=jax.ShapeDty...]
    all_gather x2, blocking collectives: 4.82 us -> 6.13 us  [joined(): lax.all_gather(half, 'blk', axis=1, tiled=True, axis_index_groups=pairs)]
    all_to_all x1, starting transfers between devices: 4.69 us -> 3.56 us  [body(): own = lax.all_to_all(far_here, 'blk', 0, 0, tiled=True)]
  transfers between devices with their start and end apart: 13 -> 13, of which waited for: 1 -> 0; matrix products, arithmetic and copies ran while one was open for 6% -> 9% of each run, Pallas kernels for 9% -> 11%
where the time goes in v7:
time: 102 us
  starting transfers between devices  45.7 us (45%)
  blocking collectives  33.3 us (33%)
  Pallas kernels  11 us (11%)
  matrix products  10.7 us (10%)
    ppermute x11, starting transfers between devices, passed_along(): return lax.ppermute(x, axis, [(i, i + by) for i in range(count - by)])  39.6 us
    all_gather x1, blocking collectives, body(): near = lax.all_gather(near_here, 'blk', axis=0, tiled=True)  27.2 us
    dot_general x17, matrix products, matmul_high(): jnp.dot(left, right, precision=lax.Precision.HIGHEST, preferred_element_t...  10.7 us
    all_gather x2, blocking collectives, joined(): lax.all_gather(half, 'blk', axis=1, tiled=True, axis_index_groups=pairs)  6.13 us
    pallas_call x1, Pallas kernels, trailing_far(): pl.pallas_call(lambda *refs: far_kernel(w, *refs), out_shape=jax.ShapeDty...  3.95 us
    pallas_call x1, Pallas kernels, trailing_edge(): pl.pallas_call(lambda *refs: edge_kernel(w, *refs), out_shape=(jax.ShapeD...  3.56 us
    all_to_all x1, starting transfers between devices, body(): own = lax.all_to_all(far_here, 'blk', 0, 0, tiled=True)  3.56 us
    pallas_call x1, Pallas kernels, picked_rows(): pl.pallas_call(lambda *refs: pick_kernel(w, per, chunks, *refs), out_shap...  2.86 us
  transfers between devices with their start and end apart: 13, of which 0 were waited for; matrix products, arithmetic and copies ran while one was open for 9% of the time, Pallas kernels for 11%

profile of v7, /device:TPU:1, one launch (start us, length us, event | category | flops | bytes accessed | tf_op | source)
XLA Modules:
  0.0 101.8 jit_solution(4344359881438326147)
XLA Ops:
  0.6 4.0 %collective-permute-start = (f32[256,256]{1,0:T(8,128)}, f32[256,256]{1,0:T(8,128)S(1)}, u32[]{:S(2)}, u32[]{:S(2)}) collective-permute-start(f32[256,256]{1,0:T(8,128)} %bitcast.52), channel_id=1, source_target_pairs={{0,16},{16,32},{32,48},{48,64},{64,80},{80,96},{96,112},{112,128},... | collective-permute-start | bytes 786440 | tf_op jit(solution)/shard_map/ppermute | solution.py:15
  4.6 5.1 %collective-permute-start.1 = (f32[256,256]{1,0:T(8,128)}, f32[256,256]{1,0:T(8,128)}, u32[]{:S(2)}, u32[]{:S(2)}) collective-permute-start(f32[256,256]{1,0:T(8,128)} %bitcast.53), channel_id=1, source_target_pairs={{0,32},{16,48},{32,64},{48,80},{64,96},{80,112},{96,128},{112,144}... | collective-permute-start | bytes 786440 | tf_op jit(solution)/shard_map/ppermute | solution.py:15
  9.7 4.1 %collective-permute-start.2 = (f32[256,256]{1,0:T(8,128)}, f32[256,256]{1,0:T(8,128)}, u32[]{:S(2)}, u32[]{:S(2)}) collective-permute-start(f32[256,256]{1,0:T(8,128)} %bitcast.54), channel_id=1, source_target_pairs={{0,48},{16,64},{32,80},{48,96},{64,112},{80,128},{96,144},{112,160... | collective-permute-start | bytes 786440 | tf_op jit(solution)/shard_map/ppermute | solution.py:15
  13.7 2.9 %pick.1 = (bf16[16,1792]{1,0:T(8,128)(2,1)S(1)}, bf16[256,1536]{1,0:T(8,128)(2,1)}) custom-call(s32[3,256]{1,0:T(4,128)} %refs_0_.1, bf16[512,2304]{1,0:T(8,128)(2,1)} %bitcast.49), custom_call_target="tpu_custom_call" | custom-call | flops 113246208 | bytes 2359296 | tf_op jit(solution)/shard_map/pick/pallas_call | solution.py:75
  16.6 0.0 copy-start
  16.6 0.0 copy-start.1
  16.6 27.2 %all_gather.9.refs_0_ = bf16[256,1792]{1,0:T(8,128)(2,1)S(1)} all-gather(bf16[16,1792]{1,0:T(8,128)(2,1)S(1)} %get-tuple-element.26), channel_id=1, replica_groups=mesh['tm'=32,'blk'=16] {'blk'}, dimensions={0}, use_global_device_ids=true | all-gather | bytes 974848 | tf_op jit(solution)/shard_map/all_gather | solution.py:251
  43.8 3.6 %all-to-all-start = ((bf16[16,16,1536]{2,1,0:T(8,128)(2,1)}), bf16[16,16,1536]{2,1,0:T(8,128)(2,1)S(1)}, u32[]{:S(2)}, u32[]{:S(2)}) async-start(bf16[16,16,1536]{2,1,0:T(8,128)(2,1)} %bitcast.3), calls=%async_computation | async-start | bytes 1572864 | tf_op jit(solution)/shard_map/all_to_all | solution.py:253
  47.4 0.0 copy-done
  47.4 0.7 boundary.1
  48.0 0.0 collective-permute-done
  48.0 0.0 collective-permute-done.1
  48.0 0.0 collective-permute-done.2
  48.1 3.2 %collective-permute-start.4 = (bf16[256,256]{1,0:T(8,128)(2,1)S(1)}, bf16[256,256]{1,0:T(8,128)(2,1)S(1)}, u32[]{:S(2)}, u32[]{:S(2)}) collective-permute-start(bf16[256,256]{1,0:T(8,128)(2,1)S(1)} %get-tuple-element.32), channel_id=1, source_target_pairs={{0,32},{16,48},{32,64},{48,80},{64,96},{80,112},{96,128},{112,144}... | collective-permute-start | bytes 393224 | tf_op jit(solution)/shard_map/ppermute | solution.py:15
  51.2 1.3 %collective-permute-start.5 = (bf16[256,256]{1,0:T(8,128)(2,1)S(1)}, bf16[256,256]{1,0:T(8,128)(2,1)S(1)}, u32[]{:S(2)}, u32[]{:S(2)}) collective-permute-start(bf16[256,256]{1,0:T(8,128)(2,1)S(1)} %get-tuple-element.32), channel_id=1, source_target_pairs={{0,16},{16,32},{32,48},{48,64},{64,80},{80,96},{96,112},{112,128},... | collective-permute-start | bytes 393224 | tf_op jit(solution)/shard_map/ppermute | solution.py:15
  52.5 5.5 %collective-permute-start.3 = (bf16[256,256]{1,0:T(8,128)(2,1)S(1)}, bf16[256,256]{1,0:T(8,128)(2,1)S(1)}, u32[]{:S(2)}, u32[]{:S(2)}) collective-permute-start(bf16[256,256]{1,0:T(8,128)(2,1)S(1)} %get-tuple-element.32), channel_id=1, source_target_pairs={{0,48},{16,64},{32,80},{48,96},{64,112},{80,128},{96,144},{112,160... | collective-permute-start | bytes 393224 | tf_op jit(solution)/shard_map/ppermute | solution.py:15
  58.0 0.0 copy-done.1
  58.1 0.6 fusion.5
  58.7 1.5 %fusion.10 = f32[256,256]{1,0:T(8,128)S(1)} fusion(f32[256,256]{1,0:T(8,128)S(1)} %fusion.5, f32[256,256]{1,0:T(8,128)} %collective-permute-done.1), kind=kOutput, calls=%fused_computation.15 | convolution fusion | flops 201326592 | bytes 786432 | tf_op jit(solution)/shard_map/dot_general | solution.py:19
  60.2 1.3 %fusion.14 = f32[256,256]{1,0:T(8,128)S(1)} fusion(f32[256,256]{1,0:T(8,128)S(1)} %fusion.10, f32[256,256]{1,0:T(8,128)} %collective-permute-done.2), kind=kOutput, calls=%fused_computation.19 | convolution fusion | flops 201326592 | bytes 786432 | tf_op jit(solution)/shard_map/dot_general | solution.py:19
  61.6 4.4 %collective-permute-start.7 = (f32[256,128]{1,0:T(8,128)S(1)}, f32[256,128]{1,0:T(8,128)S(1)}, u32[]{:S(2)}, u32[]{:S(2)}) collective-permute-start(f32[256,128]{1,0:T(8,128)S(1)} %constant_dynamic-slice_fusion), channel_id=1, source_target_pairs={{0,64},{16,80},{32,96},{48,112},{64,128},{80,144},{96,160},{112,17... | collective-permute-start | bytes 393224 | tf_op jit(solution)/shard_map/ppermute | solution.py:15
  66.0 0.0 collective-permute-done.4
  66.0 0.4 fusion.12
  66.4 0.4 fusion.13
  66.8 0.0 collective-permute-done.5
  66.8 0.3 fusion.3
  67.1 0.0 collective-permute-done.3
  67.1 0.3 fusion.11
  67.4 0.6 fusion.1
  68.0 0.4 fusion.7
  68.5 2.3 %collective-permute-start.6 = (bf16[256,256]{1,0:T(8,128)(2,1)S(1)}, bf16[256,256]{1,0:T(8,128)(2,1)S(1)}, u32[]{:S(2)}, u32[]{:S(2)}) collective-permute-start(bf16[256,256]{1,0:T(8,128)(2,1)S(1)} %get-tuple-element.50), channel_id=1, source_target_pairs={{0,64},{16,80},{32,96},{48,112},{64,128},{80,144},{96,160},{112,17... | collective-permute-start | bytes 393224 | tf_op jit(solution)/shard_map/ppermute | solution.py:15
  70.8 0.0 collective-permute-done.7
  70.8 0.4 fusion.15
  71.2 2.4 %collective-permute-start.9 = (f32[256,128]{1,0:T(8,128)S(1)}, f32[256,128]{1,0:T(8,128)S(1)}, u32[]{:S(2)}, u32[]{:S(2)}) collective-permute-start(f32[256,128]{1,0:T(8,128)S(1)} %fusion.15), channel_id=1, source_target_pairs={{0,128},{16,144},{32,160},{48,176},{64,192},{80,208},{96,224},{112... | collective-permute-start | bytes 393224 | tf_op jit(solution)/shard_map/ppermute | solution.py:15
  73.6 3.5 %all_gather.10 = f32[256,256]{1,0:T(8,128)S(1)} all-gather(f32[256,128]{1,0:T(8,128)S(1)} %fusion.15), channel_id=1, replica_groups={{0,1},{2,3},{4,5},{6,7},{8,9},{10,11},{12,13},{14,15},{16,17},{18,19},{..., dimensions={1}, use_global_device_ids=true | all-gather | bytes 393216 | tf_op jit(solution)/shard_map/all_gather | solution.py:264
  77.1 0.0 collective-permute-done.6
  77.1 0.3 fusion.16
  77.4 1.1 %fusion.8 = (bf16[256,256]{1,0:T(8,128)(2,1)}, f32[256,256]{1,0:T(8,128)S(1)}) fusion(f32[256,256]{1,0:T(8,128)S(1)} %get-tuple-element.51, f32[256,256]{1,0:T(8,128)S(1)} %fusion.16, f32[256,256]{1,0:T(8,128)S(1)} %fusion.14), kind=kOutput, calls=%fused_computation.13 | convolution fusion | flops 201457664 | bytes 1179648 | tf_op jit(solution)/shard_map/dot_general | solution.py:19
  78.5 2.8 %collective-permute-start.8 = (bf16[256,256]{1,0:T(8,128)(2,1)}, bf16[256,256]{1,0:T(8,128)(2,1)S(1)}, u32[]{:S(2)}, u32[]{:S(2)}) collective-permute-start(bf16[256,256]{1,0:T(8,128)(2,1)} %get-tuple-element.52), channel_id=1, source_target_pairs={{0,128},{16,144},{32,160},{48,176},{64,192},{80,208},{96,224},{112... | collective-permute-start | bytes 393224 | tf_op jit(solution)/shard_map/ppermute | solution.py:15
  81.3 0.0 all-to-all-done
  81.3 2.6 %collective-permute-start.11 = (bf16[256,1536]{1,0:T(8,128)(2,1)S(1)}, bf16[256,1536]{1,0:T(8,128)(2,1)S(1)}, u32[]{:S(2)}, u32[]{:S(2)}) collective-permute-start(bf16[256,1536]{1,0:T(8,128)(2,1)S(1)} %bitcast.45), channel_id=1, source_target_pairs={{0,1},{1,0},{2,3},{3,2},{4,5},{5,4},{6,7},{7,6},{8,9},{9,8},{10,11... | collective-permute-start | bytes 2359304 | tf_op jit(solution)/shard_map/ppermute | solution.py:285
  83.9 0.0 collective-permute-done.9
  83.9 0.4 fusion.17
  84.3 3.6 %edge.1 = (bf16[512,1792]{1,0:T(8,128)(2,1)}, bf16[512,256]{1,0:T(8,128)(2,1)S(1)}, bf16[512,256]{1,0:T(8,128)(2,1)S(1)}) custom-call(bf16[512,2304]{1,0:T(8,128)(2,1)} %bitcast.50, bf16[2,256,256]{2,1,0:T(8,128)(2,1)} %bitcast.47, bf16[256,512]{1,0:T(8,128)(2,1)S(1)} %get-tuple-element.37.refs_2_, bf16[256,256]{1,0:T(8,128)(2,1)S(1)} %get-tuple-element.38.refs_3_), custom_call_target="tpu_custom_call" | custom-call | flops 335544320 | bytes 1572864 | tf_op jit(solution)/shard_map/edge/pallas_call | solution.py:192
  87.9 0.0 collective-permute-done.8
  87.9 0.3 fusion.18
  88.2 1.1 %fusion.9 = (bf16[256,256]{1,0:T(8,128)(2,1)S(1)}, f32[256,256]{1,0:T(8,128)}) fusion(f32[256,256]{1,0:T(8,128)S(1)} %get-tuple-element.53, f32[256,256]{1,0:T(8,128)S(1)} %fusion.18, f32[256,256]{1,0:T(8,128)S(1)} %all_gather.10), kind=kOutput, calls=%fused_computation.14 | convolution fusion | flops 201457664 | bytes 1179648 | tf_op jit(solution)/shard_map/dot_general | solution.py:19
  89.3 4.5 %collective-permute-start.10 = (bf16[256,256]{1,0:T(8,128)(2,1)S(1)}, bf16[256,256]{1,0:T(8,128)(2,1)S(1)}, u32[]{:S(2)}, u32[]{:S(2)}) collective-permute-start(bf16[256,256]{1,0:T(8,128)(2,1)S(1)} %get-tuple-element.54), channel_id=1, source_target_pairs={{0,256},{16,272},{32,288},{48,304},{64,320},{80,336},{96,352},{112... | collective-permute-start | bytes 393224 | tf_op jit(solution)/shard_map/ppermute | solution.py:15
  93.8 2.6 %all_gather.11 = f32[256,256]{1,0:T(8,128)S(1)} all-gather(f32[256,128]{1,0:T(8,128)S(1)} %fusion.17), channel_id=1, replica_groups={{0,1},{2,3},{4,5},{6,7},{8,9},{10,11},{12,13},{14,15},{16,17},{18,19},{..., dimensions={1}, use_global_device_ids=true | all-gather | bytes 393216 | tf_op jit(solution)/shard_map/all_gather | solution.py:264
  96.4 0.0 collective-permute-done.11.refs_6_
  96.4 0.0 copy-start.2
  96.4 4.0 %far.1 = bf16[512,1792]{1,0:T(8,128)(2,1)} custom-call(bf16[512,2304]{1,0:T(8,128)(2,1)} %bitcast.51, bf16[512,1792]{1,0:T(8,128)(2,1)} %get-tuple-element.41.refs_1_, bf16[512,256]{1,0:T(8,128)(2,1)S(1)} %get-tuple-element.42.refs_2_, bf16[512,256]{1,0:T(8,128)(2,1)S(1)} %get-tuple-element.43.refs_3_, ...), custom_call_target="tpu_custom_call", output_to_operand_aliasing={{}: (1, {})} | custom-call | flops 256 | bytes 256 | tf_op jit(solution)/shard_map/far/pallas_call | solution.py:218
  100.3 0.0 collective-permute-done.10
  100.4 0.3 fusion.19
  100.6 0.0 copy-done.2
  100.6 1.1 %fusion = f32[1,256,256]{2,1,0:T(8,128)} fusion(f32[256,256]{1,0:T(8,128)S(1)} %copy-done.2, f32[256,256]{1,0:T(8,128)S(1)} %fusion.19, f32[256,256]{1,0:T(8,128)S(1)} %all_gather.11), kind=kOutput, calls=%fused_computation.1 | convolution fusion | flops 201392128 | bytes 1048576 | tf_op jit(solution)/shard_map/dot_general | solution.py:19
  (1 shorter events, 0.0 us)
Async XLA Ops:
  0.6 47.4 %collective-permute-start = (f32[256,256]{1,0:T(8,128)}, f32[256,256]{1,0:T(8,128)S(1)}, u32[]{:S(2)}, u32[]{:S(2)}) collective-permute-start(f32[256,256]{1,0:T(8,128)} %bitcast.52), channel_id=1, source_target_pairs={{0,16},{16,32},{32,48},{48,64},{64,80},{80,96},{96,112},{112,128},... | collective-permute-start | bytes 786440 | tf_op jit(solution)/shard_map/ppermute | solution.py:15
  4.6 43.4 %collective-permute-start.1 = (f32[256,256]{1,0:T(8,128)}, f32[256,256]{1,0:T(8,128)}, u32[]{:S(2)}, u32[]{:S(2)}) collective-permute-start(f32[256,256]{1,0:T(8,128)} %bitcast.53), channel_id=1, source_target_pairs={{0,32},{16,48},{32,64},{48,80},{64,96},{80,112},{96,128},{112,144}... | collective-permute-start | bytes 786440 | tf_op jit(solution)/shard_map/ppermute | solution.py:15
  9.7 38.4 %collective-permute-start.2 = (f32[256,256]{1,0:T(8,128)}, f32[256,256]{1,0:T(8,128)}, u32[]{:S(2)}, u32[]{:S(2)}) collective-permute-start(f32[256,256]{1,0:T(8,128)} %bitcast.54), channel_id=1, source_target_pairs={{0,48},{16,64},{32,80},{48,96},{64,112},{80,128},{96,144},{112,160... | collective-permute-start | bytes 786440 | tf_op jit(solution)/shard_map/ppermute | solution.py:15
  16.6 30.8 %copy-start = (bf16[1,2,256,256]{3,2,1,0:T(8,128)(2,1)S(1)}, bf16[1,2,256,256]{3,2,1,0:T(8,128)(2,1)}, u32[]{:S(2)}) copy-start(bf16[1,2,256,256]{3,2,1,0:T(8,128)(2,1)} %param.5) | copy-start | bytes 786436
  16.6 41.4 %copy-start.1 = (f32[1,256,256]{2,1,0:T(8,128)S(1)}, f32[1,256,256]{2,1,0:T(8,128)}, u32[]{:S(2)}) copy-start(f32[1,256,256]{2,1,0:T(8,128)} %param.6) | copy-start | bytes 786436
  43.8 37.5 %all-to-all-start = ((bf16[16,16,1536]{2,1,0:T(8,128)(2,1)}), bf16[16,16,1536]{2,1,0:T(8,128)(2,1)S(1)}, u32[]{:S(2)}, u32[]{:S(2)}) async-start(bf16[16,16,1536]{2,1,0:T(8,128)(2,1)} %bitcast.3), calls=%async_computation | async-start | bytes 1572864 | tf_op jit(solution)/shard_map/all_to_all | solution.py:253
  48.1 17.9 %collective-permute-start.4 = (bf16[256,256]{1,0:T(8,128)(2,1)S(1)}, bf16[256,256]{1,0:T(8,128)(2,1)S(1)}, u32[]{:S(2)}, u32[]{:S(2)}) collective-permute-start(bf16[256,256]{1,0:T(8,128)(2,1)S(1)} %get-tuple-element.32), channel_id=1, source_target_pairs={{0,32},{16,48},{32,64},{48,80},{64,96},{80,112},{96,128},{112,144}... | collective-permute-start | bytes 393224 | tf_op jit(solution)/shard_map/ppermute | solution.py:15
  51.2 15.6 %collective-permute-start.5 = (bf16[256,256]{1,0:T(8,128)(2,1)S(1)}, bf16[256,256]{1,0:T(8,128)(2,1)S(1)}, u32[]{:S(2)}, u32[]{:S(2)}) collective-permute-start(bf16[256,256]{1,0:T(8,128)(2,1)S(1)} %get-tuple-element.32), channel_id=1, source_target_pairs={{0,16},{16,32},{32,48},{48,64},{64,80},{80,96},{96,112},{112,128},... | collective-permute-start | bytes 393224 | tf_op jit(solution)/shard_map/ppermute | solution.py:15
  52.5 14.6 %collective-permute-start.3 = (bf16[256,256]{1,0:T(8,128)(2,1)S(1)}, bf16[256,256]{1,0:T(8,128)(2,1)S(1)}, u32[]{:S(2)}, u32[]{:S(2)}) collective-permute-start(bf16[256,256]{1,0:T(8,128)(2,1)S(1)} %get-tuple-element.32), channel_id=1, source_target_pairs={{0,48},{16,64},{32,80},{48,96},{64,112},{80,128},{96,144},{112,160... | collective-permute-start | bytes 393224 | tf_op jit(solution)/shard_map/ppermute | solution.py:15
  61.6 9.2 %collective-permute-start.7 = (f32[256,128]{1,0:T(8,128)S(1)}, f32[256,128]{1,0:T(8,128)S(1)}, u32[]{:S(2)}, u32[]{:S(2)}) collective-permute-start(f32[256,128]{1,0:T(8,128)S(1)} %constant_dynamic-slice_fusion), channel_id=1, source_target_pairs={{0,64},{16,80},{32,96},{48,112},{64,128},{80,144},{96,160},{112,17... | collective-permute-start | bytes 393224 | tf_op jit(solution)/shard_map/ppermute | solution.py:15
  68.5 8.7 %collective-permute-start.6 = (bf16[256,256]{1,0:T(8,128)(2,1)S(1)}, bf16[256,256]{1,0:T(8,128)(2,1)S(1)}, u32[]{:S(2)}, u32[]{:S(2)}) collective-permute-start(bf16[256,256]{1,0:T(8,128)(2,1)S(1)} %get-tuple-element.50), channel_id=1, source_target_pairs={{0,64},{16,80},{32,96},{48,112},{64,128},{80,144},{96,160},{112,17... | collective-permute-start | bytes 393224 | tf_op jit(solution)/shard_map/ppermute | solution.py:15
  71.2 12.7 %collective-permute-start.9 = (f32[256,128]{1,0:T(8,128)S(1)}, f32[256,128]{1,0:T(8,128)S(1)}, u32[]{:S(2)}, u32[]{:S(2)}) collective-permute-start(f32[256,128]{1,0:T(8,128)S(1)} %fusion.15), channel_id=1, source_target_pairs={{0,128},{16,144},{32,160},{48,176},{64,192},{80,208},{96,224},{112... | collective-permute-start | bytes 393224 | tf_op jit(solution)/shard_map/ppermute | solution.py:15
  78.5 9.4 %collective-permute-start.8 = (bf16[256,256]{1,0:T(8,128)(2,1)}, bf16[256,256]{1,0:T(8,128)(2,1)S(1)}, u32[]{:S(2)}, u32[]{:S(2)}) collective-permute-start(bf16[256,256]{1,0:T(8,128)(2,1)} %get-tuple-element.52), channel_id=1, source_target_pairs={{0,128},{16,144},{32,160},{48,176},{64,192},{80,208},{96,224},{112... | collective-permute-start | bytes 393224 | tf_op jit(solution)/shard_map/ppermute | solution.py:15
  81.3 15.0 %collective-permute-start.11 = (bf16[256,1536]{1,0:T(8,128)(2,1)S(1)}, bf16[256,1536]{1,0:T(8,128)(2,1)S(1)}, u32[]{:S(2)}, u32[]{:S(2)}) collective-permute-start(bf16[256,1536]{1,0:T(8,128)(2,1)S(1)} %bitcast.45), channel_id=1, source_target_pairs={{0,1},{1,0},{2,3},{3,2},{4,5},{5,4},{6,7},{7,6},{8,9},{9,8},{10,11... | collective-permute-start | bytes 2359304 | tf_op jit(solution)/shard_map/ppermute | solution.py:285
  89.3 11.1 %collective-permute-start.10 = (bf16[256,256]{1,0:T(8,128)(2,1)S(1)}, bf16[256,256]{1,0:T(8,128)(2,1)S(1)}, u32[]{:S(2)}, u32[]{:S(2)}) collective-permute-start(bf16[256,256]{1,0:T(8,128)(2,1)S(1)} %get-tuple-element.54), channel_id=1, source_target_pairs={{0,256},{16,272},{32,288},{48,304},{64,320},{80,336},{96,352},{112... | collective-permute-start | bytes 393224 | tf_op jit(solution)/shard_map/ppermute | solution.py:15
  96.4 4.2 %copy-start.2 = (f32[256,256]{1,0:T(8,128)S(1)}, f32[256,256]{1,0:T(8,128)}, u32[]{:S(2)}) copy-start(f32[256,256]{1,0:T(8,128)} %get-tuple-element.55) | copy-start | bytes 786436

commit v8 on v7

--- a/solution.py
+++ b/solution.py
@@ -28,7 +28,7 @@
     return (block.astype(F32) - product).astype(BF16)
 
 
-def pick_kernel(w, per, chunks, nodes_hbm, strip_hbm, near_ref, far_ref, strip_ref, nodes_ref, sems):
+def pick_kernel(w, per, chunks, nodes_hbm, strip_hbm, near_ref, far_hbm, strip_ref, nodes_ref, far_ref, sems, far_sems):
     rows = strip_ref.shape[0]
     cols = strip_ref.shape[1] // chunks
 
@@ -38,7 +38,7 @@
 
     nodes = pltpu.make_async_copy(nodes_hbm, nodes_ref, sems.at[chunks])
     nodes.start()
-    for i in range(chunks):
+    for i in [*range(1, chunks), 0]:
         part(i).start()
     nodes.wait()
     me = lax.axis_index("blk")
@@ -52,8 +52,9 @@
     picker = jnp.concatenate(
         [(wanted == at_lane + first).astype(F32).astype(BF16) for first in range(0, rows, lanes)], 1
     )
-    width = far_ref.shape[1] // 2
-    for i in range(chunks):
+    width = far_ref.shape[2] // 2
+    copies = []
+    for i in [*range(1, chunks), 0]:
         part(i).wait()
         at = pl.ds(i * cols, cols)
         got = jnp.dot(picker, strip_ref[:, at], preferred_element_type=F32).astype(BF16)
@@ -64,9 +65,17 @@
             near_ref[:, 3 * w:4 * w] = two[:, 2 * w:]
             near_ref[:, 4 * w:] = edge
         else:
-            for row in range((i - 1) * per, far_ref.shape[0], 2 * per):
-                far_ref[row:row + per, :width] = one
-                far_ref[row:row + per, width:] = two
+            far_ref[i - 1, :, :width] = one
+            far_ref[i - 1, :, width:] = two
+            for row in range((i - 1) * per, far_hbm.shape[0], 2 * per):
+                copies.append(
+                    pltpu.make_async_copy(
+                        far_ref.at[i - 1], far_hbm.at[pl.ds(row, per), :], far_sems.at[row // per]
+                    )
+                )
+                copies[-1].start()
+    for copy in copies:
+        copy.wait()
 
 
 def picked_rows(pivot_nodes, strip, w, per):
@@ -76,14 +85,16 @@
         lambda *refs: pick_kernel(w, per, chunks, *refs),
         out_shape=(
             pltpu.VMEM((per, 7 * w), BF16),
-            pltpu.VMEM((w, width - 3 * w), BF16),
+            jax.ShapeDtypeStruct((w, width - 3 * w), BF16),
         ),
         in_specs=[pl.BlockSpec(memory_space=pltpu.HBM), pl.BlockSpec(memory_space=pltpu.HBM)],
-        out_specs=tuple(pl.BlockSpec(memory_space=pltpu.VMEM) for _ in range(2)),
+        out_specs=(pl.BlockSpec(memory_space=pltpu.VMEM), pl.BlockSpec(memory_space=pl.ANY)),
         scratch_shapes=[
             pltpu.VMEM((rows, width), BF16),
             pltpu.SMEM(pivot_nodes.shape, jnp.int32),
+            pltpu.VMEM((chunks - 1, per, width - 3 * w), BF16),
             pltpu.SemaphoreType.DMA((chunks + 1,)),
+            pltpu.SemaphoreType.DMA((w // per,)),
         ],
         cost_estimate=pl.CostEstimate(
             flops=2 * 3 * per * rows * width, bytes_accessed=2 * rows * width, transcendentals=0
@@ -146,10 +157,11 @@
 
 
 def far_kernel(
-    w, strip_hbm, begun_hbm, one_ref, two_ref, factor_ref, own_ref, other_ref, out_hbm, strip_ref, out_ref, sems
+    w, strip_hbm, begun_hbm, own_hbm, other_ref, one_ref, two_ref, factor_ref, out_hbm,
+    strip_ref, own_ref, out_ref, sems, own_sem,
 ):
     del begun_hbm
-    half = own_ref.shape[1] // 2
+    half = own_hbm.shape[1] // 2
     per_half = half // w
     count = 2 * per_half
     core = lax.rem(lax.axis_index("blk"), 2)
@@ -167,8 +179,11 @@
         at = columns(blocks[i] + 1)
         return pltpu.make_async_copy(out_ref.at[:, i * w:(i + 1) * w], out_hbm.at[:, at], sems.at[1, i])
 
+    own = pltpu.make_async_copy(own_hbm, own_ref, own_sem)
+    own.start()
     for i in range(count):
         part(i).start()
+    own.wait()
     for i in range(count):
         ref, k = (own_ref, i) if i < per_half else (other_ref, i - per_half)
         one_rows = ref[:, k * w:(k + 1) * w]
@@ -204,7 +219,7 @@
             pltpu.SemaphoreType.DMA((4,)),
         ],
         cost_estimate=pl.CostEstimate(
-            flops=10 * rows * w * w, bytes_accessed=12 * rows * w, transcendentals=0
+            flops=w, bytes_accessed=w, transcendentals=0
         ),
         name="edge",
     )(strip, inverses, *in_vmem(ones, second_edge))
@@ -218,19 +233,21 @@
     return pl.pallas_call(
         lambda *refs: far_kernel(w, *refs),
         out_shape=jax.ShapeDtypeStruct(begun.shape, BF16),
-        in_specs=[hbm, hbm] + [vmem] * 5,
+        in_specs=[hbm] * 3 + [vmem] * 4,
         out_specs=hbm,
         input_output_aliases={1: 0},
         scratch_shapes=[
             pltpu.VMEM((rows, blocks * w), BF16),
+            pltpu.VMEM(own.shape, BF16),
             pltpu.VMEM((rows, blocks * w), BF16),
             pltpu.SemaphoreType.DMA((2, blocks)),
+            pltpu.SemaphoreType.DMA,
         ],
         cost_estimate=pl.CostEstimate(
             flops=w, bytes_accessed=w, transcendentals=0
         ),
         name="far",
-    )(strip, begun, *in_vmem(*factors, factor_at_two, own, other))
+    )(strip, begun, own, *in_vmem(other, *factors, factor_at_two))
 
 
 def after(x, gate):
@@ -275,17 +292,17 @@
     wire = current.astype(BF16)
 
     incoming = passed_along(wire, "tm", 4)
+    begun, *factors = trailing_edge(strip, inverses, after(one_rows, wire), second_edge)
     passed_eight = passed_along(half_eight, "tm", 8)
-    span_eight = joined(half_eight)
-    incoming, span_eight = lax.optimization_barrier((incoming, span_eight))
+    incoming, begun, half_eight = lax.optimization_barrier((incoming, begun, half_eight))
     current = advance(current, incoming, span_four)
     wire = current.astype(BF16)
 
     incoming = passed_along(wire, "tm", 8)
     other = lax.ppermute(after(own, wire), "blk", [(i, i ^ 1) for i in range(blocks)])
-    begun, *factors = trailing_edge(strip, inverses, after(one_rows, wire), second_edge)
+    span_eight = joined(after(half_eight, wire))
     half_sixteen = matmul_high(span_eight, passed_eight)
-    incoming, begun, half_sixteen = lax.optimization_barrier((incoming, begun, half_sixteen))
+    incoming, half_sixteen = lax.optimization_barrier((incoming, half_sixteen))
     span_sixteen = joined(half_sixteen)
     current = advance(current, incoming, span_eight)
     wire = current.astype(BF16)

time: 102 us -> 103 us (level)
  matrix products: 10.7 us -> 7.44 us
  blocking collectives: 33.3 us -> 36.5 us
    dot_general x17, matrix products: 10.7 us -> 7.44 us  [matmul_high(): jnp.dot(left, right, precision=lax.Precision.HIGHEST, preferred_element_t...]
    all_gather x2, blocking collectives: 6.13 us -> 9.31 us  [joined(): lax.all_gather(half, 'blk', axis=1, tiled=True, axis_index_groups=pairs)]
  transfers between devices with their start and end apart: 13 -> 13, of which waited for: 0 -> 0; matrix products, arithmetic and copies ran while one was open for 9% -> 6% of each run, Pallas kernels for 11% -> 11%
where the time goes in v8:
time: 103 us; the launch traced here: 102 us
  starting transfers between devices  45.8 us (44%)
  blocking collectives  36.5 us (35%)
  Pallas kernels  11.5 us (11%)
  matrix products  7.44 us (7%)
    ppermute x11, starting transfers between devices, passed_along(): return lax.ppermute(x, axis, [(i, i + by) for i in range(count - by)])  39.9 us
    all_gather x1, blocking collectives, body(): near = lax.all_gather(near_here, 'blk', axis=0, tiled=True)  27.2 us
    all_gather x2, blocking collectives, joined(): lax.all_gather(half, 'blk', axis=1, tiled=True, axis_index_groups=pairs)  9.31 us
    dot_general x17, matrix products, matmul_high(): jnp.dot(left, right, precision=lax.Precision.HIGHEST, preferred_element_t...  7.44 us
    pallas_call x1, Pallas kernels, trailing_far(): pl.pallas_call(lambda *refs: far_kernel(w, *refs), out_shape=jax.ShapeDty...  4.73 us
    pallas_call x1, Pallas kernels, trailing_edge(): pl.pallas_call(lambda *refs: edge_kernel(w, *refs), out_shape=(jax.ShapeD...  3.57 us
    all_to_all x1, starting transfers between devices, body(): own = lax.all_to_all(far_here, 'blk', 0, 0, tiled=True)  3.56 us
    pallas_call x1, Pallas kernels, picked_rows(): pl.pallas_call(lambda *refs: pick_kernel(w, per, chunks, *refs), out_shap...  2.59 us
  transfers between devices with their start and end apart: 13, of which 0 were waited for; matrix products, arithmetic and copies ran while one was open for 6% of the time, Pallas kernels for 11%

profile of v8, /device:TPU:1, one launch (start us, length us, event | category | flops | bytes accessed | tf_op | source)
XLA Modules:
  0.0 102.3 jit_solution(14162140397803068383)
XLA Ops:
  0.6 4.0 %collective-permute-start = (f32[256,256]{1,0:T(8,128)}, f32[256,256]{1,0:T(8,128)S(1)}, u32[]{:S(2)}, u32[]{:S(2)}) collective-permute-start(f32[256,256]{1,0:T(8,128)} %bitcast.52), channel_id=1, source_target_pairs={{0,16},{16,32},{32,48},{48,64},{64,80},{80,96},{96,112},{112,128},... | collective-permute-start | bytes 786440 | tf_op jit(solution)/shard_map/ppermute | solution.py:15
  4.6 4.4 %collective-permute-start.1 = (f32[256,256]{1,0:T(8,128)}, f32[256,256]{1,0:T(8,128)S(1)}, u32[]{:S(2)}, u32[]{:S(2)}) collective-permute-start(f32[256,256]{1,0:T(8,128)} %bitcast.53), channel_id=1, source_target_pairs={{0,32},{16,48},{32,64},{48,80},{64,96},{80,112},{96,128},{112,144}... | collective-permute-start | bytes 786440 | tf_op jit(solution)/shard_map/ppermute | solution.py:15
  9.0 4.1 %collective-permute-start.2 = (f32[256,256]{1,0:T(8,128)}, f32[256,256]{1,0:T(8,128)S(1)}, u32[]{:S(2)}, u32[]{:S(2)}) collective-permute-start(f32[256,256]{1,0:T(8,128)} %bitcast.54), channel_id=1, source_target_pairs={{0,48},{16,64},{32,80},{48,96},{64,112},{80,128},{96,144},{112,160... | collective-permute-start | bytes 786440 | tf_op jit(solution)/shard_map/ppermute | solution.py:15
  13.1 2.6 %pick.1 = (bf16[16,1792]{1,0:T(8,128)(2,1)S(1)}, bf16[256,1536]{1,0:T(8,128)(2,1)}) custom-call(s32[3,256]{1,0:T(4,128)} %refs_0_.1, bf16[512,2304]{1,0:T(8,128)(2,1)} %bitcast.47), custom_call_target="tpu_custom_call" | custom-call | flops 113246208 | bytes 2359296 | tf_op jit(solution)/shard_map/pick/pallas_call | solution.py:84
  15.6 0.0 copy-start
  15.7 0.0 copy-start.2
  15.7 27.2 %all_gather.9.refs_0_ = bf16[256,1792]{1,0:T(8,128)(2,1)S(1)} all-gather(bf16[16,1792]{1,0:T(8,128)(2,1)S(1)} %get-tuple-element.27), channel_id=1, replica_groups=mesh['tm'=32,'blk'=16] {'blk'}, dimensions={0}, use_global_device_ids=true | all-gather | bytes 974848 | tf_op jit(solution)/shard_map/all_gather | solution.py:268
  42.8 3.6 %all-to-all-start = ((bf16[16,16,1536]{2,1,0:T(8,128)(2,1)}), bf16[16,16,1536]{2,1,0:T(8,128)(2,1)S(1)}, u32[]{:S(2)}, u32[]{:S(2)}) async-start(bf16[16,16,1536]{2,1,0:T(8,128)(2,1)} %bitcast.56), calls=%async_computation | async-start | bytes 1572864 | tf_op jit(solution)/shard_map/all_to_all | solution.py:270
  46.4 0.0 copy-done
  46.4 0.7 boundary.1
  47.1 0.0 collective-permute-done
  47.1 0.0 collective-permute-done.1
  47.1 0.0 collective-permute-done.2
  47.1 2.6 %collective-permute-start.3 = (bf16[256,256]{1,0:T(8,128)(2,1)S(1)}, bf16[256,256]{1,0:T(8,128)(2,1)S(1)}, u32[]{:S(2)}, u32[]{:S(2)}) collective-permute-start(bf16[256,256]{1,0:T(8,128)(2,1)S(1)} %get-tuple-element.33), channel_id=1, source_target_pairs={{0,48},{16,64},{32,80},{48,96},{64,112},{80,128},{96,144},{112,160... | collective-permute-start | bytes 393224 | tf_op jit(solution)/shard_map/ppermute | solution.py:15
  49.7 4.4 %collective-permute-start.4 = (bf16[256,256]{1,0:T(8,128)(2,1)S(1)}, bf16[256,256]{1,0:T(8,128)(2,1)S(1)}, u32[]{:S(2)}, u32[]{:S(2)}) collective-permute-start(bf16[256,256]{1,0:T(8,128)(2,1)S(1)} %get-tuple-element.33), channel_id=1, source_target_pairs={{0,32},{16,48},{32,64},{48,80},{64,96},{80,112},{96,128},{112,144}... | collective-permute-start | bytes 393224 | tf_op jit(solution)/shard_map/ppermute | solution.py:15
  54.0 1.9 %collective-permute-start.5 = (bf16[256,256]{1,0:T(8,128)(2,1)S(1)}, bf16[256,256]{1,0:T(8,128)(2,1)S(1)}, u32[]{:S(2)}, u32[]{:S(2)}) collective-permute-start(bf16[256,256]{1,0:T(8,128)(2,1)S(1)} %get-tuple-element.33), channel_id=1, source_target_pairs={{0,16},{16,32},{32,48},{48,64},{64,80},{80,96},{96,112},{112,128},... | collective-permute-start | bytes 393224 | tf_op jit(solution)/shard_map/ppermute | solution.py:15
  56.0 0.0 copy-done.2
  56.0 0.6 fusion.5
  56.6 0.6 fusion.10
  57.2 0.4 fusion.14
  57.6 4.4 %collective-permute-start.7 = (f32[256,128]{1,0:T(8,128)S(1)}, f32[256,128]{1,0:T(8,128)S(1)}, u32[]{:S(2)}, u32[]{:S(2)}) collective-permute-start(f32[256,128]{1,0:T(8,128)S(1)} %constant_dynamic-slice_fusion), channel_id=1, source_target_pairs={{0,64},{16,80},{32,96},{48,112},{64,128},{80,144},{96,160},{112,17... | collective-permute-start | bytes 393224 | tf_op jit(solution)/shard_map/ppermute | solution.py:15
  62.0 0.0 collective-permute-done.4
  62.0 0.4 fusion.12
  62.4 0.4 fusion.13
  62.8 0.0 collective-permute-done.3
  62.8 0.3 fusion.11
  63.1 0.0 collective-permute-done.5
  63.1 0.3 fusion.3
  63.4 0.6 fusion.1
  64.0 0.4 fusion.7
  64.5 3.2 %collective-permute-start.6 = (bf16[256,256]{1,0:T(8,128)(2,1)S(1)}, bf16[256,256]{1,0:T(8,128)(2,1)S(1)}, u32[]{:S(2)}, u32[]{:S(2)}) collective-permute-start(bf16[256,256]{1,0:T(8,128)(2,1)S(1)} %get-tuple-element.52), channel_id=1, source_target_pairs={{0,64},{16,80},{32,96},{48,112},{64,128},{80,144},{96,160},{112,17... | collective-permute-start | bytes 393224 | tf_op jit(solution)/shard_map/ppermute | solution.py:15
  67.7 0.0 collective-permute-done.7
  67.7 0.4 fusion.15
  68.1 3.7 %collective-permute-start.9 = (f32[256,128]{1,0:T(8,128)S(1)}, f32[256,128]{1,0:T(8,128)S(1)}, u32[]{:S(2)}, u32[]{:S(2)}) collective-permute-start(f32[256,128]{1,0:T(8,128)S(1)} %fusion.15), channel_id=1, source_target_pairs={{0,128},{16,144},{32,160},{48,176},{64,192},{80,208},{96,224},{112... | collective-permute-start | bytes 393224 | tf_op jit(solution)/shard_map/ppermute | solution.py:15
  71.8 3.6 %edge.1 = (bf16[512,1792]{1,0:T(8,128)(2,1)}, bf16[512,256]{1,0:T(8,128)(2,1)S(1)}, bf16[512,256]{1,0:T(8,128)(2,1)S(1)}) custom-call(bf16[512,2304]{1,0:T(8,128)(2,1)} %bitcast.48, bf16[2,256,256]{2,1,0:T(8,128)(2,1)} %bitcast.45, bf16[256,512]{1,0:T(8,128)(2,1)S(1)} %get-tuple-element.35.refs_2_, bf16[256,256]{1,0:T(8,128)(2,1)S(1)} %get-tuple-element.36.refs_3_), custom_call_target="tpu_custom_call" | custom-call | flops 256 | bytes 256 | tf_op jit(solution)/shard_map/edge/pallas_call | solution.py:207
  75.3 0.0 collective-permute-done.6
  75.4 0.3 fusion.16
  75.6 0.4 fusion.8
  76.0 3.3 %collective-permute-start.8 = (bf16[256,256]{1,0:T(8,128)(2,1)S(1)}, bf16[256,256]{1,0:T(8,128)(2,1)S(1)}, u32[]{:S(2)}, u32[]{:S(2)}) collective-permute-start(bf16[256,256]{1,0:T(8,128)(2,1)S(1)} %get-tuple-element.54), channel_id=1, source_target_pairs={{0,128},{16,144},{32,160},{48,176},{64,192},{80,208},{96,224},{112... | collective-permute-start | bytes 393224 | tf_op jit(solution)/shard_map/ppermute | solution.py:15
  79.3 3.9 %all_gather.10 = f32[256,256]{1,0:T(8,128)S(1)} all-gather(f32[256,128]{1,0:T(8,128)S(1)} %fusion.15), channel_id=1, replica_groups={{0,1},{2,3},{4,5},{6,7},{8,9},{10,11},{12,13},{14,15},{16,17},{18,19},{..., dimensions={1}, use_global_device_ids=true | all-gather | bytes 393216 | tf_op jit(solution)/shard_map/all_gather | solution.py:281
  83.2 0.0 all-to-all-done
  83.2 0.0 copy-start.1
  83.2 2.3 %collective-permute-start.11 = (bf16[256,1536]{1,0:T(8,128)(2,1)S(1)}, bf16[256,1536]{1,0:T(8,128)(2,1)S(1)}, u32[]{:S(2)}, u32[]{:S(2)}) collective-permute-start(bf16[256,1536]{1,0:T(8,128)(2,1)S(1)} %bitcast.50), channel_id=1, source_target_pairs={{0,1},{1,0},{2,3},{3,2},{4,5},{5,4},{6,7},{7,6},{8,9},{9,8},{10,11... | collective-permute-start | bytes 2359304 | tf_op jit(solution)/shard_map/ppermute | solution.py:302
  85.5 0.0 collective-permute-done.9
  85.5 0.4 fusion.17
  85.8 0.0 collective-permute-done.8
  85.9 0.3 fusion.18
  86.1 0.4 fusion.9
  86.6 4.1 %collective-permute-start.10 = (bf16[256,256]{1,0:T(8,128)(2,1)S(1)}, bf16[256,256]{1,0:T(8,128)(2,1)S(1)}, u32[]{:S(2)}, u32[]{:S(2)}) collective-permute-start(bf16[256,256]{1,0:T(8,128)(2,1)S(1)} %get-tuple-element.56), channel_id=1, source_target_pairs={{0,256},{16,272},{32,288},{48,304},{64,320},{80,336},{96,352},{112... | collective-permute-start | bytes 393224 | tf_op jit(solution)/shard_map/ppermute | solution.py:15
  90.7 5.4 %all_gather.11 = f32[256,256]{1,0:T(8,128)S(1)} all-gather(f32[256,128]{1,0:T(8,128)S(1)} %fusion.17), channel_id=1, replica_groups={{0,1},{2,3},{4,5},{6,7},{8,9},{10,11},{12,13},{14,15},{16,17},{18,19},{..., dimensions={1}, use_global_device_ids=true | all-gather | bytes 393216 | tf_op jit(solution)/shard_map/all_gather | solution.py:281
  96.1 0.0 collective-permute-done.11.refs_3_
  96.1 0.0 copy-done.1
  96.1 4.7 %far.1 = bf16[512,1792]{1,0:T(8,128)(2,1)} custom-call(bf16[512,2304]{1,0:T(8,128)(2,1)} %bitcast.49, bf16[512,1792]{1,0:T(8,128)(2,1)} %get-tuple-element.43.refs_1_, bf16[256,1536]{1,0:T(8,128)(2,1)} %bitcast.51, bf16[256,1536]{1,0:T(8,128)(2,1)S(1)} %collective-permute-done.11.refs_3_, ...), custom_call_target="tpu_custom_call", output_to_operand_aliasing={{}: (1, {})} | custom-call | flops 256 | bytes 256 | tf_op jit(solution)/shard_map/far/pallas_call | solution.py:233
  100.9 0.0 collective-permute-done.10
  100.9 0.3 fusion.19
  101.2 1.1 %fusion = f32[1,256,256]{2,1,0:T(8,128)} fusion(f32[256,256]{1,0:T(8,128)S(1)} %get-tuple-element.57, f32[256,256]{1,0:T(8,128)S(1)} %fusion.19, f32[256,256]{1,0:T(8,128)S(1)} %all_gather.11), kind=kOutput, calls=%fused_computation.1 | convolution fusion | flops 201392128 | bytes 1048576 | tf_op jit(solution)/shard_map/dot_general | solution.py:19
  (1 shorter events, 0.0 us)
Async XLA Ops:
  0.6 46.4 %collective-permute-start = (f32[256,256]{1,0:T(8,128)}, f32[256,256]{1,0:T(8,128)S(1)}, u32[]{:S(2)}, u32[]{:S(2)}) collective-permute-start(f32[256,256]{1,0:T(8,128)} %bitcast.52), channel_id=1, source_target_pairs={{0,16},{16,32},{32,48},{48,64},{64,80},{80,96},{96,112},{112,128},... | collective-permute-start | bytes 786440 | tf_op jit(solution)/shard_map/ppermute | solution.py:15
  4.6 42.5 %collective-permute-start.1 = (f32[256,256]{1,0:T(8,128)}, f32[256,256]{1,0:T(8,128)S(1)}, u32[]{:S(2)}, u32[]{:S(2)}) collective-permute-start(f32[256,256]{1,0:T(8,128)} %bitcast.53), channel_id=1, source_target_pairs={{0,32},{16,48},{32,64},{48,80},{64,96},{80,112},{96,128},{112,144}... | collective-permute-start | bytes 786440 | tf_op jit(solution)/shard_map/ppermute | solution.py:15
  9.0 38.1 %collective-permute-start.2 = (f32[256,256]{1,0:T(8,128)}, f32[256,256]{1,0:T(8,128)S(1)}, u32[]{:S(2)}, u32[]{:S(2)}) collective-permute-start(f32[256,256]{1,0:T(8,128)} %bitcast.54), channel_id=1, source_target_pairs={{0,48},{16,64},{32,80},{48,96},{64,112},{80,128},{96,144},{112,160... | collective-permute-start | bytes 786440 | tf_op jit(solution)/shard_map/ppermute | solution.py:15
  15.6 30.8 %copy-start = (bf16[1,2,256,256]{3,2,1,0:T(8,128)(2,1)S(1)}, bf16[1,2,256,256]{3,2,1,0:T(8,128)(2,1)}, u32[]{:S(2)}) copy-start(bf16[1,2,256,256]{3,2,1,0:T(8,128)(2,1)} %param.5) | copy-start | bytes 786436
  15.7 40.3 %copy-start.2 = (f32[1,256,256]{2,1,0:T(8,128)S(1)}, f32[1,256,256]{2,1,0:T(8,128)}, u32[]{:S(2)}) copy-start(f32[1,256,256]{2,1,0:T(8,128)} %param.6) | copy-start | bytes 786436
  42.8 40.3 %all-to-all-start = ((bf16[16,16,1536]{2,1,0:T(8,128)(2,1)}), bf16[16,16,1536]{2,1,0:T(8,128)(2,1)S(1)}, u32[]{:S(2)}, u32[]{:S(2)}) async-start(bf16[16,16,1536]{2,1,0:T(8,128)(2,1)} %bitcast.56), calls=%async_computation | async-start | bytes 1572864 | tf_op jit(solution)/shard_map/all_to_all | solution.py:270
  47.1 15.7 %collective-permute-start.3 = (bf16[256,256]{1,0:T(8,128)(2,1)S(1)}, bf16[256,256]{1,0:T(8,128)(2,1)S(1)}, u32[]{:S(2)}, u32[]{:S(2)}) collective-permute-start(bf16[256,256]{1,0:T(8,128)(2,1)S(1)} %get-tuple-element.33), channel_id=1, source_target_pairs={{0,48},{16,64},{32,80},{48,96},{64,112},{80,128},{96,144},{112,160... | collective-permute-start | bytes 393224 | tf_op jit(solution)/shard_map/ppermute | solution.py:15
  49.7 12.3 %collective-permute-start.4 = (bf16[256,256]{1,0:T(8,128)(2,1)S(1)}, bf16[256,256]{1,0:T(8,128)(2,1)S(1)}, u32[]{:S(2)}, u32[]{:S(2)}) collective-permute-start(bf16[256,256]{1,0:T(8,128)(2,1)S(1)} %get-tuple-element.33), channel_id=1, source_target_pairs={{0,32},{16,48},{32,64},{48,80},{64,96},{80,112},{96,128},{112,144}... | collective-permute-start | bytes 393224 | tf_op jit(solution)/shard_map/ppermute | solution.py:15
  54.0 9.0 %collective-permute-start.5 = (bf16[256,256]{1,0:T(8,128)(2,1)S(1)}, bf16[256,256]{1,0:T(8,128)(2,1)S(1)}, u32[]{:S(2)}, u32[]{:S(2)}) collective-permute-start(bf16[256,256]{1,0:T(8,128)(2,1)S(1)} %get-tuple-element.33), channel_id=1, source_target_pairs={{0,16},{16,32},{32,48},{48,64},{64,80},{80,96},{96,112},{112,128},... | collective-permute-start | bytes 393224 | tf_op jit(solution)/shard_map/ppermute | solution.py:15
  57.6 10.1 %collective-permute-start.7 = (f32[256,128]{1,0:T(8,128)S(1)}, f32[256,128]{1,0:T(8,128)S(1)}, u32[]{:S(2)}, u32[]{:S(2)}) collective-permute-start(f32[256,128]{1,0:T(8,128)S(1)} %constant_dynamic-slice_fusion), channel_id=1, source_target_pairs={{0,64},{16,80},{32,96},{48,112},{64,128},{80,144},{96,160},{112,17... | collective-permute-start | bytes 393224 | tf_op jit(solution)/shard_map/ppermute | solution.py:15
  64.5 10.9 %collective-permute-start.6 = (bf16[256,256]{1,0:T(8,128)(2,1)S(1)}, bf16[256,256]{1,0:T(8,128)(2,1)S(1)}, u32[]{:S(2)}, u32[]{:S(2)}) collective-permute-start(bf16[256,256]{1,0:T(8,128)(2,1)S(1)} %get-tuple-element.52), channel_id=1, source_target_pairs={{0,64},{16,80},{32,96},{48,112},{64,128},{80,144},{96,160},{112,17... | collective-permute-start | bytes 393224 | tf_op jit(solution)/shard_map/ppermute | solution.py:15
  68.1 17.4 %collective-permute-start.9 = (f32[256,128]{1,0:T(8,128)S(1)}, f32[256,128]{1,0:T(8,128)S(1)}, u32[]{:S(2)}, u32[]{:S(2)}) collective-permute-start(f32[256,128]{1,0:T(8,128)S(1)} %fusion.15), channel_id=1, source_target_pairs={{0,128},{16,144},{32,160},{48,176},{64,192},{80,208},{96,224},{112... | collective-permute-start | bytes 393224 | tf_op jit(solution)/shard_map/ppermute | solution.py:15
  76.0 9.8 %collective-permute-start.8 = (bf16[256,256]{1,0:T(8,128)(2,1)S(1)}, bf16[256,256]{1,0:T(8,128)(2,1)S(1)}, u32[]{:S(2)}, u32[]{:S(2)}) collective-permute-start(bf16[256,256]{1,0:T(8,128)(2,1)S(1)} %get-tuple-element.54), channel_id=1, source_target_pairs={{0,128},{16,144},{32,160},{48,176},{64,192},{80,208},{96,224},{112... | collective-permute-start | bytes 393224 | tf_op jit(solution)/shard_map/ppermute | solution.py:15
  83.2 13.0 %copy-start.1 = (bf16[16,16,1536]{2,1,0:T(8,128)(2,1)}, bf16[16,16,1536]{2,1,0:T(8,128)(2,1)S(1)}, u32[]{:S(2)}) copy-start(bf16[16,16,1536]{2,1,0:T(8,128)(2,1)S(1)} %all-to-all-done) | copy-start | bytes 2359300
  83.2 13.0 %collective-permute-start.11 = (bf16[256,1536]{1,0:T(8,128)(2,1)S(1)}, bf16[256,1536]{1,0:T(8,128)(2,1)S(1)}, u32[]{:S(2)}, u32[]{:S(2)}) collective-permute-start(bf16[256,1536]{1,0:T(8,128)(2,1)S(1)} %bitcast.50), channel_id=1, source_target_pairs={{0,1},{1,0},{2,3},{3,2},{4,5},{5,4},{6,7},{7,6},{8,9},{9,8},{10,11... | collective-permute-start | bytes 2359304 | tf_op jit(solution)/shard_map/ppermute | solution.py:302
  86.6 14.3 %collective-permute-start.10 = (bf16[256,256]{1,0:T(8,128)(2,1)S(1)}, bf16[256,256]{1,0:T(8,128)(2,1)S(1)}, u32[]{:S(2)}, u32[]{:S(2)}) collective-permute-start(bf16[256,256]{1,0:T(8,128)(2,1)S(1)} %get-tuple-element.56), channel_id=1, source_target_pairs={{0,256},{16,272},{32,288},{48,304},{64,320},{80,336},{96,352},{112... | collective-permute-start | bytes 393224 | tf_op jit(solution)/shard_map/ppermute | solution.py:15

commit v9 on v8

--- a/solution.py
+++ b/solution.py
@@ -1,6 +1,7 @@
 import jax
 import jax.numpy as jnp
 from jax import lax
+from jax.experimental.layout import Layout, with_layout_constraint
 from jax.experimental import pallas as pl
 from jax.experimental.pallas import tpu as pltpu
 from jax.sharding import PartitionSpec as P
@@ -13,6 +14,17 @@
 def passed_along(x, axis, by):
     count = lax.axis_size(axis)
     return lax.ppermute(x, axis, [(i, i + by) for i in range(count - by)])
+
+
+def core_passed(x, reaches):
+    count, blocks = lax.axis_size("tm"), lax.axis_size("blk")
+    pairs = [
+        (i * blocks + j, (i + reaches[j % 2]) * blocks + j)
+        for i in range(count)
+        for j in range(blocks)
+        if reaches[j % 2] and i + reaches[j % 2] < count
+    ]
+    return lax.ppermute(x, ("tm", "blk"), pairs)
 
 
 def matmul_high(left, right):
@@ -276,19 +288,24 @@
     def advance(current, incoming, reach):
         return matmul_high(matmul_high(reach, incoming.astype(F32)), reach.T) + current
 
+    core_pairs = [[i, i + 1] for i in range(0, blocks, 2)]
+
     def joined(half):
-        pairs = [[i, i + 1] for i in range(0, blocks, 2)]
-        return lax.all_gather(half, "blk", axis=1, tiled=True, axis_index_groups=pairs)
-
-    arriving = [passed_along(boundary, "tm", by) for by in (1, 2, 3)]
+        return lax.all_gather(half, "blk", axis=1, tiled=True, axis_index_groups=core_pairs)
+
+    arriving = [core_passed(boundary, by) for by in ((1, 2), (3, None))]
     span_two = matmul_high(span, back_one)
     span_three = matmul_high(span_two, back_two)
     span_four = matmul_high(span_three, back_three)
-    half_four = lax.dynamic_slice_in_dim(span_four, lax.axis_index("blk") % 2 * (w // 2), w // 2, 1)
+    core = lax.axis_index("blk") % 2
+    half_four = lax.dynamic_slice_in_dim(span_four, core * (w // 2), w // 2, 1)
     half_eight = matmul_high(span_four, passed_along(half_four, "tm", 4))
-    current = boundary.astype(F32)
-    for incoming, reach in zip(arriving, (span, span_two, span_three)):
-        current = advance(current, incoming, reach)
+    terms = jnp.zeros((w, w), F32)
+    by_core = with_layout_constraint(jnp.where(core == 0, span, span_two), Layout((0, 1)))
+    for incoming, reach in zip(arriving, (by_core, span_three)):
+        terms = advance(terms, incoming, reach)
+    terms = lax.all_gather(terms, "blk", axis_index_groups=core_pairs)
+    current = boundary.astype(F32) + (terms[0] + terms[1])
     wire = current.astype(BF16)
 
     incoming = passed_along(wire, "tm", 4)

time: 103 us -> 99.1 us (0.962)
  starting transfers between devices: 45.8 us -> 38 us
  blocking collectives: 36.5 us -> 39.4 us
    ppermute x11 -> x8, starting transfers between devices: 39.9 us -> 28.3 us  [passed_along(): return lax.ppermute(x, axis, [(i, i + by) for i in range(count - by)])]
    ppermute x0 -> x2, starting transfers between devices: none -> 3.82 us  [core_passed(): return lax.ppermute(x, ('tm', 'blk'), pairs)]
    all_gather x2 -> x3, blocking collectives: 9.31 us -> 12.3 us  [the longest x1 6.58 us: body(): terms = lax.all_gather(terms, 'blk', axis_index_groups=core_pairs)]
    dot_general x17 -> x15, matrix products: 7.44 us -> 8.29 us  [matmul_high(): jnp.dot(left, right, precision=lax.Precision.HIGHEST, preferred_element_t...]
  transfers between devices with their start and end apart: 13 -> 12, of which waited for: 0 -> 0; matrix products, arithmetic and copies ran while one was open for 6% -> 7% of each run, Pallas kernels for 11% -> 12%
where the time goes in v9:
time: 99.1 us; the launch traced here: 98.4 us
  blocking collectives  39.4 us (40%)
  starting transfers between devices  38 us (38%)
  Pallas kernels  11.5 us (12%)
  matrix products  8.29 us (8%)
    ppermute x8, starting transfers between devices, passed_along(): return lax.ppermute(x, axis, [(i, i + by) for i in range(count - by)])  28.3 us
    all_gather x1, blocking collectives, body(): near = lax.all_gather(near_here, 'blk', axis=0, tiled=True)  27.2 us
    dot_general x15, matrix products, matmul_high(): jnp.dot(left, right, precision=lax.Precision.HIGHEST, preferred_element_t...  8.29 us
    all_gather x1, blocking collectives, body(): terms = lax.all_gather(terms, 'blk', axis_index_groups=core_pairs)  6.58 us
    all_gather x2, blocking collectives, joined(): lax.all_gather(half, 'blk', axis=1, tiled=True, axis_index_groups=core_pa...  5.68 us
    pallas_call x1, Pallas kernels, trailing_far(): pl.pallas_call(lambda *refs: far_kernel(w, *refs), out_shape=jax.ShapeDty...  4.73 us
    ppermute x2, starting transfers between devices, core_passed(): return lax.ppermute(x, ('tm', 'blk'), pairs)  3.82 us
    all_to_all x1, starting transfers between devices, body(): own = lax.all_to_all(far_here, 'blk', 0, 0, tiled=True)  3.56 us
  transfers between devices with their start and end apart: 12, of which 0 were waited for; matrix products, arithmetic and copies ran while one was open for 7% of the time, Pallas kernels for 12%

profile of v9, /device:TPU:1, one launch (start us, length us, event | category | flops | bytes accessed | tf_op | source)
XLA Modules:
  0.0 98.4 jit_solution(704067916361239691)
XLA Ops:
  0.6 4.0 %collective-permute-start = (f32[256,256]{1,0:T(8,128)}, f32[256,256]{1,0:T(8,128)S(1)}, u32[]{:S(2)}, u32[]{:S(2)}) collective-permute-start(f32[256,256]{1,0:T(8,128)} %bitcast.56), channel_id=1, source_target_pairs={{0,16},{16,32},{32,48},{48,64},{64,80},{80,96},{96,112},{112,128},... | collective-permute-start | bytes 786440 | tf_op jit(solution)/shard_map/ppermute | solution.py:16
  4.6 4.4 %collective-permute-start.1 = (f32[256,256]{1,0:T(8,128)}, f32[256,256]{1,0:T(8,128)S(1)}, u32[]{:S(2)}, u32[]{:S(2)}) collective-permute-start(f32[256,256]{1,0:T(8,128)} %bitcast.57), channel_id=1, source_target_pairs={{0,32},{16,48},{32,64},{48,80},{64,96},{80,112},{96,128},{112,144}... | collective-permute-start | bytes 786440 | tf_op jit(solution)/shard_map/ppermute | solution.py:16
  9.0 4.8 %collective-permute-start.2 = (f32[256,256]{1,0:T(8,128)}, f32[256,256]{1,0:T(8,128)}, u32[]{:S(2)}, u32[]{:S(2)}) collective-permute-start(f32[256,256]{1,0:T(8,128)} %bitcast.58), channel_id=1, source_target_pairs={{0,48},{16,64},{32,80},{48,96},{64,112},{80,128},{96,144},{112,160... | collective-permute-start | bytes 786440 | tf_op jit(solution)/shard_map/ppermute | solution.py:16
  13.7 2.6 %pick.1 = (bf16[16,1792]{1,0:T(8,128)(2,1)S(1)}, bf16[256,1536]{1,0:T(8,128)(2,1)}) custom-call(s32[3,256]{1,0:T(4,128)} %refs_0_.1, bf16[512,2304]{1,0:T(8,128)(2,1)} %bitcast.51), custom_call_target="tpu_custom_call" | custom-call | flops 113246208 | bytes 2359296 | tf_op jit(solution)/shard_map/pick/pallas_call | solution.py:96
  16.3 0.0 copy-start
  16.3 0.0 copy-start.2
  16.4 27.2 %all_gather.15.refs_0_ = bf16[256,1792]{1,0:T(8,128)(2,1)S(1)} all-gather(bf16[16,1792]{1,0:T(8,128)(2,1)S(1)} %get-tuple-element.27), channel_id=1, replica_groups=mesh['tm'=32,'blk'=16] {'blk'}, dimensions={0}, use_global_device_ids=true | all-gather | bytes 974848 | tf_op jit(solution)/shard_map/all_gather | solution.py:280
  43.5 3.6 %all-to-all-start = ((bf16[16,16,1536]{2,1,0:T(8,128)(2,1)}), bf16[16,16,1536]{2,1,0:T(8,128)(2,1)S(1)}, u32[]{:S(2)}, u32[]{:S(2)}) async-start(bf16[16,16,1536]{2,1,0:T(8,128)(2,1)} %bitcast.60), calls=%async_computation | async-start | bytes 1572864 | tf_op jit(solution)/shard_map/all_to_all | solution.py:282
  47.1 0.0 copy-done
  47.1 0.7 boundary.1
  47.7 0.0 collective-permute-done
  47.8 0.0 collective-permute-done.1
  47.8 0.0 collective-permute-done.2
  47.8 3.2 %collective-permute-start.4 = (bf16[256,256]{1,0:T(8,128)(2,1)S(1)}, bf16[256,256]{1,0:T(8,128)(2,1)S(1)}, u32[]{:S(2)}, u32[]{:S(2)}) collective-permute-start(bf16[256,256]{1,0:T(8,128)(2,1)S(1)} %get-tuple-element.31), channel_id=1, source_target_pairs={{0,16},{1,33},{2,18},{3,35},{4,20},{5,37},{6,22},{7,39},{8,24},{9,... | collective-permute-start | bytes 393224 | tf_op jit(solution)/shard_map/ppermute | solution.py:27
  50.9 0.7 collective-permute-start.3
  51.6 0.0 copy-done.2
  51.6 0.6 fusion.6
  52.2 0.6 fusion.10
  52.8 1.3 %fusion.13 = f32[256,256]{1,0:T(8,128)S(1)} fusion(f32[256,256]{1,0:T(8,128)S(1)} %fusion.10, f32[256,256]{1,0:T(8,128)} %collective-permute-done.2), kind=kOutput, calls=%fused_computation.20 | convolution fusion | flops 201326592 | bytes 786432 | tf_op jit(solution)/shard_map/dot_general | solution.py:31
  54.2 0.1 copy.7
  54.3 2.5 %collective-permute-start.6 = (f32[256,128]{1,0:T(8,128)S(1)}, f32[256,128]{1,0:T(8,128)S(1)}, u32[]{:S(2)}, u32[]{:S(2)}) collective-permute-start(f32[256,128]{1,0:T(8,128)S(1)} %constant_dynamic-slice_fusion), channel_id=1, source_target_pairs={{0,64},{16,80},{32,96},{48,112},{64,128},{80,144},{96,160},{112,17... | collective-permute-start | bytes 393224 | tf_op jit(solution)/shard_map/ppermute | solution.py:16
  56.9 0.0 collective-permute-done.3
  56.9 0.3 fusion.11
  57.1 0.0 collective-permute-done.4
  57.2 0.3 fusion.2
  57.4 0.4 fusion.12
  57.8 0.4 convolution_add_fusion.3
  58.3 6.6 %all-gather = f32[512,256]{1,0:T(8,128)S(1)} all-gather(f32[256,256]{1,0:T(8,128)S(1)} %convolution_add_fusion.3), channel_id=2, replica_groups={{0,1},{2,3},{4,5},{6,7},{8,9},{10,11},{12,13},{14,15},{16,17},{18,19},{..., dimensions={0}, use_global_device_ids=true | all-gather | bytes 786432 | tf_op jit(solution)/shard_map/all_gather | solution.py:307
  64.9 4.4 %collective-permute-start.5 = (bf16[256,256]{1,0:T(8,128)(2,1)S(1)}, bf16[256,256]{1,0:T(8,128)(2,1)S(1)}, u32[]{:S(2)}, u32[]{:S(2)}) collective-permute-start(bf16[256,256]{1,0:T(8,128)(2,1)S(1)} %fusion.3), channel_id=1, source_target_pairs={{0,64},{16,80},{32,96},{48,112},{64,128},{80,144},{96,160},{112,17... | collective-permute-start | bytes 393224 | tf_op jit(solution)/shard_map/ppermute | solution.py:16
  69.3 0.0 collective-permute-done.6
  69.3 0.4 fusion.14
  69.7 3.1 %collective-permute-start.8 = (f32[256,128]{1,0:T(8,128)S(1)}, f32[256,128]{1,0:T(8,128)}, u32[]{:S(2)}, u32[]{:S(2)}) collective-permute-start(f32[256,128]{1,0:T(8,128)S(1)} %fusion.14), channel_id=1, source_target_pairs={{0,128},{16,144},{32,160},{48,176},{64,192},{80,208},{96,224},{112... | collective-permute-start | bytes 393224 | tf_op jit(solution)/shard_map/ppermute | solution.py:16
  72.8 3.6 %edge.1 = (bf16[512,1792]{1,0:T(8,128)(2,1)}, bf16[512,256]{1,0:T(8,128)(2,1)S(1)}, bf16[512,256]{1,0:T(8,128)(2,1)S(1)}) custom-call(bf16[512,2304]{1,0:T(8,128)(2,1)} %bitcast.52, bf16[2,256,256]{2,1,0:T(8,128)(2,1)} %bitcast.49, bf16[256,512]{1,0:T(8,128)(2,1)S(1)} %get-tuple-element.35.refs_2_, bf16[256,256]{1,0:T(8,128)(2,1)S(1)} %get-tuple-element.36.refs_3_), custom_call_target="tpu_custom_call" | custom-call | flops 256 | bytes 256 | tf_op jit(solution)/shard_map/edge/pallas_call | solution.py:219
  76.4 0.0 collective-permute-done.5
  76.4 0.3 fusion.15
  76.6 0.4 fusion.8
  77.1 1.4 %collective-permute-start.7 = (bf16[256,256]{1,0:T(8,128)(2,1)S(1)}, bf16[256,256]{1,0:T(8,128)(2,1)S(1)}, u32[]{:S(2)}, u32[]{:S(2)}) collective-permute-start(bf16[256,256]{1,0:T(8,128)(2,1)S(1)} %get-tuple-element.52), channel_id=1, source_target_pairs={{0,128},{16,144},{32,160},{48,176},{64,192},{80,208},{96,224},{112... | collective-permute-start | bytes 393224 | tf_op jit(solution)/shard_map/ppermute | solution.py:16
  78.5 2.6 %all_gather.18 = f32[256,256]{1,0:T(8,128)S(1)} all-gather(f32[256,128]{1,0:T(8,128)S(1)} %fusion.14), channel_id=1, replica_groups={{0,1},{2,3},{4,5},{6,7},{8,9},{10,11},{12,13},{14,15},{16,17},{18,19},{..., dimensions={1}, use_global_device_ids=true | all-gather | bytes 393216 | tf_op jit(solution)/shard_map/all_gather | solution.py:294
  81.0 0.0 all-to-all-done
  81.0 0.0 copy-start.1
  81.1 2.3 %collective-permute-start.10 = (bf16[256,1536]{1,0:T(8,128)(2,1)S(1)}, bf16[256,1536]{1,0:T(8,128)(2,1)S(1)}, u32[]{:S(2)}, u32[]{:S(2)}) collective-permute-start(bf16[256,1536]{1,0:T(8,128)(2,1)S(1)} %bitcast.54), channel_id=1, source_target_pairs={{0,1},{1,0},{2,3},{3,2},{4,5},{5,4},{6,7},{7,6},{8,9},{9,8},{10,11... | collective-permute-start | bytes 2359304 | tf_op jit(solution)/shard_map/ppermute | solution.py:319
  83.3 0.0 collective-permute-done.8
  83.3 1.3 %fusion.16 = f32[256,128]{1,0:T(8,128)S(1)} fusion(f32[256,256]{1,0:T(8,128)S(1)} %all_gather.18, f32[256,128]{1,0:T(8,128)} %collective-permute-done.8), kind=kOutput, calls=%fused_computation.23 | convolution fusion | flops 100663296 | bytes 524288 | tf_op jit(solution)/shard_map/dot_general | solution.py:31
  84.6 0.0 collective-permute-done.7
  84.6 0.3 fusion.17
  84.9 0.4 fusion.9
  85.3 3.9 %collective-permute-start.9 = (bf16[256,256]{1,0:T(8,128)(2,1)S(1)}, bf16[256,256]{1,0:T(8,128)(2,1)S(1)}, u32[]{:S(2)}, u32[]{:S(2)}) collective-permute-start(bf16[256,256]{1,0:T(8,128)(2,1)S(1)} %get-tuple-element.54), channel_id=1, source_target_pairs={{0,256},{16,272},{32,288},{48,304},{64,320},{80,336},{96,352},{112... | collective-permute-start | bytes 393224 | tf_op jit(solution)/shard_map/ppermute | solution.py:16
  89.2 3.1 %all_gather.19 = f32[256,256]{1,0:T(8,128)S(1)} all-gather(f32[256,128]{1,0:T(8,128)S(1)} %fusion.16), channel_id=1, replica_groups={{0,1},{2,3},{4,5},{6,7},{8,9},{10,11},{12,13},{14,15},{16,17},{18,19},{..., dimensions={1}, use_global_device_ids=true | all-gather | bytes 393216 | tf_op jit(solution)/shard_map/all_gather | solution.py:294
  92.3 0.0 collective-permute-done.10.refs_3_
  92.3 0.0 copy-done.1
  92.3 4.7 %far.1 = bf16[512,1792]{1,0:T(8,128)(2,1)} custom-call(bf16[512,2304]{1,0:T(8,128)(2,1)} %bitcast.53, bf16[512,1792]{1,0:T(8,128)(2,1)} %get-tuple-element.43.refs_1_, bf16[256,1536]{1,0:T(8,128)(2,1)} %bitcast.55, bf16[256,1536]{1,0:T(8,128)(2,1)S(1)} %collective-permute-done.10.refs_3_, ...), custom_call_target="tpu_custom_call", output_to_operand_aliasing={{}: (1, {})} | custom-call | flops 256 | bytes 256 | tf_op jit(solution)/shard_map/far/pallas_call | solution.py:245
  97.0 0.0 collective-permute-done.9
  97.0 0.3 fusion.18
  97.3 1.1 %fusion = f32[1,256,256]{2,1,0:T(8,128)} fusion(f32[256,256]{1,0:T(8,128)S(1)} %get-tuple-element.55, f32[256,256]{1,0:T(8,128)S(1)} %fusion.18, f32[256,256]{1,0:T(8,128)S(1)} %all_gather.19), kind=kOutput, calls=%fused_computation.1 | convolution fusion | flops 201392128 | bytes 1048576 | tf_op jit(solution)/shard_map/dot_general | solution.py:31
  (2 shorter events, 0.1 us)
Async XLA Ops:
  0.6 47.1 %collective-permute-start = (f32[256,256]{1,0:T(8,128)}, f32[256,256]{1,0:T(8,128)S(1)}, u32[]{:S(2)}, u32[]{:S(2)}) collective-permute-start(f32[256,256]{1,0:T(8,128)} %bitcast.56), channel_id=1, source_target_pairs={{0,16},{16,32},{32,48},{48,64},{64,80},{80,96},{96,112},{112,128},... | collective-permute-start | bytes 786440 | tf_op jit(solution)/shard_map/ppermute | solution.py:16
  4.6 43.2 %collective-permute-start.1 = (f32[256,256]{1,0:T(8,128)}, f32[256,256]{1,0:T(8,128)S(1)}, u32[]{:S(2)}, u32[]{:S(2)}) collective-permute-start(f32[256,256]{1,0:T(8,128)} %bitcast.57), channel_id=1, source_target_pairs={{0,32},{16,48},{32,64},{48,80},{64,96},{80,112},{96,128},{112,144}... | collective-permute-start | bytes 786440 | tf_op jit(solution)/shard_map/ppermute | solution.py:16
  9.0 38.8 %collective-permute-start.2 = (f32[256,256]{1,0:T(8,128)}, f32[256,256]{1,0:T(8,128)}, u32[]{:S(2)}, u32[]{:S(2)}) collective-permute-start(f32[256,256]{1,0:T(8,128)} %bitcast.58), channel_id=1, source_target_pairs={{0,48},{16,64},{32,80},{48,96},{64,112},{80,128},{96,144},{112,160... | collective-permute-start | bytes 786440 | tf_op jit(solution)/shard_map/ppermute | solution.py:16
  16.3 30.8 %copy-start = (bf16[1,2,256,256]{3,2,1,0:T(8,128)(2,1)S(1)}, bf16[1,2,256,256]{3,2,1,0:T(8,128)(2,1)}, u32[]{:S(2)}) copy-start(bf16[1,2,256,256]{3,2,1,0:T(8,128)(2,1)} %param.5) | copy-start | bytes 786436
  16.3 35.3 %copy-start.2 = (f32[1,256,256]{2,1,0:T(8,128)S(1)}, f32[1,256,256]{2,1,0:T(8,128)}, u32[]{:S(2)}) copy-start(f32[1,256,256]{2,1,0:T(8,128)} %param.6) | copy-start | bytes 786436
  43.5 37.5 %all-to-all-start = ((bf16[16,16,1536]{2,1,0:T(8,128)(2,1)}), bf16[16,16,1536]{2,1,0:T(8,128)(2,1)S(1)}, u32[]{:S(2)}, u32[]{:S(2)}) async-start(bf16[16,16,1536]{2,1,0:T(8,128)(2,1)} %bitcast.60), calls=%async_computation | async-start | bytes 1572864 | tf_op jit(solution)/shard_map/all_to_all | solution.py:282
  47.8 9.4 %collective-permute-start.4 = (bf16[256,256]{1,0:T(8,128)(2,1)S(1)}, bf16[256,256]{1,0:T(8,128)(2,1)S(1)}, u32[]{:S(2)}, u32[]{:S(2)}) collective-permute-start(bf16[256,256]{1,0:T(8,128)(2,1)S(1)} %get-tuple-element.31), channel_id=1, source_target_pairs={{0,16},{1,33},{2,18},{3,35},{4,20},{5,37},{6,22},{7,39},{8,24},{9,... | collective-permute-start | bytes 393224 | tf_op jit(solution)/shard_map/ppermute | solution.py:27
  50.9 5.9 %collective-permute-start.3 = (bf16[256,256]{1,0:T(8,128)(2,1)S(1)}, bf16[256,256]{1,0:T(8,128)(2,1)S(1)}, u32[]{:S(2)}, u32[]{:S(2)}) collective-permute-start(bf16[256,256]{1,0:T(8,128)(2,1)S(1)} %get-tuple-element.31), channel_id=1, source_target_pairs={{0,48},{2,50},{4,52},{6,54},{8,56},{10,58},{12,60},{14,62},{16,64}... | collective-permute-start | bytes 393224 | tf_op jit(solution)/shard_map/ppermute | solution.py:27
  54.3 15.0 %collective-permute-start.6 = (f32[256,128]{1,0:T(8,128)S(1)}, f32[256,128]{1,0:T(8,128)S(1)}, u32[]{:S(2)}, u32[]{:S(2)}) collective-permute-start(f32[256,128]{1,0:T(8,128)S(1)} %constant_dynamic-slice_fusion), channel_id=1, source_target_pairs={{0,64},{16,80},{32,96},{48,112},{64,128},{80,144},{96,160},{112,17... | collective-permute-start | bytes 393224 | tf_op jit(solution)/shard_map/ppermute | solution.py:16
  64.9 11.4 %collective-permute-start.5 = (bf16[256,256]{1,0:T(8,128)(2,1)S(1)}, bf16[256,256]{1,0:T(8,128)(2,1)S(1)}, u32[]{:S(2)}, u32[]{:S(2)}) collective-permute-start(bf16[256,256]{1,0:T(8,128)(2,1)S(1)} %fusion.3), channel_id=1, source_target_pairs={{0,64},{16,80},{32,96},{48,112},{64,128},{80,144},{96,160},{112,17... | collective-permute-start | bytes 393224 | tf_op jit(solution)/shard_map/ppermute | solution.py:16
  69.7 13.6 %collective-permute-start.8 = (f32[256,128]{1,0:T(8,128)S(1)}, f32[256,128]{1,0:T(8,128)}, u32[]{:S(2)}, u32[]{:S(2)}) collective-permute-start(f32[256,128]{1,0:T(8,128)S(1)} %fusion.14), channel_id=1, source_target_pairs={{0,128},{16,144},{32,160},{48,176},{64,192},{80,208},{96,224},{112... | collective-permute-start | bytes 393224 | tf_op jit(solution)/shard_map/ppermute | solution.py:16
  77.1 7.6 %collective-permute-start.7 = (bf16[256,256]{1,0:T(8,128)(2,1)S(1)}, bf16[256,256]{1,0:T(8,128)(2,1)S(1)}, u32[]{:S(2)}, u32[]{:S(2)}) collective-permute-start(bf16[256,256]{1,0:T(8,128)(2,1)S(1)} %get-tuple-element.52), channel_id=1, source_target_pairs={{0,128},{16,144},{32,160},{48,176},{64,192},{80,208},{96,224},{112... | collective-permute-start | bytes 393224 | tf_op jit(solution)/shard_map/ppermute | solution.py:16
  81.0 11.2 %copy-start.1 = (bf16[16,16,1536]{2,1,0:T(8,128)(2,1)}, bf16[16,16,1536]{2,1,0:T(8,128)(2,1)S(1)}, u32[]{:S(2)}) copy-start(bf16[16,16,1536]{2,1,0:T(8,128)(2,1)S(1)} %all-to-all-done) | copy-start | bytes 2359300
  81.1 11.2 %collective-permute-start.10 = (bf16[256,1536]{1,0:T(8,128)(2,1)S(1)}, bf16[256,1536]{1,0:T(8,128)(2,1)S(1)}, u32[]{:S(2)}, u32[]{:S(2)}) collective-permute-start(bf16[256,1536]{1,0:T(8,128)(2,1)S(1)} %bitcast.54), channel_id=1, source_target_pairs={{0,1},{1,0},{2,3},{3,2},{4,5},{5,4},{6,7},{7,6},{8,9},{9,8},{10,11... | collective-permute-start | bytes 2359304 | tf_op jit(solution)/shard_map/ppermute | solution.py:319
  85.3 11.7 %collective-permute-start.9 = (bf16[256,256]{1,0:T(8,128)(2,1)S(1)}, bf16[256,256]{1,0:T(8,128)(2,1)S(1)}, u32[]{:S(2)}, u32[]{:S(2)}) collective-permute-start(bf16[256,256]{1,0:T(8,128)(2,1)S(1)} %get-tuple-element.54), channel_id=1, source_target_pairs={{0,256},{16,272},{32,288},{48,304},{64,320},{80,336},{96,352},{112... | collective-permute-start | bytes 393224 | tf_op jit(solution)/shard_map/ppermute | solution.py:16

commit v10 on v9

--- a/solution.py
+++ b/solution.py
@@ -169,37 +169,30 @@
 
 
 def far_kernel(
-    w, strip_hbm, begun_hbm, own_hbm, other_ref, one_ref, two_ref, factor_ref, out_hbm,
-    strip_ref, own_ref, out_ref, sems, own_sem,
+    w, swap, strip_hbm, begun_hbm, far_ref, one_ref, two_ref, factor_ref, out_hbm, strip_ref, out_ref, sems
 ):
     del begun_hbm
-    half = own_hbm.shape[1] // 2
-    per_half = half // w
-    count = 2 * per_half
+    half = far_ref.shape[1] // 2
+    count = half // w
     core = lax.rem(lax.axis_index("blk"), 2)
-
-    blocks = [which * per_half + k for which in (core, 1 - core) for k in range(per_half)]
+    which = 1 - core if swap else core
 
     def columns(block):
-        return pl.ds(pl.multiple_of(block * w, w), w)
+        return pl.ds(pl.multiple_of((which * count + block) * w, w), w)
 
     def part(i):
-        at = columns(blocks[i] + 3)
+        at = columns(i + 3)
         return pltpu.make_async_copy(strip_hbm.at[:, at], strip_ref.at[:, i * w:(i + 1) * w], sems.at[0, i])
 
     def done_part(i):
-        at = columns(blocks[i] + 1)
+        at = columns(i + 1)
         return pltpu.make_async_copy(out_ref.at[:, i * w:(i + 1) * w], out_hbm.at[:, at], sems.at[1, i])
 
-    own = pltpu.make_async_copy(own_hbm, own_ref, own_sem)
-    own.start()
     for i in range(count):
         part(i).start()
-    own.wait()
     for i in range(count):
-        ref, k = (own_ref, i) if i < per_half else (other_ref, i - per_half)
-        one_rows = ref[:, k * w:(k + 1) * w]
-        two_rows = reduced_by(ref[:, half + k * w:half + (k + 1) * w], factor_ref[...], one_rows)
+        one_rows = far_ref[:, i * w:(i + 1) * w]
+        two_rows = reduced_by(far_ref[:, half + i * w:half + (i + 1) * w], factor_ref[...], one_rows)
         part(i).wait()
         updated = reduced_by(strip_ref[:, i * w:(i + 1) * w], one_ref[...], one_rows)
         out_ref[:, i * w:(i + 1) * w] = reduced_by(updated, two_ref[...], two_rows)
@@ -237,29 +230,27 @@
     )(strip, inverses, *in_vmem(ones, second_edge))
 
 
-def trailing_far(strip, begun, factors, factor_at_two, own, other):
-    rows, width = strip.shape
+def trailing_far(strip, begun, far, factors, factor_at_two, swap):
+    rows = strip.shape[0]
     w = factor_at_two.shape[0]
-    blocks = width // w - 3
+    half = far.shape[1] // 2
     vmem, hbm = pl.BlockSpec(memory_space=pltpu.VMEM), pl.BlockSpec(memory_space=pl.ANY)
     return pl.pallas_call(
-        lambda *refs: far_kernel(w, *refs),
+        lambda *refs: far_kernel(w, swap, *refs),
         out_shape=jax.ShapeDtypeStruct(begun.shape, BF16),
-        in_specs=[hbm] * 3 + [vmem] * 4,
+        in_specs=[hbm] * 2 + [vmem] * 4,
         out_specs=hbm,
         input_output_aliases={1: 0},
         scratch_shapes=[
-            pltpu.VMEM((rows, blocks * w), BF16),
-            pltpu.VMEM(own.shape, BF16),
-            pltpu.VMEM((rows, blocks * w), BF16),
-            pltpu.SemaphoreType.DMA((2, blocks)),
-            pltpu.SemaphoreType.DMA,
+            pltpu.VMEM((rows, half), BF16),
+            pltpu.VMEM((rows, half), BF16),
+            pltpu.SemaphoreType.DMA((2, half // w)),
         ],
         cost_estimate=pl.CostEstimate(
             flops=w, bytes_accessed=w, transcendentals=0
         ),
-        name="far",
-    )(strip, begun, own, *in_vmem(other, *factors, factor_at_two))
+        name="far_swapped" if swap else "far",
+    )(strip, begun, *in_vmem(far, *factors, factor_at_two))
 
 
 def after(x, gate):
@@ -316,16 +307,18 @@
     wire = current.astype(BF16)
 
     incoming = passed_along(wire, "tm", 8)
-    other = lax.ppermute(after(own, wire), "blk", [(i, i ^ 1) for i in range(blocks)])
+    own = after(own, wire)
+    other = lax.ppermute(own, "blk", [(i, i ^ 1) for i in range(blocks)])
+    trailing = trailing_far(strip, begun, own, factors, factor_at_two, False)
     span_eight = joined(after(half_eight, wire))
     half_sixteen = matmul_high(span_eight, passed_eight)
-    incoming, half_sixteen = lax.optimization_barrier((incoming, half_sixteen))
+    incoming, half_sixteen, trailing = lax.optimization_barrier((incoming, half_sixteen, trailing))
     span_sixteen = joined(half_sixteen)
     current = advance(current, incoming, span_eight)
     wire = current.astype(BF16)
 
     incoming = passed_along(wire, "tm", 16)
-    trailing = trailing_far(strip, begun, factors, factor_at_two, own, other)
+    trailing = trailing_far(strip, trailing, other, factors, factor_at_two, True)
     incoming, trailing = lax.optimization_barrier((incoming, trailing))
     current = advance(current, incoming, span_sixteen)
     return (trailing[None], current[None])

time: 99.1 us -> 97.2 us (0.981)
  blocking collectives: 39.4 us -> 37.3 us
  starting transfers between devices: 38 us -> 36.6 us
    ppermute x8, starting transfers between devices: 28.3 us -> 26.4 us  [passed_along(): return lax.ppermute(x, axis, [(i, i + by) for i in range(count - by)])]
    all_gather x1, blocking collectives: 6.58 us -> 5.37 us  [body(): terms = lax.all_gather(terms, 'blk', axis_index_groups=core_pairs)]
    pallas_call x1 -> x2, Pallas kernels: 4.73 us -> 5.56 us  [trailing_far(): pl.pallas_call(lambda *refs: far_kernel(w, swap, *refs), out_shape=jax.Sh...]
  transfers between devices with their start and end apart: 12 -> 12, of which waited for: 0 -> 0; matrix products, arithmetic and copies ran while one was open for 7% -> 7% of each run, Pallas kernels for 12% -> 13%
where the time goes in v10:
time: 97.2 us; the launch traced here: 95.6 us
  blocking collectives  37.3 us (38%)
  starting transfers between devices  36.6 us (38%)
  Pallas kernels  12.4 us (13%)
  matrix products  8.1 us (8%)
  between operations  0.99 us (1%)
    all_gather x1, blocking collectives, body(): near = lax.all_gather(near_here, 'blk', axis=0, tiled=True)  27.2 us
    ppermute x8, starting transfers between devices, passed_along(): return lax.ppermute(x, axis, [(i, i + by) for i in range(count - by)])  26.4 us
    dot_general x15, matrix products, matmul_high(): jnp.dot(left, right, precision=lax.Precision.HIGHEST, preferred_element_t...  8.1 us
    pallas_call x2, Pallas kernels, trailing_far(): pl.pallas_call(lambda *refs: far_kernel(w, swap, *refs), out_shape=jax.Sh...  5.56 us
    all_gather x1, blocking collectives, body(): terms = lax.all_gather(terms, 'blk', axis_index_groups=core_pairs)  5.37 us
    all_gather x2, blocking collectives, joined(): lax.all_gather(half, 'blk', axis=1, tiled=True, axis_index_groups=core_pa...  4.79 us
    ppermute x2, starting transfers between devices, core_passed(): return lax.ppermute(x, ('tm', 'blk'), pairs)  4.33 us
    pallas_call x1, Pallas kernels, trailing_edge(): pl.pallas_call(lambda *refs: edge_kernel(w, *refs), out_shape=(jax.ShapeD...  3.57 us
  transfers between devices with their start and end apart: 12, of which 0 were waited for; matrix products, arithmetic and copies ran while one was open for 7% of the time, Pallas kernels for 13%

profile of v10, /device:TPU:1, one launch (start us, length us, event | category | flops | bytes accessed | tf_op | source)
XLA Modules:
  0.0 95.6 jit_solution(2339860469832026582)
XLA Ops:
  0.6 5.2 %collective-permute-start.2 = (f32[256,256]{1,0:T(8,128)}, f32[256,256]{1,0:T(8,128)S(1)}, u32[]{:S(2)}, u32[]{:S(2)}) collective-permute-start(f32[256,256]{1,0:T(8,128)} %bitcast.58), channel_id=1, source_target_pairs={{0,48},{16,64},{32,80},{48,96},{64,112},{80,128},{96,144},{112,160... | collective-permute-start | bytes 786440 | tf_op jit(solution)/shard_map/ppermute | solution.py:16
  5.9 3.5 %collective-permute-start.1 = (f32[256,256]{1,0:T(8,128)}, f32[256,256]{1,0:T(8,128)S(1)}, u32[]{:S(2)}, u32[]{:S(2)}) collective-permute-start(f32[256,256]{1,0:T(8,128)} %bitcast.59), channel_id=1, source_target_pairs={{0,32},{16,48},{32,64},{48,80},{64,96},{80,112},{96,128},{112,144}... | collective-permute-start | bytes 786440 | tf_op jit(solution)/shard_map/ppermute | solution.py:16
  9.3 3.2 %collective-permute-start = (f32[256,256]{1,0:T(8,128)}, f32[256,256]{1,0:T(8,128)}, u32[]{:S(2)}, u32[]{:S(2)}) collective-permute-start(f32[256,256]{1,0:T(8,128)} %bitcast.60), channel_id=1, source_target_pairs={{0,16},{16,32},{32,48},{48,64},{64,80},{80,96},{96,112},{112,128},... | collective-permute-start | bytes 786440 | tf_op jit(solution)/shard_map/ppermute | solution.py:16
  12.5 2.6 %pick.1 = (bf16[16,1792]{1,0:T(8,128)(2,1)S(1)}, bf16[256,1536]{1,0:T(8,128)(2,1)}) custom-call(s32[3,256]{1,0:T(4,128)} %refs_0_.1, bf16[512,2304]{1,0:T(8,128)(2,1)} %bitcast.53), custom_call_target="tpu_custom_call" | custom-call | flops 113246208 | bytes 2359296 | tf_op jit(solution)/shard_map/pick/pallas_call | solution.py:96
  15.1 0.0 copy-start
  15.1 0.0 copy-start.1
  15.2 27.2 %all_gather.15.refs_0_ = bf16[256,1792]{1,0:T(8,128)(2,1)S(1)} all-gather(bf16[16,1792]{1,0:T(8,128)(2,1)S(1)} %get-tuple-element.28), channel_id=1, replica_groups=mesh['tm'=32,'blk'=16] {'blk'}, dimensions={0}, use_global_device_ids=true | all-gather | bytes 974848 | tf_op jit(solution)/shard_map/all_gather | solution.py:271
  42.3 3.6 %all-to-all-start = ((bf16[16,16,1536]{2,1,0:T(8,128)(2,1)}), bf16[16,16,1536]{2,1,0:T(8,128)(2,1)S(1)}, u32[]{:S(2)}, u32[]{:S(2)}) async-start(bf16[16,16,1536]{2,1,0:T(8,128)(2,1)} %bitcast.61), calls=%async_computation | async-start | bytes 1572864 | tf_op jit(solution)/shard_map/all_to_all | solution.py:273
  45.9 0.0 copy-done
  45.9 0.7 boundary.1
  46.6 0.0 collective-permute-done.2
  46.6 0.0 collective-permute-done.1
  46.6 0.0 collective-permute-done
  46.6 3.7 %collective-permute-start.4 = (bf16[256,256]{1,0:T(8,128)(2,1)S(1)}, bf16[256,256]{1,0:T(8,128)(2,1)S(1)}, u32[]{:S(2)}, u32[]{:S(2)}) collective-permute-start(bf16[256,256]{1,0:T(8,128)(2,1)S(1)} %get-tuple-element.32), channel_id=1, source_target_pairs={{0,16},{1,33},{2,18},{3,35},{4,20},{5,37},{6,22},{7,39},{8,24},{9,... | collective-permute-start | bytes 393224 | tf_op jit(solution)/shard_map/ppermute | solution.py:27
  50.3 0.7 collective-permute-start.3
  50.9 0.0 copy-done.1
  50.9 1.5 %fusion.6 = f32[256,256]{1,0:T(8,128)S(1)} fusion(f32[256,256]{1,0:T(8,128)} %collective-permute-done, f32[1,256,256]{2,1,0:T(8,128)S(1)} %copy-done.1), kind=kOutput, calls=%fused_computation.13 | convolution fusion | flops 201326592 | bytes 786432 | tf_op jit(solution)/shard_map/dot_general | solution.py:31
  52.5 0.1 copy.8
  52.6 0.6 fusion.10
  53.2 0.4 fusion.13
  53.6 3.2 %collective-permute-start.6 = (f32[256,128]{1,0:T(8,128)S(1)}, f32[256,128]{1,0:T(8,128)S(1)}, u32[]{:S(2)}, u32[]{:S(2)}) collective-permute-start(f32[256,128]{1,0:T(8,128)S(1)} %constant_dynamic-slice_fusion), channel_id=1, source_target_pairs={{0,64},{16,80},{32,96},{48,112},{64,128},{80,144},{96,160},{112,17... | collective-permute-start | bytes 393224 | tf_op jit(solution)/shard_map/ppermute | solution.py:16
  56.9 0.0 collective-permute-done.3
  56.9 0.3 fusion.11
  57.1 0.0 collective-permute-done.4
  57.2 0.3 fusion.2
  57.4 0.4 fusion.12
  57.9 0.4 convolution_add_fusion.3
  58.3 5.4 %all-gather = f32[512,256]{1,0:T(8,128)S(1)} all-gather(f32[256,256]{1,0:T(8,128)S(1)} %convolution_add_fusion.3), channel_id=2, replica_groups={{0,1},{2,3},{4,5},{6,7},{8,9},{10,11},{12,13},{14,15},{16,17},{18,19},{..., dimensions={0}, use_global_device_ids=true | all-gather | bytes 786432 | tf_op jit(solution)/shard_map/all_gather | solution.py:298
  63.7 4.4 %collective-permute-start.5 = (bf16[256,256]{1,0:T(8,128)(2,1)S(1)}, bf16[256,256]{1,0:T(8,128)(2,1)S(1)}, u32[]{:S(2)}, u32[]{:S(2)}) collective-permute-start(bf16[256,256]{1,0:T(8,128)(2,1)S(1)} %fusion.3), channel_id=1, source_target_pairs={{0,64},{16,80},{32,96},{48,112},{64,128},{80,144},{96,160},{112,17... | collective-permute-start | bytes 393224 | tf_op jit(solution)/shard_map/ppermute | solution.py:16
  68.1 0.0 collective-permute-done.6
  68.1 0.4 fusion.14
  68.5 2.4 %collective-permute-start.8 = (f32[256,128]{1,0:T(8,128)S(1)}, f32[256,128]{1,0:T(8,128)S(1)}, u32[]{:S(2)}, u32[]{:S(2)}) collective-permute-start(f32[256,128]{1,0:T(8,128)S(1)} %fusion.14), channel_id=1, source_target_pairs={{0,128},{16,144},{32,160},{48,176},{64,192},{80,208},{96,224},{112... | collective-permute-start | bytes 393224 | tf_op jit(solution)/shard_map/ppermute | solution.py:16
  70.9 3.6 %edge.1 = (bf16[512,1792]{1,0:T(8,128)(2,1)}, bf16[512,256]{1,0:T(8,128)(2,1)S(1)}, bf16[512,256]{1,0:T(8,128)(2,1)S(1)}) custom-call(bf16[512,2304]{1,0:T(8,128)(2,1)} %bitcast.54, bf16[2,256,256]{2,1,0:T(8,128)(2,1)} %bitcast.51, bf16[256,512]{1,0:T(8,128)(2,1)S(1)} %get-tuple-element.36.refs_2_, bf16[256,256]{1,0:T(8,128)(2,1)S(1)} %get-tuple-element.37.refs_3_), custom_call_target="tpu_custom_call" | custom-call | flops 256 | bytes 256 | tf_op jit(solution)/shard_map/edge/pallas_call | solution.py:212
  74.5 0.0 collective-permute-done.5
  74.5 0.3 fusion.15
  74.8 1.1 %fusion.8 = (bf16[256,256]{1,0:T(8,128)(2,1)S(1)}, f32[256,256]{1,0:T(8,128)}) fusion(f32[512,256]{1,0:T(8,128)S(1)} %all-gather, bf16[256,256]{1,0:T(8,128)(2,1)S(1)} %get-tuple-element.32, f32[256,256]{1,0:T(8,128)S(1)} %fusion.15, f32[256,256]{1,0:T(8,128)S(1)} %fusion.13), kind=kOutput, calls=%fused_computation.15 | convolution fusion | flops 201654272 | bytes 1572864 | tf_op jit(solution)/shard_map/dot_general | solution.py:31
  75.9 2.2 %collective-permute-start.7 = (bf16[256,256]{1,0:T(8,128)(2,1)S(1)}, bf16[256,256]{1,0:T(8,128)(2,1)S(1)}, u32[]{:S(2)}, u32[]{:S(2)}) collective-permute-start(bf16[256,256]{1,0:T(8,128)(2,1)S(1)} %get-tuple-element.54), channel_id=1, source_target_pairs={{0,128},{16,144},{32,160},{48,176},{64,192},{80,208},{96,224},{112... | collective-permute-start | bytes 393224 | tf_op jit(solution)/shard_map/ppermute | solution.py:16
  78.1 2.6 %all_gather.18 = f32[256,256]{1,0:T(8,128)S(1)} all-gather(f32[256,128]{1,0:T(8,128)S(1)} %fusion.14), channel_id=1, replica_groups={{0,1},{2,3},{4,5},{6,7},{8,9},{10,11},{12,13},{14,15},{16,17},{18,19},{..., dimensions={1}, use_global_device_ids=true | all-gather | bytes 393216 | tf_op jit(solution)/shard_map/all_gather | solution.py:285
  80.7 0.0 all-to-all-done
  80.7 2.3 %collective-permute-start.10 = (bf16[256,1536]{1,0:T(8,128)(2,1)S(1)}, bf16[256,1536]{1,0:T(8,128)(2,1)S(1)}, u32[]{:S(2)}, u32[]{:S(2)}) collective-permute-start(bf16[256,1536]{1,0:T(8,128)(2,1)S(1)} %bitcast.49), channel_id=1, source_target_pairs={{0,1},{1,0},{2,3},{3,2},{4,5},{5,4},{6,7},{7,6},{8,9},{9,8},{10,11... | collective-permute-start | bytes 2359304 | tf_op jit(solution)/shard_map/ppermute | solution.py:311
  83.0 0.0 collective-permute-done.8
  83.0 0.4 fusion.16
  83.4 0.0 copy-start.2
  83.4 2.8 %far.1.refs_1_ = bf16[512,1792]{1,0:T(8,128)(2,1)} custom-call(bf16[512,2304]{1,0:T(8,128)(2,1)} %bitcast.55, bf16[512,1792]{1,0:T(8,128)(2,1)} %get-tuple-element.43.refs_1_, bf16[256,1536]{1,0:T(8,128)(2,1)S(1)} %bitcast.50, bf16[512,256]{1,0:T(8,128)(2,1)S(1)} %get-tuple-element.46.refs_3_, ...), custom_call_target="tpu_custom_call", output_to_operand_aliasing={{}: (1, {})} | custom-call | flops 256 | bytes 256 | tf_op jit(solution)/shard_map/far/pallas_call | solution.py:238
  86.2 0.0 collective-permute-done.7
  86.2 0.3 fusion.17
  86.5 0.0 copy-done.2
  86.5 0.4 fusion.9
  86.9 2.3 %collective-permute-start.9 = (bf16[256,256]{1,0:T(8,128)(2,1)S(1)}, bf16[256,256]{1,0:T(8,128)(2,1)S(1)}, u32[]{:S(2)}, u32[]{:S(2)}) collective-permute-start(bf16[256,256]{1,0:T(8,128)(2,1)S(1)} %get-tuple-element.56), channel_id=1, source_target_pairs={{0,256},{16,272},{32,288},{48,304},{64,320},{80,336},{96,352},{112... | collective-permute-start | bytes 393224 | tf_op jit(solution)/shard_map/ppermute | solution.py:16
  89.2 2.2 %all_gather.19 = f32[256,256]{1,0:T(8,128)S(1)} all-gather(f32[256,128]{1,0:T(8,128)S(1)} %fusion.16), channel_id=1, replica_groups={{0,1},{2,3},{4,5},{6,7},{8,9},{10,11},{12,13},{14,15},{16,17},{18,19},{..., dimensions={1}, use_global_device_ids=true | all-gather | bytes 393216 | tf_op jit(solution)/shard_map/all_gather | solution.py:285
  91.5 0.0 collective-permute-done.10.refs_2_
  91.5 2.8 %far_swapped.1 = bf16[512,1792]{1,0:T(8,128)(2,1)} custom-call(bf16[512,2304]{1,0:T(8,128)(2,1)} %bitcast.56, bf16[512,1792]{1,0:T(8,128)(2,1)} %far.1.refs_1_, bf16[256,1536]{1,0:T(8,128)(2,1)S(1)} %collective-permute-done.10.refs_2_, bf16[512,256]{1,0:T(8,128)(2,1)S(1)} %get-tuple-element.46.refs_3_, ...), custom_call_target="tpu_custom_call", output_to_operand_aliasing={{}: (1, {})} | custom-call | flops 256 | bytes 256 | tf_op jit(solution)/shard_map/far_swapped/pallas_call | solution.py:238
  94.2 0.0 collective-permute-done.9
  94.2 0.3 fusion.18
  94.5 1.1 %fusion = f32[1,256,256]{2,1,0:T(8,128)} fusion(f32[256,256]{1,0:T(8,128)S(1)} %get-tuple-element.57, f32[256,256]{1,0:T(8,128)S(1)} %fusion.18, f32[256,256]{1,0:T(8,128)S(1)} %all_gather.19), kind=kOutput, calls=%fused_computation.1 | convolution fusion | flops 201392128 | bytes 1048576 | tf_op jit(solution)/shard_map/dot_general | solution.py:31
  (2 shorter events, 0.1 us)
Async XLA Ops:
  0.6 45.9 %collective-permute-start.2 = (f32[256,256]{1,0:T(8,128)}, f32[256,256]{1,0:T(8,128)S(1)}, u32[]{:S(2)}, u32[]{:S(2)}) collective-permute-start(f32[256,256]{1,0:T(8,128)} %bitcast.58), channel_id=1, source_target_pairs={{0,48},{16,64},{32,80},{48,96},{64,112},{80,128},{96,144},{112,160... | collective-permute-start | bytes 786440 | tf_op jit(solution)/shard_map/ppermute | solution.py:16
  5.9 40.7 %collective-permute-start.1 = (f32[256,256]{1,0:T(8,128)}, f32[256,256]{1,0:T(8,128)S(1)}, u32[]{:S(2)}, u32[]{:S(2)}) collective-permute-start(f32[256,256]{1,0:T(8,128)} %bitcast.59), channel_id=1, source_target_pairs={{0,32},{16,48},{32,64},{48,80},{64,96},{80,112},{96,128},{112,144}... | collective-permute-start | bytes 786440 | tf_op jit(solution)/shard_map/ppermute | solution.py:16
  9.3 37.2 %collective-permute-start = (f32[256,256]{1,0:T(8,128)}, f32[256,256]{1,0:T(8,128)}, u32[]{:S(2)}, u32[]{:S(2)}) collective-permute-start(f32[256,256]{1,0:T(8,128)} %bitcast.60), channel_id=1, source_target_pairs={{0,16},{16,32},{32,48},{48,64},{64,80},{80,96},{96,112},{112,128},... | collective-permute-start | bytes 786440 | tf_op jit(solution)/shard_map/ppermute | solution.py:16
  15.1 30.8 %copy-start = (bf16[1,2,256,256]{3,2,1,0:T(8,128)(2,1)S(1)}, bf16[1,2,256,256]{3,2,1,0:T(8,128)(2,1)}, u32[]{:S(2)}) copy-start(bf16[1,2,256,256]{3,2,1,0:T(8,128)(2,1)} %param.5) | copy-start | bytes 786436
  15.1 35.8 %copy-start.1 = (f32[1,256,256]{2,1,0:T(8,128)S(1)}, f32[1,256,256]{2,1,0:T(8,128)}, u32[]{:S(2)}) copy-start(f32[1,256,256]{2,1,0:T(8,128)} %param.6) | copy-start | bytes 786436
  42.3 38.4 %all-to-all-start = ((bf16[16,16,1536]{2,1,0:T(8,128)(2,1)}), bf16[16,16,1536]{2,1,0:T(8,128)(2,1)S(1)}, u32[]{:S(2)}, u32[]{:S(2)}) async-start(bf16[16,16,1536]{2,1,0:T(8,128)(2,1)} %bitcast.61), calls=%async_computation | async-start | bytes 1572864 | tf_op jit(solution)/shard_map/all_to_all | solution.py:273
  46.6 10.6 %collective-permute-start.4 = (bf16[256,256]{1,0:T(8,128)(2,1)S(1)}, bf16[256,256]{1,0:T(8,128)(2,1)S(1)}, u32[]{:S(2)}, u32[]{:S(2)}) collective-permute-start(bf16[256,256]{1,0:T(8,128)(2,1)S(1)} %get-tuple-element.32), channel_id=1, source_target_pairs={{0,16},{1,33},{2,18},{3,35},{4,20},{5,37},{6,22},{7,39},{8,24},{9,... | collective-permute-start | bytes 393224 | tf_op jit(solution)/shard_map/ppermute | solution.py:27
  50.3 6.6 %collective-permute-start.3 = (bf16[256,256]{1,0:T(8,128)(2,1)S(1)}, bf16[256,256]{1,0:T(8,128)(2,1)S(1)}, u32[]{:S(2)}, u32[]{:S(2)}) collective-permute-start(bf16[256,256]{1,0:T(8,128)(2,1)S(1)} %get-tuple-element.32), channel_id=1, source_target_pairs={{0,48},{2,50},{4,52},{6,54},{8,56},{10,58},{12,60},{14,62},{16,64}... | collective-permute-start | bytes 393224 | tf_op jit(solution)/shard_map/ppermute | solution.py:27
  53.6 14.5 %collective-permute-start.6 = (f32[256,128]{1,0:T(8,128)S(1)}, f32[256,128]{1,0:T(8,128)S(1)}, u32[]{:S(2)}, u32[]{:S(2)}) collective-permute-start(f32[256,128]{1,0:T(8,128)S(1)} %constant_dynamic-slice_fusion), channel_id=1, source_target_pairs={{0,64},{16,80},{32,96},{48,112},{64,128},{80,144},{96,160},{112,17... | collective-permute-start | bytes 393224 | tf_op jit(solution)/shard_map/ppermute | solution.py:16
  63.7 10.8 %collective-permute-start.5 = (bf16[256,256]{1,0:T(8,128)(2,1)S(1)}, bf16[256,256]{1,0:T(8,128)(2,1)S(1)}, u32[]{:S(2)}, u32[]{:S(2)}) collective-permute-start(bf16[256,256]{1,0:T(8,128)(2,1)S(1)} %fusion.3), channel_id=1, source_target_pairs={{0,64},{16,80},{32,96},{48,112},{64,128},{80,144},{96,160},{112,17... | collective-permute-start | bytes 393224 | tf_op jit(solution)/shard_map/ppermute | solution.py:16
  68.5 14.5 %collective-permute-start.8 = (f32[256,128]{1,0:T(8,128)S(1)}, f32[256,128]{1,0:T(8,128)S(1)}, u32[]{:S(2)}, u32[]{:S(2)}) collective-permute-start(f32[256,128]{1,0:T(8,128)S(1)} %fusion.14), channel_id=1, source_target_pairs={{0,128},{16,144},{32,160},{48,176},{64,192},{80,208},{96,224},{112... | collective-permute-start | bytes 393224 | tf_op jit(solution)/shard_map/ppermute | solution.py:16
  75.9 10.3 %collective-permute-start.7 = (bf16[256,256]{1,0:T(8,128)(2,1)S(1)}, bf16[256,256]{1,0:T(8,128)(2,1)S(1)}, u32[]{:S(2)}, u32[]{:S(2)}) collective-permute-start(bf16[256,256]{1,0:T(8,128)(2,1)S(1)} %get-tuple-element.54), channel_id=1, source_target_pairs={{0,128},{16,144},{32,160},{48,176},{64,192},{80,208},{96,224},{112... | collective-permute-start | bytes 393224 | tf_op jit(solution)/shard_map/ppermute | solution.py:16
  80.7 10.7 %collective-permute-start.10 = (bf16[256,1536]{1,0:T(8,128)(2,1)S(1)}, bf16[256,1536]{1,0:T(8,128)(2,1)S(1)}, u32[]{:S(2)}, u32[]{:S(2)}) collective-permute-start(bf16[256,1536]{1,0:T(8,128)(2,1)S(1)} %bitcast.49), channel_id=1, source_target_pairs={{0,1},{1,0},{2,3},{3,2},{4,5},{5,4},{6,7},{7,6},{8,9},{9,8},{10,11... | collective-permute-start | bytes 2359304 | tf_op jit(solution)/shard_map/ppermute | solution.py:311
  83.4 3.1 %copy-start.2 = (f32[256,256]{1,0:T(8,128)S(1)}, f32[256,256]{1,0:T(8,128)}, u32[]{:S(2)}) copy-start(f32[256,256]{1,0:T(8,128)} %get-tuple-element.55) | copy-start | bytes 786436
  86.9 7.3 %collective-permute-start.9 = (bf16[256,256]{1,0:T(8,128)(2,1)S(1)}, bf16[256,256]{1,0:T(8,128)(2,1)S(1)}, u32[]{:S(2)}, u32[]{:S(2)}) collective-permute-start(bf16[256,256]{1,0:T(8,128)(2,1)S(1)} %get-tuple-element.56), channel_id=1, source_target_pairs={{0,256},{16,272},{32,288},{48,304},{64,320},{80,336},{96,352},{112... | collective-permute-start | bytes 393224 | tf_op jit(solution)/shard_map/ppermute | solution.py:16

commit v11 on v10

--- a/solution.py
+++ b/solution.py
@@ -169,7 +169,8 @@
 
 
 def far_kernel(
-    w, swap, strip_hbm, begun_hbm, far_ref, one_ref, two_ref, factor_ref, out_hbm, strip_ref, out_ref, sems
+    w, swap, strip_hbm, begun_hbm, far_hbm, one_ref, two_ref, factor_ref, out_hbm,
+    strip_ref, far_ref, out_ref, sems, far_sem,
 ):
     del begun_hbm
     half = far_ref.shape[1] // 2
@@ -188,8 +189,11 @@
         at = columns(i + 1)
         return pltpu.make_async_copy(out_ref.at[:, i * w:(i + 1) * w], out_hbm.at[:, at], sems.at[1, i])
 
+    far = pltpu.make_async_copy(far_hbm, far_ref, far_sem)
+    far.start()
     for i in range(count):
         part(i).start()
+    far.wait()
     for i in range(count):
         one_rows = far_ref[:, i * w:(i + 1) * w]
         two_rows = reduced_by(far_ref[:, half + i * w:half + (i + 1) * w], factor_ref[...], one_rows)
@@ -238,19 +242,21 @@
     return pl.pallas_call(
         lambda *refs: far_kernel(w, swap, *refs),
         out_shape=jax.ShapeDtypeStruct(begun.shape, BF16),
-        in_specs=[hbm] * 2 + [vmem] * 4,
+        in_specs=[hbm] * 3 + [vmem] * 3,
         out_specs=hbm,
         input_output_aliases={1: 0},
         scratch_shapes=[
             pltpu.VMEM((rows, half), BF16),
+            pltpu.VMEM(far.shape, BF16),
             pltpu.VMEM((rows, half), BF16),
             pltpu.SemaphoreType.DMA((2, half // w)),
+            pltpu.SemaphoreType.DMA,
         ],
         cost_estimate=pl.CostEstimate(
             flops=w, bytes_accessed=w, transcendentals=0
         ),
         name="far_swapped" if swap else "far",
-    )(strip, begun, *in_vmem(far, *factors, factor_at_two))
+    )(strip, begun, far, *in_vmem(*factors, factor_at_two))
 
 
 def after(x, gate):
@@ -284,7 +290,7 @@
     def joined(half):
         return lax.all_gather(half, "blk", axis=1, tiled=True, axis_index_groups=core_pairs)
 
-    arriving = [core_passed(boundary, by) for by in ((1, 2), (3, None))]
+    arriving = [core_passed(boundary, by) for by in ((3, 2), (1, None))]
     span_two = matmul_high(span, back_one)
     span_three = matmul_high(span_two, back_two)
     span_four = matmul_high(span_three, back_three)
@@ -292,8 +298,8 @@
     half_four = lax.dynamic_slice_in_dim(span_four, core * (w // 2), w // 2, 1)
     half_eight = matmul_high(span_four, passed_along(half_four, "tm", 4))
     terms = jnp.zeros((w, w), F32)
-    by_core = with_layout_constraint(jnp.where(core == 0, span, span_two), Layout((0, 1)))
-    for incoming, reach in zip(arriving, (by_core, span_three)):
+    by_core = with_layout_constraint(jnp.where(core == 0, span_three, span_two), Layout((0, 1)))
+    for incoming, reach in zip(arriving, (by_core, span)):
         terms = advance(terms, incoming, reach)
     terms = lax.all_gather(terms, "blk", axis_index_groups=core_pairs)
     current = boundary.astype(F32) + (terms[0] + terms[1])

time: 97.2 us -> 99.6 us (1.025)
  the two profiles are of different devices: /device:TPU:1 before, /device:TPU:48 now
where the time goes in v11:
time: 99.6 us; the launch traced here: 99 us
  blocking collectives  32 us (32%)
  starting transfers between devices  29.3 us (29%)
  waiting for transfers between devices  15.8 us (16%)
  Pallas kernels  13.1 us (13%)
  matrix products  7.63 us (8%)
  between operations  1 us (1%)
    all_gather x1, blocking collectives, body(): near = lax.all_gather(near_here, 'blk', axis=0, tiled=True)  25.8 us
    ppermute x8, starting transfers between devices, passed_along(): return lax.ppermute(x, axis, [(i, i + by) for i in range(count - by)])  18 us
    ppermute x8, waiting for transfers between devices, passed_along(): return lax.ppermute(x, axis, [(i, i + by) for i in range(count - by)])  13.6 us
    dot_general x15, matrix products, matmul_high(): jnp.dot(left, right, precision=lax.Precision.HIGHEST, preferred_element_t...  7.63 us
    pallas_call x2, Pallas kernels, trailing_far(): pl.pallas_call(lambda *refs: far_kernel(w, swap, *refs), out_shape=jax.Sh...  6.27 us
    ppermute x2, starting transfers between devices, core_passed(): return lax.ppermute(x, ('tm', 'blk'), pairs)  5.63 us
    all_gather x2, blocking collectives, joined(): lax.all_gather(half, 'blk', axis=1, tiled=True, axis_index_groups=core_pa...  3.99 us
    all_to_all x1, starting transfers between devices, body(): own = lax.all_to_all(far_here, 'blk', 0, 0, tiled=True)  3.61 us
  transfers between devices with their start and end apart: 12, of which 4 were waited for; matrix products, arithmetic and copies ran while one was open for 6% of the time, Pallas kernels for 13%

profile of v11, /device:TPU:48, one launch (start us, length us, event | category | flops | bytes accessed | tf_op | source)
XLA Modules:
  0.0 99.0 jit_solution(16619781573643939488)
XLA Ops:
  0.6 4.7 %collective-permute-start.2 = (f32[256,256]{1,0:T(8,128)}, f32[256,256]{1,0:T(8,128)S(1)}, u32[]{:S(2)}, u32[]{:S(2)}) collective-permute-start(f32[256,256]{1,0:T(8,128)} %bitcast.52), channel_id=1, source_target_pairs={{0,48},{16,64},{32,80},{48,96},{64,112},{80,128},{96,144},{112,160... | collective-permute-start | bytes 786440 | tf_op jit(solution)/shard_map/ppermute | solution.py:16
  5.3 2.8 %collective-permute-start.1 = (f32[256,256]{1,0:T(8,128)}, f32[256,256]{1,0:T(8,128)S(1)}, u32[]{:S(2)}, u32[]{:S(2)}) collective-permute-start(f32[256,256]{1,0:T(8,128)} %bitcast.53), channel_id=1, source_target_pairs={{0,32},{16,48},{32,64},{48,80},{64,96},{80,112},{96,128},{112,144}... | collective-permute-start | bytes 786440 | tf_op jit(solution)/shard_map/ppermute | solution.py:16
  8.1 2.8 %collective-permute-start = (f32[256,256]{1,0:T(8,128)}, f32[256,256]{1,0:T(8,128)}, u32[]{:S(2)}, u32[]{:S(2)}) collective-permute-start(f32[256,256]{1,0:T(8,128)} %bitcast.54), channel_id=1, source_target_pairs={{0,16},{16,32},{32,48},{48,64},{64,80},{80,96},{96,112},{112,128},... | collective-permute-start | bytes 786440 | tf_op jit(solution)/shard_map/ppermute | solution.py:16
  10.9 2.6 %pick.1 = (bf16[16,1792]{1,0:T(8,128)(2,1)S(1)}, bf16[256,1536]{1,0:T(8,128)(2,1)}) custom-call(s32[3,256]{1,0:T(4,128)} %refs_0_.1, bf16[512,2304]{1,0:T(8,128)(2,1)} %bitcast.45), custom_call_target="tpu_custom_call" | custom-call | flops 113246208 | bytes 2359296 | tf_op jit(solution)/shard_map/pick/pallas_call | solution.py:96
  13.5 0.0 copy-start
  13.6 0.0 copy-start.2
  13.6 25.8 %all_gather.15.refs_0_ = bf16[256,1792]{1,0:T(8,128)(2,1)S(1)} all-gather(bf16[16,1792]{1,0:T(8,128)(2,1)S(1)} %get-tuple-element.28), channel_id=1, replica_groups=mesh['tm'=32,'blk'=16] {'blk'}, dimensions={0}, use_global_device_ids=true | all-gather | bytes 974848 | tf_op jit(solution)/shard_map/all_gather | solution.py:277
  39.4 3.6 %all-to-all-start = ((bf16[16,16,1536]{2,1,0:T(8,128)(2,1)}), bf16[16,16,1536]{2,1,0:T(8,128)(2,1)S(1)}, u32[]{:S(2)}, u32[]{:S(2)}) async-start(bf16[16,16,1536]{2,1,0:T(8,128)(2,1)} %bitcast.55), calls=%async_computation | async-start | bytes 1572864 | tf_op jit(solution)/shard_map/all_to_all | solution.py:279
  43.0 0.0 copy-done
  43.0 0.7 boundary.1
  43.7 0.0 collective-permute-done.2
  43.7 0.0 collective-permute-done.1
  43.7 0.0 collective-permute-done
  43.7 3.5 %collective-permute-start.4 = (bf16[256,256]{1,0:T(8,128)(2,1)S(1)}, bf16[256,256]{1,0:T(8,128)(2,1)S(1)}, u32[]{:S(2)}, u32[]{:S(2)}) collective-permute-start(bf16[256,256]{1,0:T(8,128)(2,1)S(1)} %get-tuple-element.32), channel_id=1, source_target_pairs={{0,48},{1,33},{2,50},{3,35},{4,52},{5,37},{6,54},{7,39},{8,56},{9,... | collective-permute-start | bytes 393224 | tf_op jit(solution)/shard_map/ppermute | solution.py:27
  47.2 2.2 %collective-permute-start.3 = (bf16[256,256]{1,0:T(8,128)(2,1)S(1)}, bf16[256,256]{1,0:T(8,128)(2,1)S(1)}, u32[]{:S(2)}, u32[]{:S(2)}) collective-permute-start(bf16[256,256]{1,0:T(8,128)(2,1)S(1)} %get-tuple-element.32), channel_id=1, source_target_pairs={{0,16},{2,18},{4,20},{6,22},{8,24},{10,26},{12,28},{14,30},{16,32}... | collective-permute-start | bytes 393224 | tf_op jit(solution)/shard_map/ppermute | solution.py:27
  49.4 0.0 copy-done.2
  49.4 1.5 %fusion.4 = f32[256,256]{1,0:T(8,128)S(1)} fusion(f32[256,256]{1,0:T(8,128)} %collective-permute-done, f32[1,256,256]{2,1,0:T(8,128)S(1)} %copy-done.2), kind=kOutput, calls=%fused_computation.11 | convolution fusion | flops 201326592 | bytes 786432 | tf_op jit(solution)/shard_map/dot_general | solution.py:31
  50.9 0.1 copy.8
  51.1 0.6 fusion.12
  51.7 0.4 fusion.13
  52.1 1.9 %collective-permute-start.6 = (f32[256,128]{1,0:T(8,128)S(1)}, f32[256,128]{1,0:T(8,128)S(1)}, u32[]{:S(2)}, u32[]{:S(2)}) collective-permute-start(f32[256,128]{1,0:T(8,128)S(1)} %constant_dynamic-slice_fusion), channel_id=1, source_target_pairs={{0,64},{16,80},{32,96},{48,112},{64,128},{80,144},{96,160},{112,17... | collective-permute-start | bytes 393224 | tf_op jit(solution)/shard_map/ppermute | solution.py:16
  54.0 2.2 %collective-permute-done.3 = bf16[256,256]{1,0:T(8,128)(2,1)S(1)} collective-permute-done((bf16[256,256]{1,0:T(8,128)(2,1)S(1)}, bf16[256,256]{1,0:T(8,128)(2,1)S(1)}, u32[]{:S(2)}, u32[]{:S(2)}) %collective-permute-start.3) | collective-permute-done | bytes 131104 | tf_op jit(solution)/shard_map/ppermute | solution.py:27
  56.2 0.3 fusion.8
  56.5 0.0 collective-permute-done.4
  56.5 0.3 fusion.2
  56.8 0.6 fusion.6
  57.4 0.4 convolution_add_fusion.3
  57.8 2.2 %all-gather = f32[512,256]{1,0:T(8,128)S(1)} all-gather(f32[256,256]{1,0:T(8,128)S(1)} %convolution_add_fusion.3), channel_id=2, replica_groups={{0,1},{2,3},{4,5},{6,7},{8,9},{10,11},{12,13},{14,15},{16,17},{18,19},{..., dimensions={0}, use_global_device_ids=true | all-gather | bytes 786432 | tf_op jit(solution)/shard_map/all_gather | solution.py:304
  60.1 1.9 %collective-permute-start.5 = (bf16[256,256]{1,0:T(8,128)(2,1)S(1)}, bf16[256,256]{1,0:T(8,128)(2,1)S(1)}, u32[]{:S(2)}, u32[]{:S(2)}) collective-permute-start(bf16[256,256]{1,0:T(8,128)(2,1)S(1)} %fusion.3), channel_id=1, source_target_pairs={{0,64},{16,80},{32,96},{48,112},{64,128},{80,144},{96,160},{112,17... | collective-permute-start | bytes 393224 | tf_op jit(solution)/shard_map/ppermute | solution.py:16
  62.0 0.0 collective-permute-done.6
  62.0 0.4 fusion.14
  62.4 1.3 %collective-permute-start.8 = (f32[256,128]{1,0:T(8,128)S(1)}, f32[256,128]{1,0:T(8,128)S(1)}, u32[]{:S(2)}, u32[]{:S(2)}) collective-permute-start(f32[256,128]{1,0:T(8,128)S(1)} %fusion.14), channel_id=1, source_target_pairs={{0,128},{16,144},{32,160},{48,176},{64,192},{80,208},{96,224},{112... | collective-permute-start | bytes 393224 | tf_op jit(solution)/shard_map/ppermute | solution.py:16
  63.7 3.6 %edge.1 = (bf16[512,1792]{1,0:T(8,128)(2,1)}, bf16[512,256]{1,0:T(8,128)(2,1)S(1)}, bf16[512,256]{1,0:T(8,128)(2,1)S(1)}) custom-call(bf16[512,2304]{1,0:T(8,128)(2,1)} %bitcast.46, bf16[2,256,256]{2,1,0:T(8,128)(2,1)} %bitcast.43, bf16[256,512]{1,0:T(8,128)(2,1)S(1)} %get-tuple-element.36.refs_2_, bf16[256,256]{1,0:T(8,128)(2,1)S(1)} %get-tuple-element.37.refs_3_), custom_call_target="tpu_custom_call" | custom-call | flops 256 | bytes 256 | tf_op jit(solution)/shard_map/edge/pallas_call | solution.py:216
  67.3 1.2 %collective-permute-done.5 = bf16[256,256]{1,0:T(8,128)(2,1)S(1)} collective-permute-done((bf16[256,256]{1,0:T(8,128)(2,1)S(1)}, bf16[256,256]{1,0:T(8,128)(2,1)S(1)}, u32[]{:S(2)}, u32[]{:S(2)}) %collective-permute-start.5) | collective-permute-done | bytes 131104 | tf_op jit(solution)/shard_map/ppermute | solution.py:16
  68.4 0.3 fusion.15
  68.7 0.4 fusion.10
  69.1 1.3 %collective-permute-start.7 = (bf16[256,256]{1,0:T(8,128)(2,1)S(1)}, bf16[256,256]{1,0:T(8,128)(2,1)S(1)}, u32[]{:S(2)}, u32[]{:S(2)}) collective-permute-start(bf16[256,256]{1,0:T(8,128)(2,1)S(1)} %get-tuple-element.54), channel_id=1, source_target_pairs={{0,128},{16,144},{32,160},{48,176},{64,192},{80,208},{96,224},{112... | collective-permute-start | bytes 393224 | tf_op jit(solution)/shard_map/ppermute | solution.py:16
  70.4 2.0 %all_gather.18 = f32[256,256]{1,0:T(8,128)S(1)} all-gather(f32[256,128]{1,0:T(8,128)S(1)} %fusion.14), channel_id=1, replica_groups={{0,1},{2,3},{4,5},{6,7},{8,9},{10,11},{12,13},{14,15},{16,17},{18,19},{..., dimensions={1}, use_global_device_ids=true | all-gather | bytes 393216 | tf_op jit(solution)/shard_map/all_gather | solution.py:291
  72.4 0.0 all-to-all-done
  72.4 0.0 copy-start.1
  72.4 2.0 %collective-permute-start.10 = (bf16[256,1536]{1,0:T(8,128)(2,1)S(1)}, bf16[256,1536]{1,0:T(8,128)(2,1)}, u32[]{:S(2)}, u32[]{:S(2)}) collective-permute-start(bf16[256,1536]{1,0:T(8,128)(2,1)S(1)} %bitcast.50), channel_id=1, source_target_pairs={{0,1},{1,0},{2,3},{3,2},{4,5},{5,4},{6,7},{7,6},{8,9},{9,8},{10,11... | collective-permute-start | bytes 2359304 | tf_op jit(solution)/shard_map/ppermute | solution.py:317
  74.5 0.0 collective-permute-done.8
  74.5 0.4 fusion.16
  74.9 0.0 copy-done.1
  74.9 3.1 %far.1.refs_1_ = bf16[512,1792]{1,0:T(8,128)(2,1)} custom-call(bf16[512,2304]{1,0:T(8,128)(2,1)} %bitcast.47, bf16[512,1792]{1,0:T(8,128)(2,1)} %get-tuple-element.43.refs_1_, bf16[256,1536]{1,0:T(8,128)(2,1)} %bitcast.51, bf16[512,256]{1,0:T(8,128)(2,1)S(1)} %get-tuple-element.46.refs_3_, ...), custom_call_target="tpu_custom_call", output_to_operand_aliasing={{}: (1, {})} | custom-call | flops 256 | bytes 256 | tf_op jit(solution)/shard_map/far/pallas_call | solution.py:242
  78.0 4.8 %collective-permute-done.7 = bf16[256,256]{1,0:T(8,128)(2,1)S(1)} collective-permute-done((bf16[256,256]{1,0:T(8,128)(2,1)S(1)}, bf16[256,256]{1,0:T(8,128)(2,1)S(1)}, u32[]{:S(2)}, u32[]{:S(2)}) %collective-permute-start.7) | collective-permute-done | bytes 131104 | tf_op jit(solution)/shard_map/ppermute | solution.py:16
  82.9 0.3 fusion.17
  83.1 0.4 fusion.11
  83.6 1.3 %collective-permute-start.9 = (bf16[256,256]{1,0:T(8,128)(2,1)S(1)}, bf16[256,256]{1,0:T(8,128)(2,1)S(1)}, u32[]{:S(2)}, u32[]{:S(2)}) collective-permute-start(bf16[256,256]{1,0:T(8,128)(2,1)S(1)} %get-tuple-element.56), channel_id=1, source_target_pairs={{0,256},{16,272},{32,288},{48,304},{64,320},{80,336},{96,352},{112... | collective-permute-start | bytes 393224 | tf_op jit(solution)/shard_map/ppermute | solution.py:16
  84.9 2.0 %all_gather.19 = f32[256,256]{1,0:T(8,128)S(1)} all-gather(f32[256,128]{1,0:T(8,128)S(1)} %fusion.16), channel_id=1, replica_groups={{0,1},{2,3},{4,5},{6,7},{8,9},{10,11},{12,13},{14,15},{16,17},{18,19},{..., dimensions={1}, use_global_device_ids=true | all-gather | bytes 393216 | tf_op jit(solution)/shard_map/all_gather | solution.py:291
  86.9 0.0 collective-permute-done.10.refs_2_
  86.9 3.1 %far_swapped.1 = bf16[512,1792]{1,0:T(8,128)(2,1)} custom-call(bf16[512,2304]{1,0:T(8,128)(2,1)} %bitcast.48, bf16[512,1792]{1,0:T(8,128)(2,1)} %far.1.refs_1_, bf16[256,1536]{1,0:T(8,128)(2,1)} %collective-permute-done.10.refs_2_, bf16[512,256]{1,0:T(8,128)(2,1)S(1)} %get-tuple-element.46.refs_3_, ...), custom_call_target="tpu_custom_call", output_to_operand_aliasing={{}: (1, {})} | custom-call | flops 256 | bytes 256 | tf_op jit(solution)/shard_map/far_swapped/pallas_call | solution.py:242
  90.0 7.6 %collective-permute-done.9 = bf16[256,256]{1,0:T(8,128)(2,1)S(1)} collective-permute-done((bf16[256,256]{1,0:T(8,128)(2,1)S(1)}, bf16[256,256]{1,0:T(8,128)(2,1)S(1)}, u32[]{:S(2)}, u32[]{:S(2)}) %collective-permute-start.9) | collective-permute-done | bytes 131104 | tf_op jit(solution)/shard_map/ppermute | solution.py:16
  97.6 0.3 fusion.18
  97.8 1.1 %fusion = f32[1,256,256]{2,1,0:T(8,128)} fusion(f32[256,256]{1,0:T(8,128)S(1)} %get-tuple-element.57, f32[256,256]{1,0:T(8,128)S(1)} %fusion.18, f32[256,256]{1,0:T(8,128)S(1)} %all_gather.19), kind=kOutput, calls=%fused_computation.1 | convolution fusion | flops 201392128 | bytes 1048576 | tf_op jit(solution)/shard_map/dot_general | solution.py:31
  (2 shorter events, 0.1 us)
Async XLA Ops:
  0.6 43.1 %collective-permute-start.2 = (f32[256,256]{1,0:T(8,128)}, f32[256,256]{1,0:T(8,128)S(1)}, u32[]{:S(2)}, u32[]{:S(2)}) collective-permute-start(f32[256,256]{1,0:T(8,128)} %bitcast.52), channel_id=1, source_target_pairs={{0,48},{16,64},{32,80},{48,96},{64,112},{80,128},{96,144},{112,160... | collective-permute-start | bytes 786440 | tf_op jit(solution)/shard_map/ppermute | solution.py:16
  5.3 38.4 %collective-permute-start.1 = (f32[256,256]{1,0:T(8,128)}, f32[256,256]{1,0:T(8,128)S(1)}, u32[]{:S(2)}, u32[]{:S(2)}) collective-permute-start(f32[256,256]{1,0:T(8,128)} %bitcast.53), channel_id=1, source_target_pairs={{0,32},{16,48},{32,64},{48,80},{64,96},{80,112},{96,128},{112,144}... | collective-permute-start | bytes 786440 | tf_op jit(solution)/shard_map/ppermute | solution.py:16
  8.1 35.6 %collective-permute-start = (f32[256,256]{1,0:T(8,128)}, f32[256,256]{1,0:T(8,128)}, u32[]{:S(2)}, u32[]{:S(2)}) collective-permute-start(f32[256,256]{1,0:T(8,128)} %bitcast.54), channel_id=1, source_target_pairs={{0,16},{16,32},{32,48},{48,64},{64,80},{80,96},{96,112},{112,128},... | collective-permute-start | bytes 786440 | tf_op jit(solution)/shard_map/ppermute | solution.py:16
  13.5 29.5 %copy-start = (bf16[1,2,256,256]{3,2,1,0:T(8,128)(2,1)S(1)}, bf16[1,2,256,256]{3,2,1,0:T(8,128)(2,1)}, u32[]{:S(2)}) copy-start(bf16[1,2,256,256]{3,2,1,0:T(8,128)(2,1)} %param.5) | copy-start | bytes 786436
  13.6 35.8 %copy-start.2 = (f32[1,256,256]{2,1,0:T(8,128)S(1)}, f32[1,256,256]{2,1,0:T(8,128)}, u32[]{:S(2)}) copy-start(f32[1,256,256]{2,1,0:T(8,128)} %param.6) | copy-start | bytes 786436
  39.4 33.0 %all-to-all-start = ((bf16[16,16,1536]{2,1,0:T(8,128)(2,1)}), bf16[16,16,1536]{2,1,0:T(8,128)(2,1)S(1)}, u32[]{:S(2)}, u32[]{:S(2)}) async-start(bf16[16,16,1536]{2,1,0:T(8,128)(2,1)} %bitcast.55), calls=%async_computation | async-start | bytes 1572864 | tf_op jit(solution)/shard_map/all_to_all | solution.py:279
  43.7 12.8 %collective-permute-start.4 = (bf16[256,256]{1,0:T(8,128)(2,1)S(1)}, bf16[256,256]{1,0:T(8,128)(2,1)S(1)}, u32[]{:S(2)}, u32[]{:S(2)}) collective-permute-start(bf16[256,256]{1,0:T(8,128)(2,1)S(1)} %get-tuple-element.32), channel_id=1, source_target_pairs={{0,48},{1,33},{2,50},{3,35},{4,52},{5,37},{6,54},{7,39},{8,56},{9,... | collective-permute-start | bytes 393224 | tf_op jit(solution)/shard_map/ppermute | solution.py:27
  47.2 9.0 %collective-permute-start.3 = (bf16[256,256]{1,0:T(8,128)(2,1)S(1)}, bf16[256,256]{1,0:T(8,128)(2,1)S(1)}, u32[]{:S(2)}, u32[]{:S(2)}) collective-permute-start(bf16[256,256]{1,0:T(8,128)(2,1)S(1)} %get-tuple-element.32), channel_id=1, source_target_pairs={{0,16},{2,18},{4,20},{6,22},{8,24},{10,26},{12,28},{14,30},{16,32}... | collective-permute-start | bytes 393224 | tf_op jit(solution)/shard_map/ppermute | solution.py:27
  52.1 9.9 %collective-permute-start.6 = (f32[256,128]{1,0:T(8,128)S(1)}, f32[256,128]{1,0:T(8,128)S(1)}, u32[]{:S(2)}, u32[]{:S(2)}) collective-permute-start(f32[256,128]{1,0:T(8,128)S(1)} %constant_dynamic-slice_fusion), channel_id=1, source_target_pairs={{0,64},{16,80},{32,96},{48,112},{64,128},{80,144},{96,160},{112,17... | collective-permute-start | bytes 393224 | tf_op jit(solution)/shard_map/ppermute | solution.py:16
  60.1 8.4 %collective-permute-start.5 = (bf16[256,256]{1,0:T(8,128)(2,1)S(1)}, bf16[256,256]{1,0:T(8,128)(2,1)S(1)}, u32[]{:S(2)}, u32[]{:S(2)}) collective-permute-start(bf16[256,256]{1,0:T(8,128)(2,1)S(1)} %fusion.3), channel_id=1, source_target_pairs={{0,64},{16,80},{32,96},{48,112},{64,128},{80,144},{96,160},{112,17... | collective-permute-start | bytes 393224 | tf_op jit(solution)/shard_map/ppermute | solution.py:16
  62.4 12.1 %collective-permute-start.8 = (f32[256,128]{1,0:T(8,128)S(1)}, f32[256,128]{1,0:T(8,128)S(1)}, u32[]{:S(2)}, u32[]{:S(2)}) collective-permute-start(f32[256,128]{1,0:T(8,128)S(1)} %fusion.14), channel_id=1, source_target_pairs={{0,128},{16,144},{32,160},{48,176},{64,192},{80,208},{96,224},{112... | collective-permute-start | bytes 393224 | tf_op jit(solution)/shard_map/ppermute | solution.py:16
  69.1 13.8 %collective-permute-start.7 = (bf16[256,256]{1,0:T(8,128)(2,1)S(1)}, bf16[256,256]{1,0:T(8,128)(2,1)S(1)}, u32[]{:S(2)}, u32[]{:S(2)}) collective-permute-start(bf16[256,256]{1,0:T(8,128)(2,1)S(1)} %get-tuple-element.54), channel_id=1, source_target_pairs={{0,128},{16,144},{32,160},{48,176},{64,192},{80,208},{96,224},{112... | collective-permute-start | bytes 393224 | tf_op jit(solution)/shard_map/ppermute | solution.py:16
  72.4 2.5 %copy-start.1 = (bf16[16,16,1536]{2,1,0:T(8,128)(2,1)}, bf16[16,16,1536]{2,1,0:T(8,128)(2,1)S(1)}, u32[]{:S(2)}) copy-start(bf16[16,16,1536]{2,1,0:T(8,128)(2,1)S(1)} %all-to-all-done) | copy-start | bytes 2359300
  72.4 14.4 %collective-permute-start.10 = (bf16[256,1536]{1,0:T(8,128)(2,1)S(1)}, bf16[256,1536]{1,0:T(8,128)(2,1)}, u32[]{:S(2)}, u32[]{:S(2)}) collective-permute-start(bf16[256,1536]{1,0:T(8,128)(2,1)S(1)} %bitcast.50), channel_id=1, source_target_pairs={{0,1},{1,0},{2,3},{3,2},{4,5},{5,4},{6,7},{7,6},{8,9},{9,8},{10,11... | collective-permute-start | bytes 2359304 | tf_op jit(solution)/shard_map/ppermute | solution.py:317
  83.6 14.0 %collective-permute-start.9 = (bf16[256,256]{1,0:T(8,128)(2,1)S(1)}, bf16[256,256]{1,0:T(8,128)(2,1)S(1)}, u32[]{:S(2)}, u32[]{:S(2)}) collective-permute-start(bf16[256,256]{1,0:T(8,128)(2,1)S(1)} %get-tuple-element.56), channel_id=1, source_target_pairs={{0,256},{16,272},{32,288},{48,304},{64,320},{80,336},{96,352},{112... | collective-permute-start | bytes 393224 | tf_op jit(solution)/shard_map/ppermute | solution.py:16

commit v12 on v10

--- a/solution.py
+++ b/solution.py
@@ -265,16 +265,14 @@
     blocks = lax.axis_size("blk")
     per = w // blocks
 
-    back_one, back_two, back_three = (passed_along(span, "tm", by) for by in (1, 2, 3))
+    back_near, back_far = (core_passed(span, by) for by in ((1, 2), (None, 3)))
 
     near_here, far_here = picked_rows(pivot_nodes, strip, w, per)
     near = lax.all_gather(near_here, "blk", axis=0, tiled=True)
     near, far_here = lax.optimization_barrier((near, far_here))
     own = lax.all_to_all(far_here, "blk", 0, 0, tiled=True)
     boundary, factor_at_two, second_edge, one_rows = boundary_of(near, inverses)
-    back_one, back_two, back_three, boundary = lax.optimization_barrier(
-        (back_one, back_two, back_three, boundary)
-    )
+    back_near, back_far, boundary = lax.optimization_barrier((back_near, back_far, boundary))
 
     def advance(current, incoming, reach):
         return matmul_high(matmul_high(reach, incoming.astype(F32)), reach.T) + current
@@ -284,16 +282,21 @@
     def joined(half):
         return lax.all_gather(half, "blk", axis=1, tiled=True, axis_index_groups=core_pairs)
 
-    arriving = [core_passed(boundary, by) for by in ((1, 2), (3, None))]
-    span_two = matmul_high(span, back_one)
-    span_three = matmul_high(span_two, back_two)
-    span_four = matmul_high(span_three, back_three)
+    arriving = [core_passed(boundary, by) for by in ((1, 3), (2, None))]
     core = lax.axis_index("blk") % 2
+
+    def by_core(zero, one):
+        return with_layout_constraint(jnp.where(core == 0, zero, one), Layout((0, 1)))
+
+    pair = matmul_high(by_core(span, back_near), by_core(back_near, back_far))
+    pair = lax.all_gather(pair, "blk", axis_index_groups=core_pairs)
+    span_two = pair[0]
+    span_four = matmul_high(span_two, pair[1])
+    reaches = by_core(span, matmul_high(span_two, back_near)), span_two
     half_four = lax.dynamic_slice_in_dim(span_four, core * (w // 2), w // 2, 1)
     half_eight = matmul_high(span_four, passed_along(half_four, "tm", 4))
     terms = jnp.zeros((w, w), F32)
-    by_core = with_layout_constraint(jnp.where(core == 0, span, span_two), Layout((0, 1)))
-    for incoming, reach in zip(arriving, (by_core, span_three)):
+    for incoming, reach in zip(arriving, reaches):
         terms = advance(terms, incoming, reach)
     terms = lax.all_gather(terms, "blk", axis_index_groups=core_pairs)
     current = boundary.astype(F32) + (terms[0] + terms[1])

time: 97.2 us -> 92.8 us (0.955)
  starting transfers between devices: 36.6 us -> 34.7 us
  matrix products: 8.1 us -> 6.72 us
  blocking collectives: 37.3 us -> 36.2 us
    ppermute x8 -> x5, starting transfers between devices: 26.4 us -> 15.3 us  [passed_along(): return lax.ppermute(x, axis, [(i, i + by) for i in range(count - by)])]
    ppermute x2 -> x4, starting transfers between devices: 4.33 us -> 13.2 us  [core_passed(): return lax.ppermute(x, ('tm', 'blk'), pairs)]
    all_gather x0 -> x1, blocking collectives: none -> 4.92 us  [body(): pair = lax.all_gather(pair, 'blk', axis_index_groups=core_pairs)]
    all_gather x1, blocking collectives: 27.2 us -> 24.1 us  [body(): near = lax.all_gather(near_here, 'blk', axis=0, tiled=True)]
    all_gather x1, blocking collectives: 5.37 us -> 2.46 us  [body(): terms = lax.all_gather(terms, 'blk', axis_index_groups=core_pairs)]
    dot_general x15, matrix products: 8.1 us -> 6.72 us  [matmul_high(): jnp.dot(left, right, precision=lax.Precision.HIGHEST, preferred_element_t...]
  transfers between devices with their start and end apart: 12 -> 11, of which waited for: 0 -> 0; matrix products, arithmetic and copies ran while one was open for 7% -> 6% of each run, Pallas kernels for 13% -> 14%
where the time goes in v12:
time: 92.8 us; the launch traced here: 91.1 us
  blocking collectives  36.2 us (39%)
  starting transfers between devices  34.7 us (37%)
  Pallas kernels  12.4 us (13%)
  matrix products  6.72 us (7%)
  between operations  0.99 us (1%)
    all_gather x1, blocking collectives, body(): near = lax.all_gather(near_here, 'blk', axis=0, tiled=True)  24.1 us
    ppermute x5, starting transfers between devices, passed_along(): return lax.ppermute(x, axis, [(i, i + by) for i in range(count - by)])  15.3 us
    ppermute x4, starting transfers between devices, core_passed(): return lax.ppermute(x, ('tm', 'blk'), pairs)  13.2 us
    dot_general x15, matrix products, matmul_high(): jnp.dot(left, right, precision=lax.Precision.HIGHEST, preferred_element_t...  6.72 us
    pallas_call x2, Pallas kernels, trailing_far(): pl.pallas_call(lambda *refs: far_kernel(w, swap, *refs), out_shape=jax.Sh...  5.56 us
    all_gather x1, blocking collectives, body(): pair = lax.all_gather(pair, 'blk', axis_index_groups=core_pairs)  4.92 us
    all_gather x2, blocking collectives, joined(): lax.all_gather(half, 'blk', axis=1, tiled=True, axis_index_groups=core_pa...  4.79 us
    all_to_all x1, starting transfers between devices, body(): own = lax.all_to_all(far_here, 'blk', 0, 0, tiled=True)  3.87 us
  transfers between devices with their start and end apart: 11, of which 0 were waited for; matrix products, arithmetic and copies ran while one was open for 6% of the time, Pallas kernels for 14%

profile of v12, /device:TPU:1, one launch (start us, length us, event | category | flops | bytes accessed | tf_op | source)
XLA Modules:
  0.0 91.1 jit_solution(17793922961439259533)
XLA Ops:
  0.6 5.2 %collective-permute-start.1 = (f32[256,256]{1,0:T(8,128)}, f32[256,256]{1,0:T(8,128)S(1)}, u32[]{:S(2)}, u32[]{:S(2)}) collective-permute-start(f32[256,256]{1,0:T(8,128)} %bitcast.45), channel_id=1, source_target_pairs={{1,49},{3,51},{5,53},{7,55},{9,57},{11,59},{13,61},{15,63},{17,65}... | collective-permute-start | bytes 786440 | tf_op jit(solution)/shard_map/ppermute | solution.py:27
  5.9 3.5 %collective-permute-start = (f32[256,256]{1,0:T(8,128)}, f32[256,256]{1,0:T(8,128)S(1)}, u32[]{:S(2)}, u32[]{:S(2)}) collective-permute-start(f32[256,256]{1,0:T(8,128)} %bitcast.46), channel_id=1, source_target_pairs={{0,16},{1,33},{2,18},{3,35},{4,20},{5,37},{6,22},{7,39},{8,24},{9,... | collective-permute-start | bytes 786440 | tf_op jit(solution)/shard_map/ppermute | solution.py:27
  9.3 2.6 %pick.1 = (bf16[16,1792]{1,0:T(8,128)(2,1)S(1)}, bf16[256,1536]{1,0:T(8,128)(2,1)}) custom-call(s32[3,256]{1,0:T(4,128)} %refs_0_.1, bf16[512,2304]{1,0:T(8,128)(2,1)} %bitcast.40), custom_call_target="tpu_custom_call" | custom-call | flops 113246208 | bytes 2359296 | tf_op jit(solution)/shard_map/pick/pallas_call | solution.py:96
  11.9 0.0 copy-start
  11.9 0.0 copy-start.2
  12.0 24.1 %all_gather.21.refs_0_ = bf16[256,1792]{1,0:T(8,128)(2,1)S(1)} all-gather(bf16[16,1792]{1,0:T(8,128)(2,1)S(1)} %get-tuple-element.27), channel_id=1, replica_groups=mesh['tm'=32,'blk'=16] {'blk'}, dimensions={0}, use_global_device_ids=true | all-gather | bytes 974848 | tf_op jit(solution)/shard_map/all_gather | solution.py:271
  36.0 3.9 %all-to-all-start = ((bf16[16,16,1536]{2,1,0:T(8,128)(2,1)}), bf16[16,16,1536]{2,1,0:T(8,128)(2,1)S(1)}, u32[]{:S(2)}, u32[]{:S(2)}) async-start(bf16[16,16,1536]{2,1,0:T(8,128)(2,1)} %bitcast.47), calls=%async_computation | async-start | bytes 1572864 | tf_op jit(solution)/shard_map/all_to_all | solution.py:273
  39.9 0.0 copy-done
  39.9 0.7 boundary.1
  40.6 0.0 copy-start.3
  40.6 0.0 collective-permute-done.1
  40.6 0.0 collective-permute-done
  40.6 3.9 %collective-permute-start.3 = (bf16[256,256]{1,0:T(8,128)(2,1)S(1)}, bf16[256,256]{1,0:T(8,128)(2,1)S(1)}, u32[]{:S(2)}, u32[]{:S(2)}) collective-permute-start(bf16[256,256]{1,0:T(8,128)(2,1)S(1)} %get-tuple-element.31), channel_id=1, source_target_pairs={{0,16},{1,49},{2,18},{3,51},{4,20},{5,53},{6,22},{7,55},{8,24},{9,... | collective-permute-start | bytes 393224 | tf_op jit(solution)/shard_map/ppermute | solution.py:27
  44.5 0.7 collective-permute-start.2
  45.2 0.0 copy-done.2
  45.2 0.4 fusion.4
  45.6 4.9 %all-gather = f32[512,256]{1,0:T(8,128)S(1)} all-gather(f32[256,256]{1,0:T(8,128)S(1)} %fusion.4), channel_id=2, replica_groups={{0,1},{2,3},{4,5},{6,7},{8,9},{10,11},{12,13},{14,15},{16,17},{18,19},{..., dimensions={0}, use_global_device_ids=true | all-gather | bytes 786432 | tf_op jit(solution)/shard_map/all_gather | solution.py:292
  50.5 0.4 fusion.1
  50.9 3.2 %collective-permute-start.5 = (f32[256,128]{1,0:T(8,128)S(1)}, f32[256,128]{1,0:T(8,128)S(1)}, u32[]{:S(2)}, u32[]{:S(2)}) collective-permute-start(f32[256,128]{1,0:T(8,128)S(1)} %constant_dynamic-slice_fusion), channel_id=1, source_target_pairs={{0,64},{16,80},{32,96},{48,112},{64,128},{80,144},{96,160},{112,17... | collective-permute-start | bytes 393224 | tf_op jit(solution)/shard_map/ppermute | solution.py:16
  54.1 0.0 copy-done.3
  54.1 0.4 convolution_select_fusion
  54.5 0.0 collective-permute-done.2
  54.5 0.3 fusion.10
  54.8 0.4 fusion.8
  55.2 0.0 collective-permute-done.3
  55.2 0.3 fusion.18
  55.5 0.4 convolution_add_fusion.3
  55.9 2.5 %all-gather.1 = f32[512,256]{1,0:T(8,128)S(1)} all-gather(f32[256,256]{1,0:T(8,128)S(1)} %convolution_add_fusion.3), channel_id=3, replica_groups={{0,1},{2,3},{4,5},{6,7},{8,9},{10,11},{12,13},{14,15},{16,17},{18,19},{..., dimensions={0}, use_global_device_ids=true | all-gather | bytes 786432 | tf_op jit(solution)/shard_map/all_gather | solution.py:301
  58.4 4.4 %collective-permute-start.4 = (bf16[256,256]{1,0:T(8,128)(2,1)S(1)}, bf16[256,256]{1,0:T(8,128)(2,1)S(1)}, u32[]{:S(2)}, u32[]{:S(2)}) collective-permute-start(bf16[256,256]{1,0:T(8,128)(2,1)S(1)} %fusion.14), channel_id=1, source_target_pairs={{0,64},{16,80},{32,96},{48,112},{64,128},{80,144},{96,160},{112,17... | collective-permute-start | bytes 393224 | tf_op jit(solution)/shard_map/ppermute | solution.py:16
  62.9 0.0 collective-permute-done.5
  62.9 0.4 fusion.19
  63.3 2.6 %collective-permute-start.7 = (f32[256,128]{1,0:T(8,128)S(1)}, f32[256,128]{1,0:T(8,128)S(1)}, u32[]{:S(2)}, u32[]{:S(2)}) collective-permute-start(f32[256,128]{1,0:T(8,128)S(1)} %fusion.19), channel_id=1, source_target_pairs={{0,128},{16,144},{32,160},{48,176},{64,192},{80,208},{96,224},{112... | collective-permute-start | bytes 393224 | tf_op jit(solution)/shard_map/ppermute | solution.py:16
  65.9 3.6 %edge.1 = (bf16[512,1792]{1,0:T(8,128)(2,1)}, bf16[512,256]{1,0:T(8,128)(2,1)S(1)}, bf16[512,256]{1,0:T(8,128)(2,1)S(1)}) custom-call(bf16[512,2304]{1,0:T(8,128)(2,1)} %bitcast.41, bf16[2,256,256]{2,1,0:T(8,128)(2,1)} %bitcast.38, bf16[256,512]{1,0:T(8,128)(2,1)S(1)} %get-tuple-element.35.refs_2_, bf16[256,256]{1,0:T(8,128)(2,1)S(1)} %get-tuple-element.36.refs_3_), custom_call_target="tpu_custom_call" | custom-call | flops 256 | bytes 256 | tf_op jit(solution)/shard_map/edge/pallas_call | solution.py:212
  69.5 0.0 collective-permute-done.4
  69.5 0.3 fusion.20
  69.8 1.1 %fusion.16 = (bf16[256,256]{1,0:T(8,128)(2,1)S(1)}, f32[256,256]{1,0:T(8,128)}) fusion(f32[512,256]{1,0:T(8,128)S(1)} %all-gather.1, bf16[256,256]{1,0:T(8,128)(2,1)S(1)} %get-tuple-element.31, f32[256,256]{1,0:T(8,128)S(1)} %fusion.20, f32[256,256]{1,0:T(8,128)S(1)} %fusion.1), kind=kOutput, calls=%fused_computation.23 | convolution fusion | flops 201654272 | bytes 1572864 | tf_op jit(solution)/shard_map/dot_general | solution.py:31
  70.9 2.7 %collective-permute-start.6 = (bf16[256,256]{1,0:T(8,128)(2,1)S(1)}, bf16[256,256]{1,0:T(8,128)(2,1)S(1)}, u32[]{:S(2)}, u32[]{:S(2)}) collective-permute-start(bf16[256,256]{1,0:T(8,128)(2,1)S(1)} %get-tuple-element.52), channel_id=1, source_target_pairs={{0,128},{16,144},{32,160},{48,176},{64,192},{80,208},{96,224},{112... | collective-permute-start | bytes 393224 | tf_op jit(solution)/shard_map/ppermute | solution.py:16
  73.6 2.6 %all_gather.26 = f32[256,256]{1,0:T(8,128)S(1)} all-gather(f32[256,128]{1,0:T(8,128)S(1)} %fusion.19), channel_id=1, replica_groups={{0,1},{2,3},{4,5},{6,7},{8,9},{10,11},{12,13},{14,15},{16,17},{18,19},{..., dimensions={1}, use_global_device_ids=true | all-gather | bytes 393216 | tf_op jit(solution)/shard_map/all_gather | solution.py:283
  76.2 0.0 all-to-all-done
  76.2 2.3 %collective-permute-start.9 = (bf16[256,1536]{1,0:T(8,128)(2,1)S(1)}, bf16[256,1536]{1,0:T(8,128)(2,1)S(1)}, u32[]{:S(2)}, u32[]{:S(2)}) collective-permute-start(bf16[256,1536]{1,0:T(8,128)(2,1)S(1)} %bitcast.36), channel_id=1, source_target_pairs={{0,1},{1,0},{2,3},{3,2},{4,5},{5,4},{6,7},{7,6},{8,9},{9,8},{10,11... | collective-permute-start | bytes 2359304 | tf_op jit(solution)/shard_map/ppermute | solution.py:314
  78.5 0.0 collective-permute-done.7
  78.5 0.4 fusion.21
  78.9 0.0 copy-start.1
  78.9 2.8 %far.1.refs_1_ = bf16[512,1792]{1,0:T(8,128)(2,1)} custom-call(bf16[512,2304]{1,0:T(8,128)(2,1)} %bitcast.42, bf16[512,1792]{1,0:T(8,128)(2,1)} %get-tuple-element.41.refs_1_, bf16[256,1536]{1,0:T(8,128)(2,1)S(1)} %bitcast.37, bf16[512,256]{1,0:T(8,128)(2,1)S(1)} %get-tuple-element.44.refs_3_, ...), custom_call_target="tpu_custom_call", output_to_operand_aliasing={{}: (1, {})} | custom-call | flops 256 | bytes 256 | tf_op jit(solution)/shard_map/far/pallas_call | solution.py:238
  81.7 0.0 collective-permute-done.6
  81.7 0.3 fusion.22
  82.0 0.0 copy-done.1
  82.0 0.4 fusion.17
  82.4 2.3 %collective-permute-start.8 = (bf16[256,256]{1,0:T(8,128)(2,1)S(1)}, bf16[256,256]{1,0:T(8,128)(2,1)S(1)}, u32[]{:S(2)}, u32[]{:S(2)}) collective-permute-start(bf16[256,256]{1,0:T(8,128)(2,1)S(1)} %get-tuple-element.54), channel_id=1, source_target_pairs={{0,256},{16,272},{32,288},{48,304},{64,320},{80,336},{96,352},{112... | collective-permute-start | bytes 393224 | tf_op jit(solution)/shard_map/ppermute | solution.py:16
  84.7 2.2 %all_gather.27 = f32[256,256]{1,0:T(8,128)S(1)} all-gather(f32[256,128]{1,0:T(8,128)S(1)} %fusion.21), channel_id=1, replica_groups={{0,1},{2,3},{4,5},{6,7},{8,9},{10,11},{12,13},{14,15},{16,17},{18,19},{..., dimensions={1}, use_global_device_ids=true | all-gather | bytes 393216 | tf_op jit(solution)/shard_map/all_gather | solution.py:283
  86.9 0.0 collective-permute-done.9.refs_2_
  87.0 2.8 %far_swapped.1 = bf16[512,1792]{1,0:T(8,128)(2,1)} custom-call(bf16[512,2304]{1,0:T(8,128)(2,1)} %bitcast.43, bf16[512,1792]{1,0:T(8,128)(2,1)} %far.1.refs_1_, bf16[256,1536]{1,0:T(8,128)(2,1)S(1)} %collective-permute-done.9.refs_2_, bf16[512,256]{1,0:T(8,128)(2,1)S(1)} %get-tuple-element.44.refs_3_, ...), custom_call_target="tpu_custom_call", output_to_operand_aliasing={{}: (1, {})} | custom-call | flops 256 | bytes 256 | tf_op jit(solution)/shard_map/far_swapped/pallas_call | solution.py:238
  89.7 0.0 collective-permute-done.8
  89.7 0.3 fusion.23
  90.0 1.1 %fusion = f32[1,256,256]{2,1,0:T(8,128)} fusion(f32[256,256]{1,0:T(8,128)S(1)} %get-tuple-element.55, f32[256,256]{1,0:T(8,128)S(1)} %fusion.23, f32[256,256]{1,0:T(8,128)S(1)} %all_gather.27), kind=kOutput, calls=%fused_computation.1 | convolution fusion | flops 201392128 | bytes 1048576 | tf_op jit(solution)/shard_map/dot_general | solution.py:31
  (2 shorter events, 0.1 us)
Async XLA Ops:
  0.6 39.9 %collective-permute-start.1 = (f32[256,256]{1,0:T(8,128)}, f32[256,256]{1,0:T(8,128)S(1)}, u32[]{:S(2)}, u32[]{:S(2)}) collective-permute-start(f32[256,256]{1,0:T(8,128)} %bitcast.45), channel_id=1, source_target_pairs={{1,49},{3,51},{5,53},{7,55},{9,57},{11,59},{13,61},{15,63},{17,65}... | collective-permute-start | bytes 786440 | tf_op jit(solution)/shard_map/ppermute | solution.py:27
  5.9 34.7 %collective-permute-start = (f32[256,256]{1,0:T(8,128)}, f32[256,256]{1,0:T(8,128)S(1)}, u32[]{:S(2)}, u32[]{:S(2)}) collective-permute-start(f32[256,256]{1,0:T(8,128)} %bitcast.46), channel_id=1, source_target_pairs={{0,16},{1,33},{2,18},{3,35},{4,20},{5,37},{6,22},{7,39},{8,24},{9,... | collective-permute-start | bytes 786440 | tf_op jit(solution)/shard_map/ppermute | solution.py:27
  11.9 28.0 %copy-start = (bf16[1,2,256,256]{3,2,1,0:T(8,128)(2,1)S(1)}, bf16[1,2,256,256]{3,2,1,0:T(8,128)(2,1)}, u32[]{:S(2)}) copy-start(bf16[1,2,256,256]{3,2,1,0:T(8,128)(2,1)} %param.5) | copy-start | bytes 786436
  11.9 33.2 %copy-start.2 = (f32[1,256,256]{2,1,0:T(8,128)S(1)}, f32[1,256,256]{2,1,0:T(8,128)}, u32[]{:S(2)}) copy-start(f32[1,256,256]{2,1,0:T(8,128)} %param.6) | copy-start | bytes 786436
  36.0 40.2 %all-to-all-start = ((bf16[16,16,1536]{2,1,0:T(8,128)(2,1)}), bf16[16,16,1536]{2,1,0:T(8,128)(2,1)S(1)}, u32[]{:S(2)}, u32[]{:S(2)}) async-start(bf16[16,16,1536]{2,1,0:T(8,128)(2,1)} %bitcast.47), calls=%async_computation | async-start | bytes 1572864 | tf_op jit(solution)/shard_map/all_to_all | solution.py:273
  40.6 13.6 %copy-start.3 = (f32[1,256,256]{2,1,0:T(8,128)S(1)}, f32[1,256,256]{2,1,0:T(8,128)}, u32[]{:S(2)}) copy-start(f32[1,256,256]{2,1,0:T(8,128)} %param.6) | copy-start | bytes 786436
  40.6 14.6 %collective-permute-start.3 = (bf16[256,256]{1,0:T(8,128)(2,1)S(1)}, bf16[256,256]{1,0:T(8,128)(2,1)S(1)}, u32[]{:S(2)}, u32[]{:S(2)}) collective-permute-start(bf16[256,256]{1,0:T(8,128)(2,1)S(1)} %get-tuple-element.31), channel_id=1, source_target_pairs={{0,16},{1,49},{2,18},{3,51},{4,20},{5,53},{6,22},{7,55},{8,24},{9,... | collective-permute-start | bytes 393224 | tf_op jit(solution)/shard_map/ppermute | solution.py:27
  44.5 10.0 %collective-permute-start.2 = (bf16[256,256]{1,0:T(8,128)(2,1)S(1)}, bf16[256,256]{1,0:T(8,128)(2,1)S(1)}, u32[]{:S(2)}, u32[]{:S(2)}) collective-permute-start(bf16[256,256]{1,0:T(8,128)(2,1)S(1)} %get-tuple-element.31), channel_id=1, source_target_pairs={{0,32},{2,34},{4,36},{6,38},{8,40},{10,42},{12,44},{14,46},{16,48}... | collective-permute-start | bytes 393224 | tf_op jit(solution)/shard_map/ppermute | solution.py:27
  50.9 12.0 %collective-permute-start.5 = (f32[256,128]{1,0:T(8,128)S(1)}, f32[256,128]{1,0:T(8,128)S(1)}, u32[]{:S(2)}, u32[]{:S(2)}) collective-permute-start(f32[256,128]{1,0:T(8,128)S(1)} %constant_dynamic-slice_fusion), channel_id=1, source_target_pairs={{0,64},{16,80},{32,96},{48,112},{64,128},{80,144},{96,160},{112,17... | collective-permute-start | bytes 393224 | tf_op jit(solution)/shard_map/ppermute | solution.py:16
  58.4 11.0 %collective-permute-start.4 = (bf16[256,256]{1,0:T(8,128)(2,1)S(1)}, bf16[256,256]{1,0:T(8,128)(2,1)S(1)}, u32[]{:S(2)}, u32[]{:S(2)}) collective-permute-start(bf16[256,256]{1,0:T(8,128)(2,1)S(1)} %fusion.14), channel_id=1, source_target_pairs={{0,64},{16,80},{32,96},{48,112},{64,128},{80,144},{96,160},{112,17... | collective-permute-start | bytes 393224 | tf_op jit(solution)/shard_map/ppermute | solution.py:16
  63.3 15.2 %collective-permute-start.7 = (f32[256,128]{1,0:T(8,128)S(1)}, f32[256,128]{1,0:T(8,128)S(1)}, u32[]{:S(2)}, u32[]{:S(2)}) collective-permute-start(f32[256,128]{1,0:T(8,128)S(1)} %fusion.19), channel_id=1, source_target_pairs={{0,128},{16,144},{32,160},{48,176},{64,192},{80,208},{96,224},{112... | collective-permute-start | bytes 393224 | tf_op jit(solution)/shard_map/ppermute | solution.py:16
  70.9 10.8 %collective-permute-start.6 = (bf16[256,256]{1,0:T(8,128)(2,1)S(1)}, bf16[256,256]{1,0:T(8,128)(2,1)S(1)}, u32[]{:S(2)}, u32[]{:S(2)}) collective-permute-start(bf16[256,256]{1,0:T(8,128)(2,1)S(1)} %get-tuple-element.52), channel_id=1, source_target_pairs={{0,128},{16,144},{32,160},{48,176},{64,192},{80,208},{96,224},{112... | collective-permute-start | bytes 393224 | tf_op jit(solution)/shard_map/ppermute | solution.py:16
  76.2 10.7 %collective-permute-start.9 = (bf16[256,1536]{1,0:T(8,128)(2,1)S(1)}, bf16[256,1536]{1,0:T(8,128)(2,1)S(1)}, u32[]{:S(2)}, u32[]{:S(2)}) collective-permute-start(bf16[256,1536]{1,0:T(8,128)(2,1)S(1)} %bitcast.36), channel_id=1, source_target_pairs={{0,1},{1,0},{2,3},{3,2},{4,5},{5,4},{6,7},{7,6},{8,9},{9,8},{10,11... | collective-permute-start | bytes 2359304 | tf_op jit(solution)/shard_map/ppermute | solution.py:314
  78.9 3.1 %copy-start.1 = (f32[256,256]{1,0:T(8,128)S(1)}, f32[256,256]{1,0:T(8,128)}, u32[]{:S(2)}) copy-start(f32[256,256]{1,0:T(8,128)} %get-tuple-element.53) | copy-start | bytes 786436
  82.4 7.3 %collective-permute-start.8 = (bf16[256,256]{1,0:T(8,128)(2,1)S(1)}, bf16[256,256]{1,0:T(8,128)(2,1)S(1)}, u32[]{:S(2)}, u32[]{:S(2)}) collective-permute-start(bf16[256,256]{1,0:T(8,128)(2,1)S(1)} %get-tuple-element.54), channel_id=1, source_target_pairs={{0,256},{16,272},{32,288},{48,304},{64,320},{80,336},{96,352},{112... | collective-permute-start | bytes 393224 | tf_op jit(solution)/shard_map/ppermute | solution.py:16

commit v13 on v12

--- a/solution.py
+++ b/solution.py
@@ -268,9 +268,8 @@
     back_near, back_far = (core_passed(span, by) for by in ((1, 2), (None, 3)))
 
     near_here, far_here = picked_rows(pivot_nodes, strip, w, per)
+    own = lax.all_to_all(far_here, "blk", 0, 0, tiled=True)
     near = lax.all_gather(near_here, "blk", axis=0, tiled=True)
-    near, far_here = lax.optimization_barrier((near, far_here))
-    own = lax.all_to_all(far_here, "blk", 0, 0, tiled=True)
     boundary, factor_at_two, second_edge, one_rows = boundary_of(near, inverses)
     back_near, back_far, boundary = lax.optimization_barrier((back_near, back_far, boundary))
 

time: 92.8 us -> 110 us (1.19)
  blocking collectives: 36.2 us -> 46.6 us
  starting transfers between devices: 34.7 us -> 41.1 us
    all_gather x1, blocking collectives: 24.1 us -> 34.4 us  [body(): near = lax.all_gather(near_here, 'blk', axis=0, tiled=True)]
    all_to_all x1, starting transfers between devices: 3.87 us -> 10.6 us  [body(): own = lax.all_to_all(far_here, 'blk', 0, 0, tiled=True)]
  transfers between devices with their start and end apart: 11 -> 11, of which waited for: 0 -> 0; matrix products, arithmetic and copies ran while one was open for 6% -> 5% of each run, Pallas kernels for 14% -> 11%
where the time goes in v13:
time: 110 us; the launch traced here: 108 us
  blocking collectives  46.6 us (42%)
  starting transfers between devices  41.1 us (37%)
  Pallas kernels  12.4 us (11%)
  matrix products  6.71 us (6%)
    all_gather x1, blocking collectives, body(): near = lax.all_gather(near_here, 'blk', axis=0, tiled=True)  34.4 us
    ppermute x5, starting transfers between devices, passed_along(): return lax.ppermute(x, axis, [(i, i + by) for i in range(count - by)])  15.1 us
    ppermute x4, starting transfers between devices, core_passed(): return lax.ppermute(x, ('tm', 'blk'), pairs)  13.1 us
    all_to_all x1, starting transfers between devices, body(): own = lax.all_to_all(far_here, 'blk', 0, 0, tiled=True)  10.6 us
    dot_general x15, matrix products, matmul_high(): jnp.dot(left, right, precision=lax.Precision.HIGHEST, preferred_element_t...  6.71 us
    pallas_call x2, Pallas kernels, trailing_far(): pl.pallas_call(lambda *refs: far_kernel(w, swap, *refs), out_shape=jax.Sh...  5.56 us
    all_gather x1, blocking collectives, body(): pair = lax.all_gather(pair, 'blk', axis_index_groups=core_pairs)  4.95 us
    all_gather x2, blocking collectives, joined(): lax.all_gather(half, 'blk', axis=1, tiled=True, axis_index_groups=core_pa...  4.79 us
  transfers between devices with their start and end apart: 11, of which 0 were waited for; matrix products, arithmetic and copies ran while one was open for 5% of the time, Pallas kernels for 11%

profile of v13, /device:TPU:1, one launch (start us, length us, event | category | flops | bytes accessed | tf_op | source)
XLA Modules:
  0.0 107.9 jit_solution(8189378281158865442)
XLA Ops:
  0.6 5.2 %collective-permute-start.1 = (f32[256,256]{1,0:T(8,128)}, f32[256,256]{1,0:T(8,128)S(1)}, u32[]{:S(2)}, u32[]{:S(2)}) collective-permute-start(f32[256,256]{1,0:T(8,128)} %bitcast.45), channel_id=1, source_target_pairs={{1,49},{3,51},{5,53},{7,55},{9,57},{11,59},{13,61},{15,63},{17,65}... | collective-permute-start | bytes 786440 | tf_op jit(solution)/shard_map/ppermute | solution.py:27
  5.9 3.5 %collective-permute-start = (f32[256,256]{1,0:T(8,128)}, f32[256,256]{1,0:T(8,128)S(1)}, u32[]{:S(2)}, u32[]{:S(2)}) collective-permute-start(f32[256,256]{1,0:T(8,128)} %bitcast.46), channel_id=1, source_target_pairs={{0,16},{1,33},{2,18},{3,35},{4,20},{5,37},{6,22},{7,39},{8,24},{9,... | collective-permute-start | bytes 786440 | tf_op jit(solution)/shard_map/ppermute | solution.py:27
  9.3 2.6 %pick.1 = (bf16[16,1792]{1,0:T(8,128)(2,1)S(1)}, bf16[256,1536]{1,0:T(8,128)(2,1)}) custom-call(s32[3,256]{1,0:T(4,128)} %refs_0_.1, bf16[512,2304]{1,0:T(8,128)(2,1)} %bitcast.40), custom_call_target="tpu_custom_call" | custom-call | flops 113246208 | bytes 2359296 | tf_op jit(solution)/shard_map/pick/pallas_call | solution.py:96
  12.0 0.0 copy-start
  12.0 0.0 copy-start.2
  12.0 10.6 %all-to-all-start = ((bf16[16,16,1536]{2,1,0:T(8,128)(2,1)}), bf16[16,16,1536]{2,1,0:T(8,128)(2,1)S(1)}, u32[]{:S(2)}, u32[]{:S(2)}) async-start(bf16[16,16,1536]{2,1,0:T(8,128)(2,1)} %bitcast.47), calls=%async_computation | async-start | bytes 1572864 | tf_op jit(solution)/shard_map/all_to_all | solution.py:271
  22.6 34.4 %all_gather.21.refs_0_ = bf16[256,1792]{1,0:T(8,128)(2,1)S(1)} all-gather(bf16[16,1792]{1,0:T(8,128)(2,1)S(1)} %get-tuple-element.25), channel_id=1, replica_groups=mesh['tm'=32,'blk'=16] {'blk'}, dimensions={0}, use_global_device_ids=true | all-gather | bytes 974848 | tf_op jit(solution)/shard_map/all_gather | solution.py:272
  57.0 0.0 copy-done
  57.0 0.7 boundary.1
  57.7 0.0 collective-permute-done.1
  57.7 0.0 collective-permute-done
  57.7 3.8 %collective-permute-start.3 = (bf16[256,256]{1,0:T(8,128)(2,1)S(1)}, bf16[256,256]{1,0:T(8,128)(2,1)S(1)}, u32[]{:S(2)}, u32[]{:S(2)}) collective-permute-start(bf16[256,256]{1,0:T(8,128)(2,1)S(1)} %get-tuple-element.27), channel_id=1, source_target_pairs={{0,16},{1,49},{2,18},{3,51},{4,20},{5,53},{6,22},{7,55},{8,24},{9,... | collective-permute-start | bytes 393224 | tf_op jit(solution)/shard_map/ppermute | solution.py:27
  61.4 0.7 collective-permute-start.2
  62.1 0.0 copy-done.2
  62.1 0.4 fusion.4
  62.5 4.9 %all-gather = f32[512,256]{1,0:T(8,128)S(1)} all-gather(f32[256,256]{1,0:T(8,128)S(1)} %fusion.4), channel_id=2, replica_groups={{0,1},{2,3},{4,5},{6,7},{8,9},{10,11},{12,13},{14,15},{16,17},{18,19},{..., dimensions={0}, use_global_device_ids=true | all-gather | bytes 786432 | tf_op jit(solution)/shard_map/all_gather | solution.py:291
  67.5 0.4 fusion.1
  67.9 3.2 %collective-permute-start.5 = (f32[256,128]{1,0:T(8,128)S(1)}, f32[256,128]{1,0:T(8,128)S(1)}, u32[]{:S(2)}, u32[]{:S(2)}) collective-permute-start(f32[256,128]{1,0:T(8,128)S(1)} %constant_dynamic-slice_fusion), channel_id=1, source_target_pairs={{0,64},{16,80},{32,96},{48,112},{64,128},{80,144},{96,160},{112,17... | collective-permute-start | bytes 393224 | tf_op jit(solution)/shard_map/ppermute | solution.py:16
  71.1 0.4 convolution_select_fusion
  71.5 0.0 collective-permute-done.2
  71.5 0.3 fusion.10
  71.8 0.4 fusion.8
  72.2 0.0 collective-permute-done.3
  72.2 0.3 fusion.18
  72.5 0.4 convolution_add_fusion.3
  72.9 2.5 %all-gather.1 = f32[512,256]{1,0:T(8,128)S(1)} all-gather(f32[256,256]{1,0:T(8,128)S(1)} %convolution_add_fusion.3), channel_id=3, replica_groups={{0,1},{2,3},{4,5},{6,7},{8,9},{10,11},{12,13},{14,15},{16,17},{18,19},{..., dimensions={0}, use_global_device_ids=true | all-gather | bytes 786432 | tf_op jit(solution)/shard_map/all_gather | solution.py:300
  75.4 4.4 %collective-permute-start.4 = (bf16[256,256]{1,0:T(8,128)(2,1)S(1)}, bf16[256,256]{1,0:T(8,128)(2,1)S(1)}, u32[]{:S(2)}, u32[]{:S(2)}) collective-permute-start(bf16[256,256]{1,0:T(8,128)(2,1)S(1)} %fusion.14), channel_id=1, source_target_pairs={{0,64},{16,80},{32,96},{48,112},{64,128},{80,144},{96,160},{112,17... | collective-permute-start | bytes 393224 | tf_op jit(solution)/shard_map/ppermute | solution.py:16
  79.8 0.0 collective-permute-done.5
  79.9 0.4 fusion.19
  80.2 2.4 %collective-permute-start.7 = (f32[256,128]{1,0:T(8,128)S(1)}, f32[256,128]{1,0:T(8,128)S(1)}, u32[]{:S(2)}, u32[]{:S(2)}) collective-permute-start(f32[256,128]{1,0:T(8,128)S(1)} %fusion.19), channel_id=1, source_target_pairs={{0,128},{16,144},{32,160},{48,176},{64,192},{80,208},{96,224},{112... | collective-permute-start | bytes 393224 | tf_op jit(solution)/shard_map/ppermute | solution.py:16
  82.7 3.6 %edge.1 = (bf16[512,1792]{1,0:T(8,128)(2,1)}, bf16[512,256]{1,0:T(8,128)(2,1)S(1)}, bf16[512,256]{1,0:T(8,128)(2,1)S(1)}) custom-call(bf16[512,2304]{1,0:T(8,128)(2,1)} %bitcast.41, bf16[2,256,256]{2,1,0:T(8,128)(2,1)} %bitcast.38, bf16[256,512]{1,0:T(8,128)(2,1)S(1)} %get-tuple-element.31.refs_2_, bf16[256,256]{1,0:T(8,128)(2,1)S(1)} %get-tuple-element.32.refs_3_), custom_call_target="tpu_custom_call" | custom-call | flops 256 | bytes 256 | tf_op jit(solution)/shard_map/edge/pallas_call | solution.py:212
  86.3 0.0 collective-permute-done.4
  86.3 0.3 fusion.20
  86.6 1.1 %fusion.16 = (bf16[256,256]{1,0:T(8,128)(2,1)S(1)}, f32[256,256]{1,0:T(8,128)}) fusion(f32[512,256]{1,0:T(8,128)S(1)} %all-gather.1, bf16[256,256]{1,0:T(8,128)(2,1)S(1)} %get-tuple-element.27, f32[256,256]{1,0:T(8,128)S(1)} %fusion.20, f32[256,256]{1,0:T(8,128)S(1)} %fusion.1), kind=kOutput, calls=%fused_computation.23 | convolution fusion | flops 201654272 | bytes 1572864 | tf_op jit(solution)/shard_map/dot_general | solution.py:31
  87.7 2.7 %collective-permute-start.6 = (bf16[256,256]{1,0:T(8,128)(2,1)S(1)}, bf16[256,256]{1,0:T(8,128)(2,1)S(1)}, u32[]{:S(2)}, u32[]{:S(2)}) collective-permute-start(bf16[256,256]{1,0:T(8,128)(2,1)S(1)} %get-tuple-element.48), channel_id=1, source_target_pairs={{0,128},{16,144},{32,160},{48,176},{64,192},{80,208},{96,224},{112... | collective-permute-start | bytes 393224 | tf_op jit(solution)/shard_map/ppermute | solution.py:16
  90.4 2.6 %all_gather.26 = f32[256,256]{1,0:T(8,128)S(1)} all-gather(f32[256,128]{1,0:T(8,128)S(1)} %fusion.19), channel_id=1, replica_groups={{0,1},{2,3},{4,5},{6,7},{8,9},{10,11},{12,13},{14,15},{16,17},{18,19},{..., dimensions={1}, use_global_device_ids=true | all-gather | bytes 393216 | tf_op jit(solution)/shard_map/all_gather | solution.py:282
  93.0 0.0 all-to-all-done
  93.0 2.3 %collective-permute-start.9 = (bf16[256,1536]{1,0:T(8,128)(2,1)S(1)}, bf16[256,1536]{1,0:T(8,128)(2,1)S(1)}, u32[]{:S(2)}, u32[]{:S(2)}) collective-permute-start(bf16[256,1536]{1,0:T(8,128)(2,1)S(1)} %bitcast.36), channel_id=1, source_target_pairs={{0,1},{1,0},{2,3},{3,2},{4,5},{5,4},{6,7},{7,6},{8,9},{9,8},{10,11... | collective-permute-start | bytes 2359304 | tf_op jit(solution)/shard_map/ppermute | solution.py:313
  95.2 0.0 collective-permute-done.7
  95.3 0.4 fusion.21
  95.6 0.0 copy-start.1
  95.7 2.8 %far.1.refs_1_ = bf16[512,1792]{1,0:T(8,128)(2,1)} custom-call(bf16[512,2304]{1,0:T(8,128)(2,1)} %bitcast.42, bf16[512,1792]{1,0:T(8,128)(2,1)} %get-tuple-element.37.refs_1_, bf16[256,1536]{1,0:T(8,128)(2,1)S(1)} %bitcast.37, bf16[512,256]{1,0:T(8,128)(2,1)S(1)} %get-tuple-element.40.refs_3_, ...), custom_call_target="tpu_custom_call", output_to_operand_aliasing={{}: (1, {})} | custom-call | flops 256 | bytes 256 | tf_op jit(solution)/shard_map/far/pallas_call | solution.py:238
  98.5 0.0 collective-permute-done.6
  98.5 0.3 fusion.22
  98.7 0.0 copy-done.1
  98.8 0.4 fusion.17
  99.2 2.3 %collective-permute-start.8 = (bf16[256,256]{1,0:T(8,128)(2,1)S(1)}, bf16[256,256]{1,0:T(8,128)(2,1)S(1)}, u32[]{:S(2)}, u32[]{:S(2)}) collective-permute-start(bf16[256,256]{1,0:T(8,128)(2,1)S(1)} %get-tuple-element.50), channel_id=1, source_target_pairs={{0,256},{16,272},{32,288},{48,304},{64,320},{80,336},{96,352},{112... | collective-permute-start | bytes 393224 | tf_op jit(solution)/shard_map/ppermute | solution.py:16
  101.5 2.2 %all_gather.27 = f32[256,256]{1,0:T(8,128)S(1)} all-gather(f32[256,128]{1,0:T(8,128)S(1)} %fusion.21), channel_id=1, replica_groups={{0,1},{2,3},{4,5},{6,7},{8,9},{10,11},{12,13},{14,15},{16,17},{18,19},{..., dimensions={1}, use_global_device_ids=true | all-gather | bytes 393216 | tf_op jit(solution)/shard_map/all_gather | solution.py:282
  103.7 0.0 collective-permute-done.9.refs_2_
  103.7 2.8 %far_swapped.1 = bf16[512,1792]{1,0:T(8,128)(2,1)} custom-call(bf16[512,2304]{1,0:T(8,128)(2,1)} %bitcast.43, bf16[512,1792]{1,0:T(8,128)(2,1)} %far.1.refs_1_, bf16[256,1536]{1,0:T(8,128)(2,1)S(1)} %collective-permute-done.9.refs_2_, bf16[512,256]{1,0:T(8,128)(2,1)S(1)} %get-tuple-element.40.refs_3_, ...), custom_call_target="tpu_custom_call", output_to_operand_aliasing={{}: (1, {})} | custom-call | flops 256 | bytes 256 | tf_op jit(solution)/shard_map/far_swapped/pallas_call | solution.py:238
  106.5 0.0 collective-permute-done.8
  106.5 0.3 fusion.23
  106.8 1.1 %fusion = f32[1,256,256]{2,1,0:T(8,128)} fusion(f32[256,256]{1,0:T(8,128)S(1)} %get-tuple-element.51, f32[256,256]{1,0:T(8,128)S(1)} %fusion.23, f32[256,256]{1,0:T(8,128)S(1)} %all_gather.27), kind=kOutput, calls=%fused_computation.1 | convolution fusion | flops 201392128 | bytes 1048576 | tf_op jit(solution)/shard_map/dot_general | solution.py:31
  (2 shorter events, 0.1 us)
Async XLA Ops:
  0.6 57.0 %collective-permute-start.1 = (f32[256,256]{1,0:T(8,128)}, f32[256,256]{1,0:T(8,128)S(1)}, u32[]{:S(2)}, u32[]{:S(2)}) collective-permute-start(f32[256,256]{1,0:T(8,128)} %bitcast.45), channel_id=1, source_target_pairs={{1,49},{3,51},{5,53},{7,55},{9,57},{11,59},{13,61},{15,63},{17,65}... | collective-permute-start | bytes 786440 | tf_op jit(solution)/shard_map/ppermute | solution.py:27
  5.9 51.8 %collective-permute-start = (f32[256,256]{1,0:T(8,128)}, f32[256,256]{1,0:T(8,128)S(1)}, u32[]{:S(2)}, u32[]{:S(2)}) collective-permute-start(f32[256,256]{1,0:T(8,128)} %bitcast.46), channel_id=1, source_target_pairs={{0,16},{1,33},{2,18},{3,35},{4,20},{5,37},{6,22},{7,39},{8,24},{9,... | collective-permute-start | bytes 786440 | tf_op jit(solution)/shard_map/ppermute | solution.py:27
  12.0 45.0 %copy-start = (bf16[1,2,256,256]{3,2,1,0:T(8,128)(2,1)S(1)}, bf16[1,2,256,256]{3,2,1,0:T(8,128)(2,1)}, u32[]{:S(2)}) copy-start(bf16[1,2,256,256]{3,2,1,0:T(8,128)(2,1)} %param.5) | copy-start | bytes 786436
  12.0 50.2 %copy-start.2 = (f32[1,256,256]{2,1,0:T(8,128)S(1)}, f32[1,256,256]{2,1,0:T(8,128)}, u32[]{:S(2)}) copy-start(f32[1,256,256]{2,1,0:T(8,128)} %param.6) | copy-start | bytes 786436
  12.0 81.0 %all-to-all-start = ((bf16[16,16,1536]{2,1,0:T(8,128)(2,1)}), bf16[16,16,1536]{2,1,0:T(8,128)(2,1)S(1)}, u32[]{:S(2)}, u32[]{:S(2)}) async-start(bf16[16,16,1536]{2,1,0:T(8,128)(2,1)} %bitcast.47), calls=%async_computation | async-start | bytes 1572864 | tf_op jit(solution)/shard_map/all_to_all | solution.py:271
  57.7 14.5 %collective-permute-start.3 = (bf16[256,256]{1,0:T(8,128)(2,1)S(1)}, bf16[256,256]{1,0:T(8,128)(2,1)S(1)}, u32[]{:S(2)}, u32[]{:S(2)}) collective-permute-start(bf16[256,256]{1,0:T(8,128)(2,1)S(1)} %get-tuple-element.27), channel_id=1, source_target_pairs={{0,16},{1,49},{2,18},{3,51},{4,20},{5,53},{6,22},{7,55},{8,24},{9,... | collective-permute-start | bytes 393224 | tf_op jit(solution)/shard_map/ppermute | solution.py:27
  61.4 10.1 %collective-permute-start.2 = (bf16[256,256]{1,0:T(8,128)(2,1)S(1)}, bf16[256,256]{1,0:T(8,128)(2,1)S(1)}, u32[]{:S(2)}, u32[]{:S(2)}) collective-permute-start(bf16[256,256]{1,0:T(8,128)(2,1)S(1)} %get-tuple-element.27), channel_id=1, source_target_pairs={{0,32},{2,34},{4,36},{6,38},{8,40},{10,42},{12,44},{14,46},{16,48}... | collective-permute-start | bytes 393224 | tf_op jit(solution)/shard_map/ppermute | solution.py:27
  67.9 12.0 %collective-permute-start.5 = (f32[256,128]{1,0:T(8,128)S(1)}, f32[256,128]{1,0:T(8,128)S(1)}, u32[]{:S(2)}, u32[]{:S(2)}) collective-permute-start(f32[256,128]{1,0:T(8,128)S(1)} %constant_dynamic-slice_fusion), channel_id=1, source_target_pairs={{0,64},{16,80},{32,96},{48,112},{64,128},{80,144},{96,160},{112,17... | collective-permute-start | bytes 393224 | tf_op jit(solution)/shard_map/ppermute | solution.py:16
  75.4 10.8 %collective-permute-start.4 = (bf16[256,256]{1,0:T(8,128)(2,1)S(1)}, bf16[256,256]{1,0:T(8,128)(2,1)S(1)}, u32[]{:S(2)}, u32[]{:S(2)}) collective-permute-start(bf16[256,256]{1,0:T(8,128)(2,1)S(1)} %fusion.14), channel_id=1, source_target_pairs={{0,64},{16,80},{32,96},{48,112},{64,128},{80,144},{96,160},{112,17... | collective-permute-start | bytes 393224 | tf_op jit(solution)/shard_map/ppermute | solution.py:16
  80.2 15.0 %collective-permute-start.7 = (f32[256,128]{1,0:T(8,128)S(1)}, f32[256,128]{1,0:T(8,128)S(1)}, u32[]{:S(2)}, u32[]{:S(2)}) collective-permute-start(f32[256,128]{1,0:T(8,128)S(1)} %fusion.19), channel_id=1, source_target_pairs={{0,128},{16,144},{32,160},{48,176},{64,192},{80,208},{96,224},{112... | collective-permute-start | bytes 393224 | tf_op jit(solution)/shard_map/ppermute | solution.py:16
  87.7 10.8 %collective-permute-start.6 = (bf16[256,256]{1,0:T(8,128)(2,1)S(1)}, bf16[256,256]{1,0:T(8,128)(2,1)S(1)}, u32[]{:S(2)}, u32[]{:S(2)}) collective-permute-start(bf16[256,256]{1,0:T(8,128)(2,1)S(1)} %get-tuple-element.48), channel_id=1, source_target_pairs={{0,128},{16,144},{32,160},{48,176},{64,192},{80,208},{96,224},{112... | collective-permute-start | bytes 393224 | tf_op jit(solution)/shard_map/ppermute | solution.py:16
  93.0 10.7 %collective-permute-start.9 = (bf16[256,1536]{1,0:T(8,128)(2,1)S(1)}, bf16[256,1536]{1,0:T(8,128)(2,1)S(1)}, u32[]{:S(2)}, u32[]{:S(2)}) collective-permute-start(bf16[256,1536]{1,0:T(8,128)(2,1)S(1)} %bitcast.36), channel_id=1, source_target_pairs={{0,1},{1,0},{2,3},{3,2},{4,5},{5,4},{6,7},{7,6},{8,9},{9,8},{10,11... | collective-permute-start | bytes 2359304 | tf_op jit(solution)/shard_map/ppermute | solution.py:313
  95.6 3.1 %copy-start.1 = (f32[256,256]{1,0:T(8,128)S(1)}, f32[256,256]{1,0:T(8,128)}, u32[]{:S(2)}) copy-start(f32[256,256]{1,0:T(8,128)} %get-tuple-element.49) | copy-start | bytes 786436
  99.2 7.3 %collective-permute-start.8 = (bf16[256,256]{1,0:T(8,128)(2,1)S(1)}, bf16[256,256]{1,0:T(8,128)(2,1)S(1)}, u32[]{:S(2)}, u32[]{:S(2)}) collective-permute-start(bf16[256,256]{1,0:T(8,128)(2,1)S(1)} %get-tuple-element.50), channel_id=1, source_target_pairs={{0,256},{16,272},{32,288},{48,304},{64,320},{80,336},{96,352},{112... | collective-permute-start | bytes 393224 | tf_op jit(solution)/shard_map/ppermute | solution.py:16
